TPU v7x, 256 devices: a whole 4x4x8 slice. The times are simulated.
256 devices in a mesh: dp: 16 (over x, y_hi, core), zero: 16 (over y_lo, z).
Axes of the slice: x: 4, y: 4 (y_hi: 2, y_lo: 2; y = y_hi * 2 + y_lo), z: 8, core: 2. Of those that a mesh axis runs over, the one named last changes fastest.
Arguments:
- picture_embeds: bfloat16 [32768, 1024], P(('dp', 'zero')), may hold values from -4 to 4
- matched_slot: int32 [32768], P(('dp', 'zero')), may hold values from 0 to 2047, as said below
- summary_token_states: bfloat16 [32768, 1024], P(('dp', 'zero')), may hold values from -10 to 10
- feedforward_inner_activations: bfloat16 [32768, 4096], P(('dp', 'zero')), may hold values from -24 to 24
- closing_layernorm_multiplier: float32 [1024], replicated, may hold values from 0.1 to 1.9
- contracting_matrix: bfloat16 [4096, 1024], P('zero'), may hold values from -0.09375 to 0.09375
- sharpness_factor: float32 [1], replicated, may hold values from 3 to 6
- additive_shift_learned: float32 [1], replicated, may hold values from -3 to -1
Outputs:
- image_grad: float32 [32768, 1024], P(('dp', 'zero'))
- hidden_grad: bfloat16 [32768, 4096], P(('dp', 'zero'))
- down_grad: float32 [4096, 1024], P('zero', 'dp')
Inputs may be any that keep to these rules, and one draw needn't show every extreme that they name: `matched_slot`: within the 2048 images of one zero index every position 0 to 2047 is named exactly once.
All inputs are finite; a program needn't handle non-finite values.
Results may differ from a plain program's by a relative error of at most 0.005.
Values may be sent and summed in bfloat16 or wider, within the bound.
A program may use at most 128 MiB of HBM per device.

v0:
```python
import jax
import jax.numpy as jnp
from jax import lax
from jax.sharding import PartitionSpec as P


def from_behind(block, axis, distance):
    devices = range(lax.axis_size(axis))
    route = [((i - distance) % len(devices), i) for i in devices]
    return lax.ppermute(block, axis, route)


def unit_rows(values):
    return values * lax.rsqrt(jnp.sum(values * values, axis=1, keepdims=True) + 1e-06)


def text_embed(features, closing_layernorm_multiplier):
    center = features - jnp.mean(features, axis=1, keepdims=True)
    spread = jnp.mean(center * center, axis=1, keepdims=True)
    return unit_rows(center * lax.rsqrt(spread + 1e-05) * closing_layernorm_multiplier)


def tile_weights(image_b, matched_slot, caption_b, start, similarity_multiplier, shift_value):
    scores = (
        similarity_multiplier
        * lax.dot_general(
            image_b, caption_b, (((1,), (1,)), ((), ())), preferred_element_type=jnp.float32
        )
        + shift_value
    )
    places = start + jnp.arange(caption_b.shape[0], dtype=jnp.int32)
    labels = jnp.where(matched_slot[:, None] == places[None, :], 1.0, -1.0).astype(jnp.float32)
    return (-labels * jax.nn.sigmoid(-labels * scores)).astype(jnp.bfloat16)


def pair_terms(image_b, matched_slot, caption_b, start, similarity_multiplier, shift_value):
    weights = tile_weights(
        image_b, matched_slot, caption_b, start, similarity_multiplier, shift_value
    )
    image_term = similarity_multiplier * jnp.dot(
        weights, caption_b, preferred_element_type=jnp.float32
    )
    caption_term = similarity_multiplier * lax.dot_general(
        weights, image_b, (((0,), (0,)), ((), ())), preferred_element_type=jnp.float32
    )
    return (image_term, caption_term)


def shards(
    picture_embeds,
    matched_slot,
    summary_token_states,
    feedforward_inner_activations,
    closing_layernorm_multiplier,
    contracting_matrix,
    sharpness_factor,
    additive_shift_learned,
):
    similarity_multiplier = sharpness_factor[0]
    shift_value = additive_shift_learned[0]
    unit_image, image_back = jax.vjp(unit_rows, picture_embeds.astype(jnp.float32))
    image_b = unit_image.astype(jnp.bfloat16)
    caption, caption_back = jax.vjp(
        lambda feats: text_embed(feats, closing_layernorm_multiplier),
        summary_token_states.astype(jnp.float32),
    )
    caption_b = caption.astype(jnp.bfloat16)
    local_rows = picture_embeds.shape[0]
    width = picture_embeds.shape[1]
    cycle_count = lax.axis_size("dp")
    cycle_place = lax.axis_index("dp")

    def pass_grads(gathered):
        return from_behind(gathered, "dp", 1)

    def turn(step, carry):
        image_total_sum, visiting_partner, gathered = carry
        source = (cycle_place - step) % cycle_count
        image_term, caption_term = pair_terms(
            image_b,
            matched_slot,
            visiting_partner,
            source * local_rows,
            similarity_multiplier,
            shift_value,
        )
        visiting_partner = from_behind(visiting_partner, "dp", 1)
        return (image_total_sum + image_term, visiting_partner, pass_grads(gathered + caption_term))

    start_state = (
        jnp.zeros((local_rows, width), jnp.float32),
        caption_b,
        jnp.zeros((local_rows, width), jnp.float32),
    )
    image_total_sum, visiting_partner, gathered = lax.fori_loop(
        0, cycle_count - 1, turn, start_state
    )
    source = (cycle_place - (cycle_count - 1)) % cycle_count
    image_term, caption_term = pair_terms(
        image_b,
        matched_slot,
        visiting_partner,
        source * local_rows,
        similarity_multiplier,
        shift_value,
    )
    image_total_sum = image_total_sum + image_term
    caption_text_gradient = pass_grads(gathered + caption_term)
    image_grad = image_back(image_total_sum)[0]
    upstream = caption_back(caption_text_gradient)[0].astype(jnp.bfloat16)
    hidden_grad = lax.dot_general(
        upstream,
        lax.all_gather(contracting_matrix, "zero", axis=0, tiled=True),
        (((1,), (1,)), ((), ())),
        preferred_element_type=jnp.float32,
    ).astype(jnp.bfloat16)
    zero_sum = lax.psum_scatter(
        lax.dot_general(
            feedforward_inner_activations,
            upstream,
            (((0,), (0,)), ((), ())),
            preferred_element_type=jnp.float32,
        ),
        "zero",
        scatter_dimension=0,
        tiled=True,
    )
    down_grad = lax.psum_scatter(zero_sum, "dp", scatter_dimension=1, tiled=True)
    return (image_grad, hidden_grad, down_grad)


def solution(mesh):
    placed = (
        P(("dp", "zero"), None),
        P(("dp", "zero")),
        P(("dp", "zero"), None),
        P(("dp", "zero"), None),
        P(),
        P("zero", None),
        P(),
        P(),
    )
    return jax.shard_map(
        shards,
        mesh=mesh,
        in_specs=placed,
        out_specs=(P(("dp", "zero"), None), P(("dp", "zero"), None), P("zero", "dp")),
        check_vma=False,
    )
```

profile of v0, /device:TPU:57, one launch (start us, length us, event | category | flops | bytes accessed | tf_op | source)
XLA Modules:
  0.0 679.4 jit_solution(6060138698852830259)
XLA Ops:
  14.6 253.1 %while.20 = (s32[]{:T(128)}, f32[128,1024]{1,0:T(8,128)S(1)}, bf16[128,1024]{1,0:T(8,128)(2,1)S(1)}, f32[128,1024]{1,0:T(8,128)S(1)}, f32[]{:T(128)}, /*index=5*...) while((s32[]{:T(128)}, f32[128,1024]{1,0:T(8,128)S(1)}, ...), condition=%wide.region_5.6_spmd.clone, body=%wide.region_4.5_spmd.clone.sunk | while | flops 101499024 | bytes 6915960 | solution.py:95
  14.6 2.2 fusion.69
  17.7 2.5 collective-permute-start.1
  21.3 7.9 %collective-permute-done = bf16[128,1024]{1,0:T(8,128)(2,1)S(1)} collective-permute-done((bf16[128,1024]{1,0:T(8,128)(2,1)S(1)}, bf16[128,1024]{1,0:T(8,128)(2,1)S(1)}, u32[]{:S(2)}, u32[]{:S(2)}) %collective-permute-start) | collective-permute-done | bytes 262176 | tf_op jit(solution)/shard_map/while/body/eval_jaxpr/ppermute | solution.py:10
  29.2 2.2 fusion.69
  32.3 5.0 collective-permute-start.1
  38.3 7.9 %collective-permute-done = bf16[128,1024]{1,0:T(8,128)(2,1)S(1)} collective-permute-done((bf16[128,1024]{1,0:T(8,128)(2,1)S(1)}, bf16[128,1024]{1,0:T(8,128)(2,1)S(1)}, u32[]{:S(2)}, u32[]{:S(2)}) %collective-permute-start) | collective-permute-done | bytes 262176 | tf_op jit(solution)/shard_map/while/body/eval_jaxpr/ppermute | solution.py:10
  46.3 2.2 fusion.69
  49.4 5.0 collective-permute-start.1
  55.3 7.9 %collective-permute-done = bf16[128,1024]{1,0:T(8,128)(2,1)S(1)} collective-permute-done((bf16[128,1024]{1,0:T(8,128)(2,1)S(1)}, bf16[128,1024]{1,0:T(8,128)(2,1)S(1)}, u32[]{:S(2)}, u32[]{:S(2)}) %collective-permute-start) | collective-permute-done | bytes 262176 | tf_op jit(solution)/shard_map/while/body/eval_jaxpr/ppermute | solution.py:10
  66.4 5.0 collective-permute-start.1
  72.4 7.9 %collective-permute-done = bf16[128,1024]{1,0:T(8,128)(2,1)S(1)} collective-permute-done((bf16[128,1024]{1,0:T(8,128)(2,1)S(1)}, bf16[128,1024]{1,0:T(8,128)(2,1)S(1)}, u32[]{:S(2)}, u32[]{:S(2)}) %collective-permute-start) | collective-permute-done | bytes 262176 | tf_op jit(solution)/shard_map/while/body/eval_jaxpr/ppermute | solution.py:10
  80.3 2.2 fusion.69
  83.4 5.0 collective-permute-start.1
  89.4 7.9 %collective-permute-done = bf16[128,1024]{1,0:T(8,128)(2,1)S(1)} collective-permute-done((bf16[128,1024]{1,0:T(8,128)(2,1)S(1)}, bf16[128,1024]{1,0:T(8,128)(2,1)S(1)}, u32[]{:S(2)}, u32[]{:S(2)}) %collective-permute-start) | collective-permute-done | bytes 262176 | tf_op jit(solution)/shard_map/while/body/eval_jaxpr/ppermute | solution.py:10
  97.4 2.2 fusion.69
  100.5 5.0 collective-permute-start.1
  106.5 7.9 %collective-permute-done = bf16[128,1024]{1,0:T(8,128)(2,1)S(1)} collective-permute-done((bf16[128,1024]{1,0:T(8,128)(2,1)S(1)}, bf16[128,1024]{1,0:T(8,128)(2,1)S(1)}, u32[]{:S(2)}, u32[]{:S(2)}) %collective-permute-start) | collective-permute-done | bytes 262176 | tf_op jit(solution)/shard_map/while/body/eval_jaxpr/ppermute | solution.py:10
  114.4 2.2 fusion.69
  117.5 5.0 collective-permute-start.1
  123.5 7.9 %collective-permute-done = bf16[128,1024]{1,0:T(8,128)(2,1)S(1)} collective-permute-done((bf16[128,1024]{1,0:T(8,128)(2,1)S(1)}, bf16[128,1024]{1,0:T(8,128)(2,1)S(1)}, u32[]{:S(2)}, u32[]{:S(2)}) %collective-permute-start) | collective-permute-done | bytes 262176 | tf_op jit(solution)/shard_map/while/body/eval_jaxpr/ppermute | solution.py:10
  134.6 5.0 collective-permute-start.1
  140.5 7.9 %collective-permute-done = bf16[128,1024]{1,0:T(8,128)(2,1)S(1)} collective-permute-done((bf16[128,1024]{1,0:T(8,128)(2,1)S(1)}, bf16[128,1024]{1,0:T(8,128)(2,1)S(1)}, u32[]{:S(2)}, u32[]{:S(2)}) %collective-permute-start) | collective-permute-done | bytes 262176 | tf_op jit(solution)/shard_map/while/body/eval_jaxpr/ppermute | solution.py:10
  148.5 2.2 fusion.69
  151.6 5.0 collective-permute-start.1
  157.6 7.9 %collective-permute-done = bf16[128,1024]{1,0:T(8,128)(2,1)S(1)} collective-permute-done((bf16[128,1024]{1,0:T(8,128)(2,1)S(1)}, bf16[128,1024]{1,0:T(8,128)(2,1)S(1)}, u32[]{:S(2)}, u32[]{:S(2)}) %collective-permute-start) | collective-permute-done | bytes 262176 | tf_op jit(solution)/shard_map/while/body/eval_jaxpr/ppermute | solution.py:10
  168.6 5.0 collective-permute-start.1
  174.6 7.9 %collective-permute-done = bf16[128,1024]{1,0:T(8,128)(2,1)S(1)} collective-permute-done((bf16[128,1024]{1,0:T(8,128)(2,1)S(1)}, bf16[128,1024]{1,0:T(8,128)(2,1)S(1)}, u32[]{:S(2)}, u32[]{:S(2)}) %collective-permute-start) | collective-permute-done | bytes 262176 | tf_op jit(solution)/shard_map/while/body/eval_jaxpr/ppermute | solution.py:10
  182.6 2.2 fusion.69
  185.7 5.0 collective-permute-start.1
  191.6 7.9 %collective-permute-done = bf16[128,1024]{1,0:T(8,128)(2,1)S(1)} collective-permute-done((bf16[128,1024]{1,0:T(8,128)(2,1)S(1)}, bf16[128,1024]{1,0:T(8,128)(2,1)S(1)}, u32[]{:S(2)}, u32[]{:S(2)}) %collective-permute-start) | collective-permute-done | bytes 262176 | tf_op jit(solution)/shard_map/while/body/eval_jaxpr/ppermute | solution.py:10
  202.7 5.0 collective-permute-start.1
  208.7 7.9 %collective-permute-done = bf16[128,1024]{1,0:T(8,128)(2,1)S(1)} collective-permute-done((bf16[128,1024]{1,0:T(8,128)(2,1)S(1)}, bf16[128,1024]{1,0:T(8,128)(2,1)S(1)}, u32[]{:S(2)}, u32[]{:S(2)}) %collective-permute-start) | collective-permute-done | bytes 262176 | tf_op jit(solution)/shard_map/while/body/eval_jaxpr/ppermute | solution.py:10
  216.6 2.2 fusion.69
  219.7 5.0 collective-permute-start.1
  225.7 7.9 %collective-permute-done = bf16[128,1024]{1,0:T(8,128)(2,1)S(1)} collective-permute-done((bf16[128,1024]{1,0:T(8,128)(2,1)S(1)}, bf16[128,1024]{1,0:T(8,128)(2,1)S(1)}, u32[]{:S(2)}, u32[]{:S(2)}) %collective-permute-start) | collective-permute-done | bytes 262176 | tf_op jit(solution)/shard_map/while/body/eval_jaxpr/ppermute | solution.py:10
  236.8 5.0 collective-permute-start.1
  242.7 7.9 %collective-permute-done = bf16[128,1024]{1,0:T(8,128)(2,1)S(1)} collective-permute-done((bf16[128,1024]{1,0:T(8,128)(2,1)S(1)}, bf16[128,1024]{1,0:T(8,128)(2,1)S(1)}, u32[]{:S(2)}, u32[]{:S(2)}) %collective-permute-start) | collective-permute-done | bytes 262176 | tf_op jit(solution)/shard_map/while/body/eval_jaxpr/ppermute | solution.py:10
  250.7 2.2 fusion.69
  253.8 5.0 collective-permute-start.1
  259.8 7.9 %collective-permute-done = bf16[128,1024]{1,0:T(8,128)(2,1)S(1)} collective-permute-done((bf16[128,1024]{1,0:T(8,128)(2,1)S(1)}, bf16[128,1024]{1,0:T(8,128)(2,1)S(1)}, u32[]{:S(2)}, u32[]{:S(2)}) %collective-permute-start) | collective-permute-done | bytes 262176 | tf_op jit(solution)/shard_map/while/body/eval_jaxpr/ppermute | solution.py:10
  268.9 5.0 collective-permute-start.2
  273.8 6.1 collective-permute-done.2
  283.9 8.2 %convolution_bitcast_fusion = f32[4096,1024]{0,1:T(8,128)} fusion(bf16[128,4096]{1,0:T(8,128)(2,1)S(1)} %copy-done, f32[128,1024]{1,0:T(8,128)S(1)} %get-tuple-element.278, f32[128]{0:T(128)S(1)} %negate_multiply_fusion), kind=kOutput, calls=%fused_computation.14 | convolution fusion | flops 1074003968 | bytes 18350592 | tf_op jit(solution)/shard_map/dot_general | solution.py:118
  292.9 202.5 %reduce-scatter.3.cloned.1.call-done = f32[256,1024]{0,1:T(8,128)} async-done(((f32[4096,1024]{0,1:T(8,128)}), f32[256,1024]{0,1:T(8,128)}) %reduce-scatter.3.cloned.1.call-update) | async-done | bytes 1048592 | tf_op jit(solution)/shard_map/reduce_scatter | solution.py:117
  496.7 99.2 %all-gather.2.cloned.1.call-done = bf16[4096,1024]{1,0:T(8,128)(2,1)} async-done(((bf16[256,1024]{1,0:T(8,128)(2,1)}), bf16[4096,1024]{1,0:T(8,128)(2,1)}) %all-gather.2.cloned.1.call-update) | async-done | bytes 8388624 | tf_op jit(solution)/shard_map/all_gather | solution.py:113
  595.9 7.2 %convolution_convert_fusion = bf16[128,4096]{1,0:T(8,128)(2,1)} fusion(bf16[4096,1024]{1,0:T(8,128)(2,1)} %all-gather.2.cloned.1.call-done, f32[128,1024]{1,0:T(8,128)S(1)} %get-tuple-element.278, f32[128]{0:T(128)S(1)} %negate_multiply_fusion), kind=kOutput, calls=%fused_computation.15 | convolution fusion | flops 1074528256 | bytes 9961984 | tf_op jit(solution)/shard_map/dot_general | solution.py:111
  603.2 69.8 %reduce-scatter.5.cloned.1.call-done = f32[256,64]{0,1:T(8,128)} async-done(((f32[256,1024]{0,1:T(8,128)}), f32[256,64]{0,1:T(8,128)}) %reduce-scatter.5.cloned.1.call-update) | async-done | bytes 65552 | tf_op jit(solution)/shard_map/reduce_scatter | solution.py:128
  (130 shorter events, 52.9 us)
Async XLA Ops:
  7.2 276.7 %copy-start = (bf16[128,4096]{1,0:T(8,128)(2,1)S(1)}, bf16[128,4096]{1,0:T(8,128)(2,1)}, u32[]{:S(2)}) copy-start(bf16[128,4096]{1,0:T(8,128)(2,1)} %param.13) | copy-start | bytes 3145732
  7.2 488.2 %reduce-scatter.3.cloned.1.call-start = ((), (), s32[]{:S(2)}) async-start(), calls=%async_computation.3 | async-start | bytes 17825792 | tf_op jit(solution)/shard_map/reduce_scatter | solution.py:117
  14.6 265.4 %copy-start.2 = (f32[1024]{0:T(1024)S(1)}, f32[1024]{0:T(1024)}, u32[]{:S(2)}) copy-start(f32[1024]{0:T(1024)} %param.14) | copy-start | bytes 12292
  17.7 11.5 %collective-permute-start.1 = (f32[128,1024]{1,0:T(8,128)S(1)}, f32[128,1024]{1,0:T(8,128)S(1)}, u32[]{:S(2)}, u32[]{:S(2)}) collective-permute-start(f32[128,1024]{1,0:T(8,128)S(1)} %fusion.71), channel_id=1, source_target_pairs={{240,0},{0,16},{16,32},{32,48},{48,64},{64,80},{80,96},{96,112},{1... | collective-permute-start | bytes 1572872 | tf_op jit(solution)/shard_map/while/body/eval_jaxpr/ppermute | solution.py:10
  20.3 8.9 %collective-permute-start = (bf16[128,1024]{1,0:T(8,128)(2,1)S(1)}, bf16[128,1024]{1,0:T(8,128)(2,1)S(1)}, u32[]{:S(2)}, u32[]{:S(2)}) collective-permute-start(bf16[128,1024]{1,0:T(8,128)(2,1)S(1)} %copy.17), channel_id=1, source_target_pairs={{240,0},{0,16},{16,32},{32,48},{48,64},{64,80},{80,96},{96,112},{1... | collective-permute-start | bytes 786440 | tf_op jit(solution)/shard_map/while/body/eval_jaxpr/ppermute | solution.py:10
  32.3 13.9 %collective-permute-start.1 = (f32[128,1024]{1,0:T(8,128)S(1)}, f32[128,1024]{1,0:T(8,128)S(1)}, u32[]{:S(2)}, u32[]{:S(2)}) collective-permute-start(f32[128,1024]{1,0:T(8,128)S(1)} %fusion.71), channel_id=1, source_target_pairs={{240,0},{0,16},{16,32},{32,48},{48,64},{64,80},{80,96},{96,112},{1... | collective-permute-start | bytes 1572872 | tf_op jit(solution)/shard_map/while/body/eval_jaxpr/ppermute | solution.py:10
  37.3 8.9 %collective-permute-start = (bf16[128,1024]{1,0:T(8,128)(2,1)S(1)}, bf16[128,1024]{1,0:T(8,128)(2,1)S(1)}, u32[]{:S(2)}, u32[]{:S(2)}) collective-permute-start(bf16[128,1024]{1,0:T(8,128)(2,1)S(1)} %copy.17), channel_id=1, source_target_pairs={{240,0},{0,16},{16,32},{32,48},{48,64},{64,80},{80,96},{96,112},{1... | collective-permute-start | bytes 786440 | tf_op jit(solution)/shard_map/while/body/eval_jaxpr/ppermute | solution.py:10
  49.4 13.9 %collective-permute-start.1 = (f32[128,1024]{1,0:T(8,128)S(1)}, f32[128,1024]{1,0:T(8,128)S(1)}, u32[]{:S(2)}, u32[]{:S(2)}) collective-permute-start(f32[128,1024]{1,0:T(8,128)S(1)} %fusion.71), channel_id=1, source_target_pairs={{240,0},{0,16},{16,32},{32,48},{48,64},{64,80},{80,96},{96,112},{1... | collective-permute-start | bytes 1572872 | tf_op jit(solution)/shard_map/while/body/eval_jaxpr/ppermute | solution.py:10
  54.3 8.9 %collective-permute-start = (bf16[128,1024]{1,0:T(8,128)(2,1)S(1)}, bf16[128,1024]{1,0:T(8,128)(2,1)S(1)}, u32[]{:S(2)}, u32[]{:S(2)}) collective-permute-start(bf16[128,1024]{1,0:T(8,128)(2,1)S(1)} %copy.17), channel_id=1, source_target_pairs={{240,0},{0,16},{16,32},{32,48},{48,64},{64,80},{80,96},{96,112},{1... | collective-permute-start | bytes 786440 | tf_op jit(solution)/shard_map/while/body/eval_jaxpr/ppermute | solution.py:10
  66.4 13.9 %collective-permute-start.1 = (f32[128,1024]{1,0:T(8,128)S(1)}, f32[128,1024]{1,0:T(8,128)S(1)}, u32[]{:S(2)}, u32[]{:S(2)}) collective-permute-start(f32[128,1024]{1,0:T(8,128)S(1)} %fusion.71), channel_id=1, source_target_pairs={{240,0},{0,16},{16,32},{32,48},{48,64},{64,80},{80,96},{96,112},{1... | collective-permute-start | bytes 1572872 | tf_op jit(solution)/shard_map/while/body/eval_jaxpr/ppermute | solution.py:10
  71.4 8.9 %collective-permute-start = (bf16[128,1024]{1,0:T(8,128)(2,1)S(1)}, bf16[128,1024]{1,0:T(8,128)(2,1)S(1)}, u32[]{:S(2)}, u32[]{:S(2)}) collective-permute-start(bf16[128,1024]{1,0:T(8,128)(2,1)S(1)} %copy.17), channel_id=1, source_target_pairs={{240,0},{0,16},{16,32},{32,48},{48,64},{64,80},{80,96},{96,112},{1... | collective-permute-start | bytes 786440 | tf_op jit(solution)/shard_map/while/body/eval_jaxpr/ppermute | solution.py:10
  83.4 13.9 %collective-permute-start.1 = (f32[128,1024]{1,0:T(8,128)S(1)}, f32[128,1024]{1,0:T(8,128)S(1)}, u32[]{:S(2)}, u32[]{:S(2)}) collective-permute-start(f32[128,1024]{1,0:T(8,128)S(1)} %fusion.71), channel_id=1, source_target_pairs={{240,0},{0,16},{16,32},{32,48},{48,64},{64,80},{80,96},{96,112},{1... | collective-permute-start | bytes 1572872 | tf_op jit(solution)/shard_map/while/body/eval_jaxpr/ppermute | solution.py:10
  88.4 8.9 %collective-permute-start = (bf16[128,1024]{1,0:T(8,128)(2,1)S(1)}, bf16[128,1024]{1,0:T(8,128)(2,1)S(1)}, u32[]{:S(2)}, u32[]{:S(2)}) collective-permute-start(bf16[128,1024]{1,0:T(8,128)(2,1)S(1)} %copy.17), channel_id=1, source_target_pairs={{240,0},{0,16},{16,32},{32,48},{48,64},{64,80},{80,96},{96,112},{1... | collective-permute-start | bytes 786440 | tf_op jit(solution)/shard_map/while/body/eval_jaxpr/ppermute | solution.py:10
  100.5 13.9 %collective-permute-start.1 = (f32[128,1024]{1,0:T(8,128)S(1)}, f32[128,1024]{1,0:T(8,128)S(1)}, u32[]{:S(2)}, u32[]{:S(2)}) collective-permute-start(f32[128,1024]{1,0:T(8,128)S(1)} %fusion.71), channel_id=1, source_target_pairs={{240,0},{0,16},{16,32},{32,48},{48,64},{64,80},{80,96},{96,112},{1... | collective-permute-start | bytes 1572872 | tf_op jit(solution)/shard_map/while/body/eval_jaxpr/ppermute | solution.py:10
  105.4 8.9 %collective-permute-start = (bf16[128,1024]{1,0:T(8,128)(2,1)S(1)}, bf16[128,1024]{1,0:T(8,128)(2,1)S(1)}, u32[]{:S(2)}, u32[]{:S(2)}) collective-permute-start(bf16[128,1024]{1,0:T(8,128)(2,1)S(1)} %copy.17), channel_id=1, source_target_pairs={{240,0},{0,16},{16,32},{32,48},{48,64},{64,80},{80,96},{96,112},{1... | collective-permute-start | bytes 786440 | tf_op jit(solution)/shard_map/while/body/eval_jaxpr/ppermute | solution.py:10
  117.5 13.9 %collective-permute-start.1 = (f32[128,1024]{1,0:T(8,128)S(1)}, f32[128,1024]{1,0:T(8,128)S(1)}, u32[]{:S(2)}, u32[]{:S(2)}) collective-permute-start(f32[128,1024]{1,0:T(8,128)S(1)} %fusion.71), channel_id=1, source_target_pairs={{240,0},{0,16},{16,32},{32,48},{48,64},{64,80},{80,96},{96,112},{1... | collective-permute-start | bytes 1572872 | tf_op jit(solution)/shard_map/while/body/eval_jaxpr/ppermute | solution.py:10
  122.5 8.9 %collective-permute-start = (bf16[128,1024]{1,0:T(8,128)(2,1)S(1)}, bf16[128,1024]{1,0:T(8,128)(2,1)S(1)}, u32[]{:S(2)}, u32[]{:S(2)}) collective-permute-start(bf16[128,1024]{1,0:T(8,128)(2,1)S(1)} %copy.17), channel_id=1, source_target_pairs={{240,0},{0,16},{16,32},{32,48},{48,64},{64,80},{80,96},{96,112},{1... | collective-permute-start | bytes 786440 | tf_op jit(solution)/shard_map/while/body/eval_jaxpr/ppermute | solution.py:10
  134.6 13.9 %collective-permute-start.1 = (f32[128,1024]{1,0:T(8,128)S(1)}, f32[128,1024]{1,0:T(8,128)S(1)}, u32[]{:S(2)}, u32[]{:S(2)}) collective-permute-start(f32[128,1024]{1,0:T(8,128)S(1)} %fusion.71), channel_id=1, source_target_pairs={{240,0},{0,16},{16,32},{32,48},{48,64},{64,80},{80,96},{96,112},{1... | collective-permute-start | bytes 1572872 | tf_op jit(solution)/shard_map/while/body/eval_jaxpr/ppermute | solution.py:10
  139.5 8.9 %collective-permute-start = (bf16[128,1024]{1,0:T(8,128)(2,1)S(1)}, bf16[128,1024]{1,0:T(8,128)(2,1)S(1)}, u32[]{:S(2)}, u32[]{:S(2)}) collective-permute-start(bf16[128,1024]{1,0:T(8,128)(2,1)S(1)} %copy.17), channel_id=1, source_target_pairs={{240,0},{0,16},{16,32},{32,48},{48,64},{64,80},{80,96},{96,112},{1... | collective-permute-start | bytes 786440 | tf_op jit(solution)/shard_map/while/body/eval_jaxpr/ppermute | solution.py:10
  151.6 13.9 %collective-permute-start.1 = (f32[128,1024]{1,0:T(8,128)S(1)}, f32[128,1024]{1,0:T(8,128)S(1)}, u32[]{:S(2)}, u32[]{:S(2)}) collective-permute-start(f32[128,1024]{1,0:T(8,128)S(1)} %fusion.71), channel_id=1, source_target_pairs={{240,0},{0,16},{16,32},{32,48},{48,64},{64,80},{80,96},{96,112},{1... | collective-permute-start | bytes 1572872 | tf_op jit(solution)/shard_map/while/body/eval_jaxpr/ppermute | solution.py:10
  156.6 8.9 %collective-permute-start = (bf16[128,1024]{1,0:T(8,128)(2,1)S(1)}, bf16[128,1024]{1,0:T(8,128)(2,1)S(1)}, u32[]{:S(2)}, u32[]{:S(2)}) collective-permute-start(bf16[128,1024]{1,0:T(8,128)(2,1)S(1)} %copy.17), channel_id=1, source_target_pairs={{240,0},{0,16},{16,32},{32,48},{48,64},{64,80},{80,96},{96,112},{1... | collective-permute-start | bytes 786440 | tf_op jit(solution)/shard_map/while/body/eval_jaxpr/ppermute | solution.py:10
  168.6 13.9 %collective-permute-start.1 = (f32[128,1024]{1,0:T(8,128)S(1)}, f32[128,1024]{1,0:T(8,128)S(1)}, u32[]{:S(2)}, u32[]{:S(2)}) collective-permute-start(f32[128,1024]{1,0:T(8,128)S(1)} %fusion.71), channel_id=1, source_target_pairs={{240,0},{0,16},{16,32},{32,48},{48,64},{64,80},{80,96},{96,112},{1... | collective-permute-start | bytes 1572872 | tf_op jit(solution)/shard_map/while/body/eval_jaxpr/ppermute | solution.py:10
  173.6 8.9 %collective-permute-start = (bf16[128,1024]{1,0:T(8,128)(2,1)S(1)}, bf16[128,1024]{1,0:T(8,128)(2,1)S(1)}, u32[]{:S(2)}, u32[]{:S(2)}) collective-permute-start(bf16[128,1024]{1,0:T(8,128)(2,1)S(1)} %copy.17), channel_id=1, source_target_pairs={{240,0},{0,16},{16,32},{32,48},{48,64},{64,80},{80,96},{96,112},{1... | collective-permute-start | bytes 786440 | tf_op jit(solution)/shard_map/while/body/eval_jaxpr/ppermute | solution.py:10
  185.7 13.9 %collective-permute-start.1 = (f32[128,1024]{1,0:T(8,128)S(1)}, f32[128,1024]{1,0:T(8,128)S(1)}, u32[]{:S(2)}, u32[]{:S(2)}) collective-permute-start(f32[128,1024]{1,0:T(8,128)S(1)} %fusion.71), channel_id=1, source_target_pairs={{240,0},{0,16},{16,32},{32,48},{48,64},{64,80},{80,96},{96,112},{1... | collective-permute-start | bytes 1572872 | tf_op jit(solution)/shard_map/while/body/eval_jaxpr/ppermute | solution.py:10
  190.6 8.9 %collective-permute-start = (bf16[128,1024]{1,0:T(8,128)(2,1)S(1)}, bf16[128,1024]{1,0:T(8,128)(2,1)S(1)}, u32[]{:S(2)}, u32[]{:S(2)}) collective-permute-start(bf16[128,1024]{1,0:T(8,128)(2,1)S(1)} %copy.17), channel_id=1, source_target_pairs={{240,0},{0,16},{16,32},{32,48},{48,64},{64,80},{80,96},{96,112},{1... | collective-permute-start | bytes 786440 | tf_op jit(solution)/shard_map/while/body/eval_jaxpr/ppermute | solution.py:10
  202.7 13.9 %collective-permute-start.1 = (f32[128,1024]{1,0:T(8,128)S(1)}, f32[128,1024]{1,0:T(8,128)S(1)}, u32[]{:S(2)}, u32[]{:S(2)}) collective-permute-start(f32[128,1024]{1,0:T(8,128)S(1)} %fusion.71), channel_id=1, source_target_pairs={{240,0},{0,16},{16,32},{32,48},{48,64},{64,80},{80,96},{96,112},{1... | collective-permute-start | bytes 1572872 | tf_op jit(solution)/shard_map/while/body/eval_jaxpr/ppermute | solution.py:10
  207.7 8.9 %collective-permute-start = (bf16[128,1024]{1,0:T(8,128)(2,1)S(1)}, bf16[128,1024]{1,0:T(8,128)(2,1)S(1)}, u32[]{:S(2)}, u32[]{:S(2)}) collective-permute-start(bf16[128,1024]{1,0:T(8,128)(2,1)S(1)} %copy.17), channel_id=1, source_target_pairs={{240,0},{0,16},{16,32},{32,48},{48,64},{64,80},{80,96},{96,112},{1... | collective-permute-start | bytes 786440 | tf_op jit(solution)/shard_map/while/body/eval_jaxpr/ppermute | solution.py:10
  219.7 13.9 %collective-permute-start.1 = (f32[128,1024]{1,0:T(8,128)S(1)}, f32[128,1024]{1,0:T(8,128)S(1)}, u32[]{:S(2)}, u32[]{:S(2)}) collective-permute-start(f32[128,1024]{1,0:T(8,128)S(1)} %fusion.71), channel_id=1, source_target_pairs={{240,0},{0,16},{16,32},{32,48},{48,64},{64,80},{80,96},{96,112},{1... | collective-permute-start | bytes 1572872 | tf_op jit(solution)/shard_map/while/body/eval_jaxpr/ppermute | solution.py:10
  224.7 8.9 %collective-permute-start = (bf16[128,1024]{1,0:T(8,128)(2,1)S(1)}, bf16[128,1024]{1,0:T(8,128)(2,1)S(1)}, u32[]{:S(2)}, u32[]{:S(2)}) collective-permute-start(bf16[128,1024]{1,0:T(8,128)(2,1)S(1)} %copy.17), channel_id=1, source_target_pairs={{240,0},{0,16},{16,32},{32,48},{48,64},{64,80},{80,96},{96,112},{1... | collective-permute-start | bytes 786440 | tf_op jit(solution)/shard_map/while/body/eval_jaxpr/ppermute | solution.py:10
  236.8 13.9 %collective-permute-start.1 = (f32[128,1024]{1,0:T(8,128)S(1)}, f32[128,1024]{1,0:T(8,128)S(1)}, u32[]{:S(2)}, u32[]{:S(2)}) collective-permute-start(f32[128,1024]{1,0:T(8,128)S(1)} %fusion.71), channel_id=1, source_target_pairs={{240,0},{0,16},{16,32},{32,48},{48,64},{64,80},{80,96},{96,112},{1... | collective-permute-start | bytes 1572872 | tf_op jit(solution)/shard_map/while/body/eval_jaxpr/ppermute | solution.py:10
  241.7 8.9 %collective-permute-start = (bf16[128,1024]{1,0:T(8,128)(2,1)S(1)}, bf16[128,1024]{1,0:T(8,128)(2,1)S(1)}, u32[]{:S(2)}, u32[]{:S(2)}) collective-permute-start(bf16[128,1024]{1,0:T(8,128)(2,1)S(1)} %copy.17), channel_id=1, source_target_pairs={{240,0},{0,16},{16,32},{32,48},{48,64},{64,80},{80,96},{96,112},{1... | collective-permute-start | bytes 786440 | tf_op jit(solution)/shard_map/while/body/eval_jaxpr/ppermute | solution.py:10
  253.8 13.9 %collective-permute-start.1 = (f32[128,1024]{1,0:T(8,128)S(1)}, f32[128,1024]{1,0:T(8,128)S(1)}, u32[]{:S(2)}, u32[]{:S(2)}) collective-permute-start(f32[128,1024]{1,0:T(8,128)S(1)} %fusion.71), channel_id=1, source_target_pairs={{240,0},{0,16},{16,32},{32,48},{48,64},{64,80},{80,96},{96,112},{1... | collective-permute-start | bytes 1572872 | tf_op jit(solution)/shard_map/while/body/eval_jaxpr/ppermute | solution.py:10
  258.8 8.9 %collective-permute-start = (bf16[128,1024]{1,0:T(8,128)(2,1)S(1)}, bf16[128,1024]{1,0:T(8,128)(2,1)S(1)}, u32[]{:S(2)}, u32[]{:S(2)}) collective-permute-start(bf16[128,1024]{1,0:T(8,128)(2,1)S(1)} %copy.17), channel_id=1, source_target_pairs={{240,0},{0,16},{16,32},{32,48},{48,64},{64,80},{80,96},{96,112},{1... | collective-permute-start | bytes 786440 | tf_op jit(solution)/shard_map/while/body/eval_jaxpr/ppermute | solution.py:10
  268.9 11.1 %collective-permute-start.2 = (f32[128,1024]{1,0:T(8,128)S(1)}, f32[128,1024]{1,0:T(8,128)S(1)}, u32[]{:S(2)}, u32[]{:S(2)}) collective-permute-start(f32[128,1024]{1,0:T(8,128)S(1)} %fusion.11), channel_id=1, source_target_pairs={{240,0},{0,16},{16,32},{32,48},{48,64},{64,80},{80,96},{96,112},{1... | collective-permute-start | bytes 1572872 | tf_op jit(solution)/shard_map/ppermute | solution.py:10
  292.1 203.4 %copy-start.1 = (bf16[128,1024]{1,0:T(8,128)(2,1)S(1)}, bf16[128,1024]{1,0:T(8,128)(2,1)}, u32[]{:S(2)}) copy-start(bf16[128,1024]{1,0:T(8,128)(2,1)} %param.10) | copy-start | bytes 786436
  292.1 303.8 %all-gather.2.cloned.1.call-start = ((), (), s32[]{:S(2)}) async-start(), calls=%async_computation.2 | async-start | bytes 8912896 | tf_op jit(solution)/shard_map/all_gather | solution.py:113
  292.8 380.1 %reduce-scatter.5.cloned.1.call-start = ((), (), s32[]{:S(2)}) async-start(), calls=%async_computation.4 | async-start | bytes 1114112 | tf_op jit(solution)/shard_map/reduce_scatter | solution.py:128
Sparse Core Ops, SparseCore 0:
  292.2 203.1 reduce-scatter.2
  497.2 98.6 all-gather.1
  600.6 72.2 reduce-scatter.4
where the time goes:
time: 683 us; the launch traced here: 679 us
  waiting for transfers between devices  497 us (73%)
  starting transfers between devices  78.5 us (11%)
  matrix products  76.9 us (11%)
  between operations  15.2 us (2%)
  other arithmetic  10.8 us (2%)
    reduce_scatter x1, waiting for transfers between devices, shards(): lax.psum_scatter(lax.dot_general(feedforward_inner_activations, upstream,...  203 us
    ppermute x31, waiting for transfers between devices, from_behind(): return lax.ppermute(block, axis, route)  125 us
    all_gather x1, waiting for transfers between devices, shards(): lax.all_gather(contracting_matrix, 'zero', axis=0, tiled=True)  99.2 us
    ppermute x31, starting transfers between devices, from_behind(): return lax.ppermute(block, axis, route)  78.4 us
    reduce_scatter x1, waiting for transfers between devices, shards(): lax.psum_scatter(zero_sum, 'dp', scatter_dimension=1, tiled=True)  69.8 us
    dot_general x16, matrix products, tile_weights(): lax.dot_general(image_b, caption_b, (((1,), (1,)), ((), ())), preferred_e...  33.9 us
    dot_general x16, matrix products, pair_terms(): jnp.dot(weights, caption_b, preferred_element_type=jnp.float32)  13.9 us
  transfers between devices with their start and end apart: 34, of which 19 were waited for; matrix products, arithmetic and copies ran while one was open for 3% of the time, Pallas kernels for 0%

commit v1 on v0

v1 whole, which is shorter than its diff:
```python
import jax
import jax.numpy as jnp
from jax import lax
from jax.sharding import PartitionSpec as P


def unit_rows(values):
    return values * lax.rsqrt(jnp.sum(values * values, axis=1, keepdims=True) + 1e-06)


def text_embed(features, closing_layernorm_multiplier):
    center = features - jnp.mean(features, axis=1, keepdims=True)
    spread = jnp.mean(center * center, axis=1, keepdims=True)
    return unit_rows(center * lax.rsqrt(spread + 1e-05) * closing_layernorm_multiplier)


def sigmoid_weights(scores, labels):
    return (-labels * jax.nn.sigmoid(-labels * scores)).astype(jnp.bfloat16)


def shards(
    picture_embeds,
    matched_slot,
    summary_token_states,
    feedforward_inner_activations,
    closing_layernorm_multiplier,
    contracting_matrix,
    sharpness_factor,
    additive_shift_learned,
):
    similarity_multiplier = sharpness_factor[0]
    shift_value = additive_shift_learned[0]
    local_rows, width = picture_embeds.shape
    own_start = lax.axis_index("dp") * local_rows

    ffa_cols = lax.all_to_all(
        feedforward_inner_activations, "zero", split_axis=1, concat_axis=0, tiled=True
    )

    both = jnp.concatenate([picture_embeds, summary_token_states], axis=1)
    both_g = lax.all_gather(both, "dp", axis=0, tiled=True)
    slot_g = lax.all_gather(matched_slot, "dp", axis=0, tiled=True)
    image_b_g = unit_rows(both_g[:, :width].astype(jnp.float32)).astype(jnp.bfloat16)
    caption_b_g = text_embed(
        both_g[:, width:].astype(jnp.float32), closing_layernorm_multiplier
    ).astype(jnp.bfloat16)

    unit_image, image_back = jax.vjp(unit_rows, picture_embeds.astype(jnp.float32))
    image_b = unit_image.astype(jnp.bfloat16)
    caption, caption_back = jax.vjp(
        lambda feats: text_embed(feats, closing_layernorm_multiplier),
        summary_token_states.astype(jnp.float32),
    )
    caption_b = caption.astype(jnp.bfloat16)
    group_rows = caption_b_g.shape[0]

    scores_i = (
        similarity_multiplier
        * lax.dot_general(
            image_b, caption_b_g, (((1,), (1,)), ((), ())), preferred_element_type=jnp.float32
        )
        + shift_value
    )
    places = jnp.arange(group_rows, dtype=jnp.int32)
    labels_i = jnp.where(matched_slot[:, None] == places[None, :], 1.0, -1.0)
    weights_i = sigmoid_weights(scores_i, labels_i)
    image_term = similarity_multiplier * jnp.dot(
        weights_i, caption_b_g, preferred_element_type=jnp.float32
    )

    scores_c = (
        similarity_multiplier
        * lax.dot_general(
            image_b_g, caption_b, (((1,), (1,)), ((), ())), preferred_element_type=jnp.float32
        )
        + shift_value
    )
    own_places = own_start + jnp.arange(local_rows, dtype=jnp.int32)
    labels_c = jnp.where(slot_g[:, None] == own_places[None, :], 1.0, -1.0)
    weights_c = sigmoid_weights(scores_c, labels_c)
    caption_term = similarity_multiplier * lax.dot_general(
        weights_c, image_b_g, (((0,), (0,)), ((), ())), preferred_element_type=jnp.float32
    )

    image_grad = image_back(image_term)[0]
    upstream = caption_back(caption_term)[0].astype(jnp.bfloat16)

    upstream_g = lax.all_gather(upstream, "zero", axis=0, tiled=True)
    hidden_part = lax.dot_general(
        upstream_g,
        contracting_matrix,
        (((1,), (1,)), ((), ())),
        preferred_element_type=jnp.float32,
    ).astype(jnp.bfloat16)
    hidden_grad = lax.all_to_all(hidden_part, "zero", split_axis=0, concat_axis=1, tiled=True)
    zero_sum = lax.dot_general(
        ffa_cols, upstream_g, (((0,), (0,)), ((), ())), preferred_element_type=jnp.float32
    )
    down_grad = lax.psum_scatter(zero_sum, "dp", scatter_dimension=1, tiled=True)
    return (image_grad, hidden_grad, down_grad)


def solution(mesh):
    placed = (
        P(("dp", "zero"), None),
        P(("dp", "zero")),
        P(("dp", "zero"), None),
        P(("dp", "zero"), None),
        P(),
        P("zero", None),
        P(),
        P(),
    )
    return jax.shard_map(
        shards,
        mesh=mesh,
        in_specs=placed,
        out_specs=(P(("dp", "zero"), None), P(("dp", "zero"), None), P("zero", "dp")),
        check_vma=False,
    )
```

time: 683 us -> 295 us (0.43)
  waiting for transfers between devices: 497 us -> 196 us
  starting transfers between devices: 78.5 us -> 13.7 us
  matrix products: 76.9 us -> 23.3 us
  blocking collectives: 0 us -> 20.7 us
  other arithmetic: 10.8 us -> 19.1 us
    reduce_scatter x1 -> x0, waiting for transfers between devices: 203 us -> none  [shards(): lax.psum_scatter(lax.dot_general(feedforward_inner_activations, upstream,...]
    ppermute x31 -> x0, waiting for transfers between devices: 125 us -> none  [from_behind(): return lax.ppermute(block, axis, route)]
    ppermute x31 -> x0, starting transfers between devices: 78.4 us -> none  [from_behind(): return lax.ppermute(block, axis, route)]
    dot_general x50 -> x4, matrix products: 76.9 us -> 23.3 us  [the longest x1 7.87 us: shards(): jnp.dot(weights_i, caption_b_g, preferred_element_type=jnp.float32)]
    all_to_all x0 -> x2, waiting for transfers between devices: none -> 36.2 us  [the longest x1 31.6 us: shards(): lax.all_to_all(feedforward_inner_activations, 'zero', split_axis=1, conca...]
    all_gather x0 -> x1, blocking collectives: none -> 20.7 us  [shards(): slot_g = lax.all_gather(matched_slot, 'dp', axis=0, tiled=True)]
    all_to_all x0 -> x2, starting transfers between devices: none -> 13.4 us  [the longest x1 7.84 us: shards(): lax.all_to_all(feedforward_inner_activations, 'zero', split_axis=1, conca...]
    reduce_sum x2 -> x4, other arithmetic: 2.3 us -> 9.52 us  [unit_rows(): jnp.sum(values * values, axis=1, keepdims=True) + 1e-06]
  transfers between devices with their start and end apart: 34 -> 5, of which waited for: 19 -> 5; matrix products, arithmetic and copies ran while one was open for 3% -> 8% of each run, Pallas kernels for 0% -> 0%
where the time goes in v1:
time: 295 us; the launch traced here: 291 us
  waiting for transfers between devices  196 us (66%)
  matrix products  23.3 us (8%)
  blocking collectives  20.7 us (7%)
  other arithmetic  19.1 us (6%)
  between operations  15.2 us (5%)
  starting transfers between devices  13.7 us (5%)
  local copies, waits for them, and re-layouts  2.95 us (1%)
    reduce_scatter x1, waiting for transfers between devices, shards(): lax.psum_scatter(zero_sum, 'dp', scatter_dimension=1, tiled=True)  65.1 us
    all_gather x1, waiting for transfers between devices, shards(): both_g = lax.all_gather(both, 'dp', axis=0, tiled=True)  55.6 us
    all_gather x1, waiting for transfers between devices, shards(): upstream_g = lax.all_gather(upstream, 'zero', axis=0, tiled=True)  39.3 us
    all_to_all x1, waiting for transfers between devices, shards(): lax.all_to_all(feedforward_inner_activations, 'zero', split_axis=1, conca...  31.6 us
    all_gather x1, blocking collectives, shards(): slot_g = lax.all_gather(matched_slot, 'dp', axis=0, tiled=True)  20.7 us
    reduce_sum x4, other arithmetic, unit_rows(): jnp.sum(values * values, axis=1, keepdims=True) + 1e-06  9.52 us
    dot_general x1, matrix products, shards(): jnp.dot(weights_i, caption_b_g, preferred_element_type=jnp.float32)  7.87 us
    all_to_all x1, starting transfers between devices, shards(): lax.all_to_all(feedforward_inner_activations, 'zero', split_axis=1, conca...  7.84 us
  transfers between devices with their start and end apart: 5, of which 5 were waited for; matrix products, arithmetic and copies ran while one was open for 8% of the time, Pallas kernels for 0%

profile of v1, /device:TPU:57, one launch (start us, length us, event | category | flops | bytes accessed | tf_op | source)
XLA Modules:
  0.0 291.3 jit_solution(3951360067263233612)
XLA Ops:
  7.2 0.0 copy-start
  7.2 0.0 copy-start.1
  7.2 0.0 copy-start.4
  7.2 0.0 all-gather.4.cloned.1.call-start
  7.2 1.9 pad_maximum_fusion
  9.2 0.0 all-gather.4.cloned.1.call-update
  9.2 0.0 all-gather.6.cloned.1.call-start
  10.5 20.7 %all-gather = s32[16,1,128]{2,1,0:T(1,128)S(1)} all-gather(s32[1,1,128]{2,1,0:T(1,128)} %bitcast.26), channel_id=1, replica_groups=mesh['dp'=16,'zero'=16] {'dp'}, dimensions={0}, use_global_device_ids=true | all-gather | bytes 8704 | tf_op jit(solution)/shard_map/all_gather | solution.py:42
  31.3 1.1 convert_reduce_fusion.1
  32.4 1.2 fusion.39
  33.6 1.2 fusion.45
  34.8 55.6 %all-gather.4.cloned.1.call-done = bf16[2048,2048]{1,0:T(8,128)(2,1)} async-done(((bf16[128,2048]{1,0:T(8,128)(2,1)}), bf16[2048,2048]{1,0:T(8,128)(2,1)}) %all-gather.4.cloned.1.call-update) | async-done | bytes 8388624 | tf_op jit(solution)/shard_map/all_gather | solution.py:41
  90.3 2.8 convert_reduce_fusion
  93.1 4.6 %fusion.8 = (f32[2048]{0:T(1024)S(1)}, f32[2048]{0:T(1024)S(1)}) fusion(bf16[2048,2048]{1,0:T(8,128)(2,1)} %all-gather.4.cloned.1.call-done, f32[2048]{0:T(1024)S(1)} %broadcast_multiply_fusion), kind=kLoop, calls=%fused_computation.12 | loop fusion | flops 14675968 | bytes 8413184 | tf_op jit(solution)/shard_map/reduce_sum | solution.py:8
  97.7 0.0 copy-done.1
  97.7 0.0 copy-done.4
  97.8 0.0 copy-start.3
  97.8 0.0 copy-start.2
  97.8 6.5 %fusion.47 = (f32[128]{0:T(128)S(1)}, f32[128,1024]{1,0:T(8,128)S(1)}) fusion(bf16[128,1024]{1,0:T(8,128)(2,1)S(1)} %copy-done.1, f32[1024]{0:T(1024)S(1)} %copy-done.4, f32[128]{0:T(128)S(1)} %fusion.78, f32[128]{0:T(128)S(1)} %broadcast_multiply_fusion.1, f32[2048]{0:T(1024)S(1)} %add_rsqrt_fusion, bf16[2048,2048]{1,0:T(8,128)(2,1)} %all-gather.4.cloned.1.call-done, ...), kind=kOutput, calls=%fused_computation.61 | convolution fusion | flops 1090912128 | bytes 9475072 | tf_op jit(solution)/shard_map/dot_general | solution.py:81
  104.3 0.3 fusion.48
  104.6 0.4 fusion.83
  105.1 0.8 add_convert_fusion
  105.9 0.0 all-gather.6.cloned.1.call-update
  105.9 0.0 copy-done.3
  105.9 1.3 copy.17
  107.2 7.8 %all-to-all-start.1 = ((bf16[128,16,256]{0,2,1:T(8,128)(2,1)}), bf16[128,16,256]{0,2,1:T(8,128)(2,1)S(1)}, u32[]{:S(2)}, u32[]{:S(2)}) async-start(bf16[128,16,256]{0,2,1:T(8,128)(2,1)} %bitcast.6), calls=%async_computation.1 | async-start | bytes 2097152 | tf_op jit(solution)/shard_map/all_to_all | solution.py:36
  115.1 0.0 copy-done.2
  115.1 0.1 fusion.50
  115.2 31.6 %all-to-all-done.1 = bf16[128,16,256]{0,2,1:T(8,128)(2,1)S(1)} async-done(((bf16[128,16,256]{0,2,1:T(8,128)(2,1)}), bf16[128,16,256]{0,2,1:T(8,128)(2,1)S(1)}, u32[]{:S(2)}, u32[]{:S(2)}) %all-to-all-start.1) | async-done | bytes 1048608 | tf_op jit(solution)/shard_map/all_to_all | solution.py:36
  146.8 0.5 copy.18
  147.3 3.6 %fusion.6 = f32[2048]{0:T(1024)S(1)} fusion(f32[1024]{0:T(1024)S(1)} %copy-done.4, f32[2048]{0:T(1024)S(1)} %add_rsqrt_fusion.2, f32[2048]{0:T(1024)S(1)} %broadcast_multiply_fusion, bf16[2048,2048]{1,0:T(8,128)(2,1)} %all-gather.4.cloned.1.call-done), kind=kLoop, calls=%fused_computation.10 | loop fusion | flops 12580864 | bytes 4222976 | tf_op jit(solution)/shard_map/reduce_sum | solution.py:8
  151.0 0.0 copy-start.5
  151.0 39.3 %all-gather.6.cloned.1.call-done = bf16[2048,1024]{1,0:T(8,128)(2,1)} async-done(((bf16[128,1024]{1,0:T(8,128)(2,1)}), bf16[2048,1024]{1,0:T(8,128)(2,1)}) %all-gather.6.cloned.1.call-update) | async-done | bytes 4194320 | tf_op jit(solution)/shard_map/all_gather | solution.py:88
  190.3 0.0 copy-done
  190.3 4.5 %convolution_convert_fusion = bf16[2048,256]{1,0:T(8,128)(2,1)} fusion(bf16[2048,1024]{1,0:T(8,128)(2,1)} %all-gather.6.cloned.1.call-done, bf16[256,1024]{1,0:T(8,128)(2,1)S(1)} %copy-done), kind=kOutput, calls=%fused_computation.14 | convolution fusion | flops 1074266112 | bytes 5767168 | tf_op jit(solution)/shard_map/dot_general | solution.py:89
  194.7 5.6 %all-to-all-start = ((bf16[16,128,256]{2,1,0:T(8,128)(2,1)}), bf16[16,128,256]{2,1,0:T(8,128)(2,1)S(1)}, u32[]{:S(2)}, u32[]{:S(2)}) async-start(bf16[16,128,256]{2,1,0:T(8,128)(2,1)} %bitcast.4), calls=%async_computation | async-start | bytes 2097152 | tf_op jit(solution)/shard_map/all_to_all | solution.py:95
  200.3 0.2 reduce-scatter.2.cloned.1.call-start
  200.5 4.5 %convolution_bitcast_fusion = f32[256,1024]{0,1:T(8,128)} fusion(bf16[2048,1024]{1,0:T(8,128)(2,1)} %all-gather.6.cloned.1.call-done, bf16[2048,256]{1,0:T(8,128)(2,1)S(1)} %bitcast.23), kind=kOutput, calls=%fused_computation.33 | convolution fusion | flops 1073741824 | bytes 6291456 | tf_op jit(solution)/shard_map/dot_general | solution.py:96
  205.1 0.0 reduce-scatter.2.cloned.1.call-update
  205.1 0.0 copy-done.5
  205.1 7.9 %fusion.52 = (f32[128]{0:T(128)S(1)}, f32[128,1024]{1,0:T(8,128)S(1)}) fusion(bf16[128,1024]{1,0:T(8,128)(2,1)S(1)} %copy-done.2, f32[2048]{0:T(1024)S(1)} %add_rsqrt_fusion.1, f32[1024]{0:T(1024)S(1)} %copy-done.4, f32[2048]{0:T(1024)S(1)} %add_rsqrt_fusion.2, f32[2048]{0:T(1024)S(1)} %broadcast_multiply_fusion, ...), kind=kOutput, calls=%fused_computation.66 | convolution fusion | flops 1102708608 | bytes 9497600 | tf_op jit(solution)/shard_map/dot_general | solution.py:67
  213.0 1.0 add_add_fusion.2
  213.9 4.6 %all-to-all-done = bf16[16,128,256]{2,1,0:T(8,128)(2,1)S(1)} async-done(((bf16[16,128,256]{2,1,0:T(8,128)(2,1)}), bf16[16,128,256]{2,1,0:T(8,128)(2,1)S(1)}, u32[]{:S(2)}, u32[]{:S(2)}) %all-to-all-start) | async-done | bytes 1048608 | tf_op jit(solution)/shard_map/all_to_all | solution.py:95
  218.6 1.1 copy.19
  219.6 65.1 %reduce-scatter.2.cloned.1.call-done = f32[256,64]{0,1:T(8,128)} async-done(((f32[256,1024]{0,1:T(8,128)}), f32[256,64]{0,1:T(8,128)}) %reduce-scatter.2.cloned.1.call-update) | async-done | bytes 65552 | tf_op jit(solution)/shard_map/reduce_scatter | solution.py:99
  (13 shorter events, 0.1 us)
Async XLA Ops:
  7.2 183.1 %copy-start = (bf16[256,1024]{1,0:T(8,128)(2,1)S(1)}, bf16[256,1024]{1,0:T(8,128)(2,1)}, u32[]{:S(2)}) copy-start(bf16[256,1024]{1,0:T(8,128)(2,1)} %param.13) | copy-start | bytes 1572868
  7.2 90.6 %copy-start.1 = (bf16[128,1024]{1,0:T(8,128)(2,1)S(1)}, bf16[128,1024]{1,0:T(8,128)(2,1)}, u32[]{:S(2)}) copy-start(bf16[128,1024]{1,0:T(8,128)(2,1)} %param.10) | copy-start | bytes 786436
  7.2 90.6 %copy-start.4 = (f32[1024]{0:T(1024)S(1)}, f32[1024]{0:T(1024)}, u32[]{:S(2)}) copy-start(f32[1024]{0:T(1024)} %param.12) | copy-start | bytes 12292
  7.2 83.1 %all-gather.4.cloned.1.call-start = ((), (), s32[]{:S(2)}) async-start(), calls=%async_computation.3 | async-start | bytes 8912896 | tf_op jit(solution)/shard_map/all_gather | solution.py:41
  9.2 181.1 %all-gather.6.cloned.1.call-start = ((), (), s32[]{:S(2)}) async-start(), calls=%async_computation.4 | async-start | bytes 4456448 | tf_op jit(solution)/shard_map/all_gather | solution.py:88
  97.8 8.2 %copy-start.3 = (bf16[128,4096]{1,0:T(8,128)(2,1)S(1)}, bf16[128,4096]{1,0:T(8,128)(2,1)}, u32[]{:S(2)}) copy-start(bf16[128,4096]{1,0:T(8,128)(2,1)} %param.11) | copy-start | bytes 3145732
  97.8 17.3 %copy-start.2 = (bf16[128,1024]{1,0:T(8,128)(2,1)S(1)}, bf16[128,1024]{1,0:T(8,128)(2,1)}, u32[]{:S(2)}) copy-start(bf16[128,1024]{1,0:T(8,128)(2,1)} %param.8) | copy-start | bytes 786436
  107.2 39.6 %all-to-all-start.1 = ((bf16[128,16,256]{0,2,1:T(8,128)(2,1)}), bf16[128,16,256]{0,2,1:T(8,128)(2,1)S(1)}, u32[]{:S(2)}, u32[]{:S(2)}) async-start(bf16[128,16,256]{0,2,1:T(8,128)(2,1)} %bitcast.6), calls=%async_computation.1 | async-start | bytes 2097152 | tf_op jit(solution)/shard_map/all_to_all | solution.py:36
  151.0 54.1 %copy-start.5 = (s32[128]{0:T(128)S(1)}, s32[128]{0:T(128)}, u32[]{:S(2)}) copy-start(s32[128]{0:T(128)} %param.9) | copy-start | bytes 1540
  194.7 23.8 %all-to-all-start = ((bf16[16,128,256]{2,1,0:T(8,128)(2,1)}), bf16[16,128,256]{2,1,0:T(8,128)(2,1)S(1)}, u32[]{:S(2)}, u32[]{:S(2)}) async-start(bf16[16,128,256]{2,1,0:T(8,128)(2,1)} %bitcast.4), calls=%async_computation | async-start | bytes 2097152 | tf_op jit(solution)/shard_map/all_to_all | solution.py:95
  200.3 84.4 %reduce-scatter.2.cloned.1.call-start = ((), (), s32[]{:S(2)}) async-start(), calls=%async_computation.5 | async-start | bytes 1114112 | tf_op jit(solution)/shard_map/reduce_scatter | solution.py:99
Sparse Core Ops, SparseCore 0:
  11.3 78.9 all-gather.3
  106.0 84.2 all-gather.5
  205.8 78.8 reduce-scatter.1

commit v2 on v1

--- a/solution.py
+++ b/solution.py
@@ -37,12 +37,18 @@
         feedforward_inner_activations, "zero", split_axis=1, concat_axis=0, tiled=True
     )
 
-    both = jnp.concatenate([picture_embeds, summary_token_states], axis=1)
+    digits = jnp.zeros((local_rows, 128), jnp.bfloat16)
+    digits = digits.at[:, 0].set((matched_slot // 256).astype(jnp.bfloat16))
+    digits = digits.at[:, 1].set((matched_slot % 256).astype(jnp.bfloat16))
+    both = jnp.concatenate([picture_embeds, summary_token_states, digits], axis=1)
     both_g = lax.all_gather(both, "dp", axis=0, tiled=True)
-    slot_g = lax.all_gather(matched_slot, "dp", axis=0, tiled=True)
+    ffa_cols, both_g = lax.optimization_barrier((ffa_cols, both_g))
+    slot_g = both_g[:, 2 * width].astype(jnp.int32) * 256 + both_g[:, 2 * width + 1].astype(
+        jnp.int32
+    )
     image_b_g = unit_rows(both_g[:, :width].astype(jnp.float32)).astype(jnp.bfloat16)
     caption_b_g = text_embed(
-        both_g[:, width:].astype(jnp.float32), closing_layernorm_multiplier
+        both_g[:, width : 2 * width].astype(jnp.float32), closing_layernorm_multiplier
     ).astype(jnp.bfloat16)
 
     unit_image, image_back = jax.vjp(unit_rows, picture_embeds.astype(jnp.float32))
@@ -85,7 +91,15 @@
     image_grad = image_back(image_term)[0]
     upstream = caption_back(caption_term)[0].astype(jnp.bfloat16)
 
-    upstream_g = lax.all_gather(upstream, "zero", axis=0, tiled=True)
+    zero_size = lax.axis_size("zero")
+    upstream_rep = jnp.broadcast_to(upstream[None], (zero_size,) + upstream.shape)
+    upstream_g = lax.all_to_all(
+        upstream_rep.reshape((zero_size * local_rows, width)),
+        "zero",
+        split_axis=0,
+        concat_axis=0,
+        tiled=True,
+    )
     hidden_part = lax.dot_general(
         upstream_g,
         contracting_matrix,
@@ -96,7 +110,9 @@
     zero_sum = lax.dot_general(
         ffa_cols, upstream_g, (((0,), (0,)), ((), ())), preferred_element_type=jnp.float32
     )
-    down_grad = lax.psum_scatter(zero_sum, "dp", scatter_dimension=1, tiled=True)
+    dp_size = lax.axis_size("dp")
+    down_parts = lax.all_to_all(zero_sum, "dp", split_axis=1, concat_axis=0, tiled=True)
+    down_grad = jnp.sum(down_parts.reshape((dp_size,) + (zero_sum.shape[0], -1)), axis=0)
     return (image_grad, hidden_grad, down_grad)
 
 

time: 295 us -> 300 us (1.017)
  waiting for transfers between devices: 196 us -> 95.9 us
  blocking collectives: 20.7 us -> 101 us
  local copies, waits for them, and re-layouts: 2.95 us -> 18 us
  starting transfers between devices: 13.7 us -> 20.9 us
    all_to_all x0 -> x1, blocking collectives: none -> 101 us  [shards(): lax.all_to_all(upstream_rep.reshape((zero_size * local_rows, width)), 'ze...]
    reduce_scatter x1 -> x0, waiting for transfers between devices: 65.1 us -> none  [shards(): lax.psum_scatter(zero_sum, 'dp', scatter_dimension=1, tiled=True)]
    all_gather x1 -> x0, waiting for transfers between devices: 39.3 us -> none  [shards(): upstream_g = lax.all_gather(upstream, 'zero', axis=0, tiled=True)]
    all_gather x1 -> x0, blocking collectives: 20.7 us -> none  [shards(): slot_g = lax.all_gather(matched_slot, 'dp', axis=0, tiled=True)]
    all_to_all x0 -> x1, waiting for transfers between devices: none -> 10.7 us  [shards(): lax.all_to_all(zero_sum, 'dp', split_axis=1, concat_axis=0, tiled=True)]
    all_to_all x1, waiting for transfers between devices: 31.6 us -> 21 us  [shards(): lax.all_to_all(feedforward_inner_activations, 'zero', split_axis=1, conca...]
    all_to_all x1, waiting for transfers between devices: 4.62 us -> 14.5 us  [shards(): lax.all_to_all(hidden_part, 'zero', split_axis=0, concat_axis=1, tiled=True)]
    all_to_all x0 -> x1, starting transfers between devices: none -> 7.55 us  [shards(): lax.all_to_all(zero_sum, 'dp', split_axis=1, concat_axis=0, tiled=True)]
  transfers between devices with their start and end apart: 5 -> 4, of which waited for: 5 -> 4; matrix products, arithmetic and copies ran while one was open for 8% -> 6% of each run, Pallas kernels for 0% -> 0%
where the time goes in v2:
time: 300 us; the launch traced here: 295 us
  blocking collectives  101 us (34%)
  waiting for transfers between devices  95.9 us (32%)
  matrix products  23.3 us (8%)
  starting transfers between devices  20.9 us (7%)
  other arithmetic  20.7 us (7%)
  local copies, waits for them, and re-layouts  18 us (6%)
  between operations  15.5 us (5%)
    all_to_all x1, blocking collectives, shards(): lax.all_to_all(upstream_rep.reshape((zero_size * local_rows, width)), 'ze...  101 us
    all_gather x1, waiting for transfers between devices, shards(): both_g = lax.all_gather(both, 'dp', axis=0, tiled=True)  49.7 us
    all_to_all x1, waiting for transfers between devices, shards(): lax.all_to_all(feedforward_inner_activations, 'zero', split_axis=1, conca...  21 us
    all_to_all x1, waiting for transfers between devices, shards(): lax.all_to_all(hidden_part, 'zero', split_axis=0, concat_axis=1, tiled=True)  14.5 us
    all_to_all x1, waiting for transfers between devices, shards(): lax.all_to_all(zero_sum, 'dp', split_axis=1, concat_axis=0, tiled=True)  10.7 us
    all_to_all x1, starting transfers between devices, shards(): lax.all_to_all(feedforward_inner_activations, 'zero', split_axis=1, conca...  8.93 us
    dot_general x1, matrix products, shards(): jnp.dot(weights_i, caption_b_g, preferred_element_type=jnp.float32)  7.88 us
    all_to_all x1, starting transfers between devices, shards(): lax.all_to_all(zero_sum, 'dp', split_axis=1, concat_axis=0, tiled=True)  7.55 us
  transfers between devices with their start and end apart: 4, of which 4 were waited for; matrix products, arithmetic and copies ran while one was open for 6% of the time, Pallas kernels for 0%

profile of v2, /device:TPU:57, one launch (start us, length us, event | category | flops | bytes accessed | tf_op | source)
XLA Modules:
  0.0 295.1 jit_solution(10581804253873701716)
XLA Ops:
  7.2 0.0 copy-start
  7.2 0.0 copy-start.2
  7.2 0.0 copy-start.4
  7.2 0.0 all-gather.2.cloned.1.call-start
  7.2 0.6 compare_reduce_fusion
  7.9 0.6 compare_reduce_fusion.1
  8.5 2.0 fusion.81
  10.5 0.1 copy.24
  10.7 2.0 pad_maximum_fusion
  12.6 0.0 all-gather.2.cloned.1.call-update
  12.6 1.6 copy.22
  14.3 1.3 copy.23
  15.6 8.9 %all-to-all-start = ((bf16[128,16,256]{2,0,1:T(8,128)(2,1)}), bf16[128,16,256]{2,0,1:T(8,128)(2,1)S(1)}, u32[]{:S(2)}, u32[]{:S(2)}) async-start(bf16[128,16,256]{2,0,1:T(8,128)(2,1)} %copy.23), calls=%async_computation | async-start | bytes 2097152 | tf_op jit(solution)/shard_map/all_to_all | solution.py:36
  25.8 1.1 convert_reduce_fusion.1
  26.9 0.0 copy-done.2
  26.9 0.2 fusion.41
  27.1 0.0 copy-done.4
  27.1 0.2 fusion.47
  27.4 21.0 %all-to-all-done = bf16[128,16,256]{2,0,1:T(8,128)(2,1)S(1)} async-done(((bf16[128,16,256]{2,0,1:T(8,128)(2,1)}), bf16[128,16,256]{2,0,1:T(8,128)(2,1)S(1)}, u32[]{:S(2)}, u32[]{:S(2)}) %all-to-all-start) | async-done | bytes 1048608 | tf_op jit(solution)/shard_map/all_to_all | solution.py:36
  48.3 49.7 %all-gather.2.cloned.1.call-done = bf16[2048,2176]{1,0:T(8,128)(2,1)} async-done(((bf16[128,2176]{1,0:T(8,128)(2,1)}), bf16[2048,2176]{1,0:T(8,128)(2,1)}) %all-gather.2.cloned.1.call-update) | async-done | bytes 8912912 | tf_op jit(solution)/shard_map/all_gather | solution.py:44
  98.1 3.0 %convert_reduce_fusion = f32[2048]{0:T(1024)S(1)} fusion(bf16[2048,2176]{1,0:T(8,128)(2,1)} %all-gather.2.cloned.1.call-done), kind=kLoop, calls=%fused_computation.3 | loop fusion | flops 4192256 | bytes 4202496 | tf_op jit(solution)/shard_map/reduce_sum | solution.py:12
  101.1 2.2 add_reduce_fusion
  103.3 3.0 %fusion.2 = f32[2048]{0:T(1024)S(1)} fusion(f32[2048]{0:T(1024)S(1)} %broadcast_multiply_fusion, bf16[2048,2176]{1,0:T(8,128)(2,1)} %all-gather.2.cloned.1.call-done), kind=kLoop, calls=%fused_computation.6 | loop fusion | flops 8386560 | bytes 4210688 | tf_op jit(solution)/shard_map/reduce_sum | solution.py:13
  106.3 0.0 copy-done.1
  106.3 3.0 %fusion.8 = (f32[2048]{0:T(1024)S(1)}, f32[2048]{0:T(1024)S(1)}) fusion(bf16[2048,2176]{1,0:T(8,128)(2,1)S(1)} %copy-done.1, f32[1024]{0:T(1024)S(1)} %copy-done.4, f32[2048]{0:T(1024)S(1)} %add_rsqrt_fusion.2, f32[2048]{0:T(1024)S(1)} %broadcast_multiply_fusion), kind=kLoop, calls=%fused_computation.12 | loop fusion | flops 18870272 | bytes 8425472 | tf_op jit(solution)/shard_map/reduce_sum | solution.py:8
  109.4 6.5 %fusion.49 = (f32[128]{0:T(128)S(1)}, f32[128,1024]{1,0:T(8,128)S(1)}) fusion(bf16[128,1024]{1,0:T(8,128)(2,1)S(1)} %copy-done.2, f32[1024]{0:T(1024)S(1)} %copy-done.4, f32[128]{0:T(128)S(1)} %fusion.83, f32[128]{0:T(128)S(1)} %broadcast_multiply_fusion.1, f32[2048]{0:T(1024)S(1)} %get-tuple-element.41, ...), kind=kOutput, calls=%fused_computation.64 | convolution fusion | flops 1090912128 | bytes 9475072 | tf_op jit(solution)/shard_map/dot_general | solution.py:87
  115.9 0.3 fusion.50
  116.3 0.4 fusion.88
  116.7 0.1 add_convert_fusion
  116.8 0.2 copy.25
  117.0 0.8 broadcast_in_dim.57
  117.8 100.9 %all_to_all.57 = bf16[16,128,1024]{1,2,0:T(8,128)(2,1)} all-to-all(bf16[16,128,1024]{1,2,0:T(8,128)(2,1)S(1)} %broadcast_in_dim.57), channel_id=1, replica_groups=mesh['dp'=16,'zero'=16] {'zero'}, dimensions={0} | all-to-all | bytes 8388608 | tf_op jit(solution)/shard_map/all_to_all | solution.py:96
  218.7 6.3 %copy.26 = bf16[16,128,1024]{2,1,0:T(8,128)(2,1)} copy(bf16[16,128,1024]{1,2,0:T(8,128)(2,1)} %all_to_all.57) | data formatting | bytes 8388608 | tf_op jit(solution)/shard_map/all_to_all | solution.py:96
  225.0 6.5 %copy.28 = bf16[1024,2048]{1,0:T(8,128)(2,1)} copy(bf16[1024,2048]{0,1:T(8,128)(2,1)} %bitcast.28) | data formatting | bytes 8388608 | tf_op jit(solution)/shard_map/dot_general | solution.py:110
  231.5 4.4 %fusion.30 = f32[256,16,64]{0,2,1:T(8,128)} fusion(bf16[16,64,2048]{2,1,0:T(8,128)(2,1)} %bitcast.30, bf16[2048,256]{1,0:T(8,128)(2,1)S(1)} %bitcast.33), kind=kOutput, calls=%fused_computation.35 | convolution fusion | flops 1073741824 | bytes 6291456 | tf_op jit(solution)/shard_map/dot_general | solution.py:110
  235.9 7.6 %all-to-all-start.3 = ((f32[256,16,64]{0,2,1:T(8,128)}), f32[256,16,64]{0,2,1:T(8,128)S(1)}, u32[]{:S(2)}, u32[]{:S(2)}) async-start(f32[256,16,64]{0,2,1:T(8,128)} %fusion.30), calls=%async_computation.3 | async-start | bytes 2097152 | tf_op jit(solution)/shard_map/all_to_all | solution.py:114
  243.5 0.0 copy-done
  243.5 4.5 %convolution_convert_fusion = bf16[2048,256]{1,0:T(8,128)(2,1)} fusion(bf16[2048,1024]{1,0:T(8,128)(2,1)} %bitcast.29, bf16[256,1024]{1,0:T(8,128)(2,1)S(1)} %copy-done), kind=kOutput, calls=%fused_computation.14 | convolution fusion | flops 1074266112 | bytes 5767168 | tf_op jit(solution)/shard_map/dot_general | solution.py:103
  247.9 10.7 %all-to-all-done.3 = f32[256,16,64]{0,2,1:T(8,128)S(1)} async-done(((f32[256,16,64]{0,2,1:T(8,128)}), f32[256,16,64]{0,2,1:T(8,128)S(1)}, u32[]{:S(2)}, u32[]{:S(2)}) %all-to-all-start.3) | async-done | bytes 1048608 | tf_op jit(solution)/shard_map/all_to_all | solution.py:114
  258.6 4.4 %all-to-all-start.2 = ((bf16[16,128,256]{2,1,0:T(8,128)(2,1)}), bf16[16,128,256]{2,1,0:T(8,128)(2,1)S(1)}, u32[]{:S(2)}, u32[]{:S(2)}) async-start(bf16[16,128,256]{2,1,0:T(8,128)(2,1)} %bitcast.34), calls=%async_computation.2 | async-start | bytes 2097152 | tf_op jit(solution)/shard_map/all_to_all | solution.py:109
  263.0 0.0 copy-done.3
  263.0 0.1 fusion.52
  263.1 0.0 copy-done.5
  263.1 7.9 %fusion.54 = (f32[128]{0:T(128)S(1)}, f32[128,1024]{1,0:T(8,128)S(1)}) fusion(bf16[128,1024]{1,0:T(8,128)(2,1)S(1)} %copy-done.3, f32[2048]{0:T(1024)S(1)} %get-tuple-element.42, f32[1024]{0:T(1024)S(1)} %copy-done.4, f32[2048]{0:T(1024)S(1)} %add_rsqrt_fusion.2, f32[2048]{0:T(1024)S(1)} %broadcast_multiply_fusion, ...), kind=kOutput, calls=%fused_computation.69 | convolution fusion | flops 1102708608 | bytes 9497600 | tf_op jit(solution)/shard_map/dot_general | solution.py:73
  271.0 1.0 add_add_fusion.2
  272.0 0.7 reduce_sum.145
  272.7 14.5 %all-to-all-done.2 = bf16[16,128,256]{2,1,0:T(8,128)(2,1)S(1)} async-done(((bf16[16,128,256]{2,1,0:T(8,128)(2,1)}), bf16[16,128,256]{2,1,0:T(8,128)(2,1)S(1)}, u32[]{:S(2)}, u32[]{:S(2)}) %all-to-all-start.2) | async-done | bytes 1048608 | tf_op jit(solution)/shard_map/all_to_all | solution.py:109
  287.2 1.1 copy.29
  (17 shorter events, 0.1 us)
Async XLA Ops:
  7.2 236.3 %copy-start = (bf16[256,1024]{1,0:T(8,128)(2,1)S(1)}, bf16[256,1024]{1,0:T(8,128)(2,1)}, u32[]{:S(2)}) copy-start(bf16[256,1024]{1,0:T(8,128)(2,1)} %param.17) | copy-start | bytes 1572868
  7.2 19.7 %copy-start.2 = (bf16[128,1024]{1,0:T(8,128)(2,1)S(1)}, bf16[128,1024]{1,0:T(8,128)(2,1)}, u32[]{:S(2)}) copy-start(bf16[128,1024]{1,0:T(8,128)(2,1)} %param.14) | copy-start | bytes 786436
  7.2 19.9 %copy-start.4 = (f32[1024]{0:T(1024)S(1)}, f32[1024]{0:T(1024)}, u32[]{:S(2)}) copy-start(f32[1024]{0:T(1024)} %param.16) | copy-start | bytes 12292
  7.2 90.9 %all-gather.2.cloned.1.call-start = ((), (), s32[]{:S(2)}) async-start(), calls=%async_computation.4 | async-start | bytes 9469952 | tf_op jit(solution)/shard_map/all_gather | solution.py:44
  15.6 32.8 %all-to-all-start = ((bf16[128,16,256]{2,0,1:T(8,128)(2,1)}), bf16[128,16,256]{2,0,1:T(8,128)(2,1)S(1)}, u32[]{:S(2)}, u32[]{:S(2)}) async-start(bf16[128,16,256]{2,0,1:T(8,128)(2,1)} %copy.23), calls=%async_computation | async-start | bytes 2097152 | tf_op jit(solution)/shard_map/all_to_all | solution.py:36
  98.1 8.2 %copy-start.1 = (bf16[2048,2176]{1,0:T(8,128)(2,1)S(1)}, bf16[2048,2176]{1,0:T(8,128)(2,1)}, u32[]{:S(2)}) copy-start(bf16[2048,2176]{1,0:T(8,128)(2,1)} %all-gather.2.cloned.1.call-done) | copy-start | bytes 26738692
  235.9 27.0 %copy-start.3 = (bf16[128,1024]{1,0:T(8,128)(2,1)S(1)}, bf16[128,1024]{1,0:T(8,128)(2,1)}, u32[]{:S(2)}) copy-start(bf16[128,1024]{1,0:T(8,128)(2,1)} %param.12) | copy-start | bytes 786436
  235.9 27.2 %copy-start.5 = (s32[128]{0:T(128)S(1)}, s32[128]{0:T(128)}, u32[]{:S(2)}) copy-start(s32[128]{0:T(128)} %param.13) | copy-start | bytes 1540
  235.9 22.7 %all-to-all-start.3 = ((f32[256,16,64]{0,2,1:T(8,128)}), f32[256,16,64]{0,2,1:T(8,128)S(1)}, u32[]{:S(2)}, u32[]{:S(2)}) async-start(f32[256,16,64]{0,2,1:T(8,128)} %fusion.30), calls=%async_computation.3 | async-start | bytes 2097152 | tf_op jit(solution)/shard_map/all_to_all | solution.py:114
  258.6 28.6 %all-to-all-start.2 = ((bf16[16,128,256]{2,1,0:T(8,128)(2,1)}), bf16[16,128,256]{2,1,0:T(8,128)(2,1)S(1)}, u32[]{:S(2)}, u32[]{:S(2)}) async-start(bf16[16,128,256]{2,1,0:T(8,128)(2,1)} %bitcast.34), calls=%async_computation.2 | async-start | bytes 2097152 | tf_op jit(solution)/shard_map/all_to_all | solution.py:109
Sparse Core Ops, SparseCore 0:
  12.8 85.2 all-gather.1

commit v3 on v1

v3 whole, which is shorter than its diff:
```python
import jax
import jax.numpy as jnp
from jax import lax
from jax.sharding import PartitionSpec as P


def unit_rows(values):
    return values * lax.rsqrt(jnp.sum(values * values, axis=1, keepdims=True) + 1e-06)


def text_embed(features, closing_layernorm_multiplier):
    center = features - jnp.mean(features, axis=1, keepdims=True)
    spread = jnp.mean(center * center, axis=1, keepdims=True)
    return unit_rows(center * lax.rsqrt(spread + 1e-05) * closing_layernorm_multiplier)


def sigmoid_weights(scores, labels):
    return (-labels * jax.nn.sigmoid(-labels * scores)).astype(jnp.bfloat16)


def shards(
    picture_embeds,
    matched_slot,
    summary_token_states,
    feedforward_inner_activations,
    closing_layernorm_multiplier,
    contracting_matrix,
    sharpness_factor,
    additive_shift_learned,
):
    similarity_multiplier = sharpness_factor[0]
    shift_value = additive_shift_learned[0]
    local_rows, width = picture_embeds.shape

    dp_size = lax.axis_size("dp")
    zero_size = lax.axis_size("zero")
    dp_place = lax.axis_index("dp")
    own_start = dp_place * local_rows
    transpose_route = [
        (a * zero_size + b, b * zero_size + a) for a in range(dp_size) for b in range(zero_size)
    ]

    ffa_cols = lax.all_to_all(
        feedforward_inner_activations, "dp", split_axis=1, concat_axis=0, tiled=True
    )
    weight_block = lax.ppermute(contracting_matrix, ("dp", "zero"), transpose_route)

    digits = jnp.zeros((local_rows, 128), jnp.bfloat16)
    digits = digits.at[:, 0].set((matched_slot // 256).astype(jnp.bfloat16))
    digits = digits.at[:, 1].set((matched_slot % 256).astype(jnp.bfloat16))
    both = jnp.concatenate([picture_embeds, summary_token_states, digits], axis=1)
    both_g = lax.all_gather(both, "dp", axis=0, tiled=True)
    ffa_cols, weight_block, both_g = lax.optimization_barrier((ffa_cols, weight_block, both_g))
    slot_g = both_g[:, 2 * width].astype(jnp.int32) * 256 + both_g[:, 2 * width + 1].astype(
        jnp.int32
    )
    image_b_g = unit_rows(both_g[:, :width].astype(jnp.float32)).astype(jnp.bfloat16)
    caption_g, caption_back = jax.vjp(
        lambda feats: text_embed(feats, closing_layernorm_multiplier),
        both_g[:, width : 2 * width].astype(jnp.float32),
    )
    caption_b_g = caption_g.astype(jnp.bfloat16)
    group_rows = caption_b_g.shape[0]

    unit_image, image_back = jax.vjp(unit_rows, picture_embeds.astype(jnp.float32))

    scores = (
        similarity_multiplier
        * lax.dot_general(
            image_b_g, caption_b_g, (((1,), (1,)), ((), ())), preferred_element_type=jnp.float32
        )
        + shift_value
    )
    places = jnp.arange(group_rows, dtype=jnp.int32)
    labels = jnp.where(slot_g[:, None] == places[None, :], 1.0, -1.0)
    weights = sigmoid_weights(scores, labels)
    own_weights = lax.dynamic_slice_in_dim(weights, own_start, local_rows, axis=0)
    image_term = similarity_multiplier * jnp.dot(
        own_weights, caption_b_g, preferred_element_type=jnp.float32
    )
    caption_term = similarity_multiplier * lax.dot_general(
        weights, image_b_g, (((0,), (0,)), ((), ())), preferred_element_type=jnp.float32
    )

    image_grad = image_back(image_term)[0]
    upstream_g = caption_back(caption_term)[0].astype(jnp.bfloat16)

    hidden_part = lax.dot_general(
        upstream_g,
        weight_block,
        (((1,), (1,)), ((), ())),
        preferred_element_type=jnp.float32,
    ).astype(jnp.bfloat16)
    hidden_grad = lax.all_to_all(hidden_part, "dp", split_axis=0, concat_axis=1, tiled=True)
    group_sum = lax.dot_general(
        ffa_cols, upstream_g, (((0,), (0,)), ((), ())), preferred_element_type=jnp.float32
    )
    down_parts = lax.all_to_all(group_sum, "zero", split_axis=1, concat_axis=0, tiled=True)
    down_block = jnp.sum(down_parts.reshape((zero_size,) + (group_sum.shape[0], -1)), axis=0)
    down_grad = lax.ppermute(down_block, ("dp", "zero"), transpose_route)
    return (image_grad, hidden_grad, down_grad)


def solution(mesh):
    placed = (
        P(("dp", "zero"), None),
        P(("dp", "zero")),
        P(("dp", "zero"), None),
        P(("dp", "zero"), None),
        P(),
        P("zero", None),
        P(),
        P(),
    )
    return jax.shard_map(
        shards,
        mesh=mesh,
        in_specs=placed,
        out_specs=(P(("dp", "zero"), None), P(("dp", "zero"), None), P("zero", "dp")),
        check_vma=False,
    )
```

time: 295 us -> 255 us (0.86)
  waiting for transfers between devices: 196 us -> 123 us
  starting transfers between devices: 13.7 us -> 37.2 us
  blocking collectives: 20.7 us -> 0 us
  matrix products: 23.3 us -> 42.9 us
  other arithmetic: 19.1 us -> 26.4 us
  local copies, waits for them, and re-layouts: 2.95 us -> 7.57 us
    reduce_scatter x1 -> x0, waiting for transfers between devices: 65.1 us -> none  [shards(): lax.psum_scatter(zero_sum, 'dp', scatter_dimension=1, tiled=True)]
    all_gather x1 -> x0, waiting for transfers between devices: 39.3 us -> none  [shards(): upstream_g = lax.all_gather(upstream, 'zero', axis=0, tiled=True)]
    all_to_all x2 -> x3, waiting for transfers between devices: 36.2 us -> 60.3 us  [the longest x1 35.6 us: shards(): lax.all_to_all(feedforward_inner_activations, 'dp', split_axis=1, concat_...]
    dot_general x3 -> x4, matrix products: 18.8 us -> 40.1 us  [the longest x1 18.2 us: shards(): lax.dot_general(image_b_g, caption_b_g, (((1,), (1,)), ((), ())), preferr...]
    all_gather x1 -> x0, blocking collectives: 20.7 us -> none  [shards(): slot_g = lax.all_gather(matched_slot, 'dp', axis=0, tiled=True)]
    ppermute x0 -> x2, starting transfers between devices: none -> 12.4 us  [the longest x1 7.18 us: shards(): lax.ppermute(contracting_matrix, ('dp', 'zero'), transpose_route)]
    all_to_all x2 -> x3, starting transfers between devices: 13.4 us -> 24.7 us  [the longest x1 9.31 us: shards(): lax.all_to_all(hidden_part, 'dp', split_axis=0, concat_axis=1, tiled=True)]
    all_gather x1, waiting for transfers between devices: 55.6 us -> 62.8 us  [shards(): both_g = lax.all_gather(both, 'dp', axis=0, tiled=True)]
  transfers between devices with their start and end apart: 5 -> 6, of which waited for: 5 -> 4; matrix products, arithmetic and copies ran while one was open for 8% -> 6% of each run, Pallas kernels for 0% -> 0%
where the time goes in v3:
time: 255 us; the launch traced here: 253 us
  waiting for transfers between devices  123 us (48%)
  matrix products  42.9 us (17%)
  starting transfers between devices  37.2 us (15%)
  other arithmetic  26.4 us (10%)
  between operations  15.5 us (6%)
  local copies, waits for them, and re-layouts  7.57 us (3%)
    all_gather x1, waiting for transfers between devices, shards(): both_g = lax.all_gather(both, 'dp', axis=0, tiled=True)  62.8 us
    all_to_all x1, waiting for transfers between devices, shards(): lax.all_to_all(feedforward_inner_activations, 'dp', split_axis=1, concat_...  35.6 us
    all_to_all x1, waiting for transfers between devices, shards(): lax.all_to_all(group_sum, 'zero', split_axis=1, concat_axis=0, tiled=True)  18.4 us
    dot_general x1, matrix products, shards(): lax.dot_general(image_b_g, caption_b_g, (((1,), (1,)), ((), ())), preferr...  18.2 us
    dot_general x1, matrix products, shards(): lax.dot_general(weights, image_b_g, (((0,), (0,)), ((), ())), preferred_e...  11.9 us
    all_to_all x1, starting transfers between devices, shards(): lax.all_to_all(hidden_part, 'dp', split_axis=0, concat_axis=1, tiled=True)  9.31 us
    all_to_all x1, starting transfers between devices, shards(): lax.all_to_all(group_sum, 'zero', split_axis=1, concat_axis=0, tiled=True)  7.84 us
    reduce_sum x2, other arithmetic, text_embed(): center = features - jnp.mean(features, axis=1, keepdims=True)  7.6 us
  transfers between devices with their start and end apart: 6, of which 4 were waited for; matrix products, arithmetic and copies ran while one was open for 6% of the time, Pallas kernels for 0%

profile of v3, /device:TPU:57, one launch (start us, length us, event | category | flops | bytes accessed | tf_op | source)
XLA Modules:
  0.0 252.8 jit_solution(212489842081570415)
XLA Ops:
  7.2 0.0 all-gather.2.cloned.1.call-start
  7.2 0.6 compare_reduce_fusion.1
  7.8 0.6 compare_reduce_fusion
  8.5 1.1 copy.21
  9.6 0.0 copy-start.3
  9.6 1.1 copy.20
  10.8 2.0 fusion.26
  12.8 0.9 pad_maximum_fusion
  13.7 0.0 all-gather.2.cloned.1.call-update
  13.7 2.3 copy.18
  16.0 7.6 %all-to-all-start = ((bf16[128,16,256]{0,2,1:T(8,128)(2,1)}), bf16[128,16,256]{0,2,1:T(8,128)(2,1)S(1)}, u32[]{:S(2)}, u32[]{:S(2)}) async-start(bf16[128,16,256]{0,2,1:T(8,128)(2,1)} %bitcast.1), calls=%async_computation | async-start | bytes 2097152 | tf_op jit(solution)/shard_map/all_to_all | solution.py:43
  23.6 7.2 %collective-permute-start = (bf16[256,1024]{1,0:T(8,128)(2,1)}, bf16[256,1024]{1,0:T(8,128)(2,1)S(1)}, u32[]{:S(2)}, u32[]{:S(2)}) collective-permute-start(bf16[256,1024]{1,0:T(8,128)(2,1)} %param.17), channel_id=1, source_target_pairs={{0,0},{1,16},{2,32},{3,48},{4,64},{5,80},{6,96},{7,112},{8,128},{9... | collective-permute-start | bytes 1572872 | tf_op jit(solution)/shard_map/ppermute | solution.py:46
  32.1 35.6 %all-to-all-done = bf16[128,16,256]{0,2,1:T(8,128)(2,1)S(1)} async-done(((bf16[128,16,256]{0,2,1:T(8,128)(2,1)}), bf16[128,16,256]{0,2,1:T(8,128)(2,1)S(1)}, u32[]{:S(2)}, u32[]{:S(2)}) %all-to-all-start) | async-done | bytes 1048608 | tf_op jit(solution)/shard_map/all_to_all | solution.py:43
  67.7 0.5 copy.19
  68.2 0.0 collective-permute-done
  68.2 62.8 %all-gather.2.cloned.1.call-done = bf16[2048,2176]{0,1:T(8,128)(2,1)} async-done(((bf16[128,2176]{0,1:T(8,128)(2,1)}), bf16[2048,2176]{0,1:T(8,128)(2,1)}) %all-gather.2.cloned.1.call-update) | async-done | bytes 8912912 | tf_op jit(solution)/shard_map/all_gather | solution.py:52
  131.0 0.0 copy-start
  131.0 3.0 %convert_reduce_fusion = f32[2048]{0:T(1024)S(1)} fusion(bf16[2048,2176]{0,1:T(8,128)(2,1)} %all-gather.2.cloned.1.call-done), kind=kLoop, calls=%fused_computation.5 | loop fusion | flops 4192256 | bytes 4202496 | tf_op jit(solution)/shard_map/jvp()/reduce_sum | solution.py:12
  134.0 1.3 convert_add_fusion
  135.3 3.3 %fusion.6 = f32[2048]{0:T(1024)S(1)} fusion(f32[2048]{0:T(1024)S(1)} %broadcast_multiply_fusion, bf16[2048,2176]{0,1:T(8,128)(2,1)} %all-gather.2.cloned.1.call-done), kind=kLoop, calls=%fused_computation.14 | loop fusion | flops 8386560 | bytes 4210688 | tf_op jit(solution)/shard_map/jvp()/reduce_sum | solution.py:13
  138.7 0.0 copy-done.3
  138.7 5.1 %fusion.12 = (f32[2048]{0:T(1024)S(1)}, f32[2048]{0:T(1024)S(1)}) fusion(f32[1024]{0:T(1024)S(1)} %copy-done.3, f32[2048]{0:T(1024)S(1)} %fusion.24, f32[2048]{0:T(1024)S(1)} %broadcast_multiply_fusion, bf16[2048,2176]{0,1:T(8,128)(2,1)} %all-gather.2.cloned.1.call-done), kind=kLoop, calls=%fused_computation.20 | loop fusion | flops 18870272 | bytes 8425472 | tf_op jit(solution)/shard_map/jvp()/reduce_sum | solution.py:8
  143.8 0.0 copy-done
  143.8 18.2 %multiply_convert_fusion = bf16[2048,2048]{1,0:T(8,128)(2,1)} fusion(f32[]{:T(128)} %bitcast.23, f32[]{:T(128)} %bitcast.19, s32[2048]{0:T(1024)S(1)} %bitcast.28, f32[2048]{0:T(1024)S(1)} %get-tuple-element.46, bf16[2048,2176]{0,1:T(8,128)(2,1)S(1)} %copy-done, f32[2048]{0:T(1024)S(1)} %get-tuple-element.47, f32[1024]{0:T(1024)S(1)} %copy-done.3, ...), kind=kOutput, calls=%fused_computation | convolution fusion | flops 8654946304 | bytes 16822280 | tf_op jit(solution)/shard_map/dot_general | solution.py:69
  162.0 11.9 %fusion.14 = (f32[2048]{0:T(1024)S(1)}, f32[2048,1024]{0,1:T(8,128)S(1)}) fusion(f32[]{:T(128)} %bitcast.22, f32[1024]{0:T(1024)S(1)} %copy-done.3, f32[2048]{0:T(1024)S(1)} %fusion.24, f32[2048]{0:T(1024)S(1)} %broadcast_multiply_fusion, bf16[2048,2176]{0,1:T(8,128)(2,1)S(1)} %copy-done, bf16[2048,2048]{1,0:T(8,128)(2,1)} %multiply_convert_fusion, ...), kind=kOutput, calls=%fused_computation.22 | convolution fusion | flops 8610904064 | bytes 25202692 | tf_op jit(solution)/shard_map/dot_general | solution.py:81
  173.9 3.9 %fusion.15 = f32[2048]{0:T(1024)S(1)} fusion(f32[2048,1024]{0,1:T(8,128)S(1)} %get-tuple-element.45, f32[2048]{0:T(1024)S(1)} %multiply_multiply_fusion.1, f32[]{:T(128)} %bitcast.21, f32[2048]{0:T(1024)S(1)} %get-tuple-element.47, f32[1024]{0:T(1024)S(1)} %copy-done.3, f32[2048]{0:T(1024)S(1)} %fusion.24, f32[2048]{0:T(1024)S(1)} %broadcast_multiply_fusion, ...), kind=kLoop, calls=%fused_computation.23 | loop fusion | flops 25163776 | bytes 12627972 | tf_op jit(solution)/shard_map/transpose(jvp())/reduce_sum | solution.py:14
  177.8 4.6 %fusion.31 = (f32[2048]{0:T(1024)S(1)}, f32[2048,1024]{0,1:T(8,128)S(1)}) fusion(f32[2048]{0:T(1024)S(1)} %multiply_multiply_fusion, f32[2048]{0:T(1024)S(1)} %multiply_multiply_fusion.1, f32[1024]{0:T(1024)S(1)} %copy-done.3, f32[2048]{0:T(1024)S(1)} %fusion.24, f32[2048]{0:T(1024)S(1)} %broadcast_multiply_fusion, bf16[2048,2176]{0,1:T(8,128)(2,1)S(1)} %copy-done, ...), kind=kLoop, calls=%fused_computation.63 | loop fusion | flops 31455232 | bytes 21024772 | tf_op jit(solution)/shard_map/transpose(jvp())/reduce_sum | solution.py:12
  182.5 0.0 copy-start.1
  182.5 2.9 %fusion.20 = f32[256,1024]{0,1:T(8,128)} fusion(bf16[2048,256]{1,0:T(8,128)(2,1)S(1)} %bitcast.26, f32[2048,1024]{0,1:T(8,128)S(1)} %get-tuple-element.38, f32[2048]{0:T(1024)S(1)} %negate_multiply_fusion), kind=kOutput, calls=%fused_computation.28 | convolution fusion | flops 1077936128 | bytes 10493952 | tf_op jit(solution)/shard_map/dot_general | solution.py:95
  185.4 0.8 copy-done.1
  186.1 7.8 %all-to-all-start.2 = ((f32[256,16,64]{0,2,1:T(8,128)}), f32[256,16,64]{0,2,1:T(8,128)S(1)}, u32[]{:S(2)}, u32[]{:S(2)}) async-start(f32[256,16,64]{0,2,1:T(8,128)} %bitcast.10), calls=%async_computation.2 | async-start | bytes 2097152 | tf_op jit(solution)/shard_map/all_to_all | solution.py:98
  194.0 0.0 copy-start.2
  194.0 5.8 %convolution_convert_fusion = bf16[2048,256]{1,0:T(8,128)(2,1)} fusion(bf16[256,1024]{1,0:T(8,128)(2,1)S(1)} %collective-permute-done, f32[2048,1024]{0,1:T(8,128)} %copy-done.1, f32[2048]{0:T(1024)S(1)} %negate_multiply_fusion), kind=kOutput, calls=%fused_computation.27 | convolution fusion | flops 1078460416 | bytes 9969664 | tf_op jit(solution)/shard_map/dot_general | solution.py:88
  199.7 18.4 %all-to-all-done.2 = f32[256,16,64]{0,2,1:T(8,128)S(1)} async-done(((f32[256,16,64]{0,2,1:T(8,128)}), f32[256,16,64]{0,2,1:T(8,128)S(1)}, u32[]{:S(2)}, u32[]{:S(2)}) %all-to-all-start.2) | async-done | bytes 1048608 | tf_op jit(solution)/shard_map/all_to_all | solution.py:98
  218.1 9.3 %all-to-all-start.1 = ((bf16[16,128,256]{2,1,0:T(8,128)(2,1)}), bf16[16,128,256]{2,1,0:T(8,128)(2,1)S(1)}, u32[]{:S(2)}, u32[]{:S(2)}) async-start(bf16[16,128,256]{2,1,0:T(8,128)(2,1)} %bitcast.8), calls=%async_computation.1 | async-start | bytes 2097152 | tf_op jit(solution)/shard_map/all_to_all | solution.py:94
  227.5 0.0 copy-done.2
  227.5 4.2 %fusion.21 = (f32[128]{0:T(128)S(1)}, f32[128]{0:T(128)S(1)}, f32[128,1024]{1,0:T(8,128)S(1)}) fusion(bf16[128,1024]{1,0:T(8,128)(2,1)S(1)} %copy-done.2, f32[2048]{0:T(1024)S(1)} %get-tuple-element.47, f32[1024]{0:T(1024)S(1)} %copy-done.3, f32[2048]{0:T(1024)S(1)} %fusion.24, f32[2048]{0:T(1024)S(1)} %broadcast_multiply_fusion, ...), kind=kOutput, calls=%fused_computation.35 | convolution fusion | flops 550240000 | bytes 5535236 | tf_op jit(solution)/shard_map/dot_general | solution.py:78
  231.7 0.1 reduce_sum.115
  231.8 5.2 %collective-permute-start.1 = (f32[256,64]{0,1:T(8,128)S(1)}, f32[256,64]{0,1:T(8,128)S(1)}, u32[]{:S(2)}, u32[]{:S(2)}) collective-permute-start(f32[256,64]{0,1:T(8,128)S(1)} %reduce_sum.115), channel_id=1, source_target_pairs={{0,0},{1,16},{2,32},{3,48},{4,64},{5,80},{6,96},{7,112},{8,128},{9... | collective-permute-start | bytes 196616 | tf_op jit(solution)/shard_map/ppermute | solution.py:100
  237.0 1.0 add_add_fusion.2
  238.0 6.3 %all-to-all-done.1 = bf16[16,128,256]{2,1,0:T(8,128)(2,1)S(1)} async-done(((bf16[16,128,256]{2,1,0:T(8,128)(2,1)}), bf16[16,128,256]{2,1,0:T(8,128)(2,1)S(1)}, u32[]{:S(2)}, u32[]{:S(2)}) %all-to-all-start.1) | async-done | bytes 1048608 | tf_op jit(solution)/shard_map/all_to_all | solution.py:94
  244.3 1.1 copy.25
  245.4 0.0 collective-permute-done.1
  245.4 0.6 copy.30
  (9 shorter events, 0.1 us)
Async XLA Ops:
  7.2 123.9 %all-gather.2.cloned.1.call-start = ((), (), s32[]{:S(2)}) async-start(), calls=%async_computation.3 | async-start | bytes 9469952 | tf_op jit(solution)/shard_map/all_gather | solution.py:52
  9.6 129.0 %copy-start.3 = (f32[1024]{0:T(1024)S(1)}, f32[1024]{0:T(1024)}, u32[]{:S(2)}) copy-start(f32[1024]{0:T(1024)} %param.16) | copy-start | bytes 12292
  16.0 51.7 %all-to-all-start = ((bf16[128,16,256]{0,2,1:T(8,128)(2,1)}), bf16[128,16,256]{0,2,1:T(8,128)(2,1)S(1)}, u32[]{:S(2)}, u32[]{:S(2)}) async-start(bf16[128,16,256]{0,2,1:T(8,128)(2,1)} %bitcast.1), calls=%async_computation | async-start | bytes 2097152 | tf_op jit(solution)/shard_map/all_to_all | solution.py:43
  23.6 44.6 %collective-permute-start = (bf16[256,1024]{1,0:T(8,128)(2,1)}, bf16[256,1024]{1,0:T(8,128)(2,1)S(1)}, u32[]{:S(2)}, u32[]{:S(2)}) collective-permute-start(bf16[256,1024]{1,0:T(8,128)(2,1)} %param.17), channel_id=1, source_target_pairs={{0,0},{1,16},{2,32},{3,48},{4,64},{5,80},{6,96},{7,112},{8,128},{9... | collective-permute-start | bytes 1572872 | tf_op jit(solution)/shard_map/ppermute | solution.py:46
  131.0 12.8 %copy-start = (bf16[2048,2176]{0,1:T(8,128)(2,1)S(1)}, bf16[2048,2176]{0,1:T(8,128)(2,1)}, u32[]{:S(2)}) copy-start(bf16[2048,2176]{0,1:T(8,128)(2,1)} %all-gather.2.cloned.1.call-done) | copy-start | bytes 26738692
  182.5 3.6 %copy-start.1 = (f32[2048,1024]{0,1:T(8,128)}, f32[2048,1024]{0,1:T(8,128)S(1)}, u32[]{:S(2)}) copy-start(f32[2048,1024]{0,1:T(8,128)S(1)} %get-tuple-element.38) | copy-start | bytes 25165828
  186.1 32.0 %all-to-all-start.2 = ((f32[256,16,64]{0,2,1:T(8,128)}), f32[256,16,64]{0,2,1:T(8,128)S(1)}, u32[]{:S(2)}, u32[]{:S(2)}) async-start(f32[256,16,64]{0,2,1:T(8,128)} %bitcast.10), calls=%async_computation.2 | async-start | bytes 2097152 | tf_op jit(solution)/shard_map/all_to_all | solution.py:98
  194.0 33.5 %copy-start.2 = (bf16[128,1024]{1,0:T(8,128)(2,1)S(1)}, bf16[128,1024]{1,0:T(8,128)(2,1)}, u32[]{:S(2)}) copy-start(bf16[128,1024]{1,0:T(8,128)(2,1)} %param.12) | copy-start | bytes 786436
  218.1 26.1 %all-to-all-start.1 = ((bf16[16,128,256]{2,1,0:T(8,128)(2,1)}), bf16[16,128,256]{2,1,0:T(8,128)(2,1)S(1)}, u32[]{:S(2)}, u32[]{:S(2)}) async-start(bf16[16,128,256]{2,1,0:T(8,128)(2,1)} %bitcast.8), calls=%async_computation.1 | async-start | bytes 2097152 | tf_op jit(solution)/shard_map/all_to_all | solution.py:94
  231.8 13.6 %collective-permute-start.1 = (f32[256,64]{0,1:T(8,128)S(1)}, f32[256,64]{0,1:T(8,128)S(1)}, u32[]{:S(2)}, u32[]{:S(2)}) collective-permute-start(f32[256,64]{0,1:T(8,128)S(1)} %reduce_sum.115), channel_id=1, source_target_pairs={{0,0},{1,16},{2,32},{3,48},{4,64},{5,80},{6,96},{7,112},{8,128},{9... | collective-permute-start | bytes 196616 | tf_op jit(solution)/shard_map/ppermute | solution.py:100
Sparse Core Ops, SparseCore 0:
  13.8 117.1 all-gather.1

commit v4 on v3

--- a/solution.py
+++ b/solution.py
@@ -40,17 +40,17 @@
         (a * zero_size + b, b * zero_size + a) for a in range(dp_size) for b in range(zero_size)
     ]
 
-    ffa_cols = lax.all_to_all(
-        feedforward_inner_activations, "dp", split_axis=1, concat_axis=0, tiled=True
-    )
-    weight_block = lax.ppermute(contracting_matrix, ("dp", "zero"), transpose_route)
-
     digits = jnp.zeros((local_rows, 128), jnp.bfloat16)
     digits = digits.at[:, 0].set((matched_slot // 256).astype(jnp.bfloat16))
     digits = digits.at[:, 1].set((matched_slot % 256).astype(jnp.bfloat16))
     both = jnp.concatenate([picture_embeds, summary_token_states, digits], axis=1)
     both_g = lax.all_gather(both, "dp", axis=0, tiled=True)
-    ffa_cols, weight_block, both_g = lax.optimization_barrier((ffa_cols, weight_block, both_g))
+
+    ffa_in, weight_in, both_g = lax.optimization_barrier(
+        (feedforward_inner_activations, contracting_matrix, both_g)
+    )
+    ffa_cols = lax.all_to_all(ffa_in, "dp", split_axis=1, concat_axis=0, tiled=True)
+    weight_block = lax.ppermute(weight_in, ("dp", "zero"), transpose_route)
     slot_g = both_g[:, 2 * width].astype(jnp.int32) * 256 + both_g[:, 2 * width + 1].astype(
         jnp.int32
     )

time: 255 us -> 285 us (1.12); the launches traced: 253 us -> 280 us
  waiting for transfers between devices: 123 us -> 148 us
  other arithmetic: 26.4 us -> 32.3 us
    ppermute x1, waiting for transfers between devices: 0.01 us -> 51.1 us  [shards(): weight_block = lax.ppermute(weight_in, ('dp', 'zero'), transpose_route)]
    all_to_all x1, waiting for transfers between devices: 35.6 us -> 4.55 us  [shards(): lax.all_to_all(ffa_in, 'dp', split_axis=1, concat_axis=0, tiled=True)]
    all_gather x1, waiting for transfers between devices: 62.8 us -> 87.9 us  [shards(): both_g = lax.all_gather(both, 'dp', axis=0, tiled=True)]
    all_to_all x1, waiting for transfers between devices: 18.4 us -> 0.01 us  [shards(): lax.all_to_all(group_sum, 'zero', split_axis=1, concat_axis=0, tiled=True)]
    convert_element_type x0 -> x1, other arithmetic: none -> 3.17 us  [shards(): upstream_g = caption_back(caption_term)[0].astype(jnp.bfloat16)]
    unnamed x12 -> x15, local copies, waits for them, and re-layouts: 5.92 us -> 2.89 us
  transfers between devices with their start and end apart: 6 -> 6, of which waited for: 4 -> 4; matrix products, arithmetic and copies ran while one was open for 6% -> 8% of each run, Pallas kernels for 0% -> 0%
where the time goes in v4:
time: 285 us; the launch traced here: 280 us
  waiting for transfers between devices  148 us (52%)
  matrix products  43.4 us (15%)
  starting transfers between devices  35.4 us (12%)
  other arithmetic  32.3 us (11%)
  between operations  15.5 us (5%)
  local copies, waits for them, and re-layouts  5.09 us (2%)
    all_gather x1, waiting for transfers between devices, shards(): both_g = lax.all_gather(both, 'dp', axis=0, tiled=True)  87.9 us
    ppermute x1, waiting for transfers between devices, shards(): weight_block = lax.ppermute(weight_in, ('dp', 'zero'), transpose_route)  51.1 us
    dot_general x1, matrix products, shards(): lax.dot_general(image_b_g, caption_b_g, (((1,), (1,)), ((), ())), preferr...  18.3 us
    dot_general x1, matrix products, shards(): lax.dot_general(weights, image_b_g, (((0,), (0,)), ((), ())), preferred_e...  11.9 us
    reduce_sum x2, other arithmetic, text_embed(): center = features - jnp.mean(features, axis=1, keepdims=True)  10.4 us
    all_to_all x1, starting transfers between devices, shards(): lax.all_to_all(hidden_part, 'dp', split_axis=0, concat_axis=1, tiled=True)  8.84 us
    all_to_all x1, starting transfers between devices, shards(): lax.all_to_all(group_sum, 'zero', split_axis=1, concat_axis=0, tiled=True)  7.93 us
    ppermute x1, starting transfers between devices, shards(): down_grad = lax.ppermute(down_block, ('dp', 'zero'), transpose_route)  6.58 us
  transfers between devices with their start and end apart: 6, of which 4 were waited for; matrix products, arithmetic and copies ran while one was open for 8% of the time, Pallas kernels for 0%

profile of v4, /device:TPU:57, one launch (start us, length us, event | category | flops | bytes accessed | tf_op | source)
XLA Modules:
  0.0 279.6 jit_solution(1317905749165161730)
XLA Ops:
  7.2 0.0 copy-start.4
  7.2 0.0 all-gather.2.cloned.1.call-start
  7.2 0.6 compare_reduce_fusion
  7.9 0.6 compare_reduce_fusion.1
  8.5 1.1 copy.12
  9.6 1.1 copy.11
  10.8 2.0 fusion.25
  12.8 0.8 pad_maximum_fusion
  13.6 0.0 all-gather.2.cloned.1.call-update
  14.9 87.9 %all-gather.2.cloned.1.call-done = bf16[2048,2176]{0,1:T(8,128)(2,1)} async-done(((bf16[128,2176]{0,1:T(8,128)(2,1)}), bf16[2048,2176]{0,1:T(8,128)(2,1)}) %all-gather.2.cloned.1.call-update) | async-done | bytes 8912912 | tf_op jit(solution)/shard_map/all_gather | solution.py:47
  102.9 0.0 copy-start
  102.9 3.0 %convert_reduce_fusion = f32[2048]{0:T(1024)S(1)} fusion(bf16[2048,2176]{0,1:T(8,128)(2,1)} %all-gather.2.cloned.1.call-done), kind=kLoop, calls=%fused_computation.5 | loop fusion | flops 4192256 | bytes 4202496 | tf_op jit(solution)/shard_map/jvp()/reduce_sum | solution.py:12
  105.8 1.3 convert_add_fusion
  107.2 3.3 %fusion.6 = f32[2048]{0:T(1024)S(1)} fusion(f32[2048]{0:T(1024)S(1)} %broadcast_multiply_fusion, bf16[2048,2176]{0,1:T(8,128)(2,1)} %all-gather.2.cloned.1.call-done), kind=kLoop, calls=%fused_computation.14 | loop fusion | flops 8386560 | bytes 4210688 | tf_op jit(solution)/shard_map/jvp()/reduce_sum | solution.py:13
  110.5 0.0 copy-done.4
  110.5 5.1 %fusion.12 = (f32[2048]{0:T(1024)S(1)}, f32[2048]{0:T(1024)S(1)}) fusion(f32[1024]{0:T(1024)S(1)} %copy-done.4, f32[2048]{0:T(1024)S(1)} %fusion.23, f32[2048]{0:T(1024)S(1)} %broadcast_multiply_fusion, bf16[2048,2176]{0,1:T(8,128)(2,1)} %all-gather.2.cloned.1.call-done), kind=kLoop, calls=%fused_computation.20 | loop fusion | flops 18870272 | bytes 8425472 | tf_op jit(solution)/shard_map/jvp()/reduce_sum | solution.py:8
  115.6 0.0 copy-done
  115.6 18.3 %multiply_convert_fusion = bf16[2048,2048]{1,0:T(8,128)(2,1)} fusion(f32[]{:T(128)} %bitcast.33, f32[]{:T(128)} %bitcast.29, s32[2048]{0:T(1024)S(1)} %bitcast.39, f32[2048]{0:T(1024)S(1)} %get-tuple-element.46, bf16[2048,2176]{0,1:T(8,128)(2,1)S(1)} %copy-done, f32[2048]{0:T(1024)S(1)} %get-tuple-element.47, f32[1024]{0:T(1024)S(1)} %copy-done.4, ...), kind=kOutput, calls=%fused_computation | convolution fusion | flops 8654946304 | bytes 16822280 | tf_op jit(solution)/shard_map/dot_general | solution.py:69
  134.0 11.9 %fusion.14 = (f32[2048]{0:T(1024)S(1)}, f32[2048,1024]{0,1:T(8,128)S(1)}) fusion(f32[]{:T(128)} %bitcast.32, f32[1024]{0:T(1024)S(1)} %copy-done.4, f32[2048]{0:T(1024)S(1)} %fusion.23, f32[2048]{0:T(1024)S(1)} %broadcast_multiply_fusion, bf16[2048,2176]{0,1:T(8,128)(2,1)S(1)} %copy-done, bf16[2048,2048]{1,0:T(8,128)(2,1)} %multiply_convert_fusion, ...), kind=kOutput, calls=%fused_computation.22 | convolution fusion | flops 8610904064 | bytes 25202692 | tf_op jit(solution)/shard_map/dot_general | solution.py:81
  145.9 0.0 copy-start.1
  145.9 0.0 copy-start.2
  145.9 3.9 %fusion.15 = f32[2048]{0:T(1024)S(1)} fusion(f32[2048,1024]{0,1:T(8,128)S(1)} %get-tuple-element.45, f32[2048]{0:T(1024)S(1)} %multiply_multiply_fusion.1, f32[]{:T(128)} %bitcast.31, f32[2048]{0:T(1024)S(1)} %get-tuple-element.47, f32[1024]{0:T(1024)S(1)} %copy-done.4, f32[2048]{0:T(1024)S(1)} %fusion.23, f32[2048]{0:T(1024)S(1)} %broadcast_multiply_fusion, ...), kind=kLoop, calls=%fused_computation.23 | loop fusion | flops 25163776 | bytes 12627972 | tf_op jit(solution)/shard_map/transpose(jvp())/reduce_sum | solution.py:14
  149.8 0.0 copy-done.1
  149.8 0.0 copy-done.2
  149.8 1.1 copy.18
  150.9 6.2 %all-to-all-start.1 = ((bf16[128,16,256]{2,0,1:T(8,128)(2,1)}), bf16[128,16,256]{2,0,1:T(8,128)(2,1)S(1)}, u32[]{:S(2)}, u32[]{:S(2)}) async-start(bf16[128,16,256]{2,0,1:T(8,128)(2,1)} %bitcast.27), calls=%async_computation.1 | async-start | bytes 2097152 | tf_op jit(solution)/shard_map/all_to_all | solution.py:52
  157.1 7.4 %fusion.30 = (f32[2048]{0:T(1024)S(1)}, f32[2048,1024]{0,1:T(8,128)S(1)}) fusion(f32[2048]{0:T(1024)S(1)} %multiply_multiply_fusion, f32[2048]{0:T(1024)S(1)} %multiply_multiply_fusion.1, f32[1024]{0:T(1024)S(1)} %copy-done.4, f32[2048]{0:T(1024)S(1)} %fusion.23, f32[2048]{0:T(1024)S(1)} %broadcast_multiply_fusion, ...), kind=kLoop, calls=%fused_computation.63 | loop fusion | flops 31455232 | bytes 21024772 | tf_op jit(solution)/shard_map/transpose(jvp())/reduce_sum | solution.py:12
  164.5 3.2 %add_convert_fusion = bf16[2048,1024]{0,1:T(8,128)(2,1)} fusion(f32[2048,1024]{0,1:T(8,128)S(1)} %get-tuple-element.38, f32[2048]{0:T(1024)S(1)} %negate_multiply_fusion), kind=kLoop, calls=%fused_computation.25 | loop fusion | flops 4194304 | bytes 12591104 | tf_op jit(solution)/shard_map/convert_element_type | solution.py:86
  167.7 0.0 copy-start.5
  167.7 4.6 %all-to-all-done.1 = bf16[128,16,256]{2,0,1:T(8,128)(2,1)S(1)} async-done(((bf16[128,16,256]{2,0,1:T(8,128)(2,1)}), bf16[128,16,256]{2,0,1:T(8,128)(2,1)S(1)}, u32[]{:S(2)}, u32[]{:S(2)}) %all-to-all-start.1) | async-done | bytes 1048608 | tf_op jit(solution)/shard_map/all_to_all | solution.py:52
  172.3 4.5 %fusion.31 = f32[256,16,64]{0,2,1:T(8,128)} fusion(bf16[2048,256,1]{1,0,2:T(8,128)(2,1)S(1)} %bitcast.37, bf16[16,64,2048]{2,1,0:T(8,128)(2,1)} %bitcast.35), kind=kOutput, calls=%fused_computation.64 | convolution fusion | flops 1073741824 | bytes 6291456 | tf_op jit(solution)/shard_map/dot_general | solution.py:95
  176.7 0.0 copy-start.3
  176.7 7.9 %all-to-all-start.2 = ((f32[256,16,64]{0,2,1:T(8,128)}), f32[256,16,64]{0,2,1:T(8,128)S(1)}, u32[]{:S(2)}, u32[]{:S(2)}) async-start(f32[256,16,64]{0,2,1:T(8,128)} %fusion.31), calls=%async_computation.2 | async-start | bytes 2097152 | tf_op jit(solution)/shard_map/all_to_all | solution.py:98
  184.7 0.0 copy-done.5
  184.7 5.8 %collective-permute-start = (bf16[256,1024]{1,0:T(8,128)(2,1)S(1)}, bf16[256,1024]{1,0:T(8,128)(2,1)S(1)}, u32[]{:S(2)}, u32[]{:S(2)}) collective-permute-start(bf16[256,1024]{1,0:T(8,128)(2,1)S(1)} %copy-done.5), channel_id=1, source_target_pairs={{0,0},{1,16},{2,32},{3,48},{4,64},{5,80},{6,96},{7,112},{8,128},{9... | collective-permute-start | bytes 1572872 | tf_op jit(solution)/shard_map/ppermute | solution.py:53
  190.5 51.1 %collective-permute-done = bf16[256,1024]{1,0:T(8,128)(2,1)S(1)} collective-permute-done((bf16[256,1024]{1,0:T(8,128)(2,1)S(1)}, bf16[256,1024]{1,0:T(8,128)(2,1)S(1)}, u32[]{:S(2)}, u32[]{:S(2)}) %collective-permute-start) | collective-permute-done | bytes 524320 | tf_op jit(solution)/shard_map/ppermute | solution.py:53
  241.6 4.5 %convolution_convert_fusion = bf16[2048,256]{1,0:T(8,128)(2,1)} fusion(bf16[2048,1024]{0,1:T(8,128)(2,1)} %add_convert_fusion, bf16[256,1024]{1,0:T(8,128)(2,1)S(1)} %collective-permute-done), kind=kOutput, calls=%fused_computation.27 | convolution fusion | flops 1074266112 | bytes 5767168 | tf_op jit(solution)/shard_map/dot_general | solution.py:88
  246.1 0.0 all-to-all-done.2
  246.1 8.8 %all-to-all-start = ((bf16[16,128,256]{2,1,0:T(8,128)(2,1)}), bf16[16,128,256]{2,1,0:T(8,128)(2,1)S(1)}, u32[]{:S(2)}, u32[]{:S(2)}) async-start(bf16[16,128,256]{2,1,0:T(8,128)(2,1)} %bitcast.5), calls=%async_computation | async-start | bytes 2097152 | tf_op jit(solution)/shard_map/all_to_all | solution.py:94
  254.9 0.0 copy-done.3
  254.9 4.2 %fusion.20 = (f32[128]{0:T(128)S(1)}, f32[128]{0:T(128)S(1)}, f32[128,1024]{1,0:T(8,128)S(1)}) fusion(bf16[128,1024]{1,0:T(8,128)(2,1)S(1)} %copy-done.3, f32[2048]{0:T(1024)S(1)} %get-tuple-element.47, f32[1024]{0:T(1024)S(1)} %copy-done.4, f32[2048]{0:T(1024)S(1)} %fusion.23, f32[2048]{0:T(1024)S(1)} %broadcast_multiply_fusion, ...), kind=kOutput, calls=%fused_computation.35 | convolution fusion | flops 550240000 | bytes 5535236 | tf_op jit(solution)/shard_map/dot_general | solution.py:78
  259.1 0.1 reduce_sum.115
  259.2 6.6 %collective-permute-start.1 = (f32[256,64]{0,1:T(8,128)S(1)}, f32[256,64]{0,1:T(8,128)S(1)}, u32[]{:S(2)}, u32[]{:S(2)}) collective-permute-start(f32[256,64]{0,1:T(8,128)S(1)} %reduce_sum.115), channel_id=1, source_target_pairs={{0,0},{1,16},{2,32},{3,48},{4,64},{5,80},{6,96},{7,112},{8,128},{9... | collective-permute-start | bytes 196616 | tf_op jit(solution)/shard_map/ppermute | solution.py:100
  265.8 0.9 add_add_fusion.2
  266.8 4.3 %all-to-all-done = bf16[16,128,256]{2,1,0:T(8,128)(2,1)S(1)} async-done(((bf16[16,128,256]{2,1,0:T(8,128)(2,1)}), bf16[16,128,256]{2,1,0:T(8,128)(2,1)S(1)}, u32[]{:S(2)}, u32[]{:S(2)}) %all-to-all-start) | async-done | bytes 1048608 | tf_op jit(solution)/shard_map/all_to_all | solution.py:94
  271.0 1.1 copy.16
  272.1 0.0 collective-permute-done.1
  272.1 0.6 copy.23
  (9 shorter events, 0.1 us)
Async XLA Ops:
  7.2 103.3 %copy-start.4 = (f32[1024]{0:T(1024)S(1)}, f32[1024]{0:T(1024)}, u32[]{:S(2)}) copy-start(f32[1024]{0:T(1024)} %param.16) | copy-start | bytes 12292
  7.2 95.7 %all-gather.2.cloned.1.call-start = ((), (), s32[]{:S(2)}) async-start(), calls=%async_computation.3 | async-start | bytes 9469952 | tf_op jit(solution)/shard_map/all_gather | solution.py:47
  102.9 12.8 %copy-start = (bf16[2048,2176]{0,1:T(8,128)(2,1)S(1)}, bf16[2048,2176]{0,1:T(8,128)(2,1)}, u32[]{:S(2)}) copy-start(bf16[2048,2176]{0,1:T(8,128)(2,1)} %all-gather.2.cloned.1.call-done) | copy-start | bytes 26738692
  145.9 3.9 %copy-start.1 = (f32[2048,1024]{0,1:T(8,128)}, f32[2048,1024]{0,1:T(8,128)S(1)}, u32[]{:S(2)}) copy-start(f32[2048,1024]{0,1:T(8,128)S(1)} %get-tuple-element.45) | copy-start | bytes 25165828
  145.9 4.0 %copy-start.2 = (bf16[128,4096]{1,0:T(8,128)(2,1)S(1)}, bf16[128,4096]{1,0:T(8,128)(2,1)}, u32[]{:S(2)}) copy-start(bf16[128,4096]{1,0:T(8,128)(2,1)} %param.15) | copy-start | bytes 3145732
  150.9 21.4 %all-to-all-start.1 = ((bf16[128,16,256]{2,0,1:T(8,128)(2,1)}), bf16[128,16,256]{2,0,1:T(8,128)(2,1)S(1)}, u32[]{:S(2)}, u32[]{:S(2)}) async-start(bf16[128,16,256]{2,0,1:T(8,128)(2,1)} %bitcast.27), calls=%async_computation.1 | async-start | bytes 2097152 | tf_op jit(solution)/shard_map/all_to_all | solution.py:52
  167.7 17.0 %copy-start.5 = (bf16[256,1024]{1,0:T(8,128)(2,1)S(1)}, bf16[256,1024]{1,0:T(8,128)(2,1)}, u32[]{:S(2)}) copy-start(bf16[256,1024]{1,0:T(8,128)(2,1)} %param.17) | copy-start | bytes 1572868
  176.7 78.2 %copy-start.3 = (bf16[128,1024]{1,0:T(8,128)(2,1)S(1)}, bf16[128,1024]{1,0:T(8,128)(2,1)}, u32[]{:S(2)}) copy-start(bf16[128,1024]{1,0:T(8,128)(2,1)} %param.12) | copy-start | bytes 786436
  176.7 69.3 %all-to-all-start.2 = ((f32[256,16,64]{0,2,1:T(8,128)}), f32[256,16,64]{0,2,1:T(8,128)S(1)}, u32[]{:S(2)}, u32[]{:S(2)}) async-start(f32[256,16,64]{0,2,1:T(8,128)} %fusion.31), calls=%async_computation.2 | async-start | bytes 2097152 | tf_op jit(solution)/shard_map/all_to_all | solution.py:98
  184.7 56.9 %collective-permute-start = (bf16[256,1024]{1,0:T(8,128)(2,1)S(1)}, bf16[256,1024]{1,0:T(8,128)(2,1)S(1)}, u32[]{:S(2)}, u32[]{:S(2)}) collective-permute-start(bf16[256,1024]{1,0:T(8,128)(2,1)S(1)} %copy-done.5), channel_id=1, source_target_pairs={{0,0},{1,16},{2,32},{3,48},{4,64},{5,80},{6,96},{7,112},{8,128},{9... | collective-permute-start | bytes 1572872 | tf_op jit(solution)/shard_map/ppermute | solution.py:53
  246.1 25.0 %all-to-all-start = ((bf16[16,128,256]{2,1,0:T(8,128)(2,1)}), bf16[16,128,256]{2,1,0:T(8,128)(2,1)S(1)}, u32[]{:S(2)}, u32[]{:S(2)}) async-start(bf16[16,128,256]{2,1,0:T(8,128)(2,1)} %bitcast.5), calls=%async_computation | async-start | bytes 2097152 | tf_op jit(solution)/shard_map/all_to_all | solution.py:94
  259.2 12.9 %collective-permute-start.1 = (f32[256,64]{0,1:T(8,128)S(1)}, f32[256,64]{0,1:T(8,128)S(1)}, u32[]{:S(2)}, u32[]{:S(2)}) collective-permute-start(f32[256,64]{0,1:T(8,128)S(1)} %reduce_sum.115), channel_id=1, source_target_pairs={{0,0},{1,16},{2,32},{3,48},{4,64},{5,80},{6,96},{7,112},{8,128},{9... | collective-permute-start | bytes 196616 | tf_op jit(solution)/shard_map/ppermute | solution.py:100
Sparse Core Ops, SparseCore 0:
  13.8 89.0 all-gather.1

commit v5 on v3

--- a/solution.py
+++ b/solution.py
@@ -1,7 +1,100 @@
+import functools
+
 import jax
 import jax.numpy as jnp
 from jax import lax
+from jax.experimental import pallas as pl
+from jax.experimental.pallas import tpu as pltpu
 from jax.sharding import PartitionSpec as P
+
+MESH = pl.DeviceIdType.MESH
+
+
+def gather_kernel(chips, block_ref, out_ref, send_sem, recv_sem, local_sem):
+    me = lax.axis_index("dp")
+    zz = lax.axis_index("zero")
+    core = me % 2
+    chip = me // 2
+    sibling = me + 1 - 2 * core
+
+    def peer(k):
+        return ((chip + k) % chips) * 2 + core
+
+    def source(k):
+        return ((chip + chips - k) % chips) * 2 + core
+
+    barrier = pltpu.get_barrier_semaphore()
+    pl.semaphore_signal(barrier, inc=1, device_id=(sibling, zz), device_id_type=MESH)
+    for k in range(1, chips):
+        pl.semaphore_signal(barrier, inc=1, device_id=(peer(k), zz), device_id_type=MESH)
+    pl.semaphore_wait(barrier, chips)
+
+    local = pltpu.make_async_copy(block_ref, out_ref.at[me], local_sem)
+    local.start()
+    sends = []
+    for k in range(1, chips):
+        copy = pltpu.make_async_remote_copy(
+            src_ref=block_ref,
+            dst_ref=out_ref.at[me],
+            send_sem=send_sem.at[k],
+            recv_sem=recv_sem.at[me],
+            device_id=(peer(k), zz),
+            device_id_type=MESH,
+        )
+        copy.start()
+        sends.append(copy)
+    copy = pltpu.make_async_remote_copy(
+        src_ref=block_ref,
+        dst_ref=out_ref.at[me],
+        send_sem=send_sem.at[0],
+        recv_sem=recv_sem.at[me],
+        device_id=(sibling, zz),
+        device_id_type=MESH,
+    )
+    copy.start()
+    sends.append(copy)
+    for k in range(1, chips):
+        s = source(k)
+        arrived = pltpu.make_async_remote_copy(
+            src_ref=out_ref.at[s],
+            dst_ref=out_ref.at[s],
+            send_sem=send_sem.at[chips + k],
+            recv_sem=recv_sem.at[s],
+            device_id=(sibling, zz),
+            device_id_type=MESH,
+        )
+        arrived.wait_recv()
+        arrived.start()
+        sends.append(arrived)
+    for k in range(chips):
+        t = ((chip + k) % chips) * 2 + (1 - core)
+        pltpu.make_async_remote_copy(
+            src_ref=out_ref.at[t],
+            dst_ref=out_ref.at[t],
+            send_sem=send_sem.at[0],
+            recv_sem=recv_sem.at[t],
+            device_id=(sibling, zz),
+            device_id_type=MESH,
+        ).wait_recv()
+    for copy in sends:
+        copy.wait_send()
+    local.wait()
+
+
+def gather_dp(block):
+    dp_size = lax.axis_size("dp")
+    return pl.pallas_call(
+        functools.partial(gather_kernel, dp_size // 2),
+        out_shape=jax.ShapeDtypeStruct((dp_size,) + block.shape, block.dtype),
+        in_specs=[pl.BlockSpec(memory_space=pl.ANY)],
+        out_specs=pl.BlockSpec(memory_space=pl.ANY),
+        scratch_shapes=[
+            pltpu.SemaphoreType.DMA((dp_size,)),
+            pltpu.SemaphoreType.DMA((dp_size,)),
+            pltpu.SemaphoreType.DMA(()),
+        ],
+        compiler_params=pltpu.CompilerParams(collective_id=0, has_side_effects=True),
+    )(block)
 
 
 def unit_rows(values):
@@ -49,7 +142,7 @@
     digits = digits.at[:, 0].set((matched_slot // 256).astype(jnp.bfloat16))
     digits = digits.at[:, 1].set((matched_slot % 256).astype(jnp.bfloat16))
     both = jnp.concatenate([picture_embeds, summary_token_states, digits], axis=1)
-    both_g = lax.all_gather(both, "dp", axis=0, tiled=True)
+    both_g = gather_dp(both).reshape((-1, both.shape[1]))
     ffa_cols, weight_block, both_g = lax.optimization_barrier((ffa_cols, weight_block, both_g))
     slot_g = both_g[:, 2 * width].astype(jnp.int32) * 256 + both_g[:, 2 * width + 1].astype(
         jnp.int32

time: 255 us -> 254 us (level)
  waiting for transfers between devices: 123 us -> 25.5 us
  Pallas kernels: 0 us -> 89 us
  between operations: 15.5 us -> 2.12 us
  local copies, waits for them, and re-layouts: 7.57 us -> 18.3 us
  starting transfers between devices: 37.2 us -> 43.9 us
    pallas_call x0 -> x1, Pallas kernels: none -> 89 us  [gather_dp(): pl.pallas_call(functools.partial(gather_kernel, dp_size // 2), out_shape=...]
    all_gather x1 -> x0, waiting for transfers between devices: 62.8 us -> none  [shards(): both_g = lax.all_gather(both, 'dp', axis=0, tiled=True)]
    all_to_all x1, waiting for transfers between devices: 35.6 us -> 0.01 us  [shards(): lax.all_to_all(feedforward_inner_activations, 'dp', split_axis=1, concat_...]
    optimization_barrier x0 -> x1, local copies, waits for them, and re-layouts: none -> 12.6 us  [shards(): lax.optimization_barrier((ffa_cols, weight_block, both_g))]
    all_to_all x1, starting transfers between devices: 7.84 us -> 13 us  [shards(): lax.all_to_all(group_sum, 'zero', split_axis=1, concat_axis=0, tiled=True)]
    dot_general x1, matrix products: 11.9 us -> 14.7 us  [shards(): lax.dot_general(weights, image_b_g, (((0,), (0,)), ((), ())), preferred_e...]
    unnamed x12 -> x10, local copies, waits for them, and re-layouts: 5.92 us -> 3.65 us
    reduce_sum x1 -> x2, other arithmetic: 5.1 us -> 5.43 us  [unit_rows(): jnp.sum(values * values, axis=1, keepdims=True) + 1e-06]
  transfers between devices with their start and end apart: 6 -> 5, of which waited for: 4 -> 2; matrix products, arithmetic and copies ran while one was open for 6% -> 7% of each run, Pallas kernels for 0% -> 35%
where the time goes in v5:
time: 254 us; the launch traced here: 251 us
  Pallas kernels  89 us (35%)
  matrix products  44.7 us (18%)
  starting transfers between devices  43.9 us (17%)
  other arithmetic  27.7 us (11%)
  waiting for transfers between devices  25.5 us (10%)
  local copies, waits for them, and re-layouts  18.3 us (7%)
    pallas_call x1, Pallas kernels, gather_dp(): pl.pallas_call(functools.partial(gather_kernel, dp_size // 2), out_shape=...  89 us
    all_to_all x1, waiting for transfers between devices, shards(): lax.all_to_all(group_sum, 'zero', split_axis=1, concat_axis=0, tiled=True)  19.1 us
    dot_general x1, matrix products, shards(): lax.dot_general(image_b_g, caption_b_g, (((1,), (1,)), ((), ())), preferr...  17.1 us
    dot_general x1, matrix products, shards(): lax.dot_general(weights, image_b_g, (((0,), (0,)), ((), ())), preferred_e...  14.7 us
    all_to_all x1, starting transfers between devices, shards(): lax.all_to_all(group_sum, 'zero', split_axis=1, concat_axis=0, tiled=True)  13 us
    optimization_barrier x1, local copies, waits for them, and re-layouts, shards(): lax.optimization_barrier((ffa_cols, weight_block, both_g))  12.6 us
    all_to_all x1, starting transfers between devices, shards(): lax.all_to_all(hidden_part, 'dp', split_axis=0, concat_axis=1, tiled=True)  11 us
    reduce_sum x2, other arithmetic, text_embed(): center = features - jnp.mean(features, axis=1, keepdims=True)  8.04 us
  transfers between devices with their start and end apart: 5, of which 2 were waited for; matrix products, arithmetic and copies ran while one was open for 7% of the time, Pallas kernels for 35%

profile of v5, /device:TPU:57, one launch (start us, length us, event | category | flops | bytes accessed | tf_op | source)
XLA Modules:
  0.0 251.2 jit_solution(15493588492524579415)
XLA Ops:
  0.6 2.3 copy.22
  2.9 7.6 %all-to-all-start = ((bf16[128,16,256]{0,2,1:T(8,128)(2,1)}), bf16[128,16,256]{0,2,1:T(8,128)(2,1)S(1)}, u32[]{:S(2)}, u32[]{:S(2)}) async-start(bf16[128,16,256]{0,2,1:T(8,128)(2,1)} %bitcast.1), calls=%async_computation | async-start | bytes 2097152 | tf_op jit(solution)/shard_map/all_to_all | solution.py:136
  10.5 7.2 %collective-permute-start = (bf16[256,1024]{1,0:T(8,128)(2,1)}, bf16[256,1024]{1,0:T(8,128)(2,1)S(1)}, u32[]{:S(2)}, u32[]{:S(2)}) collective-permute-start(bf16[256,1024]{1,0:T(8,128)(2,1)} %param.17), channel_id=1, source_target_pairs={{0,0},{1,16},{2,32},{3,48},{4,64},{5,80},{6,96},{7,112},{8,128},{9... | collective-permute-start | bytes 1572872 | tf_op jit(solution)/shard_map/ppermute | solution.py:139
  17.7 0.6 compare_reduce_fusion
  18.3 0.6 compare_reduce_fusion.1
  19.0 2.0 fusion.28
  20.9 0.1 copy.24
  21.1 0.1 copy.25
  21.2 0.2 scatter.9
  21.4 1.9 pad_maximum_fusion.block_ref
  23.3 89.0 %shard_map.103 = bf16[16,128,2176]{2,1,0:T(8,128)(2,1)} custom-call(bf16[128,2176]{1,0:T(8,128)(2,1)} %pad_maximum_fusion.block_ref), custom_call_target="tpu_custom_call" | custom-call | tf_op jit(solution)/shard_map/pallas_call | solution.py:86
  113.6 0.0 all-to-all-done
  113.6 0.5 copy.23
  114.1 0.0 collective-permute-done
  114.1 12.6 %copy.26 = bf16[2048,2176]{0,1:T(8,128)(2,1)} copy(bf16[2048,2176]{1,0:T(8,128)(2,1)} %bitcast.25) | data formatting | bytes 17825792 | tf_op jit(solution)/shard_map/optimization_barrier | solution.py:146
  126.7 0.0 copy-start
  126.7 0.0 copy-start.3
  126.7 3.2 %fusion.4 = f32[2048]{0:T(1024)S(1)} fusion(bf16[2048,2176]{1,0:T(8,128)(2,1)} %bitcast.26), kind=kLoop, calls=%fused_computation.12 | loop fusion | flops 6289408 | bytes 4202496 | tf_op jit(solution)/shard_map/reduce_sum | solution.py:101
  130.0 3.4 %convert_reduce_fusion = f32[2048]{0:T(1024)S(1)} fusion(bf16[2048,2176]{0,1:T(8,128)(2,1)} %copy.26), kind=kLoop, calls=%fused_computation.5 | loop fusion | flops 4192256 | bytes 4202496 | tf_op jit(solution)/shard_map/jvp()/reduce_sum | solution.py:105
  133.4 0.9 fusion.24
  134.3 3.3 %fusion.6 = f32[2048]{0:T(1024)S(1)} fusion(f32[2048]{0:T(1024)S(1)} %broadcast_multiply_fusion, bf16[2048,2176]{0,1:T(8,128)(2,1)} %copy.26), kind=kLoop, calls=%fused_computation.14 | loop fusion | flops 8386560 | bytes 4210688 | tf_op jit(solution)/shard_map/jvp()/reduce_sum | solution.py:106
  137.6 0.0 copy-done
  137.6 0.0 copy-done.3
  137.6 2.2 fusion.12
  139.9 17.1 %multiply_convert_fusion = bf16[2048,2048]{1,0:T(8,128)(2,1)} fusion(f32[]{:T(128)} %bitcast.24, f32[]{:T(128)} %bitcast.20, s32[2048]{0:T(1024)S(1)} %bitcast.33, f32[2048]{0:T(1024)S(1)} %get-tuple-element.44, bf16[2048,2176]{1,0:T(8,128)(2,1)} %bitcast.27, f32[2048]{0:T(1024)S(1)} %get-tuple-element.45, f32[1024]{0:T(1024)S(1)} %copy-done.3, ...), kind=kOutput, calls=%fused_computation | convolution fusion | flops 8654946304 | bytes 16823296 | tf_op jit(solution)/shard_map/dot_general | solution.py:162
  157.0 14.7 %fusion.14 = (f32[2048]{0:T(1024)S(1)}, f32[2048,1024]{0,1:T(8,128)S(1)}) fusion(f32[]{:T(128)} %bitcast.23, f32[1024]{0:T(1024)S(1)} %copy-done.3, f32[2048]{0:T(1024)S(1)} %fusion.26, f32[2048]{0:T(1024)S(1)} %broadcast_multiply_fusion, bf16[2048,2176]{0,1:T(8,128)(2,1)S(1)} %copy-done, bf16[2048,2048]{1,0:T(8,128)(2,1)} %multiply_convert_fusion, ...), kind=kOutput, calls=%fused_computation.22 | convolution fusion | flops 8610904064 | bytes 25203200 | tf_op jit(solution)/shard_map/dot_general | solution.py:174
  171.7 3.9 %fusion.15 = f32[2048]{0:T(1024)S(1)} fusion(f32[2048,1024]{0,1:T(8,128)S(1)} %get-tuple-element.43, f32[2048]{0:T(1024)S(1)} %multiply_multiply_fusion.1, f32[]{:T(128)} %bitcast.22, f32[2048]{0:T(1024)S(1)} %get-tuple-element.45, f32[1024]{0:T(1024)S(1)} %copy-done.3, f32[2048]{0:T(1024)S(1)} %fusion.26, f32[2048]{0:T(1024)S(1)} %broadcast_multiply_fusion, ...), kind=kLoop, calls=%fused_computation.23 | loop fusion | flops 25163776 | bytes 12627972 | tf_op jit(solution)/shard_map/transpose(jvp())/reduce_sum | solution.py:107
  175.6 4.6 %fusion.33 = (f32[2048]{0:T(1024)S(1)}, f32[2048,1024]{0,1:T(8,128)S(1)}) fusion(f32[2048]{0:T(1024)S(1)} %multiply_multiply_fusion, f32[2048]{0:T(1024)S(1)} %multiply_multiply_fusion.1, f32[1024]{0:T(1024)S(1)} %copy-done.3, f32[2048]{0:T(1024)S(1)} %fusion.26, f32[2048]{0:T(1024)S(1)} %broadcast_multiply_fusion, bf16[2048,2176]{0,1:T(8,128)(2,1)S(1)} %copy-done, ...), kind=kLoop, calls=%fused_computation.66 | loop fusion | flops 31455232 | bytes 21024772 | tf_op jit(solution)/shard_map/transpose(jvp())/reduce_sum | solution.py:105
  180.3 0.0 copy-start.1
  180.3 2.9 %fusion.17 = f32[256,1024]{0,1:T(8,128)} fusion(bf16[2048,256]{1,0:T(8,128)(2,1)S(1)} %bitcast.31, f32[2048,1024]{0,1:T(8,128)S(1)} %get-tuple-element.36, f32[2048]{0:T(1024)S(1)} %negate_multiply_fusion), kind=kOutput, calls=%fused_computation.27 | convolution fusion | flops 1077936128 | bytes 10493952 | tf_op jit(solution)/shard_map/dot_general | solution.py:188
  183.2 0.7 copy-done.1
  183.9 13.0 %all-to-all-start.2 = ((f32[256,16,64]{0,2,1:T(8,128)}), f32[256,16,64]{0,2,1:T(8,128)S(1)}, u32[]{:S(2)}, u32[]{:S(2)}) async-start(f32[256,16,64]{0,2,1:T(8,128)} %bitcast.11), calls=%async_computation.2 | async-start | bytes 2097152 | tf_op jit(solution)/shard_map/all_to_all | solution.py:191
  196.9 0.0 copy-start.2
  196.9 5.7 %convolution_convert_fusion = bf16[2048,256]{1,0:T(8,128)(2,1)} fusion(bf16[256,1024]{1,0:T(8,128)(2,1)S(1)} %collective-permute-done, f32[2048,1024]{0,1:T(8,128)} %copy-done.1, f32[2048]{0:T(1024)S(1)} %negate_multiply_fusion), kind=kOutput, calls=%fused_computation.26 | convolution fusion | flops 1078460416 | bytes 9969664 | tf_op jit(solution)/shard_map/dot_general | solution.py:181
  202.6 19.1 %all-to-all-done.2 = f32[256,16,64]{0,2,1:T(8,128)S(1)} async-done(((f32[256,16,64]{0,2,1:T(8,128)}), f32[256,16,64]{0,2,1:T(8,128)S(1)}, u32[]{:S(2)}, u32[]{:S(2)}) %all-to-all-start.2) | async-done | bytes 1048608 | tf_op jit(solution)/shard_map/all_to_all | solution.py:191
  221.7 11.0 %all-to-all-start.1 = ((bf16[16,128,256]{2,1,0:T(8,128)(2,1)}), bf16[16,128,256]{2,1,0:T(8,128)(2,1)S(1)}, u32[]{:S(2)}, u32[]{:S(2)}) async-start(bf16[16,128,256]{2,1,0:T(8,128)(2,1)} %bitcast.9), calls=%async_computation.1 | async-start | bytes 2097152 | tf_op jit(solution)/shard_map/all_to_all | solution.py:187
  232.7 0.0 copy-done.2
  232.7 4.2 %fusion.21 = (f32[128]{0:T(128)S(1)}, f32[128]{0:T(128)S(1)}, f32[128,1024]{1,0:T(8,128)S(1)}) fusion(bf16[128,1024]{1,0:T(8,128)(2,1)S(1)} %copy-done.2, f32[2048]{0:T(1024)S(1)} %get-tuple-element.45, f32[1024]{0:T(1024)S(1)} %copy-done.3, f32[2048]{0:T(1024)S(1)} %fusion.26, f32[2048]{0:T(1024)S(1)} %broadcast_multiply_fusion, ...), kind=kOutput, calls=%fused_computation.35 | convolution fusion | flops 550240000 | bytes 5535236 | tf_op jit(solution)/shard_map/dot_general | solution.py:171
  236.9 0.1 reduce_sum.115
  237.0 5.2 %collective-permute-start.1 = (f32[256,64]{0,1:T(8,128)S(1)}, f32[256,64]{0,1:T(8,128)S(1)}, u32[]{:S(2)}, u32[]{:S(2)}) collective-permute-start(f32[256,64]{0,1:T(8,128)S(1)} %reduce_sum.115), channel_id=1, source_target_pairs={{0,0},{1,16},{2,32},{3,48},{4,64},{5,80},{6,96},{7,112},{8,128},{9... | collective-permute-start | bytes 196616 | tf_op jit(solution)/shard_map/ppermute | solution.py:193
  242.3 1.0 add_add_fusion.2
  243.2 6.3 %all-to-all-done.1 = bf16[16,128,256]{2,1,0:T(8,128)(2,1)S(1)} async-done(((bf16[16,128,256]{2,1,0:T(8,128)(2,1)}), bf16[16,128,256]{2,1,0:T(8,128)(2,1)S(1)}, u32[]{:S(2)}, u32[]{:S(2)}) %all-to-all-start.1) | async-done | bytes 1048608 | tf_op jit(solution)/shard_map/all_to_all | solution.py:187
  249.5 1.1 copy.32
  250.6 0.0 collective-permute-done.1
  250.6 0.6 copy.37
  (8 shorter events, 0.1 us)
Async XLA Ops:
  2.9 110.7 %all-to-all-start = ((bf16[128,16,256]{0,2,1:T(8,128)(2,1)}), bf16[128,16,256]{0,2,1:T(8,128)(2,1)S(1)}, u32[]{:S(2)}, u32[]{:S(2)}) async-start(bf16[128,16,256]{0,2,1:T(8,128)(2,1)} %bitcast.1), calls=%async_computation | async-start | bytes 2097152 | tf_op jit(solution)/shard_map/all_to_all | solution.py:136
  10.5 103.6 %collective-permute-start = (bf16[256,1024]{1,0:T(8,128)(2,1)}, bf16[256,1024]{1,0:T(8,128)(2,1)S(1)}, u32[]{:S(2)}, u32[]{:S(2)}) collective-permute-start(bf16[256,1024]{1,0:T(8,128)(2,1)} %param.17), channel_id=1, source_target_pairs={{0,0},{1,16},{2,32},{3,48},{4,64},{5,80},{6,96},{7,112},{8,128},{9... | collective-permute-start | bytes 1572872 | tf_op jit(solution)/shard_map/ppermute | solution.py:139
  126.7 10.9 %copy-start = (bf16[2048,2176]{0,1:T(8,128)(2,1)S(1)}, bf16[2048,2176]{0,1:T(8,128)(2,1)}, u32[]{:S(2)}) copy-start(bf16[2048,2176]{0,1:T(8,128)(2,1)} %copy.26) | copy-start | bytes 26738692
  126.7 10.9 %copy-start.3 = (f32[1024]{0:T(1024)S(1)}, f32[1024]{0:T(1024)}, u32[]{:S(2)}) copy-start(f32[1024]{0:T(1024)} %param.16) | copy-start | bytes 12292
  180.3 3.6 %copy-start.1 = (f32[2048,1024]{0,1:T(8,128)}, f32[2048,1024]{0,1:T(8,128)S(1)}, u32[]{:S(2)}) copy-start(f32[2048,1024]{0,1:T(8,128)S(1)} %get-tuple-element.36) | copy-start | bytes 25165828
  183.9 37.8 %all-to-all-start.2 = ((f32[256,16,64]{0,2,1:T(8,128)}), f32[256,16,64]{0,2,1:T(8,128)S(1)}, u32[]{:S(2)}, u32[]{:S(2)}) async-start(f32[256,16,64]{0,2,1:T(8,128)} %bitcast.11), calls=%async_computation.2 | async-start | bytes 2097152 | tf_op jit(solution)/shard_map/all_to_all | solution.py:191
  196.9 35.9 %copy-start.2 = (bf16[128,1024]{1,0:T(8,128)(2,1)S(1)}, bf16[128,1024]{1,0:T(8,128)(2,1)}, u32[]{:S(2)}) copy-start(bf16[128,1024]{1,0:T(8,128)(2,1)} %param.12) | copy-start | bytes 786436
  221.7 27.8 %all-to-all-start.1 = ((bf16[16,128,256]{2,1,0:T(8,128)(2,1)}), bf16[16,128,256]{2,1,0:T(8,128)(2,1)S(1)}, u32[]{:S(2)}, u32[]{:S(2)}) async-start(bf16[16,128,256]{2,1,0:T(8,128)(2,1)} %bitcast.9), calls=%async_computation.1 | async-start | bytes 2097152 | tf_op jit(solution)/shard_map/all_to_all | solution.py:187
  237.0 13.6 %collective-permute-start.1 = (f32[256,64]{0,1:T(8,128)S(1)}, f32[256,64]{0,1:T(8,128)S(1)}, u32[]{:S(2)}, u32[]{:S(2)}) collective-permute-start(f32[256,64]{0,1:T(8,128)S(1)} %reduce_sum.115), channel_id=1, source_target_pairs={{0,0},{1,16},{2,32},{3,48},{4,64},{5,80},{6,96},{7,112},{8,128},{9... | collective-permute-start | bytes 196616 | tf_op jit(solution)/shard_map/ppermute | solution.py:193

commit v6 on v5

--- a/solution.py
+++ b/solution.py
@@ -97,6 +97,127 @@
     )(block)
 
 
+def tail_kernel(
+    n, hidden_ref, sums_ref, hidden_out, slots_out,
+    send_h, recv_h, send_d, recv_d, local_h, local_d,
+):
+    a = lax.axis_index("dp")
+    b = lax.axis_index("zero")
+    rows = hidden_ref.shape[0] // n
+    cols = hidden_ref.shape[1]
+    diagonal = a == b
+
+    barrier = pltpu.get_barrier_semaphore()
+    for j in range(1, n):
+        pl.semaphore_signal(barrier, inc=1, device_id=((a + j) % n, b), device_id_type=MESH)
+        pl.semaphore_signal(barrier, inc=1, device_id=((a + j) % n, a), device_id_type=MESH)
+        pl.semaphore_signal(barrier, inc=1, device_id=(b, (b + j) % n), device_id_type=MESH)
+
+    @pl.when(jnp.logical_not(diagonal))
+    def _():
+        pl.semaphore_signal(barrier, inc=1, device_id=(a, a), device_id_type=MESH)
+        pl.semaphore_signal(barrier, inc=1, device_id=(b, b), device_id_type=MESH)
+
+    pl.semaphore_wait(barrier, 3 * (n - 1) + 2 - 2 * diagonal.astype(jnp.int32))
+
+    def hidden_copy(j):
+        k = (a + j) % n
+        return pltpu.make_async_remote_copy(
+            src_ref=hidden_ref.at[pl.ds(pl.multiple_of(k * rows, rows), rows), :],
+            dst_ref=hidden_out.at[:, pl.ds(pl.multiple_of(a * cols, cols), cols)],
+            send_sem=send_h.at[j],
+            recv_sem=recv_h.at[a],
+            device_id=(k, b),
+            device_id_type=MESH,
+        )
+
+    def sum_copy(j):
+        k = (a + j) % n
+        return pltpu.make_async_remote_copy(
+            src_ref=sums_ref.at[k],
+            dst_ref=slots_out.at[b],
+            send_sem=send_d.at[j],
+            recv_sem=recv_d.at[b],
+            device_id=(k, a),
+            device_id_type=MESH,
+        )
+
+    own_hidden = pltpu.make_async_copy(
+        hidden_ref.at[pl.ds(pl.multiple_of(a * rows, rows), rows), :], hidden_out.at[:, pl.ds(pl.multiple_of(a * cols, cols), cols)], local_h
+    )
+    own_hidden.start()
+    own_sum = pltpu.make_async_copy(sums_ref.at[a], slots_out.at[b], local_d)
+
+    @pl.when(diagonal)
+    def _():
+        own_sum.start()
+
+    @pl.when(jnp.logical_not(diagonal))
+    def _():
+        sum_copy(0).start()
+
+    for j in range(1, n):
+        hidden_copy(j).start()
+        sum_copy(j).start()
+
+    for j in range(1, n):
+        k = (a + n - j) % n
+        pltpu.make_async_remote_copy(
+            src_ref=hidden_ref.at[pl.ds(0, rows), :],
+            dst_ref=hidden_out.at[:, pl.ds(pl.multiple_of(k * cols, cols), cols)],
+            send_sem=send_h.at[0],
+            recv_sem=recv_h.at[k],
+            device_id=(k, b),
+            device_id_type=MESH,
+        ).wait_recv()
+        z = (b + j) % n
+        pltpu.make_async_remote_copy(
+            src_ref=sums_ref.at[0],
+            dst_ref=slots_out.at[z],
+            send_sem=send_d.at[0],
+            recv_sem=recv_d.at[z],
+            device_id=(b, z),
+            device_id_type=MESH,
+        ).wait_recv()
+
+    @pl.when(diagonal)
+    def _():
+        own_sum.wait()
+
+    @pl.when(jnp.logical_not(diagonal))
+    def _():
+        pltpu.make_async_remote_copy(
+            src_ref=sums_ref.at[0],
+            dst_ref=slots_out.at[b],
+            send_sem=send_d.at[0],
+            recv_sem=recv_d.at[b],
+            device_id=(b, b),
+            device_id_type=MESH,
+        ).wait_recv()
+        sum_copy(0).wait_send()
+
+    for j in range(1, n):
+        hidden_copy(j).wait_send()
+        sum_copy(j).wait_send()
+    own_hidden.wait()
+
+
+def exchange_tail(hidden_part, group_sum):
+    n = lax.axis_size("dp")
+    rows = hidden_part.shape[0] // n
+    return pl.pallas_call(
+        functools.partial(tail_kernel, n),
+        out_shape=(
+            jax.ShapeDtypeStruct((rows, n * hidden_part.shape[1]), hidden_part.dtype),
+            jax.ShapeDtypeStruct(group_sum.shape, group_sum.dtype),
+        ),
+        in_specs=[pl.BlockSpec(memory_space=pl.ANY)] * 2,
+        out_specs=(pl.BlockSpec(memory_space=pl.ANY), pl.BlockSpec(memory_space=pl.ANY)),
+        scratch_shapes=[pltpu.SemaphoreType.DMA((n,))] * 4 + [pltpu.SemaphoreType.DMA(())] * 2,
+        compiler_params=pltpu.CompilerParams(collective_id=1, has_side_effects=True),
+    )(hidden_part, group_sum)
+
+
 def unit_rows(values):
     return values * lax.rsqrt(jnp.sum(values * values, axis=1, keepdims=True) + 1e-06)
 
@@ -144,9 +265,10 @@
     both = jnp.concatenate([picture_embeds, summary_token_states, digits], axis=1)
     both_g = gather_dp(both).reshape((-1, both.shape[1]))
     ffa_cols, weight_block, both_g = lax.optimization_barrier((ffa_cols, weight_block, both_g))
-    slot_g = both_g[:, 2 * width].astype(jnp.int32) * 256 + both_g[:, 2 * width + 1].astype(
-        jnp.int32
-    )
+    digit_weights = jnp.zeros((128,), jnp.float32).at[0].set(256.0).at[1].set(1.0)
+    slot_g = jnp.sum(
+        both_g[:, 2 * width :].astype(jnp.float32) * digit_weights[None, :], axis=1
+    ).astype(jnp.int32)
     image_b_g = unit_rows(both_g[:, :width].astype(jnp.float32)).astype(jnp.bfloat16)
     caption_g, caption_back = jax.vjp(
         lambda feats: text_embed(feats, closing_layernorm_multiplier),
@@ -184,13 +306,12 @@
         (((1,), (1,)), ((), ())),
         preferred_element_type=jnp.float32,
     ).astype(jnp.bfloat16)
-    hidden_grad = lax.all_to_all(hidden_part, "dp", split_axis=0, concat_axis=1, tiled=True)
     group_sum = lax.dot_general(
         ffa_cols, upstream_g, (((0,), (0,)), ((), ())), preferred_element_type=jnp.float32
     )
-    down_parts = lax.all_to_all(group_sum, "zero", split_axis=1, concat_axis=0, tiled=True)
-    down_block = jnp.sum(down_parts.reshape((zero_size,) + (group_sum.shape[0], -1)), axis=0)
-    down_grad = lax.ppermute(down_block, ("dp", "zero"), transpose_route)
+    sum_slabs = group_sum.reshape((group_sum.shape[0], dp_size, -1)).transpose((1, 0, 2))
+    hidden_grad, down_slots = exchange_tail(hidden_part, sum_slabs)
+    down_grad = jnp.sum(down_slots, axis=0)
     return (image_grad, hidden_grad, down_grad)
 
 

time: 254 us -> 360 us (1.42)
  Pallas kernels: 89 us -> 244 us
  starting transfers between devices: 43.9 us -> 14.8 us
  waiting for transfers between devices: 25.5 us -> 0.01 us
    pallas_call x0 -> x1, Pallas kernels: none -> 155 us  [exchange_tail(): pl.pallas_call(functools.partial(tail_kernel, n), out_shape=(jax.ShapeDty...]
    all_to_all x2 -> x0, waiting for transfers between devices: 25.5 us -> none  [the longest x1 19.1 us: shards(): lax.all_to_all(group_sum, 'zero', split_axis=1, concat_axis=0, tiled=True)]
    all_to_all x2 -> x0, starting transfers between devices: 23.9 us -> none  [the longest x1 13 us: shards(): lax.all_to_all(group_sum, 'zero', split_axis=1, concat_axis=0, tiled=True)]
    ppermute x1 -> x0, starting transfers between devices: 5.23 us -> none  [shards(): down_grad = lax.ppermute(down_block, ('dp', 'zero'), transpose_route)]
  transfers between devices with their start and end apart: 5 -> 2, of which waited for: 2 -> 0; matrix products, arithmetic and copies ran while one was open for 7% -> 2% of each run, Pallas kernels for 35% -> 25%
where the time goes in v6:
time: 360 us; the launch traced here: 355 us
  Pallas kernels  244 us (68%)
  matrix products  43.1 us (12%)
  other arithmetic  30 us (8%)
  local copies, waits for them, and re-layouts  21.4 us (6%)
  starting transfers between devices  14.8 us (4%)
    pallas_call x1, Pallas kernels, exchange_tail(): pl.pallas_call(functools.partial(tail_kernel, n), out_shape=(jax.ShapeDty...  155 us
    pallas_call x1, Pallas kernels, gather_dp(): pl.pallas_call(functools.partial(gather_kernel, dp_size // 2), out_shape=...  89 us
    dot_general x1, matrix products, shards(): lax.dot_general(image_b_g, caption_b_g, (((1,), (1,)), ((), ())), preferr...  17.2 us
    dot_general x1, matrix products, shards(): lax.dot_general(weights, image_b_g, (((0,), (0,)), ((), ())), preferred_e...  14.7 us
    optimization_barrier x1, local copies, waits for them, and re-layouts, shards(): lax.optimization_barrier((ffa_cols, weight_block, both_g))  12.6 us
    reduce_sum x2, other arithmetic, text_embed(): center = features - jnp.mean(features, axis=1, keepdims=True)  8.05 us
    all_to_all x1, starting transfers between devices, shards(): lax.all_to_all(feedforward_inner_activations, 'dp', split_axis=1, concat_...  7.59 us
  transfers between devices with their start and end apart: 2, of which 0 were waited for; matrix products, arithmetic and copies ran while one was open for 2% of the time, Pallas kernels for 25%

profile of v6, /device:TPU:57, one launch (start us, length us, event | category | flops | bytes accessed | tf_op | source)
XLA Modules:
  0.0 355.2 jit_solution(14595144446118145543)
XLA Ops:
  0.6 2.3 copy.26
  2.9 7.6 %all-to-all-start = ((bf16[128,16,256]{0,2,1:T(8,128)(2,1)}), bf16[128,16,256]{0,2,1:T(8,128)(2,1)S(1)}, u32[]{:S(2)}, u32[]{:S(2)}) async-start(bf16[128,16,256]{0,2,1:T(8,128)(2,1)} %bitcast.1), calls=%async_computation | async-start | bytes 2097152 | tf_op jit(solution)/shard_map/all_to_all | solution.py:257
  10.5 7.2 %collective-permute-start = (bf16[256,1024]{1,0:T(8,128)(2,1)}, bf16[256,1024]{1,0:T(8,128)(2,1)S(1)}, u32[]{:S(2)}, u32[]{:S(2)}) collective-permute-start(bf16[256,1024]{1,0:T(8,128)(2,1)} %param.21), channel_id=1, source_target_pairs={{0,0},{1,16},{2,32},{3,48},{4,64},{5,80},{6,96},{7,112},{8,128},{9... | collective-permute-start | bytes 1572872 | tf_op jit(solution)/shard_map/ppermute | solution.py:260
  17.7 0.6 compare_reduce_fusion
  18.3 0.6 compare_reduce_fusion.1
  19.0 2.0 fusion.26
  20.9 0.1 copy.28
  21.1 0.1 copy.29
  21.2 0.2 scatter.9
  21.4 1.9 pad_maximum_fusion.block_ref
  23.3 89.0 %shard_map.103 = bf16[16,128,2176]{2,1,0:T(8,128)(2,1)} custom-call(bf16[128,2176]{1,0:T(8,128)(2,1)} %pad_maximum_fusion.block_ref), custom_call_target="tpu_custom_call" | custom-call | tf_op jit(solution)/shard_map/pallas_call | solution.py:86
  113.6 0.0 all-to-all-done
  113.6 0.5 copy.27
  114.1 0.0 collective-permute-done
  114.1 12.6 %copy.30 = bf16[2048,2176]{0,1:T(8,128)(2,1)} copy(bf16[2048,2176]{1,0:T(8,128)(2,1)} %bitcast.21) | data formatting | bytes 17825792 | tf_op jit(solution)/shard_map/optimization_barrier | solution.py:267
  126.7 0.0 copy-start.5
  126.7 0.0 copy-start
  126.7 0.0 copy-start.4
  126.8 3.2 fusion.4
  130.0 3.4 convert_reduce_fusion
  133.4 3.3 fusion.6
  136.8 0.0 copy-done.5
  136.8 1.4 multiply_reduce_fusion
  138.2 0.0 copy-done
  138.2 0.0 copy-done.4
  138.2 2.2 fusion.12
  140.4 17.2 %multiply_convert_fusion = bf16[2048,2048]{1,0:T(8,128)(2,1)} fusion(f32[]{:T(128)} %bitcast.20, f32[]{:T(128)} %bitcast.16, s32[2048]{0:T(1024)S(1)} %convert_element_type.43, f32[2048]{0:T(1024)S(1)} %get-tuple-element.75, bf16[2048,2176]{1,0:T(8,128)(2,1)} %bitcast.24, f32[2048]{0:T(1024)S(1)} %get-tuple-element.76, f32[1024]{0:T(1024)S(1)} %copy-done.4, ...), kind=kOutput, calls=%fused_computation | convolution fusion | flops 8654946304 | bytes 16823296 | tf_op jit(solution)/shard_map/dot_general | solution.py:284
  157.6 14.7 %fusion.14 = (f32[2048]{0:T(1024)S(1)}, f32[2048,1024]{0,1:T(8,128)S(1)}) fusion(f32[]{:T(128)} %bitcast.19, f32[1024]{0:T(1024)S(1)} %copy-done.4, f32[2048]{0:T(1024)S(1)} %fusion.24, f32[2048]{0:T(1024)S(1)} %broadcast_multiply_fusion, bf16[2048,2176]{0,1:T(8,128)(2,1)S(1)} %copy-done, bf16[2048,2048]{1,0:T(8,128)(2,1)} %multiply_convert_fusion, ...), kind=kOutput, calls=%fused_computation.22 | convolution fusion | flops 8610904064 | bytes 25203200 | tf_op jit(solution)/shard_map/dot_general | solution.py:296
  172.3 3.9 %fusion.15 = f32[2048]{0:T(1024)S(1)} fusion(f32[2048,1024]{0,1:T(8,128)S(1)} %get-tuple-element.74, f32[2048]{0:T(1024)S(1)} %multiply_multiply_fusion.1, f32[]{:T(128)} %bitcast.18, f32[2048]{0:T(1024)S(1)} %get-tuple-element.76, f32[1024]{0:T(1024)S(1)} %copy-done.4, f32[2048]{0:T(1024)S(1)} %fusion.24, f32[2048]{0:T(1024)S(1)} %broadcast_multiply_fusion, ...), kind=kLoop, calls=%fused_computation.23 | loop fusion | flops 25163776 | bytes 12627972 | tf_op jit(solution)/shard_map/transpose(jvp())/reduce_sum | solution.py:228
  176.3 4.6 %fusion.31 = (f32[2048]{0:T(1024)S(1)}, f32[2048,1024]{0,1:T(8,128)S(1)}) fusion(f32[2048]{0:T(1024)S(1)} %multiply_multiply_fusion, f32[2048]{0:T(1024)S(1)} %multiply_multiply_fusion.1, f32[1024]{0:T(1024)S(1)} %copy-done.4, f32[2048]{0:T(1024)S(1)} %fusion.24, f32[2048]{0:T(1024)S(1)} %broadcast_multiply_fusion, bf16[2048,2176]{0,1:T(8,128)(2,1)S(1)} %copy-done, ...), kind=kLoop, calls=%fused_computation.63 | loop fusion | flops 31455232 | bytes 21024772 | tf_op jit(solution)/shard_map/transpose(jvp())/reduce_sum | solution.py:226
  180.9 0.0 copy-start.1
  180.9 1.3 fusion.17
  182.2 1.9 copy-done.1
  184.1 1.9 copy.32
  186.0 0.0 copy-start.3
  186.0 5.7 %convolution_convert_fusion.hidden_ref = bf16[2048,256]{1,0:T(8,128)(2,1)} fusion(bf16[256,1024]{1,0:T(8,128)(2,1)S(1)} %collective-permute-done, f32[2048,1024]{0,1:T(8,128)} %copy-done.1, f32[2048]{0:T(1024)S(1)} %negate_multiply_fusion), kind=kOutput, calls=%fused_computation.26 | convolution fusion | flops 1078460416 | bytes 9969664 | tf_op jit(solution)/shard_map/dot_general | solution.py:303
  191.8 154.9 %shard_map.104 = (bf16[128,4096]{1,0:T(8,128)(2,1)}, f32[16,256,64]{2,1,0:T(8,128)}) custom-call(bf16[2048,256]{1,0:T(8,128)(2,1)} %convolution_convert_fusion.hidden_ref, f32[16,256,64]{2,1,0:T(8,128)} %bitcast.26), custom_call_target="tpu_custom_call" | custom-call | tf_op jit(solution)/shard_map/pallas_call | solution.py:208
  346.6 1.7 reduce_sum.125
  348.4 0.0 copy-start.2
  348.4 0.7 copy.33
  349.1 0.0 copy-done.3
  349.1 4.2 %fusion.21 = (f32[128]{0:T(128)S(1)}, f32[128]{0:T(128)S(1)}, f32[128,1024]{1,0:T(8,128)S(1)}) fusion(bf16[128,1024]{1,0:T(8,128)(2,1)S(1)} %copy-done.3, f32[2048]{0:T(1024)S(1)} %get-tuple-element.76, f32[1024]{0:T(1024)S(1)} %copy-done.4, f32[2048]{0:T(1024)S(1)} %fusion.24, f32[2048]{0:T(1024)S(1)} %broadcast_multiply_fusion, ...), kind=kOutput, calls=%fused_computation.36 | convolution fusion | flops 550240000 | bytes 5535236 | tf_op jit(solution)/shard_map/dot_general | solution.py:293
  353.3 0.9 add_add_fusion.2
  354.3 0.0 copy-done.2
  354.3 1.0 copy.39
  (9 shorter events, 0.1 us)
Async XLA Ops:
  2.9 110.7 %all-to-all-start = ((bf16[128,16,256]{0,2,1:T(8,128)(2,1)}), bf16[128,16,256]{0,2,1:T(8,128)(2,1)S(1)}, u32[]{:S(2)}, u32[]{:S(2)}) async-start(bf16[128,16,256]{0,2,1:T(8,128)(2,1)} %bitcast.1), calls=%async_computation | async-start | bytes 2097152 | tf_op jit(solution)/shard_map/all_to_all | solution.py:257
  10.5 103.6 %collective-permute-start = (bf16[256,1024]{1,0:T(8,128)(2,1)}, bf16[256,1024]{1,0:T(8,128)(2,1)S(1)}, u32[]{:S(2)}, u32[]{:S(2)}) collective-permute-start(bf16[256,1024]{1,0:T(8,128)(2,1)} %param.21), channel_id=1, source_target_pairs={{0,0},{1,16},{2,32},{3,48},{4,64},{5,80},{6,96},{7,112},{8,128},{9... | collective-permute-start | bytes 1572872 | tf_op jit(solution)/shard_map/ppermute | solution.py:260
  126.7 10.0 %copy-start.5 = (f32[128]{0:T(128)S(1)}, f32[128]{0:T(128)}, u32[]{:S(2)}) copy-start(f32[128]{0:T(128)} %constant.156.clone.1) | copy-start | bytes 1540
  126.7 11.4 %copy-start = (bf16[2048,2176]{0,1:T(8,128)(2,1)S(1)}, bf16[2048,2176]{0,1:T(8,128)(2,1)}, u32[]{:S(2)}) copy-start(bf16[2048,2176]{0,1:T(8,128)(2,1)} %copy.30) | copy-start | bytes 26738692
  126.7 11.4 %copy-start.4 = (f32[1024]{0:T(1024)S(1)}, f32[1024]{0:T(1024)}, u32[]{:S(2)}) copy-start(f32[1024]{0:T(1024)} %param.20) | copy-start | bytes 12292
  180.9 3.2 copy-start.1
  186.0 163.1 %copy-start.3 = (bf16[128,1024]{1,0:T(8,128)(2,1)S(1)}, bf16[128,1024]{1,0:T(8,128)(2,1)}, u32[]{:S(2)}) copy-start(bf16[128,1024]{1,0:T(8,128)(2,1)} %param.16) | copy-start | bytes 786436
  348.4 5.9 %copy-start.2 = (bf16[128,4096]{1,0:T(8,128)(2,1)S(1)}, bf16[128,4096]{1,0:T(8,128)(2,1)}, u32[]{:S(2)}) copy-start(bf16[128,4096]{1,0:T(8,128)(2,1)} %get-tuple-element.81) | copy-start | bytes 3145732

commit v7 on v6

--- a/solution.py
+++ b/solution.py
@@ -103,28 +103,19 @@
 ):
     a = lax.axis_index("dp")
     b = lax.axis_index("zero")
-    rows = hidden_ref.shape[0] // n
-    cols = hidden_ref.shape[1]
-    diagonal = a == b
+    rows = hidden_out.shape[1]
 
     barrier = pltpu.get_barrier_semaphore()
     for j in range(1, n):
         pl.semaphore_signal(barrier, inc=1, device_id=((a + j) % n, b), device_id_type=MESH)
-        pl.semaphore_signal(barrier, inc=1, device_id=((a + j) % n, a), device_id_type=MESH)
-        pl.semaphore_signal(barrier, inc=1, device_id=(b, (b + j) % n), device_id_type=MESH)
-
-    @pl.when(jnp.logical_not(diagonal))
-    def _():
-        pl.semaphore_signal(barrier, inc=1, device_id=(a, a), device_id_type=MESH)
-        pl.semaphore_signal(barrier, inc=1, device_id=(b, b), device_id_type=MESH)
-
-    pl.semaphore_wait(barrier, 3 * (n - 1) + 2 - 2 * diagonal.astype(jnp.int32))
+        pl.semaphore_signal(barrier, inc=1, device_id=(a, (b + j) % n), device_id_type=MESH)
+    pl.semaphore_wait(barrier, 2 * (n - 1))
 
     def hidden_copy(j):
         k = (a + j) % n
         return pltpu.make_async_remote_copy(
             src_ref=hidden_ref.at[pl.ds(pl.multiple_of(k * rows, rows), rows), :],
-            dst_ref=hidden_out.at[:, pl.ds(pl.multiple_of(a * cols, cols), cols)],
+            dst_ref=hidden_out.at[a],
             send_sem=send_h.at[j],
             recv_sem=recv_h.at[a],
             device_id=(k, b),
@@ -132,74 +123,50 @@
         )
 
     def sum_copy(j):
-        k = (a + j) % n
+        k = (b + j) % n
         return pltpu.make_async_remote_copy(
             src_ref=sums_ref.at[k],
             dst_ref=slots_out.at[b],
             send_sem=send_d.at[j],
             recv_sem=recv_d.at[b],
-            device_id=(k, a),
+            device_id=(a, k),
             device_id_type=MESH,
         )
 
     own_hidden = pltpu.make_async_copy(
-        hidden_ref.at[pl.ds(pl.multiple_of(a * rows, rows), rows), :], hidden_out.at[:, pl.ds(pl.multiple_of(a * cols, cols), cols)], local_h
-    )
+        hidden_ref.at[pl.ds(pl.multiple_of(a * rows, rows), rows), :], hidden_out.at[a], local_h
+    )
+    own_sum = pltpu.make_async_copy(sums_ref.at[b], slots_out.at[b], local_d)
     own_hidden.start()
-    own_sum = pltpu.make_async_copy(sums_ref.at[a], slots_out.at[b], local_d)
-
-    @pl.when(diagonal)
-    def _():
-        own_sum.start()
-
-    @pl.when(jnp.logical_not(diagonal))
-    def _():
-        sum_copy(0).start()
-
+    own_sum.start()
     for j in range(1, n):
+        sum_copy(j).start()
         hidden_copy(j).start()
-        sum_copy(j).start()
 
     for j in range(1, n):
         k = (a + n - j) % n
         pltpu.make_async_remote_copy(
             src_ref=hidden_ref.at[pl.ds(0, rows), :],
-            dst_ref=hidden_out.at[:, pl.ds(pl.multiple_of(k * cols, cols), cols)],
+            dst_ref=hidden_out.at[k],
             send_sem=send_h.at[0],
             recv_sem=recv_h.at[k],
             device_id=(k, b),
             device_id_type=MESH,
         ).wait_recv()
-        z = (b + j) % n
+        z = (b + n - j) % n
         pltpu.make_async_remote_copy(
             src_ref=sums_ref.at[0],
             dst_ref=slots_out.at[z],
             send_sem=send_d.at[0],
             recv_sem=recv_d.at[z],
-            device_id=(b, z),
+            device_id=(a, z),
             device_id_type=MESH,
         ).wait_recv()
-
-    @pl.when(diagonal)
-    def _():
-        own_sum.wait()
-
-    @pl.when(jnp.logical_not(diagonal))
-    def _():
-        pltpu.make_async_remote_copy(
-            src_ref=sums_ref.at[0],
-            dst_ref=slots_out.at[b],
-            send_sem=send_d.at[0],
-            recv_sem=recv_d.at[b],
-            device_id=(b, b),
-            device_id_type=MESH,
-        ).wait_recv()
-        sum_copy(0).wait_send()
-
     for j in range(1, n):
         hidden_copy(j).wait_send()
         sum_copy(j).wait_send()
     own_hidden.wait()
+    own_sum.wait()
 
 
 def exchange_tail(hidden_part, group_sum):
@@ -208,7 +175,7 @@
     return pl.pallas_call(
         functools.partial(tail_kernel, n),
         out_shape=(
-            jax.ShapeDtypeStruct((rows, n * hidden_part.shape[1]), hidden_part.dtype),
+            jax.ShapeDtypeStruct((n, rows, hidden_part.shape[1]), hidden_part.dtype),
             jax.ShapeDtypeStruct(group_sum.shape, group_sum.dtype),
         ),
         in_specs=[pl.BlockSpec(memory_space=pl.ANY)] * 2,
@@ -309,9 +276,10 @@
     group_sum = lax.dot_general(
         ffa_cols, upstream_g, (((0,), (0,)), ((), ())), preferred_element_type=jnp.float32
     )
-    sum_slabs = group_sum.reshape((group_sum.shape[0], dp_size, -1)).transpose((1, 0, 2))
-    hidden_grad, down_slots = exchange_tail(hidden_part, sum_slabs)
-    down_grad = jnp.sum(down_slots, axis=0)
+    sum_slabs = group_sum.reshape((group_sum.shape[0], zero_size, -1)).transpose((1, 0, 2))
+    hidden_slots, down_slots = exchange_tail(hidden_part, sum_slabs)
+    hidden_grad = hidden_slots.transpose((1, 0, 2)).reshape((local_rows, -1))
+    down_grad = lax.ppermute(jnp.sum(down_slots, axis=0), ("dp", "zero"), transpose_route)
     return (image_grad, hidden_grad, down_grad)
 
 

time: 360 us -> 281 us (0.78)
  the two profiles are of different devices: /device:TPU:57 before, /device:TPU:24 now
where the time goes in v7:
time: 281 us; the launch traced here: 280 us
  Pallas kernels  155 us (55%)
  matrix products  43.1 us (15%)
  other arithmetic  30.2 us (11%)
  starting transfers between devices  27.4 us (10%)
  local copies, waits for them, and re-layouts  22.4 us (8%)
    pallas_call x1, Pallas kernels, gather_dp(): pl.pallas_call(functools.partial(gather_kernel, dp_size // 2), out_shape=...  87.8 us
    pallas_call x1, Pallas kernels, exchange_tail(): pl.pallas_call(functools.partial(tail_kernel, n), out_shape=(jax.ShapeDty...  66.9 us
    dot_general x1, matrix products, shards(): lax.dot_general(image_b_g, caption_b_g, (((1,), (1,)), ((), ())), preferr...  17.2 us
    dot_general x1, matrix products, shards(): lax.dot_general(weights, image_b_g, (((0,), (0,)), ((), ())), preferred_e...  14.7 us
    ppermute x1, starting transfers between devices, shards(): lax.ppermute(jnp.sum(down_slots, axis=0), ('dp', 'zero'), transpose_route)  12.6 us
    optimization_barrier x1, local copies, waits for them, and re-layouts, shards(): lax.optimization_barrier((ffa_cols, weight_block, both_g))  12.6 us
    reduce_sum x2, other arithmetic, text_embed(): center = features - jnp.mean(features, axis=1, keepdims=True)  8.27 us
    ppermute x1, starting transfers between devices, shards(): lax.ppermute(contracting_matrix, ('dp', 'zero'), transpose_route)  7.46 us
  transfers between devices with their start and end apart: 3, of which 0 were waited for; matrix products, arithmetic and copies ran while one was open for 5% of the time, Pallas kernels for 31%

profile of v7, /device:TPU:24, one launch (start us, length us, event | category | flops | bytes accessed | tf_op | source)
XLA Modules:
  0.0 279.9 jit_solution(10605464749633867883)
XLA Ops:
  0.6 2.3 copy.30
  2.9 7.3 %all-to-all-start = ((bf16[128,16,256]{0,2,1:T(8,128)(2,1)}), bf16[128,16,256]{0,2,1:T(8,128)(2,1)S(1)}, u32[]{:S(2)}, u32[]{:S(2)}) async-start(bf16[128,16,256]{0,2,1:T(8,128)(2,1)} %bitcast.1), calls=%async_computation | async-start | bytes 2097152 | tf_op jit(solution)/shard_map/all_to_all | solution.py:224
  10.2 7.5 %collective-permute-start = (bf16[256,1024]{1,0:T(8,128)(2,1)}, bf16[256,1024]{1,0:T(8,128)(2,1)S(1)}, u32[]{:S(2)}, u32[]{:S(2)}) collective-permute-start(bf16[256,1024]{1,0:T(8,128)(2,1)} %param.21), channel_id=1, source_target_pairs={{0,0},{1,16},{2,32},{3,48},{4,64},{5,80},{6,96},{7,112},{8,128},{9... | collective-permute-start | bytes 1572872 | tf_op jit(solution)/shard_map/ppermute | solution.py:227
  17.6 0.6 compare_reduce_fusion
  18.3 0.6 compare_reduce_fusion.1
  18.9 2.0 fusion.26
  20.9 0.1 copy.32
  21.0 0.1 copy.33
  21.2 0.2 scatter.9
  21.4 1.9 pad_maximum_fusion.block_ref
  23.2 87.8 %shard_map.103 = bf16[16,128,2176]{2,1,0:T(8,128)(2,1)} custom-call(bf16[128,2176]{1,0:T(8,128)(2,1)} %pad_maximum_fusion.block_ref), custom_call_target="tpu_custom_call" | custom-call | tf_op jit(solution)/shard_map/pallas_call | solution.py:86
  112.3 0.0 all-to-all-done
  112.4 0.5 copy.31
  112.9 0.0 collective-permute-done
  112.9 12.6 %copy.34 = bf16[2048,2176]{0,1:T(8,128)(2,1)} copy(bf16[2048,2176]{1,0:T(8,128)(2,1)} %bitcast.23) | data formatting | bytes 17825792 | tf_op jit(solution)/shard_map/optimization_barrier | solution.py:234
  125.5 0.0 copy-start.5
  125.5 0.0 copy-start
  125.5 0.0 copy-start.4
  125.5 3.2 %fusion.4 = f32[2048]{0:T(1024)S(1)} fusion(bf16[2048,2176]{1,0:T(8,128)(2,1)} %bitcast.24), kind=kLoop, calls=%fused_computation.12 | loop fusion | flops 6289408 | bytes 4202496 | tf_op jit(solution)/shard_map/reduce_sum | solution.py:189
  128.7 3.4 %convert_reduce_fusion = f32[2048]{0:T(1024)S(1)} fusion(bf16[2048,2176]{0,1:T(8,128)(2,1)} %copy.34), kind=kLoop, calls=%fused_computation.5 | loop fusion | flops 4192256 | bytes 4202496 | tf_op jit(solution)/shard_map/jvp()/reduce_sum | solution.py:193
  132.2 3.3 %fusion.6 = f32[2048]{0:T(1024)S(1)} fusion(f32[2048]{0:T(1024)S(1)} %broadcast_multiply_fusion, bf16[2048,2176]{0,1:T(8,128)(2,1)} %copy.34), kind=kLoop, calls=%fused_computation.14 | loop fusion | flops 8386560 | bytes 4210688 | tf_op jit(solution)/shard_map/jvp()/reduce_sum | solution.py:194
  135.5 0.0 copy-done.5
  135.5 1.4 multiply_reduce_fusion
  136.9 0.0 copy-done
  137.0 0.0 copy-done.4
  137.0 2.2 fusion.12
  139.2 17.2 %multiply_convert_fusion = bf16[2048,2048]{1,0:T(8,128)(2,1)} fusion(f32[]{:T(128)} %bitcast.22, f32[]{:T(128)} %bitcast.18, s32[2048]{0:T(1024)S(1)} %convert_element_type.43, f32[2048]{0:T(1024)S(1)} %get-tuple-element.81, bf16[2048,2176]{1,0:T(8,128)(2,1)} %bitcast.26, f32[2048]{0:T(1024)S(1)} %get-tuple-element.82, f32[1024]{0:T(1024)S(1)} %copy-done.4, ...), kind=kOutput, calls=%fused_computation | convolution fusion | flops 8654946304 | bytes 16823296 | tf_op jit(solution)/shard_map/dot_general | solution.py:251
  156.4 14.7 %fusion.14 = (f32[2048]{0:T(1024)S(1)}, f32[2048,1024]{0,1:T(8,128)S(1)}) fusion(f32[]{:T(128)} %bitcast.21, f32[1024]{0:T(1024)S(1)} %copy-done.4, f32[2048]{0:T(1024)S(1)} %fusion.24, f32[2048]{0:T(1024)S(1)} %broadcast_multiply_fusion, bf16[2048,2176]{0,1:T(8,128)(2,1)S(1)} %copy-done, bf16[2048,2048]{1,0:T(8,128)(2,1)} %multiply_convert_fusion, ...), kind=kOutput, calls=%fused_computation.22 | convolution fusion | flops 8610904064 | bytes 25203200 | tf_op jit(solution)/shard_map/dot_general | solution.py:263
  171.1 3.9 %fusion.15 = f32[2048]{0:T(1024)S(1)} fusion(f32[2048,1024]{0,1:T(8,128)S(1)} %get-tuple-element.80, f32[2048]{0:T(1024)S(1)} %multiply_multiply_fusion.1, f32[]{:T(128)} %bitcast.20, f32[2048]{0:T(1024)S(1)} %get-tuple-element.82, f32[1024]{0:T(1024)S(1)} %copy-done.4, f32[2048]{0:T(1024)S(1)} %fusion.24, f32[2048]{0:T(1024)S(1)} %broadcast_multiply_fusion, ...), kind=kLoop, calls=%fused_computation.23 | loop fusion | flops 25163776 | bytes 12627972 | tf_op jit(solution)/shard_map/transpose(jvp())/reduce_sum | solution.py:195
  175.0 4.8 %fusion.31 = (f32[2048]{0:T(1024)S(1)}, f32[2048,1024]{0,1:T(8,128)S(1)}) fusion(f32[2048]{0:T(1024)S(1)} %multiply_multiply_fusion, f32[2048]{0:T(1024)S(1)} %multiply_multiply_fusion.1, f32[1024]{0:T(1024)S(1)} %copy-done.4, f32[2048]{0:T(1024)S(1)} %fusion.24, f32[2048]{0:T(1024)S(1)} %broadcast_multiply_fusion, bf16[2048,2176]{0,1:T(8,128)(2,1)S(1)} %copy-done, ...), kind=kLoop, calls=%fused_computation.63 | loop fusion | flops 31455232 | bytes 21024772 | tf_op jit(solution)/shard_map/transpose(jvp())/reduce_sum | solution.py:193
  179.9 0.0 copy-start.1
  179.9 1.3 fusion.17
  181.2 1.9 copy-done.1
  183.1 1.9 copy.36
  185.0 0.0 copy-start.3
  185.0 5.7 %convolution_convert_fusion.hidden_ref = bf16[2048,256]{1,0:T(8,128)(2,1)} fusion(bf16[256,1024]{1,0:T(8,128)(2,1)S(1)} %collective-permute-done, f32[2048,1024]{0,1:T(8,128)} %copy-done.1, f32[2048]{0:T(1024)S(1)} %negate_multiply_fusion), kind=kOutput, calls=%fused_computation.26 | convolution fusion | flops 1078460416 | bytes 9969664 | tf_op jit(solution)/shard_map/dot_general | solution.py:270
  190.8 66.9 %shard_map.104 = (bf16[16,128,256]{2,1,0:T(8,128)(2,1)}, f32[16,256,64]{2,1,0:T(8,128)}) custom-call(bf16[2048,256]{1,0:T(8,128)(2,1)} %convolution_convert_fusion.hidden_ref, f32[16,256,64]{2,1,0:T(8,128)} %bitcast.28), custom_call_target="tpu_custom_call" | custom-call | tf_op jit(solution)/shard_map/pallas_call | solution.py:175
  257.6 1.7 reduce_sum.125
  259.4 0.0 copy-start.2
  259.4 12.6 %collective-permute-start.1 = (f32[256,64]{1,0:T(8,128)S(1)}, f32[256,64]{1,0:T(8,128)S(1)}, u32[]{:S(2)}, u32[]{:S(2)}) collective-permute-start(f32[256,64]{1,0:T(8,128)S(1)} %reduce_sum.125), channel_id=1, source_target_pairs={{0,0},{1,16},{2,32},{3,48},{4,64},{5,80},{6,96},{7,112},{8,128},{9... | collective-permute-start | bytes 196616 | tf_op jit(solution)/shard_map/ppermute | solution.py:282
  272.0 0.0 copy-done.3
  272.0 4.2 %fusion.21 = (f32[128]{0:T(128)S(1)}, f32[128]{0:T(128)S(1)}, f32[128,1024]{1,0:T(8,128)S(1)}) fusion(bf16[128,1024]{1,0:T(8,128)(2,1)S(1)} %copy-done.3, f32[2048]{0:T(1024)S(1)} %get-tuple-element.82, f32[1024]{0:T(1024)S(1)} %copy-done.4, f32[2048]{0:T(1024)S(1)} %fusion.24, f32[2048]{0:T(1024)S(1)} %broadcast_multiply_fusion, ...), kind=kOutput, calls=%fused_computation.36 | convolution fusion | flops 550240000 | bytes 5535236 | tf_op jit(solution)/shard_map/dot_general | solution.py:260
  276.3 0.9 add_add_fusion.2
  277.2 0.0 copy-done.2
  277.2 0.7 copy.37
  277.9 1.3 copy.38
  279.2 0.0 collective-permute-done.1
  279.2 0.7 copy.39
  (9 shorter events, 0.1 us)
Async XLA Ops:
  2.9 109.5 %all-to-all-start = ((bf16[128,16,256]{0,2,1:T(8,128)(2,1)}), bf16[128,16,256]{0,2,1:T(8,128)(2,1)S(1)}, u32[]{:S(2)}, u32[]{:S(2)}) async-start(bf16[128,16,256]{0,2,1:T(8,128)(2,1)} %bitcast.1), calls=%async_computation | async-start | bytes 2097152 | tf_op jit(solution)/shard_map/all_to_all | solution.py:224
  10.2 102.7 %collective-permute-start = (bf16[256,1024]{1,0:T(8,128)(2,1)}, bf16[256,1024]{1,0:T(8,128)(2,1)S(1)}, u32[]{:S(2)}, u32[]{:S(2)}) collective-permute-start(bf16[256,1024]{1,0:T(8,128)(2,1)} %param.21), channel_id=1, source_target_pairs={{0,0},{1,16},{2,32},{3,48},{4,64},{5,80},{6,96},{7,112},{8,128},{9... | collective-permute-start | bytes 1572872 | tf_op jit(solution)/shard_map/ppermute | solution.py:227
  125.5 10.0 %copy-start.5 = (f32[128]{0:T(128)S(1)}, f32[128]{0:T(128)}, u32[]{:S(2)}) copy-start(f32[128]{0:T(128)} %constant.156.clone.1) | copy-start | bytes 1540
  125.5 11.4 %copy-start = (bf16[2048,2176]{0,1:T(8,128)(2,1)S(1)}, bf16[2048,2176]{0,1:T(8,128)(2,1)}, u32[]{:S(2)}) copy-start(bf16[2048,2176]{0,1:T(8,128)(2,1)} %copy.34) | copy-start | bytes 26738692
  125.5 11.4 %copy-start.4 = (f32[1024]{0:T(1024)S(1)}, f32[1024]{0:T(1024)}, u32[]{:S(2)}) copy-start(f32[1024]{0:T(1024)} %param.20) | copy-start | bytes 12292
  179.9 3.2 %copy-start.1 = (f32[2048,1024]{0,1:T(8,128)}, f32[2048,1024]{0,1:T(8,128)S(1)}, u32[]{:S(2)}) copy-start(f32[2048,1024]{0,1:T(8,128)S(1)} %get-tuple-element.73) | copy-start | bytes 25165828
  185.0 87.0 %copy-start.3 = (bf16[128,1024]{1,0:T(8,128)(2,1)S(1)}, bf16[128,1024]{1,0:T(8,128)(2,1)}, u32[]{:S(2)}) copy-start(bf16[128,1024]{1,0:T(8,128)(2,1)} %param.16) | copy-start | bytes 786436
  259.4 17.8 %copy-start.2 = (bf16[16,128,256]{2,1,0:T(8,128)(2,1)S(1)}, bf16[16,128,256]{2,1,0:T(8,128)(2,1)}, u32[]{:S(2)}) copy-start(bf16[16,128,256]{2,1,0:T(8,128)(2,1)} %get-tuple-element.59) | copy-start | bytes 3145732
  259.4 19.8 %collective-permute-start.1 = (f32[256,64]{1,0:T(8,128)S(1)}, f32[256,64]{1,0:T(8,128)S(1)}, u32[]{:S(2)}, u32[]{:S(2)}) collective-permute-start(f32[256,64]{1,0:T(8,128)S(1)} %reduce_sum.125), channel_id=1, source_target_pairs={{0,0},{1,16},{2,32},{3,48},{4,64},{5,80},{6,96},{7,112},{8,128},{9... | collective-permute-start | bytes 196616 | tf_op jit(solution)/shard_map/ppermute | solution.py:282

commit v8 on v5

--- a/solution.py
+++ b/solution.py
@@ -97,6 +97,84 @@
     )(block)
 
 
+def contrast_kernel(
+    scale_ref, shift_ref, own_slot_ref, slot_ref, images_ref, captions_ref,
+    caption_out, image_out,
+):
+    jb = pl.program_id(0)
+    tc = captions_ref.shape[0]
+    rows = own_slot_ref.shape[0]
+    chunk = 512
+    scale = scale_ref[0]
+    shift = shift_ref[0]
+    captions = captions_ref[...]
+    places = jb * tc + lax.broadcasted_iota(jnp.int32, (tc, 1), 0)
+
+    def weights_of(scores, positive):
+        labels = jnp.where(positive, 1.0, -1.0)
+        return (-labels * jax.nn.sigmoid(-labels * scores)).astype(jnp.bfloat16)
+
+    def body(ib, acc):
+        start = pl.multiple_of(ib * chunk, chunk)
+        images = images_ref[pl.ds(start, chunk), :]
+        scores = scale * lax.dot_general(
+            captions, images, (((1,), (1,)), ((), ())), preferred_element_type=jnp.float32
+        ) + shift
+        weights = weights_of(scores, slot_ref[:, pl.ds(start, chunk)] == places)
+        return acc + jnp.dot(weights, images, preferred_element_type=jnp.float32)
+
+    acc = lax.fori_loop(
+        0, images_ref.shape[0] // chunk, body, jnp.zeros(caption_out.shape, jnp.float32)
+    )
+    caption_out[...] = scale * acc
+
+    own_start = pl.multiple_of(lax.axis_index("dp") * rows, rows)
+    own = images_ref[pl.ds(own_start, rows), :]
+    own_scores = scale * lax.dot_general(
+        own, captions, (((1,), (1,)), ((), ())), preferred_element_type=jnp.float32
+    ) + shift
+    columns = jb * tc + lax.broadcasted_iota(jnp.int32, (1, tc), 1)
+    own_weights = weights_of(own_scores, own_slot_ref[...] == columns)
+
+    @pl.when(jb == 0)
+    def _():
+        image_out[...] = jnp.zeros_like(image_out)
+
+    image_out[...] += scale * jnp.dot(own_weights, captions, preferred_element_type=jnp.float32)
+
+
+def contrast_group(scale, shift, own_slot, slot_g, image_b_g, caption_b_g):
+    group_rows, width = caption_b_g.shape
+    rows = own_slot.shape[0]
+    tc = 256
+    return pl.pallas_call(
+        contrast_kernel,
+        grid=(group_rows // tc,),
+        out_shape=(
+            jax.ShapeDtypeStruct((group_rows, width), jnp.float32),
+            jax.ShapeDtypeStruct((rows, width), jnp.float32),
+        ),
+        in_specs=[
+            pl.BlockSpec(memory_space=pltpu.SMEM),
+            pl.BlockSpec(memory_space=pltpu.SMEM),
+            pl.BlockSpec((rows, 1), lambda j: (0, 0)),
+            pl.BlockSpec((1, group_rows), lambda j: (0, 0)),
+            pl.BlockSpec((group_rows, width), lambda j: (0, 0)),
+            pl.BlockSpec((tc, width), lambda j: (j, 0)),
+        ],
+        out_specs=(
+            pl.BlockSpec((tc, width), lambda j: (j, 0)),
+            pl.BlockSpec((rows, width), lambda j: (0, 0)),
+        ),
+        compiler_params=pltpu.CompilerParams(dimension_semantics=("arbitrary",)),
+        cost_estimate=pl.CostEstimate(
+            flops=4 * group_rows * (group_rows + rows) * width,
+            bytes_accessed=2 * group_rows * width * 2 + (group_rows + rows) * width * 4,
+            transcendentals=group_rows * (group_rows + rows),
+        ),
+    )(scale, shift, own_slot.reshape((rows, 1)), slot_g.reshape((1, group_rows)), image_b_g, caption_b_g)
+
+
 def unit_rows(values):
     return values * lax.rsqrt(jnp.sum(values * values, axis=1, keepdims=True) + 1e-06)
 
@@ -157,22 +235,8 @@
 
     unit_image, image_back = jax.vjp(unit_rows, picture_embeds.astype(jnp.float32))
 
-    scores = (
-        similarity_multiplier
-        * lax.dot_general(
-            image_b_g, caption_b_g, (((1,), (1,)), ((), ())), preferred_element_type=jnp.float32
-        )
-        + shift_value
-    )
-    places = jnp.arange(group_rows, dtype=jnp.int32)
-    labels = jnp.where(slot_g[:, None] == places[None, :], 1.0, -1.0)
-    weights = sigmoid_weights(scores, labels)
-    own_weights = lax.dynamic_slice_in_dim(weights, own_start, local_rows, axis=0)
-    image_term = similarity_multiplier * jnp.dot(
-        own_weights, caption_b_g, preferred_element_type=jnp.float32
-    )
-    caption_term = similarity_multiplier * lax.dot_general(
-        weights, image_b_g, (((0,), (0,)), ((), ())), preferred_element_type=jnp.float32
+    caption_term, image_term = contrast_group(
+        sharpness_factor, additive_shift_learned, matched_slot, slot_g, image_b_g, caption_b_g
     )
 
     image_grad = image_back(image_term)[0]

time: 254 us -> 269 us (1.059)
  Pallas kernels: 89 us -> 130 us
  matrix products: 44.7 us -> 9.02 us
  other arithmetic: 27.7 us -> 41 us
  local copies, waits for them, and re-layouts: 18.3 us -> 10.8 us
  waiting for transfers between devices: 25.5 us -> 31.9 us
    pallas_call x0 -> x1, Pallas kernels: none -> 43.8 us  [contrast_group(): pl.pallas_call(contrast_kernel, grid=(group_rows // tc,), out_shape=(jax....]
    dot_general x3 -> x0, matrix products: 36 us -> none  [the longest x1 17.1 us: shards(): lax.dot_general(image_b_g, caption_b_g, (((1,), (1,)), ((), ())), preferr...]
    optimization_barrier x1 -> x0, local copies, waits for them, and re-layouts: 12.6 us -> none  [shards(): lax.optimization_barrier((ffa_cols, weight_block, both_g))]
    all_to_all x1, waiting for transfers between devices: 6.32 us -> 12.7 us  [shards(): lax.all_to_all(hidden_part, 'dp', split_axis=0, concat_axis=1, tiled=True)]
    reduce_sum x0 -> x1, other arithmetic: none -> 5.84 us  [unit_rows(): values * lax.rsqrt(jnp.sum(values * values, axis=1, keepdims=True) + 1e-06)]
    convert_element_type x0 -> x1, other arithmetic: none -> 4.89 us  [shards(): caption_b_g = caption_g.astype(jnp.bfloat16)]
    unnamed x10 -> x18, local copies, waits for them, and re-layouts: 3.65 us -> 7.3 us
    pallas_call x1, Pallas kernels: 89 us -> 85.7 us  [gather_dp(): pl.pallas_call(functools.partial(gather_kernel, dp_size // 2), out_shape=...]
  transfers between devices with their start and end apart: 5 -> 5, of which waited for: 2 -> 2; matrix products, arithmetic and copies ran while one was open for 7% -> 6% of each run, Pallas kernels for 35% -> 32%
where the time goes in v8:
time: 269 us
  Pallas kernels  130 us (48%)
  starting transfers between devices  44.5 us (17%)
  other arithmetic  41 us (15%)
  waiting for transfers between devices  31.9 us (12%)
  local copies, waits for them, and re-layouts  10.8 us (4%)
  matrix products  9.02 us (3%)
    pallas_call x1, Pallas kernels, gather_dp(): pl.pallas_call(functools.partial(gather_kernel, dp_size // 2), out_shape=...  85.7 us
    pallas_call x1, Pallas kernels, contrast_group(): pl.pallas_call(contrast_kernel, grid=(group_rows // tc,), out_shape=(jax....  43.8 us
    all_to_all x1, waiting for transfers between devices, shards(): lax.all_to_all(group_sum, 'zero', split_axis=1, concat_axis=0, tiled=True)  19.1 us
    all_to_all x1, starting transfers between devices, shards(): lax.all_to_all(hidden_part, 'dp', split_axis=0, concat_axis=1, tiled=True)  12.8 us
    all_to_all x1, waiting for transfers between devices, shards(): lax.all_to_all(hidden_part, 'dp', split_axis=0, concat_axis=1, tiled=True)  12.7 us
    all_to_all x1, starting transfers between devices, shards(): lax.all_to_all(group_sum, 'zero', split_axis=1, concat_axis=0, tiled=True)  11.7 us
    reduce_sum x2, other arithmetic, text_embed(): center = features - jnp.mean(features, axis=1, keepdims=True)  9.66 us
    all_to_all x1, starting transfers between devices, shards(): lax.all_to_all(feedforward_inner_activations, 'dp', split_axis=1, concat_...  7.59 us
  transfers between devices with their start and end apart: 5, of which 2 were waited for; matrix products, arithmetic and copies ran while one was open for 6% of the time, Pallas kernels for 32%

profile of v8, /device:TPU:57, one launch (start us, length us, event | category | flops | bytes accessed | tf_op | source)
XLA Modules:
  0.0 268.8 jit_solution(5933342904835349946)
XLA Ops:
  0.6 2.3 copy.20
  2.9 7.6 %all-to-all-start = ((bf16[128,16,256]{0,2,1:T(8,128)(2,1)}), bf16[128,16,256]{0,2,1:T(8,128)(2,1)S(1)}, u32[]{:S(2)}, u32[]{:S(2)}) async-start(bf16[128,16,256]{0,2,1:T(8,128)(2,1)} %bitcast.1), calls=%async_computation | async-start | bytes 2097152 | tf_op jit(solution)/shard_map/all_to_all | solution.py:214
  10.5 7.2 %collective-permute-start = (bf16[256,1024]{1,0:T(8,128)(2,1)}, bf16[256,1024]{1,0:T(8,128)(2,1)S(1)}, u32[]{:S(2)}, u32[]{:S(2)}) collective-permute-start(bf16[256,1024]{1,0:T(8,128)(2,1)} %param.17), channel_id=1, source_target_pairs={{0,0},{1,16},{2,32},{3,48},{4,64},{5,80},{6,96},{7,112},{8,128},{9... | collective-permute-start | bytes 1572872 | tf_op jit(solution)/shard_map/ppermute | solution.py:217
  19.0 0.6 compare_reduce_fusion.1
  19.6 0.6 compare_reduce_fusion
  20.3 2.0 fusion.21
  22.2 0.1 copy.23
  22.3 0.1 copy.22
  22.5 1.4 copy.24.own_slot_ref
  23.9 0.2 scatter.9
  24.1 1.9 pad_maximum_fusion.block_ref
  26.0 85.7 %shard_map.103 = bf16[16,128,2176]{2,1,0:T(8,128)(2,1)} custom-call(bf16[128,2176]{1,0:T(8,128)(2,1)} %pad_maximum_fusion.block_ref), custom_call_target="tpu_custom_call" | custom-call | tf_op jit(solution)/shard_map/pallas_call | solution.py:86
  111.7 0.0 all-to-all-done
  111.7 0.5 copy.21
  112.2 0.0 copy-start
  112.3 0.0 collective-permute-done
  112.3 0.0 copy-start.6
  112.3 3.0 %convert_reduce_fusion = f32[2048]{0:T(1024)S(1)} fusion(bf16[2048,2176]{1,0:T(8,128)(2,1)} %bitcast.17), kind=kLoop, calls=%fused_computation.3 | loop fusion | flops 4192256 | bytes 4202496 | tf_op jit(solution)/shard_map/jvp()/reduce_sum | solution.py:183
  115.3 3.0 %add_reduce_fusion = s32[2048]{0:T(1024)} fusion(bf16[2048,2176]{1,0:T(8,128)(2,1)} %bitcast.18), kind=kLoop, calls=%fused_computation.25 | loop fusion | flops 8192 | bytes 16384 | tf_op jit(solution)/shard_map/add | solution.py:225
  118.3 3.0 %fusion.6 = f32[2048]{0:T(1024)S(1)} fusion(f32[2048]{0:T(1024)S(1)} %broadcast_multiply_fusion, bf16[2048,2176]{1,0:T(8,128)(2,1)} %bitcast.19), kind=kLoop, calls=%fused_computation.12 | loop fusion | flops 8386560 | bytes 4210688 | tf_op jit(solution)/shard_map/jvp()/reduce_sum | solution.py:184
  121.3 0.0 copy-done.5
  121.3 0.0 copy-done
  121.3 2.8 %fusion.12 = (f32[2048]{0:T(1024)S(1)}, f32[2048]{0:T(1024)S(1)}) fusion(f32[1024]{0:T(1024)S(1)} %copy-done.5, f32[2048]{0:T(1024)S(1)} %fusion.19, f32[2048]{0:T(1024)S(1)} %broadcast_multiply_fusion, bf16[2048,2176]{1,0:T(8,128)(2,1)S(1)} %bitcast.23), kind=kLoop, calls=%fused_computation.18 | loop fusion | flops 18870272 | bytes 8425472 | tf_op jit(solution)/shard_map/jvp()/reduce_sum | solution.py:179
  124.1 0.0 copy-done.6
  124.2 4.9 %fusion.13 = (bf16[2048,1024]{1,0:T(8,128)(2,1)}, bf16[2048,1024]{1,0:T(8,128)(2,1)}) fusion(f32[2048]{0:T(1024)S(1)} %get-tuple-element.50, f32[1024]{0:T(1024)S(1)} %copy-done.5, f32[2048]{0:T(1024)S(1)} %fusion.19, f32[2048]{0:T(1024)S(1)} %broadcast_multiply_fusion, bf16[2048,2176]{1,0:T(8,128)(2,1)S(1)} %bitcast.24, f32[2048]{0:T(1024)S(1)} %get-tuple-element.49), kind=kLoop, calls=%fused_computation.19 | loop fusion | flops 18874368 | bytes 16814080 | tf_op jit(solution)/shard_map/convert_element_type | solution.py:233
  129.0 43.8 %shard_map.104 = (f32[2048,1024]{1,0:T(8,128)}, f32[128,1024]{1,0:T(8,128)}) custom-call(f32[1]{0:T(128)S(6)} %copy.31.scale_ref, f32[1]{0:T(128)S(6)} %copy.32.shift_ref, s32[128,1]{1,0:T(8,128)} %copy.24.own_slot_ref, s32[1,2048]{1,0:T(1,128)} %bitcast.30, bf16[2048,1024]{1,0:T(8,128)(2,1)} %get-tuple-element.44.images_ref, ...), custom_call_target="tpu_custom_call" | custom-call | flops 18253611008 | bytes 17301504 | tf_op jit(solution)/shard_map/pallas_call | solution.py:150
  172.9 5.8 %fusion.14 = f32[2048]{0:T(1024)S(1)} fusion(f32[2048,1024]{1,0:T(8,128)} %get-tuple-element.34, f32[1024]{0:T(1024)S(1)} %copy-done.5, f32[2048]{0:T(1024)S(1)} %fusion.19, f32[2048]{0:T(1024)S(1)} %broadcast_multiply_fusion, bf16[2048,2176]{1,0:T(8,128)(2,1)} %bitcast.20), kind=kLoop, calls=%fused_computation.20 | loop fusion | flops 12580864 | bytes 12611584 | tf_op jit(solution)/shard_map/transpose(jvp())/reduce_sum | solution.py:179
  178.8 1.2 copy-done.1
  179.9 5.4 %fusion.15 = f32[2048]{0:T(1024)S(1)} fusion(f32[2048,1024]{1,0:T(8,128)S(1)} %copy-done.1, f32[2048]{0:T(1024)S(1)} %multiply_multiply_fusion.1, f32[2048]{0:T(1024)S(1)} %get-tuple-element.50, f32[1024]{0:T(1024)S(1)} %copy-done.5, f32[2048]{0:T(1024)S(1)} %fusion.19, f32[2048]{0:T(1024)S(1)} %broadcast_multiply_fusion, bf16[2048,2176]{1,0:T(8,128)(2,1)} %bitcast.21), kind=kLoop, calls=%fused_computation.21 | loop fusion | flops 23066624 | bytes 12627968 | tf_op jit(solution)/shard_map/transpose(jvp())/reduce_sum | solution.py:185
  185.4 6.6 %fusion.24 = (f32[2048]{0:T(1024)S(1)}, f32[2048,1024]{1,0:T(8,128)S(1)}) fusion(f32[2048]{0:T(1024)S(1)} %multiply_multiply_fusion, f32[2048]{0:T(1024)S(1)} %multiply_multiply_fusion.1, f32[1024]{0:T(1024)S(1)} %copy-done.5, f32[2048]{0:T(1024)S(1)} %fusion.19, f32[2048]{0:T(1024)S(1)} %broadcast_multiply_fusion, bf16[2048,2176]{1,0:T(8,128)(2,1)} %bitcast.22, ...), kind=kLoop, calls=%fused_computation.57 | loop fusion | flops 29358080 | bytes 21024768 | tf_op jit(solution)/shard_map/transpose(jvp())/reduce_sum | solution.py:183
  192.0 0.0 copy-start.7
  192.1 3.2 %copy-done.2 = f32[2048,1024]{1,0:T(8,128)} copy-done((f32[2048,1024]{1,0:T(8,128)}, f32[2048,1024]{1,0:T(8,128)S(1)}, u32[]{:S(2)}) %copy-start.2) | copy-done | bytes 8388632
  195.2 3.3 %fusion.23 = f32[256,1024]{0,1:T(8,128)} fusion(bf16[2048,256]{1,0:T(8,128)(2,1)S(1)} %bitcast.27, f32[2048,1024]{1,0:T(8,128)S(1)} %get-tuple-element.42, f32[2048]{0:T(1024)S(1)} %negate_multiply_fusion), kind=kOutput, calls=%fused_computation.56 | convolution fusion | flops 1077936128 | bytes 10493952 | tf_op jit(solution)/shard_map/dot_general | solution.py:252
  198.5 11.7 %all-to-all-start.2 = ((f32[256,16,64]{0,2,1:T(8,128)}), f32[256,16,64]{0,2,1:T(8,128)S(1)}, u32[]{:S(2)}, u32[]{:S(2)}) async-start(f32[256,16,64]{0,2,1:T(8,128)} %bitcast.9), calls=%async_computation.2 | async-start | bytes 2097152 | tf_op jit(solution)/shard_map/all_to_all | solution.py:255
  210.3 0.0 copy-start.3
  210.3 0.0 copy-start.4
  210.3 5.7 %convolution_convert_fusion = bf16[2048,256]{1,0:T(8,128)(2,1)} fusion(bf16[256,1024]{1,0:T(8,128)(2,1)S(1)} %copy-done.7, f32[2048,1024]{1,0:T(8,128)} %copy-done.2, f32[2048]{0:T(1024)S(1)} %negate_multiply_fusion), kind=kOutput, calls=%fused_computation.24 | convolution fusion | flops 1078460416 | bytes 9969664 | tf_op jit(solution)/shard_map/dot_general | solution.py:245
  216.0 19.1 %all-to-all-done.2 = f32[256,16,64]{0,2,1:T(8,128)S(1)} async-done(((f32[256,16,64]{0,2,1:T(8,128)}), f32[256,16,64]{0,2,1:T(8,128)S(1)}, u32[]{:S(2)}, u32[]{:S(2)}) %all-to-all-start.2) | async-done | bytes 1048608 | tf_op jit(solution)/shard_map/all_to_all | solution.py:255
  235.1 12.8 %all-to-all-start.1 = ((bf16[16,128,256]{2,1,0:T(8,128)(2,1)}), bf16[16,128,256]{2,1,0:T(8,128)(2,1)S(1)}, u32[]{:S(2)}, u32[]{:S(2)}) async-start(bf16[16,128,256]{2,1,0:T(8,128)(2,1)} %bitcast.28), calls=%async_computation.1 | async-start | bytes 2097152 | tf_op jit(solution)/shard_map/all_to_all | solution.py:251
  247.9 0.0 copy-done.3
  247.9 0.2 fusion.17
  248.1 0.1 reduce_sum.115
  248.2 5.2 %collective-permute-start.1 = (f32[256,64]{0,1:T(8,128)S(1)}, f32[256,64]{0,1:T(8,128)S(1)}, u32[]{:S(2)}, u32[]{:S(2)}) collective-permute-start(f32[256,64]{0,1:T(8,128)S(1)} %reduce_sum.115), channel_id=1, source_target_pairs={{0,0},{1,16},{2,32},{3,48},{4,64},{5,80},{6,96},{7,112},{8,128},{9... | collective-permute-start | bytes 196616 | tf_op jit(solution)/shard_map/ppermute | solution.py:257
  253.4 0.9 add_add_fusion.2
  254.4 12.7 %all-to-all-done.1 = bf16[16,128,256]{2,1,0:T(8,128)(2,1)S(1)} async-done(((bf16[16,128,256]{2,1,0:T(8,128)(2,1)}), bf16[16,128,256]{2,1,0:T(8,128)(2,1)S(1)}, u32[]{:S(2)}, u32[]{:S(2)}) %all-to-all-start.1) | async-done | bytes 1048608 | tf_op jit(solution)/shard_map/all_to_all | solution.py:251
  267.1 1.1 copy.28
  268.2 0.0 collective-permute-done.1
  268.2 0.6 copy.33
  (13 shorter events, 0.1 us)
Async XLA Ops:
  2.9 108.8 %all-to-all-start = ((bf16[128,16,256]{0,2,1:T(8,128)(2,1)}), bf16[128,16,256]{0,2,1:T(8,128)(2,1)S(1)}, u32[]{:S(2)}, u32[]{:S(2)}) async-start(bf16[128,16,256]{0,2,1:T(8,128)(2,1)} %bitcast.1), calls=%async_computation | async-start | bytes 2097152 | tf_op jit(solution)/shard_map/all_to_all | solution.py:214
  10.5 101.8 %collective-permute-start = (bf16[256,1024]{1,0:T(8,128)(2,1)}, bf16[256,1024]{1,0:T(8,128)(2,1)S(1)}, u32[]{:S(2)}, u32[]{:S(2)}) collective-permute-start(bf16[256,1024]{1,0:T(8,128)(2,1)} %param.17), channel_id=1, source_target_pairs={{0,0},{1,16},{2,32},{3,48},{4,64},{5,80},{6,96},{7,112},{8,128},{9... | collective-permute-start | bytes 1572872 | tf_op jit(solution)/shard_map/ppermute | solution.py:217
  26.0 95.3 %copy-start.5 = (f32[1024]{0:T(1024)S(1)}, f32[1024]{0:T(1024)}, u32[]{:S(2)}) copy-start(f32[1024]{0:T(1024)} %param.16) | copy-start | bytes 12292
  112.2 9.0 %copy-start = (bf16[16,128,2176]{2,1,0:T(8,128)(2,1)S(1)}, bf16[16,128,2176]{2,1,0:T(8,128)(2,1)}, u32[]{:S(2)}) copy-start(bf16[16,128,2176]{2,1,0:T(8,128)(2,1)} %shard_map.103) | copy-start | bytes 26738692
  112.3 11.9 %copy-start.6 = (bf16[256,1024]{1,0:T(8,128)(2,1)}, bf16[256,1024]{1,0:T(8,128)(2,1)S(1)}, u32[]{:S(2)}) copy-start(bf16[256,1024]{1,0:T(8,128)(2,1)S(1)} %collective-permute-done) | copy-start | bytes 1572868
  172.9 7.1 %copy-start.1 = (f32[2048,1024]{1,0:T(8,128)S(1)}, f32[2048,1024]{1,0:T(8,128)}, u32[]{:S(2)}) copy-start(f32[2048,1024]{1,0:T(8,128)} %get-tuple-element.34) | copy-start | bytes 25165828
  192.0 3.2 %copy-start.2 = (f32[2048,1024]{1,0:T(8,128)}, f32[2048,1024]{1,0:T(8,128)S(1)}, u32[]{:S(2)}) copy-start(f32[2048,1024]{1,0:T(8,128)S(1)} %get-tuple-element.42) | copy-start | bytes 25165828
  192.0 18.2 %copy-start.7 = (bf16[256,1024]{1,0:T(8,128)(2,1)S(1)}, bf16[256,1024]{1,0:T(8,128)(2,1)}, u32[]{:S(2)}) copy-start(bf16[256,1024]{1,0:T(8,128)(2,1)} %copy-done.6) | copy-start | bytes 1572868
  198.5 36.6 %all-to-all-start.2 = ((f32[256,16,64]{0,2,1:T(8,128)}), f32[256,16,64]{0,2,1:T(8,128)S(1)}, u32[]{:S(2)}, u32[]{:S(2)}) async-start(f32[256,16,64]{0,2,1:T(8,128)} %bitcast.9), calls=%async_computation.2 | async-start | bytes 2097152 | tf_op jit(solution)/shard_map/all_to_all | solution.py:255
  210.3 37.7 %copy-start.3 = (bf16[128,1024]{1,0:T(8,128)(2,1)S(1)}, bf16[128,1024]{1,0:T(8,128)(2,1)}, u32[]{:S(2)}) copy-start(bf16[128,1024]{1,0:T(8,128)(2,1)} %param.12) | copy-start | bytes 786436
  210.3 37.7 %copy-start.4 = (f32[128,1024]{1,0:T(8,128)S(1)}, f32[128,1024]{1,0:T(8,128)}, u32[]{:S(2)}) copy-start(f32[128,1024]{1,0:T(8,128)} %get-tuple-element.33) | copy-start | bytes 1572868
  235.1 32.0 %all-to-all-start.1 = ((bf16[16,128,256]{2,1,0:T(8,128)(2,1)}), bf16[16,128,256]{2,1,0:T(8,128)(2,1)S(1)}, u32[]{:S(2)}, u32[]{:S(2)}) async-start(bf16[16,128,256]{2,1,0:T(8,128)(2,1)} %bitcast.28), calls=%async_computation.1 | async-start | bytes 2097152 | tf_op jit(solution)/shard_map/all_to_all | solution.py:251
  248.2 20.0 %collective-permute-start.1 = (f32[256,64]{0,1:T(8,128)S(1)}, f32[256,64]{0,1:T(8,128)S(1)}, u32[]{:S(2)}, u32[]{:S(2)}) collective-permute-start(f32[256,64]{0,1:T(8,128)S(1)} %reduce_sum.115), channel_id=1, source_target_pairs={{0,0},{1,16},{2,32},{3,48},{4,64},{5,80},{6,96},{7,112},{8,128},{9... | collective-permute-start | bytes 196616 | tf_op jit(solution)/shard_map/ppermute | solution.py:257

commit v9 on v8

--- a/solution.py
+++ b/solution.py
@@ -98,12 +98,12 @@
 
 
 def contrast_kernel(
-    scale_ref, shift_ref, own_slot_ref, slot_ref, images_ref, captions_ref,
+    scale_ref, shift_ref, own_slot_ref, slot_ref, images_ref, images_t_ref, captions_ref,
     caption_out, image_out,
 ):
     jb = pl.program_id(0)
     tc = captions_ref.shape[0]
-    rows = own_slot_ref.shape[0]
+    rows = own_slot_ref.shape[1]
     chunk = 512
     scale = scale_ref[0]
     shift = shift_ref[0]
@@ -117,8 +117,8 @@
     def body(ib, acc):
         start = pl.multiple_of(ib * chunk, chunk)
         images = images_ref[pl.ds(start, chunk), :]
-        scores = scale * lax.dot_general(
-            captions, images, (((1,), (1,)), ((), ())), preferred_element_type=jnp.float32
+        scores = scale * jnp.dot(
+            captions, images_t_ref[:, pl.ds(start, chunk)], preferred_element_type=jnp.float32
         ) + shift
         weights = weights_of(scores, slot_ref[:, pl.ds(start, chunk)] == places)
         return acc + jnp.dot(weights, images, preferred_element_type=jnp.float32)
@@ -129,18 +129,18 @@
     caption_out[...] = scale * acc
 
     own_start = pl.multiple_of(lax.axis_index("dp") * rows, rows)
-    own = images_ref[pl.ds(own_start, rows), :]
-    own_scores = scale * lax.dot_general(
-        own, captions, (((1,), (1,)), ((), ())), preferred_element_type=jnp.float32
+    own_scores = scale * jnp.dot(
+        captions, images_t_ref[:, pl.ds(own_start, rows)], preferred_element_type=jnp.float32
     ) + shift
-    columns = jb * tc + lax.broadcasted_iota(jnp.int32, (1, tc), 1)
-    own_weights = weights_of(own_scores, own_slot_ref[...] == columns)
+    own_weights = weights_of(own_scores, own_slot_ref[...] == places)
 
     @pl.when(jb == 0)
     def _():
         image_out[...] = jnp.zeros_like(image_out)
 
-    image_out[...] += scale * jnp.dot(own_weights, captions, preferred_element_type=jnp.float32)
+    image_out[...] += scale * jnp.dot(
+        own_weights.T, captions, preferred_element_type=jnp.float32
+    )
 
 
 def contrast_group(scale, shift, own_slot, slot_g, image_b_g, caption_b_g):
@@ -157,9 +157,10 @@
         in_specs=[
             pl.BlockSpec(memory_space=pltpu.SMEM),
             pl.BlockSpec(memory_space=pltpu.SMEM),
-            pl.BlockSpec((rows, 1), lambda j: (0, 0)),
+            pl.BlockSpec((1, rows), lambda j: (0, 0)),
             pl.BlockSpec((1, group_rows), lambda j: (0, 0)),
             pl.BlockSpec((group_rows, width), lambda j: (0, 0)),
+            pl.BlockSpec((width, group_rows), lambda j: (0, 0)),
             pl.BlockSpec((tc, width), lambda j: (j, 0)),
         ],
         out_specs=(
@@ -172,7 +173,15 @@
             bytes_accessed=2 * group_rows * width * 2 + (group_rows + rows) * width * 4,
             transcendentals=group_rows * (group_rows + rows),
         ),
-    )(scale, shift, own_slot.reshape((rows, 1)), slot_g.reshape((1, group_rows)), image_b_g, caption_b_g)
+    )(
+        scale,
+        shift,
+        own_slot.reshape((1, rows)),
+        slot_g.reshape((1, group_rows)),
+        image_b_g,
+        image_b_g.T,
+        caption_b_g,
+    )
 
 
 def unit_rows(values):

time: 269 us -> 275 us (1.022)
  local copies, waits for them, and re-layouts: 10.8 us -> 15.9 us
    transpose x0 -> x1, local copies, waits for them, and re-layouts: none -> 6.5 us  [contrast_group(): return pl.pallas_call(contrast_kernel, grid=(group_rows // tc,), out_shap...]
    unnamed x18 -> x14, local copies, waits for them, and re-layouts: 7.3 us -> 7.3 us
  transfers between devices with their start and end apart: 5 -> 5, of which waited for: 2 -> 2; matrix products, arithmetic and copies ran while one was open for 6% -> 5% of each run, Pallas kernels for 32% -> 32%
where the time goes in v9:
time: 275 us; the launch traced here: 274 us
  Pallas kernels  130 us (47%)
  starting transfers between devices  44.3 us (16%)
  other arithmetic  40.8 us (15%)
  waiting for transfers between devices  31.9 us (12%)
  local copies, waits for them, and re-layouts  15.9 us (6%)
  matrix products  9.01 us (3%)
    pallas_call x1, Pallas kernels, gather_dp(): pl.pallas_call(functools.partial(gather_kernel, dp_size // 2), out_shape=...  87 us
    pallas_call x1, Pallas kernels, contrast_group(): pl.pallas_call(contrast_kernel, grid=(group_rows // tc,), out_shape=(jax....  43.1 us
    all_to_all x1, waiting for transfers between devices, shards(): lax.all_to_all(group_sum, 'zero', split_axis=1, concat_axis=0, tiled=True)  19.1 us
    all_to_all x1, starting transfers between devices, shards(): lax.all_to_all(hidden_part, 'dp', split_axis=0, concat_axis=1, tiled=True)  13.6 us
    all_to_all x1, waiting for transfers between devices, shards(): lax.all_to_all(hidden_part, 'dp', split_axis=0, concat_axis=1, tiled=True)  12.7 us
    all_to_all x1, starting transfers between devices, shards(): lax.all_to_all(group_sum, 'zero', split_axis=1, concat_axis=0, tiled=True)  10.7 us
    reduce_sum x2, other arithmetic, text_embed(): center = features - jnp.mean(features, axis=1, keepdims=True)  9.57 us
    all_to_all x1, starting transfers between devices, shards(): lax.all_to_all(feedforward_inner_activations, 'dp', split_axis=1, concat_...  7.59 us
  transfers between devices with their start and end apart: 5, of which 2 were waited for; matrix products, arithmetic and copies ran while one was open for 5% of the time, Pallas kernels for 32%

profile of v9, /device:TPU:57, one launch (start us, length us, event | category | flops | bytes accessed | tf_op | source)
XLA Modules:
  0.0 274.2 jit_solution(15813401095582611863)
XLA Ops:
  0.6 2.3 copy.20
  2.9 7.6 %all-to-all-start = ((bf16[128,16,256]{0,2,1:T(8,128)(2,1)}), bf16[128,16,256]{0,2,1:T(8,128)(2,1)S(1)}, u32[]{:S(2)}, u32[]{:S(2)}) async-start(bf16[128,16,256]{0,2,1:T(8,128)(2,1)} %bitcast.1), calls=%async_computation | async-start | bytes 2097152 | tf_op jit(solution)/shard_map/all_to_all | solution.py:223
  10.5 7.2 %collective-permute-start = (bf16[256,1024]{1,0:T(8,128)(2,1)}, bf16[256,1024]{1,0:T(8,128)(2,1)S(1)}, u32[]{:S(2)}, u32[]{:S(2)}) collective-permute-start(bf16[256,1024]{1,0:T(8,128)(2,1)} %param.17), channel_id=1, source_target_pairs={{0,0},{1,16},{2,32},{3,48},{4,64},{5,80},{6,96},{7,112},{8,128},{9... | collective-permute-start | bytes 1572872 | tf_op jit(solution)/shard_map/ppermute | solution.py:226
  19.0 0.6 compare_reduce_fusion.1
  19.6 0.6 compare_reduce_fusion
  20.3 2.0 fusion.21
  22.2 0.1 copy.23
  22.3 0.1 copy.22
  22.5 0.2 scatter.9
  22.7 1.9 pad_maximum_fusion.block_ref
  24.6 0.0 copy-start.5
  24.6 87.0 %shard_map.103 = bf16[16,128,2176]{2,1,0:T(8,128)(2,1)} custom-call(bf16[128,2176]{1,0:T(8,128)(2,1)} %pad_maximum_fusion.block_ref), custom_call_target="tpu_custom_call" | custom-call | tf_op jit(solution)/shard_map/pallas_call | solution.py:86
  111.7 0.0 all-to-all-done
  111.7 0.5 copy.21
  112.2 0.0 copy-start
  112.3 0.0 collective-permute-done
  112.3 3.0 %convert_reduce_fusion = f32[2048]{0:T(1024)S(1)} fusion(bf16[2048,2176]{1,0:T(8,128)(2,1)} %bitcast.18), kind=kLoop, calls=%fused_computation.3 | loop fusion | flops 4192256 | bytes 4202496 | tf_op jit(solution)/shard_map/jvp()/reduce_sum | solution.py:192
  115.2 2.9 %add_reduce_fusion = s32[2048]{0:T(1024)} fusion(bf16[2048,2176]{1,0:T(8,128)(2,1)} %bitcast.19), kind=kLoop, calls=%fused_computation.25 | loop fusion | flops 8192 | bytes 16384 | tf_op jit(solution)/shard_map/add | solution.py:234
  118.1 3.0 %fusion.6 = f32[2048]{0:T(1024)S(1)} fusion(f32[2048]{0:T(1024)S(1)} %broadcast_multiply_fusion, bf16[2048,2176]{1,0:T(8,128)(2,1)} %bitcast.20), kind=kLoop, calls=%fused_computation.12 | loop fusion | flops 8386560 | bytes 4210688 | tf_op jit(solution)/shard_map/jvp()/reduce_sum | solution.py:193
  121.1 0.0 copy-done.5
  121.1 0.0 copy-done
  121.1 2.8 %fusion.12 = (f32[2048]{0:T(1024)S(1)}, f32[2048]{0:T(1024)S(1)}) fusion(f32[1024]{0:T(1024)S(1)} %copy-done.5, f32[2048]{0:T(1024)S(1)} %fusion.19, f32[2048]{0:T(1024)S(1)} %broadcast_multiply_fusion, bf16[2048,2176]{1,0:T(8,128)(2,1)S(1)} %bitcast.24), kind=kLoop, calls=%fused_computation.18 | loop fusion | flops 18870272 | bytes 8425472 | tf_op jit(solution)/shard_map/jvp()/reduce_sum | solution.py:188
  123.9 4.9 %fusion.13 = (bf16[2048,1024]{1,0:T(8,128)(2,1)}, bf16[2048,1024]{1,0:T(8,128)(2,1)}) fusion(f32[2048]{0:T(1024)S(1)} %get-tuple-element.50, f32[1024]{0:T(1024)S(1)} %copy-done.5, f32[2048]{0:T(1024)S(1)} %fusion.19, f32[2048]{0:T(1024)S(1)} %broadcast_multiply_fusion, bf16[2048,2176]{1,0:T(8,128)(2,1)S(1)} %bitcast.25, f32[2048]{0:T(1024)S(1)} %get-tuple-element.49), kind=kLoop, calls=%fused_computation.19 | loop fusion | flops 18874368 | bytes 16814080 | tf_op jit(solution)/shard_map/convert_element_type | solution.py:242
  128.8 6.5 %copy.24.images_t_ref = bf16[1024,2048]{1,0:T(8,128)(2,1)} copy(bf16[1024,2048]{0,1:T(8,128)(2,1)} %bitcast.26) | data formatting | bytes 8388608 | tf_op jit(solution)/shard_map/transpose | solution.py:182
  135.3 43.1 %shard_map.104 = (f32[2048,1024]{1,0:T(8,128)}, f32[128,1024]{1,0:T(8,128)}) custom-call(f32[1]{0:T(128)S(6)} %copy.31.scale_ref, f32[1]{0:T(128)S(6)} %copy.32.shift_ref, s32[1,128]{1,0:T(1,128)} %bitcast.33, s32[1,2048]{1,0:T(1,128)} %bitcast.32, bf16[2048,1024]{1,0:T(8,128)(2,1)} %get-tuple-element.44.images_ref, bf16[1024,2048]{1,0:T(8,128)(2,1)} %copy.24.images_t_ref, ...), custom_call_target="tpu_custom_call" | custom-call | flops 18253611008 | bytes 17301504 | tf_op jit(solution)/shard_map/pallas_call | solution.py:150
  178.4 0.0 copy-start.1
  178.4 5.8 %fusion.14 = f32[2048]{0:T(1024)S(1)} fusion(f32[2048,1024]{1,0:T(8,128)} %get-tuple-element.34, f32[1024]{0:T(1024)S(1)} %copy-done.5, f32[2048]{0:T(1024)S(1)} %fusion.19, f32[2048]{0:T(1024)S(1)} %broadcast_multiply_fusion, bf16[2048,2176]{1,0:T(8,128)(2,1)} %bitcast.21), kind=kLoop, calls=%fused_computation.20 | loop fusion | flops 12580864 | bytes 12611584 | tf_op jit(solution)/shard_map/transpose(jvp())/reduce_sum | solution.py:188
  184.3 1.2 copy-done.1
  185.5 5.4 %fusion.15 = f32[2048]{0:T(1024)S(1)} fusion(f32[2048,1024]{1,0:T(8,128)S(1)} %copy-done.1, f32[2048]{0:T(1024)S(1)} %multiply_multiply_fusion.1, f32[2048]{0:T(1024)S(1)} %get-tuple-element.50, f32[1024]{0:T(1024)S(1)} %copy-done.5, f32[2048]{0:T(1024)S(1)} %fusion.19, f32[2048]{0:T(1024)S(1)} %broadcast_multiply_fusion, bf16[2048,2176]{1,0:T(8,128)(2,1)} %bitcast.22), kind=kLoop, calls=%fused_computation.21 | loop fusion | flops 23066624 | bytes 12627968 | tf_op jit(solution)/shard_map/transpose(jvp())/reduce_sum | solution.py:194
  190.9 6.6 %fusion.24 = (f32[2048]{0:T(1024)S(1)}, f32[2048,1024]{1,0:T(8,128)S(1)}) fusion(f32[2048]{0:T(1024)S(1)} %multiply_multiply_fusion, f32[2048]{0:T(1024)S(1)} %multiply_multiply_fusion.1, f32[1024]{0:T(1024)S(1)} %copy-done.5, f32[2048]{0:T(1024)S(1)} %fusion.19, f32[2048]{0:T(1024)S(1)} %broadcast_multiply_fusion, bf16[2048,2176]{1,0:T(8,128)(2,1)} %bitcast.23, ...), kind=kLoop, calls=%fused_computation.57 | loop fusion | flops 29358080 | bytes 21024768 | tf_op jit(solution)/shard_map/transpose(jvp())/reduce_sum | solution.py:192
  197.6 0.0 copy-start.2
  197.6 3.2 %copy-done.2 = f32[2048,1024]{1,0:T(8,128)} copy-done((f32[2048,1024]{1,0:T(8,128)}, f32[2048,1024]{1,0:T(8,128)S(1)}, u32[]{:S(2)}) %copy-start.2) | copy-done | bytes 8388632
  200.8 3.3 %fusion.23 = f32[256,1024]{0,1:T(8,128)} fusion(bf16[2048,256]{1,0:T(8,128)(2,1)S(1)} %bitcast.29, f32[2048,1024]{1,0:T(8,128)S(1)} %get-tuple-element.42, f32[2048]{0:T(1024)S(1)} %negate_multiply_fusion), kind=kOutput, calls=%fused_computation.56 | convolution fusion | flops 1077936128 | bytes 10493952 | tf_op jit(solution)/shard_map/dot_general | solution.py:261
  204.1 10.7 %all-to-all-start.2 = ((f32[256,16,64]{0,2,1:T(8,128)}), f32[256,16,64]{0,2,1:T(8,128)S(1)}, u32[]{:S(2)}, u32[]{:S(2)}) async-start(f32[256,16,64]{0,2,1:T(8,128)} %bitcast.10), calls=%async_computation.2 | async-start | bytes 2097152 | tf_op jit(solution)/shard_map/all_to_all | solution.py:264
  214.8 0.0 copy-start.4
  214.8 5.7 %convolution_convert_fusion = bf16[2048,256]{1,0:T(8,128)(2,1)} fusion(bf16[256,1024]{1,0:T(8,128)(2,1)S(1)} %collective-permute-done, f32[2048,1024]{1,0:T(8,128)} %copy-done.2, f32[2048]{0:T(1024)S(1)} %negate_multiply_fusion), kind=kOutput, calls=%fused_computation.24 | convolution fusion | flops 1078460416 | bytes 9969664 | tf_op jit(solution)/shard_map/dot_general | solution.py:254
  220.5 19.1 %all-to-all-done.2 = f32[256,16,64]{0,2,1:T(8,128)S(1)} async-done(((f32[256,16,64]{0,2,1:T(8,128)}), f32[256,16,64]{0,2,1:T(8,128)S(1)}, u32[]{:S(2)}, u32[]{:S(2)}) %all-to-all-start.2) | async-done | bytes 1048608 | tf_op jit(solution)/shard_map/all_to_all | solution.py:264
  239.6 13.6 %all-to-all-start.1 = ((bf16[16,128,256]{2,1,0:T(8,128)(2,1)}), bf16[16,128,256]{2,1,0:T(8,128)(2,1)S(1)}, u32[]{:S(2)}, u32[]{:S(2)}) async-start(bf16[16,128,256]{2,1,0:T(8,128)(2,1)} %bitcast.30), calls=%async_computation.1 | async-start | bytes 2097152 | tf_op jit(solution)/shard_map/all_to_all | solution.py:260
  253.3 0.0 copy-done.3
  253.3 0.0 copy-done.4
  253.3 0.2 fusion.17
  253.5 0.1 reduce_sum.115
  253.5 5.2 %collective-permute-start.1 = (f32[256,64]{0,1:T(8,128)S(1)}, f32[256,64]{0,1:T(8,128)S(1)}, u32[]{:S(2)}, u32[]{:S(2)}) collective-permute-start(f32[256,64]{0,1:T(8,128)S(1)} %reduce_sum.115), channel_id=1, source_target_pairs={{0,0},{1,16},{2,32},{3,48},{4,64},{5,80},{6,96},{7,112},{8,128},{9... | collective-permute-start | bytes 196616 | tf_op jit(solution)/shard_map/ppermute | solution.py:266
  258.8 0.9 add_add_fusion.2
  259.7 12.7 %all-to-all-done.1 = bf16[16,128,256]{2,1,0:T(8,128)(2,1)S(1)} async-done(((bf16[16,128,256]{2,1,0:T(8,128)(2,1)}), bf16[16,128,256]{2,1,0:T(8,128)(2,1)S(1)}, u32[]{:S(2)}, u32[]{:S(2)}) %all-to-all-start.1) | async-done | bytes 1048608 | tf_op jit(solution)/shard_map/all_to_all | solution.py:260
  272.5 1.1 copy.28
  273.5 0.0 collective-permute-done.1
  273.5 0.6 copy.33
  (9 shorter events, 0.1 us)
Async XLA Ops:
  2.9 108.8 %all-to-all-start = ((bf16[128,16,256]{0,2,1:T(8,128)(2,1)}), bf16[128,16,256]{0,2,1:T(8,128)(2,1)S(1)}, u32[]{:S(2)}, u32[]{:S(2)}) async-start(bf16[128,16,256]{0,2,1:T(8,128)(2,1)} %bitcast.1), calls=%async_computation | async-start | bytes 2097152 | tf_op jit(solution)/shard_map/all_to_all | solution.py:223
  10.5 101.8 %collective-permute-start = (bf16[256,1024]{1,0:T(8,128)(2,1)}, bf16[256,1024]{1,0:T(8,128)(2,1)S(1)}, u32[]{:S(2)}, u32[]{:S(2)}) collective-permute-start(bf16[256,1024]{1,0:T(8,128)(2,1)} %param.17), channel_id=1, source_target_pairs={{0,0},{1,16},{2,32},{3,48},{4,64},{5,80},{6,96},{7,112},{8,128},{9... | collective-permute-start | bytes 1572872 | tf_op jit(solution)/shard_map/ppermute | solution.py:226
  24.6 96.4 %copy-start.5 = (f32[1024]{0:T(1024)S(1)}, f32[1024]{0:T(1024)}, u32[]{:S(2)}) copy-start(f32[1024]{0:T(1024)} %param.16) | copy-start | bytes 12292
  112.2 8.8 %copy-start = (bf16[16,128,2176]{2,1,0:T(8,128)(2,1)S(1)}, bf16[16,128,2176]{2,1,0:T(8,128)(2,1)}, u32[]{:S(2)}) copy-start(bf16[16,128,2176]{2,1,0:T(8,128)(2,1)} %shard_map.103) | copy-start | bytes 26738692
  178.4 7.1 %copy-start.1 = (f32[2048,1024]{1,0:T(8,128)S(1)}, f32[2048,1024]{1,0:T(8,128)}, u32[]{:S(2)}) copy-start(f32[2048,1024]{1,0:T(8,128)} %get-tuple-element.34) | copy-start | bytes 25165828
  197.6 3.2 %copy-start.2 = (f32[2048,1024]{1,0:T(8,128)}, f32[2048,1024]{1,0:T(8,128)S(1)}, u32[]{:S(2)}) copy-start(f32[2048,1024]{1,0:T(8,128)S(1)} %get-tuple-element.42) | copy-start | bytes 25165828
  204.1 35.6 %all-to-all-start.2 = ((f32[256,16,64]{0,2,1:T(8,128)}), f32[256,16,64]{0,2,1:T(8,128)S(1)}, u32[]{:S(2)}, u32[]{:S(2)}) async-start(f32[256,16,64]{0,2,1:T(8,128)} %bitcast.10), calls=%async_computation.2 | async-start | bytes 2097152 | tf_op jit(solution)/shard_map/all_to_all | solution.py:264
  214.8 38.5 %copy-start.3 = (bf16[128,1024]{1,0:T(8,128)(2,1)S(1)}, bf16[128,1024]{1,0:T(8,128)(2,1)}, u32[]{:S(2)}) copy-start(bf16[128,1024]{1,0:T(8,128)(2,1)} %param.12) | copy-start | bytes 786436
  214.8 38.5 %copy-start.4 = (f32[128,1024]{1,0:T(8,128)S(1)}, f32[128,1024]{1,0:T(8,128)}, u32[]{:S(2)}) copy-start(f32[128,1024]{1,0:T(8,128)} %get-tuple-element.33) | copy-start | bytes 1572868
  239.6 32.8 %all-to-all-start.1 = ((bf16[16,128,256]{2,1,0:T(8,128)(2,1)}), bf16[16,128,256]{2,1,0:T(8,128)(2,1)S(1)}, u32[]{:S(2)}, u32[]{:S(2)}) async-start(bf16[16,128,256]{2,1,0:T(8,128)(2,1)} %bitcast.30), calls=%async_computation.1 | async-start | bytes 2097152 | tf_op jit(solution)/shard_map/all_to_all | solution.py:260
  253.5 20.0 %collective-permute-start.1 = (f32[256,64]{0,1:T(8,128)S(1)}, f32[256,64]{0,1:T(8,128)S(1)}, u32[]{:S(2)}, u32[]{:S(2)}) collective-permute-start(f32[256,64]{0,1:T(8,128)S(1)} %reduce_sum.115), channel_id=1, source_target_pairs={{0,0},{1,16},{2,32},{3,48},{4,64},{5,80},{6,96},{7,112},{8,128},{9... | collective-permute-start | bytes 196616 | tf_op jit(solution)/shard_map/ppermute | solution.py:266

commit v10 on v8

--- a/solution.py
+++ b/solution.py
@@ -106,21 +106,22 @@
     rows = own_slot_ref.shape[0]
     chunk = 512
     scale = scale_ref[0]
-    shift = shift_ref[0]
+    half_scale = 0.5 * scale
+    half_shift = 0.5 * shift_ref[0]
     captions = captions_ref[...]
     places = jb * tc + lax.broadcasted_iota(jnp.int32, (tc, 1), 0)
 
-    def weights_of(scores, positive):
-        labels = jnp.where(positive, 1.0, -1.0)
-        return (-labels * jax.nn.sigmoid(-labels * scores)).astype(jnp.bfloat16)
+    def weights_of(products, positive):
+        half = 0.5 * jnp.tanh(half_scale * products + half_shift)
+        return jnp.where(positive, half - 0.5, half + 0.5).astype(jnp.bfloat16)
 
     def body(ib, acc):
         start = pl.multiple_of(ib * chunk, chunk)
         images = images_ref[pl.ds(start, chunk), :]
-        scores = scale * lax.dot_general(
+        products = lax.dot_general(
             captions, images, (((1,), (1,)), ((), ())), preferred_element_type=jnp.float32
-        ) + shift
-        weights = weights_of(scores, slot_ref[:, pl.ds(start, chunk)] == places)
+        )
+        weights = weights_of(products, slot_ref[:, pl.ds(start, chunk)] == places)
         return acc + jnp.dot(weights, images, preferred_element_type=jnp.float32)
 
     acc = lax.fori_loop(
@@ -130,9 +131,9 @@
 
     own_start = pl.multiple_of(lax.axis_index("dp") * rows, rows)
     own = images_ref[pl.ds(own_start, rows), :]
-    own_scores = scale * lax.dot_general(
+    own_scores = lax.dot_general(
         own, captions, (((1,), (1,)), ((), ())), preferred_element_type=jnp.float32
-    ) + shift
+    )
     columns = jb * tc + lax.broadcasted_iota(jnp.int32, (1, tc), 1)
     own_weights = weights_of(own_scores, own_slot_ref[...] == columns)
 

time: 269 us -> 268 us (level)
  no operation moved by 1% of the time
where the time goes in v10:
time: 268 us; the launch traced here: 267 us
  Pallas kernels  128 us (48%)
  starting transfers between devices  44.6 us (17%)
  other arithmetic  41 us (15%)
  waiting for transfers between devices  31.5 us (12%)
  local copies, waits for them, and re-layouts  10.8 us (4%)
  matrix products  9.02 us (3%)
    pallas_call x1, Pallas kernels, gather_dp(): pl.pallas_call(functools.partial(gather_kernel, dp_size // 2), out_shape=...  85.7 us
    pallas_call x1, Pallas kernels, contrast_group(): pl.pallas_call(contrast_kernel, grid=(group_rows // tc,), out_shape=(jax....  42.5 us
    all_to_all x1, waiting for transfers between devices, shards(): lax.all_to_all(group_sum, 'zero', split_axis=1, concat_axis=0, tiled=True)  18.8 us
    all_to_all x1, starting transfers between devices, shards(): lax.all_to_all(hidden_part, 'dp', split_axis=0, concat_axis=1, tiled=True)  13 us
    all_to_all x1, waiting for transfers between devices, shards(): lax.all_to_all(hidden_part, 'dp', split_axis=0, concat_axis=1, tiled=True)  12.7 us
    all_to_all x1, starting transfers between devices, shards(): lax.all_to_all(group_sum, 'zero', split_axis=1, concat_axis=0, tiled=True)  11.6 us
    reduce_sum x2, other arithmetic, text_embed(): center = features - jnp.mean(features, axis=1, keepdims=True)  9.66 us
    all_to_all x1, starting transfers between devices, shards(): lax.all_to_all(feedforward_inner_activations, 'dp', split_axis=1, concat_...  7.59 us
  transfers between devices with their start and end apart: 5, of which 2 were waited for; matrix products, arithmetic and copies ran while one was open for 6% of the time, Pallas kernels for 32%

profile of v10, /device:TPU:57, one launch (start us, length us, event | category | flops | bytes accessed | tf_op | source)
XLA Modules:
  0.0 267.3 jit_solution(2050872214186002859)
XLA Ops:
  0.6 2.3 copy.20
  2.9 7.6 %all-to-all-start = ((bf16[128,16,256]{0,2,1:T(8,128)(2,1)}), bf16[128,16,256]{0,2,1:T(8,128)(2,1)S(1)}, u32[]{:S(2)}, u32[]{:S(2)}) async-start(bf16[128,16,256]{0,2,1:T(8,128)(2,1)} %bitcast.1), calls=%async_computation | async-start | bytes 2097152 | tf_op jit(solution)/shard_map/all_to_all | solution.py:215
  10.5 7.2 %collective-permute-start = (bf16[256,1024]{1,0:T(8,128)(2,1)}, bf16[256,1024]{1,0:T(8,128)(2,1)S(1)}, u32[]{:S(2)}, u32[]{:S(2)}) collective-permute-start(bf16[256,1024]{1,0:T(8,128)(2,1)} %param.17), channel_id=1, source_target_pairs={{0,0},{1,16},{2,32},{3,48},{4,64},{5,80},{6,96},{7,112},{8,128},{9... | collective-permute-start | bytes 1572872 | tf_op jit(solution)/shard_map/ppermute | solution.py:218
  19.0 0.6 compare_reduce_fusion.1
  19.6 0.6 compare_reduce_fusion
  20.3 2.0 fusion.21
  22.2 0.1 copy.23
  22.3 0.1 copy.22
  22.5 1.4 copy.24.own_slot_ref
  23.9 0.2 scatter.9
  24.1 1.9 pad_maximum_fusion.block_ref
  26.0 85.7 %shard_map.103 = bf16[16,128,2176]{2,1,0:T(8,128)(2,1)} custom-call(bf16[128,2176]{1,0:T(8,128)(2,1)} %pad_maximum_fusion.block_ref), custom_call_target="tpu_custom_call" | custom-call | tf_op jit(solution)/shard_map/pallas_call | solution.py:86
  111.7 0.0 all-to-all-done
  111.7 0.5 copy.21
  112.2 0.0 copy-start
  112.3 0.0 collective-permute-done
  112.3 0.0 copy-start.6
  112.3 3.0 %convert_reduce_fusion = f32[2048]{0:T(1024)S(1)} fusion(bf16[2048,2176]{1,0:T(8,128)(2,1)} %bitcast.17), kind=kLoop, calls=%fused_computation.3 | loop fusion | flops 4192256 | bytes 4202496 | tf_op jit(solution)/shard_map/jvp()/reduce_sum | solution.py:184
  115.3 3.0 %add_reduce_fusion = s32[2048]{0:T(1024)} fusion(bf16[2048,2176]{1,0:T(8,128)(2,1)} %bitcast.18), kind=kLoop, calls=%fused_computation.25 | loop fusion | flops 8192 | bytes 16384 | tf_op jit(solution)/shard_map/add | solution.py:226
  118.3 3.0 %fusion.6 = f32[2048]{0:T(1024)S(1)} fusion(f32[2048]{0:T(1024)S(1)} %broadcast_multiply_fusion, bf16[2048,2176]{1,0:T(8,128)(2,1)} %bitcast.19), kind=kLoop, calls=%fused_computation.12 | loop fusion | flops 8386560 | bytes 4210688 | tf_op jit(solution)/shard_map/jvp()/reduce_sum | solution.py:185
  121.3 0.0 copy-done.5
  121.3 0.0 copy-done
  121.3 2.8 %fusion.12 = (f32[2048]{0:T(1024)S(1)}, f32[2048]{0:T(1024)S(1)}) fusion(f32[1024]{0:T(1024)S(1)} %copy-done.5, f32[2048]{0:T(1024)S(1)} %fusion.19, f32[2048]{0:T(1024)S(1)} %broadcast_multiply_fusion, bf16[2048,2176]{1,0:T(8,128)(2,1)S(1)} %bitcast.23), kind=kLoop, calls=%fused_computation.18 | loop fusion | flops 18870272 | bytes 8425472 | tf_op jit(solution)/shard_map/jvp()/reduce_sum | solution.py:180
  124.1 0.0 copy-done.6
  124.2 4.9 %fusion.13 = (bf16[2048,1024]{1,0:T(8,128)(2,1)}, bf16[2048,1024]{1,0:T(8,128)(2,1)}) fusion(f32[2048]{0:T(1024)S(1)} %get-tuple-element.50, f32[1024]{0:T(1024)S(1)} %copy-done.5, f32[2048]{0:T(1024)S(1)} %fusion.19, f32[2048]{0:T(1024)S(1)} %broadcast_multiply_fusion, bf16[2048,2176]{1,0:T(8,128)(2,1)S(1)} %bitcast.24, f32[2048]{0:T(1024)S(1)} %get-tuple-element.49), kind=kLoop, calls=%fused_computation.19 | loop fusion | flops 18874368 | bytes 16814080 | tf_op jit(solution)/shard_map/convert_element_type | solution.py:234
  129.0 42.5 %shard_map.104 = (f32[2048,1024]{1,0:T(8,128)}, f32[128,1024]{1,0:T(8,128)}) custom-call(f32[1]{0:T(128)S(6)} %copy.31.scale_ref, f32[1]{0:T(128)S(6)} %copy.32.shift_ref, s32[128,1]{1,0:T(8,128)} %copy.24.own_slot_ref, s32[1,2048]{1,0:T(1,128)} %bitcast.30, bf16[2048,1024]{1,0:T(8,128)(2,1)} %get-tuple-element.44.images_ref, ...), custom_call_target="tpu_custom_call" | custom-call | flops 18253611008 | bytes 17301504 | tf_op jit(solution)/shard_map/pallas_call | solution.py:151
  171.6 5.8 %fusion.14 = f32[2048]{0:T(1024)S(1)} fusion(f32[2048,1024]{1,0:T(8,128)} %get-tuple-element.34, f32[1024]{0:T(1024)S(1)} %copy-done.5, f32[2048]{0:T(1024)S(1)} %fusion.19, f32[2048]{0:T(1024)S(1)} %broadcast_multiply_fusion, bf16[2048,2176]{1,0:T(8,128)(2,1)} %bitcast.20), kind=kLoop, calls=%fused_computation.20 | loop fusion | flops 12580864 | bytes 12611584 | tf_op jit(solution)/shard_map/transpose(jvp())/reduce_sum | solution.py:180
  177.4 1.2 copy-done.1
  178.6 5.4 %fusion.15 = f32[2048]{0:T(1024)S(1)} fusion(f32[2048,1024]{1,0:T(8,128)S(1)} %copy-done.1, f32[2048]{0:T(1024)S(1)} %multiply_multiply_fusion.1, f32[2048]{0:T(1024)S(1)} %get-tuple-element.50, f32[1024]{0:T(1024)S(1)} %copy-done.5, f32[2048]{0:T(1024)S(1)} %fusion.19, f32[2048]{0:T(1024)S(1)} %broadcast_multiply_fusion, bf16[2048,2176]{1,0:T(8,128)(2,1)} %bitcast.21), kind=kLoop, calls=%fused_computation.21 | loop fusion | flops 23066624 | bytes 12627968 | tf_op jit(solution)/shard_map/transpose(jvp())/reduce_sum | solution.py:186
  184.1 6.6 %fusion.24 = (f32[2048]{0:T(1024)S(1)}, f32[2048,1024]{1,0:T(8,128)S(1)}) fusion(f32[2048]{0:T(1024)S(1)} %multiply_multiply_fusion, f32[2048]{0:T(1024)S(1)} %multiply_multiply_fusion.1, f32[1024]{0:T(1024)S(1)} %copy-done.5, f32[2048]{0:T(1024)S(1)} %fusion.19, f32[2048]{0:T(1024)S(1)} %broadcast_multiply_fusion, bf16[2048,2176]{1,0:T(8,128)(2,1)} %bitcast.22, ...), kind=kLoop, calls=%fused_computation.57 | loop fusion | flops 29358080 | bytes 21024768 | tf_op jit(solution)/shard_map/transpose(jvp())/reduce_sum | solution.py:184
  190.7 0.0 copy-start.2
  190.7 0.0 copy-start.7
  190.7 3.2 %copy-done.2 = f32[2048,1024]{1,0:T(8,128)} copy-done((f32[2048,1024]{1,0:T(8,128)}, f32[2048,1024]{1,0:T(8,128)S(1)}, u32[]{:S(2)}) %copy-start.2) | copy-done | bytes 8388632
  193.9 3.3 %fusion.23 = f32[256,1024]{0,1:T(8,128)} fusion(bf16[2048,256]{1,0:T(8,128)(2,1)S(1)} %bitcast.27, f32[2048,1024]{1,0:T(8,128)S(1)} %get-tuple-element.42, f32[2048]{0:T(1024)S(1)} %negate_multiply_fusion), kind=kOutput, calls=%fused_computation.56 | convolution fusion | flops 1077936128 | bytes 10493952 | tf_op jit(solution)/shard_map/dot_general | solution.py:253
  197.2 11.6 %all-to-all-start.2 = ((f32[256,16,64]{0,2,1:T(8,128)}), f32[256,16,64]{0,2,1:T(8,128)S(1)}, u32[]{:S(2)}, u32[]{:S(2)}) async-start(f32[256,16,64]{0,2,1:T(8,128)} %bitcast.9), calls=%async_computation.2 | async-start | bytes 2097152 | tf_op jit(solution)/shard_map/all_to_all | solution.py:256
  208.8 0.0 copy-start.3
  208.8 0.0 copy-start.4
  208.8 5.7 %convolution_convert_fusion = bf16[2048,256]{1,0:T(8,128)(2,1)} fusion(bf16[256,1024]{1,0:T(8,128)(2,1)S(1)} %copy-done.7, f32[2048,1024]{1,0:T(8,128)} %copy-done.2, f32[2048]{0:T(1024)S(1)} %negate_multiply_fusion), kind=kOutput, calls=%fused_computation.24 | convolution fusion | flops 1078460416 | bytes 9969664 | tf_op jit(solution)/shard_map/dot_general | solution.py:246
  214.5 18.8 %all-to-all-done.2 = f32[256,16,64]{0,2,1:T(8,128)S(1)} async-done(((f32[256,16,64]{0,2,1:T(8,128)}), f32[256,16,64]{0,2,1:T(8,128)S(1)}, u32[]{:S(2)}, u32[]{:S(2)}) %all-to-all-start.2) | async-done | bytes 1048608 | tf_op jit(solution)/shard_map/all_to_all | solution.py:256
  233.3 13.0 %all-to-all-start.1 = ((bf16[16,128,256]{2,1,0:T(8,128)(2,1)}), bf16[16,128,256]{2,1,0:T(8,128)(2,1)S(1)}, u32[]{:S(2)}, u32[]{:S(2)}) async-start(bf16[16,128,256]{2,1,0:T(8,128)(2,1)} %bitcast.28), calls=%async_computation.1 | async-start | bytes 2097152 | tf_op jit(solution)/shard_map/all_to_all | solution.py:252
  246.4 0.2 fusion.17
  246.5 0.1 reduce_sum.115
  246.6 5.2 %collective-permute-start.1 = (f32[256,64]{0,1:T(8,128)S(1)}, f32[256,64]{0,1:T(8,128)S(1)}, u32[]{:S(2)}, u32[]{:S(2)}) collective-permute-start(f32[256,64]{0,1:T(8,128)S(1)} %reduce_sum.115), channel_id=1, source_target_pairs={{0,0},{1,16},{2,32},{3,48},{4,64},{5,80},{6,96},{7,112},{8,128},{9... | collective-permute-start | bytes 196616 | tf_op jit(solution)/shard_map/ppermute | solution.py:258
  251.9 0.9 add_add_fusion.2
  252.8 12.7 %all-to-all-done.1 = bf16[16,128,256]{2,1,0:T(8,128)(2,1)S(1)} async-done(((bf16[16,128,256]{2,1,0:T(8,128)(2,1)}), bf16[16,128,256]{2,1,0:T(8,128)(2,1)S(1)}, u32[]{:S(2)}, u32[]{:S(2)}) %all-to-all-start.1) | async-done | bytes 1048608 | tf_op jit(solution)/shard_map/all_to_all | solution.py:252
  265.6 1.1 copy.28
  266.6 0.0 collective-permute-done.1
  266.6 0.6 copy.33
  (13 shorter events, 0.1 us)
Async XLA Ops:
  2.9 108.8 %all-to-all-start = ((bf16[128,16,256]{0,2,1:T(8,128)(2,1)}), bf16[128,16,256]{0,2,1:T(8,128)(2,1)S(1)}, u32[]{:S(2)}, u32[]{:S(2)}) async-start(bf16[128,16,256]{0,2,1:T(8,128)(2,1)} %bitcast.1), calls=%async_computation | async-start | bytes 2097152 | tf_op jit(solution)/shard_map/all_to_all | solution.py:215
  10.5 101.8 %collective-permute-start = (bf16[256,1024]{1,0:T(8,128)(2,1)}, bf16[256,1024]{1,0:T(8,128)(2,1)S(1)}, u32[]{:S(2)}, u32[]{:S(2)}) collective-permute-start(bf16[256,1024]{1,0:T(8,128)(2,1)} %param.17), channel_id=1, source_target_pairs={{0,0},{1,16},{2,32},{3,48},{4,64},{5,80},{6,96},{7,112},{8,128},{9... | collective-permute-start | bytes 1572872 | tf_op jit(solution)/shard_map/ppermute | solution.py:218
  26.0 95.3 %copy-start.5 = (f32[1024]{0:T(1024)S(1)}, f32[1024]{0:T(1024)}, u32[]{:S(2)}) copy-start(f32[1024]{0:T(1024)} %param.16) | copy-start | bytes 12292
  112.2 9.0 %copy-start = (bf16[16,128,2176]{2,1,0:T(8,128)(2,1)S(1)}, bf16[16,128,2176]{2,1,0:T(8,128)(2,1)}, u32[]{:S(2)}) copy-start(bf16[16,128,2176]{2,1,0:T(8,128)(2,1)} %shard_map.103) | copy-start | bytes 26738692
  112.3 11.9 %copy-start.6 = (bf16[256,1024]{1,0:T(8,128)(2,1)}, bf16[256,1024]{1,0:T(8,128)(2,1)S(1)}, u32[]{:S(2)}) copy-start(bf16[256,1024]{1,0:T(8,128)(2,1)S(1)} %collective-permute-done) | copy-start | bytes 1572868
  171.6 7.1 %copy-start.1 = (f32[2048,1024]{1,0:T(8,128)S(1)}, f32[2048,1024]{1,0:T(8,128)}, u32[]{:S(2)}) copy-start(f32[2048,1024]{1,0:T(8,128)} %get-tuple-element.34) | copy-start | bytes 25165828
  190.7 3.2 %copy-start.2 = (f32[2048,1024]{1,0:T(8,128)}, f32[2048,1024]{1,0:T(8,128)S(1)}, u32[]{:S(2)}) copy-start(f32[2048,1024]{1,0:T(8,128)S(1)} %get-tuple-element.42) | copy-start | bytes 25165828
  190.7 18.1 %copy-start.7 = (bf16[256,1024]{1,0:T(8,128)(2,1)S(1)}, bf16[256,1024]{1,0:T(8,128)(2,1)}, u32[]{:S(2)}) copy-start(bf16[256,1024]{1,0:T(8,128)(2,1)} %copy-done.6) | copy-start | bytes 1572868
  197.2 36.1 %all-to-all-start.2 = ((f32[256,16,64]{0,2,1:T(8,128)}), f32[256,16,64]{0,2,1:T(8,128)S(1)}, u32[]{:S(2)}, u32[]{:S(2)}) async-start(f32[256,16,64]{0,2,1:T(8,128)} %bitcast.9), calls=%async_computation.2 | async-start | bytes 2097152 | tf_op jit(solution)/shard_map/all_to_all | solution.py:256
  208.8 37.6 %copy-start.3 = (bf16[128,1024]{1,0:T(8,128)(2,1)S(1)}, bf16[128,1024]{1,0:T(8,128)(2,1)}, u32[]{:S(2)}) copy-start(bf16[128,1024]{1,0:T(8,128)(2,1)} %param.12) | copy-start | bytes 786436
  208.8 37.6 %copy-start.4 = (f32[128,1024]{1,0:T(8,128)S(1)}, f32[128,1024]{1,0:T(8,128)}, u32[]{:S(2)}) copy-start(f32[128,1024]{1,0:T(8,128)} %get-tuple-element.33) | copy-start | bytes 1572868
  233.3 32.2 %all-to-all-start.1 = ((bf16[16,128,256]{2,1,0:T(8,128)(2,1)}), bf16[16,128,256]{2,1,0:T(8,128)(2,1)S(1)}, u32[]{:S(2)}, u32[]{:S(2)}) async-start(bf16[16,128,256]{2,1,0:T(8,128)(2,1)} %bitcast.28), calls=%async_computation.1 | async-start | bytes 2097152 | tf_op jit(solution)/shard_map/all_to_all | solution.py:252
  246.6 20.0 %collective-permute-start.1 = (f32[256,64]{0,1:T(8,128)S(1)}, f32[256,64]{0,1:T(8,128)S(1)}, u32[]{:S(2)}, u32[]{:S(2)}) collective-permute-start(f32[256,64]{0,1:T(8,128)S(1)} %reduce_sum.115), channel_id=1, source_target_pairs={{0,0},{1,16},{2,32},{3,48},{4,64},{5,80},{6,96},{7,112},{8,128},{9... | collective-permute-start | bytes 196616 | tf_op jit(solution)/shard_map/ppermute | solution.py:258

commit v11 on v10

--- a/solution.py
+++ b/solution.py
@@ -104,7 +104,6 @@
     jb = pl.program_id(0)
     tc = captions_ref.shape[0]
     rows = own_slot_ref.shape[0]
-    chunk = 512
     scale = scale_ref[0]
     half_scale = 0.5 * scale
     half_shift = 0.5 * shift_ref[0]
@@ -115,18 +114,12 @@
         half = 0.5 * jnp.tanh(half_scale * products + half_shift)
         return jnp.where(positive, half - 0.5, half + 0.5).astype(jnp.bfloat16)
 
-    def body(ib, acc):
-        start = pl.multiple_of(ib * chunk, chunk)
-        images = images_ref[pl.ds(start, chunk), :]
-        products = lax.dot_general(
-            captions, images, (((1,), (1,)), ((), ())), preferred_element_type=jnp.float32
-        )
-        weights = weights_of(products, slot_ref[:, pl.ds(start, chunk)] == places)
-        return acc + jnp.dot(weights, images, preferred_element_type=jnp.float32)
-
-    acc = lax.fori_loop(
-        0, images_ref.shape[0] // chunk, body, jnp.zeros(caption_out.shape, jnp.float32)
-    )
+    images = images_ref[...]
+    products = lax.dot_general(
+        captions, images, (((1,), (1,)), ((), ())), preferred_element_type=jnp.float32
+    )
+    weights = weights_of(products, slot_ref[...] == places)
+    acc = jnp.dot(weights, images, preferred_element_type=jnp.float32)
     caption_out[...] = scale * acc
 
     own_start = pl.multiple_of(lax.axis_index("dp") * rows, rows)

time: 268 us -> 253 us (0.944)
  Pallas kernels: 128 us -> 113 us
    pallas_call x1, Pallas kernels: 42.5 us -> 27.4 us  [contrast_group(): pl.pallas_call(contrast_kernel, grid=(group_rows // tc,), out_shape=(jax....]
  transfers between devices with their start and end apart: 5 -> 5, of which waited for: 2 -> 2; matrix products, arithmetic and copies ran while one was open for 6% -> 6% of each run, Pallas kernels for 32% -> 34%
where the time goes in v11:
time: 253 us
  Pallas kernels  113 us (45%)
  starting transfers between devices  44.7 us (18%)
  other arithmetic  41.2 us (16%)
  waiting for transfers between devices  31.6 us (12%)
  local copies, waits for them, and re-layouts  10.8 us (4%)
  matrix products  9.02 us (4%)
    pallas_call x1, Pallas kernels, gather_dp(): pl.pallas_call(functools.partial(gather_kernel, dp_size // 2), out_shape=...  85.7 us
    pallas_call x1, Pallas kernels, contrast_group(): pl.pallas_call(contrast_kernel, grid=(group_rows // tc,), out_shape=(jax....  27.4 us
    all_to_all x1, waiting for transfers between devices, shards(): lax.all_to_all(group_sum, 'zero', split_axis=1, concat_axis=0, tiled=True)  18.8 us
    all_to_all x1, starting transfers between devices, shards(): lax.all_to_all(hidden_part, 'dp', split_axis=0, concat_axis=1, tiled=True)  13.1 us
    all_to_all x1, waiting for transfers between devices, shards(): lax.all_to_all(hidden_part, 'dp', split_axis=0, concat_axis=1, tiled=True)  12.8 us
    all_to_all x1, starting transfers between devices, shards(): lax.all_to_all(group_sum, 'zero', split_axis=1, concat_axis=0, tiled=True)  11.7 us
    reduce_sum x2, other arithmetic, text_embed(): center = features - jnp.mean(features, axis=1, keepdims=True)  9.84 us
    all_to_all x1, starting transfers between devices, shards(): lax.all_to_all(feedforward_inner_activations, 'dp', split_axis=1, concat_...  7.59 us
  transfers between devices with their start and end apart: 5, of which 2 were waited for; matrix products, arithmetic and copies ran while one was open for 6% of the time, Pallas kernels for 34%

profile of v11, /device:TPU:57, one launch (start us, length us, event | category | flops | bytes accessed | tf_op | source)
XLA Modules:
  0.0 252.6 jit_solution(6108534116285385472)
XLA Ops:
  0.6 2.3 copy.20
  2.9 7.6 %all-to-all-start = ((bf16[128,16,256]{0,2,1:T(8,128)(2,1)}), bf16[128,16,256]{0,2,1:T(8,128)(2,1)S(1)}, u32[]{:S(2)}, u32[]{:S(2)}) async-start(bf16[128,16,256]{0,2,1:T(8,128)(2,1)} %bitcast.1), calls=%async_computation | async-start | bytes 2097152 | tf_op jit(solution)/shard_map/all_to_all | solution.py:208
  10.5 7.2 %collective-permute-start = (bf16[256,1024]{1,0:T(8,128)(2,1)}, bf16[256,1024]{1,0:T(8,128)(2,1)S(1)}, u32[]{:S(2)}, u32[]{:S(2)}) collective-permute-start(bf16[256,1024]{1,0:T(8,128)(2,1)} %param.17), channel_id=1, source_target_pairs={{0,0},{1,16},{2,32},{3,48},{4,64},{5,80},{6,96},{7,112},{8,128},{9... | collective-permute-start | bytes 1572872 | tf_op jit(solution)/shard_map/ppermute | solution.py:211
  19.0 0.6 compare_reduce_fusion.1
  19.6 0.6 compare_reduce_fusion
  20.3 2.0 fusion.21
  22.2 0.1 copy.23
  22.3 0.1 copy.22
  22.5 1.4 copy.24.own_slot_ref
  23.9 0.2 scatter.9
  24.1 1.9 pad_maximum_fusion.block_ref
  26.0 85.7 %shard_map.103 = bf16[16,128,2176]{2,1,0:T(8,128)(2,1)} custom-call(bf16[128,2176]{1,0:T(8,128)(2,1)} %pad_maximum_fusion.block_ref), custom_call_target="tpu_custom_call" | custom-call | tf_op jit(solution)/shard_map/pallas_call | solution.py:86
  111.7 0.0 all-to-all-done
  111.7 0.5 copy.21
  112.2 0.0 copy-start
  112.3 0.0 collective-permute-done
  112.3 0.0 copy-start.6
  112.3 3.0 %convert_reduce_fusion = f32[2048]{0:T(1024)S(1)} fusion(bf16[2048,2176]{1,0:T(8,128)(2,1)} %bitcast.17), kind=kLoop, calls=%fused_computation.3 | loop fusion | flops 4192256 | bytes 4202496 | tf_op jit(solution)/shard_map/jvp()/reduce_sum | solution.py:177
  115.3 3.0 %add_reduce_fusion = s32[2048]{0:T(1024)} fusion(bf16[2048,2176]{1,0:T(8,128)(2,1)} %bitcast.18), kind=kLoop, calls=%fused_computation.25 | loop fusion | flops 8192 | bytes 16384 | tf_op jit(solution)/shard_map/add | solution.py:219
  118.3 3.0 %fusion.6 = f32[2048]{0:T(1024)S(1)} fusion(f32[2048]{0:T(1024)S(1)} %broadcast_multiply_fusion, bf16[2048,2176]{1,0:T(8,128)(2,1)} %bitcast.19), kind=kLoop, calls=%fused_computation.12 | loop fusion | flops 8386560 | bytes 4210688 | tf_op jit(solution)/shard_map/jvp()/reduce_sum | solution.py:178
  121.3 0.0 copy-done.5
  121.3 0.0 copy-done
  121.3 2.8 %fusion.12 = (f32[2048]{0:T(1024)S(1)}, f32[2048]{0:T(1024)S(1)}) fusion(f32[1024]{0:T(1024)S(1)} %copy-done.5, f32[2048]{0:T(1024)S(1)} %fusion.19, f32[2048]{0:T(1024)S(1)} %broadcast_multiply_fusion, bf16[2048,2176]{1,0:T(8,128)(2,1)S(1)} %bitcast.23), kind=kLoop, calls=%fused_computation.18 | loop fusion | flops 18870272 | bytes 8425472 | tf_op jit(solution)/shard_map/jvp()/reduce_sum | solution.py:173
  124.1 0.0 copy-done.6
  124.2 4.9 %fusion.13 = (bf16[2048,1024]{1,0:T(8,128)(2,1)}, bf16[2048,1024]{1,0:T(8,128)(2,1)}) fusion(f32[2048]{0:T(1024)S(1)} %get-tuple-element.50, f32[1024]{0:T(1024)S(1)} %copy-done.5, f32[2048]{0:T(1024)S(1)} %fusion.19, f32[2048]{0:T(1024)S(1)} %broadcast_multiply_fusion, bf16[2048,2176]{1,0:T(8,128)(2,1)S(1)} %bitcast.24, f32[2048]{0:T(1024)S(1)} %get-tuple-element.49), kind=kLoop, calls=%fused_computation.19 | loop fusion | flops 18874368 | bytes 16814080 | tf_op jit(solution)/shard_map/convert_element_type | solution.py:227
  129.0 27.4 %shard_map.104 = (f32[2048,1024]{1,0:T(8,128)}, f32[128,1024]{1,0:T(8,128)}) custom-call(f32[1]{0:T(128)S(6)} %copy.31.scale_ref, f32[1]{0:T(128)S(6)} %copy.32.shift_ref, s32[128,1]{1,0:T(8,128)} %copy.24.own_slot_ref, s32[1,2048]{1,0:T(1,128)} %bitcast.30, bf16[2048,1024]{1,0:T(8,128)(2,1)} %get-tuple-element.44.images_ref, ...), custom_call_target="tpu_custom_call" | custom-call | flops 18253611008 | bytes 17301504 | tf_op jit(solution)/shard_map/pallas_call | solution.py:144
  156.5 5.8 %fusion.14 = f32[2048]{0:T(1024)S(1)} fusion(f32[2048,1024]{1,0:T(8,128)} %get-tuple-element.34, f32[1024]{0:T(1024)S(1)} %copy-done.5, f32[2048]{0:T(1024)S(1)} %fusion.19, f32[2048]{0:T(1024)S(1)} %broadcast_multiply_fusion, bf16[2048,2176]{1,0:T(8,128)(2,1)} %bitcast.20), kind=kLoop, calls=%fused_computation.20 | loop fusion | flops 12580864 | bytes 12611584 | tf_op jit(solution)/shard_map/transpose(jvp())/reduce_sum | solution.py:173
  162.3 1.2 copy-done.1
  163.5 5.4 %fusion.15 = f32[2048]{0:T(1024)S(1)} fusion(f32[2048,1024]{1,0:T(8,128)S(1)} %copy-done.1, f32[2048]{0:T(1024)S(1)} %multiply_multiply_fusion.1, f32[2048]{0:T(1024)S(1)} %get-tuple-element.50, f32[1024]{0:T(1024)S(1)} %copy-done.5, f32[2048]{0:T(1024)S(1)} %fusion.19, f32[2048]{0:T(1024)S(1)} %broadcast_multiply_fusion, bf16[2048,2176]{1,0:T(8,128)(2,1)} %bitcast.21), kind=kLoop, calls=%fused_computation.21 | loop fusion | flops 23066624 | bytes 12627968 | tf_op jit(solution)/shard_map/transpose(jvp())/reduce_sum | solution.py:179
  169.0 6.8 %fusion.24 = (f32[2048]{0:T(1024)S(1)}, f32[2048,1024]{1,0:T(8,128)S(1)}) fusion(f32[2048]{0:T(1024)S(1)} %multiply_multiply_fusion, f32[2048]{0:T(1024)S(1)} %multiply_multiply_fusion.1, f32[1024]{0:T(1024)S(1)} %copy-done.5, f32[2048]{0:T(1024)S(1)} %fusion.19, f32[2048]{0:T(1024)S(1)} %broadcast_multiply_fusion, bf16[2048,2176]{1,0:T(8,128)(2,1)} %bitcast.22, ...), kind=kLoop, calls=%fused_computation.57 | loop fusion | flops 29358080 | bytes 21024768 | tf_op jit(solution)/shard_map/transpose(jvp())/reduce_sum | solution.py:177
  175.8 0.0 copy-start.2
  175.8 0.0 copy-start.7
  175.8 3.2 %copy-done.2 = f32[2048,1024]{1,0:T(8,128)} copy-done((f32[2048,1024]{1,0:T(8,128)}, f32[2048,1024]{1,0:T(8,128)S(1)}, u32[]{:S(2)}) %copy-start.2) | copy-done | bytes 8388632
  179.0 3.3 %fusion.23 = f32[256,1024]{0,1:T(8,128)} fusion(bf16[2048,256]{1,0:T(8,128)(2,1)S(1)} %bitcast.27, f32[2048,1024]{1,0:T(8,128)S(1)} %get-tuple-element.42, f32[2048]{0:T(1024)S(1)} %negate_multiply_fusion), kind=kOutput, calls=%fused_computation.56 | convolution fusion | flops 1077936128 | bytes 10493952 | tf_op jit(solution)/shard_map/dot_general | solution.py:246
  182.3 11.7 %all-to-all-start.2 = ((f32[256,16,64]{0,2,1:T(8,128)}), f32[256,16,64]{0,2,1:T(8,128)S(1)}, u32[]{:S(2)}, u32[]{:S(2)}) async-start(f32[256,16,64]{0,2,1:T(8,128)} %bitcast.9), calls=%async_computation.2 | async-start | bytes 2097152 | tf_op jit(solution)/shard_map/all_to_all | solution.py:249
  194.0 0.0 copy-start.3
  194.0 0.0 copy-start.4
  194.0 5.7 %convolution_convert_fusion = bf16[2048,256]{1,0:T(8,128)(2,1)} fusion(bf16[256,1024]{1,0:T(8,128)(2,1)S(1)} %copy-done.7, f32[2048,1024]{1,0:T(8,128)} %copy-done.2, f32[2048]{0:T(1024)S(1)} %negate_multiply_fusion), kind=kOutput, calls=%fused_computation.24 | convolution fusion | flops 1078460416 | bytes 9969664 | tf_op jit(solution)/shard_map/dot_general | solution.py:239
  199.8 18.8 %all-to-all-done.2 = f32[256,16,64]{0,2,1:T(8,128)S(1)} async-done(((f32[256,16,64]{0,2,1:T(8,128)}), f32[256,16,64]{0,2,1:T(8,128)S(1)}, u32[]{:S(2)}, u32[]{:S(2)}) %all-to-all-start.2) | async-done | bytes 1048608 | tf_op jit(solution)/shard_map/all_to_all | solution.py:249
  218.6 13.1 %all-to-all-start.1 = ((bf16[16,128,256]{2,1,0:T(8,128)(2,1)}), bf16[16,128,256]{2,1,0:T(8,128)(2,1)S(1)}, u32[]{:S(2)}, u32[]{:S(2)}) async-start(bf16[16,128,256]{2,1,0:T(8,128)(2,1)} %bitcast.28), calls=%async_computation.1 | async-start | bytes 2097152 | tf_op jit(solution)/shard_map/all_to_all | solution.py:245
  231.7 0.2 fusion.17
  231.9 0.1 reduce_sum.115
  231.9 5.2 %collective-permute-start.1 = (f32[256,64]{0,1:T(8,128)S(1)}, f32[256,64]{0,1:T(8,128)S(1)}, u32[]{:S(2)}, u32[]{:S(2)}) collective-permute-start(f32[256,64]{0,1:T(8,128)S(1)} %reduce_sum.115), channel_id=1, source_target_pairs={{0,0},{1,16},{2,32},{3,48},{4,64},{5,80},{6,96},{7,112},{8,128},{9... | collective-permute-start | bytes 196616 | tf_op jit(solution)/shard_map/ppermute | solution.py:251
  237.1 0.9 add_add_fusion.2
  238.1 12.8 %all-to-all-done.1 = bf16[16,128,256]{2,1,0:T(8,128)(2,1)S(1)} async-done(((bf16[16,128,256]{2,1,0:T(8,128)(2,1)}), bf16[16,128,256]{2,1,0:T(8,128)(2,1)S(1)}, u32[]{:S(2)}, u32[]{:S(2)}) %all-to-all-start.1) | async-done | bytes 1048608 | tf_op jit(solution)/shard_map/all_to_all | solution.py:245
  250.9 1.1 copy.28
  252.0 0.0 collective-permute-done.1
  252.0 0.6 copy.33
  (13 shorter events, 0.1 us)
Async XLA Ops:
  2.9 108.8 %all-to-all-start = ((bf16[128,16,256]{0,2,1:T(8,128)(2,1)}), bf16[128,16,256]{0,2,1:T(8,128)(2,1)S(1)}, u32[]{:S(2)}, u32[]{:S(2)}) async-start(bf16[128,16,256]{0,2,1:T(8,128)(2,1)} %bitcast.1), calls=%async_computation | async-start | bytes 2097152 | tf_op jit(solution)/shard_map/all_to_all | solution.py:208
  10.5 101.8 %collective-permute-start = (bf16[256,1024]{1,0:T(8,128)(2,1)}, bf16[256,1024]{1,0:T(8,128)(2,1)S(1)}, u32[]{:S(2)}, u32[]{:S(2)}) collective-permute-start(bf16[256,1024]{1,0:T(8,128)(2,1)} %param.17), channel_id=1, source_target_pairs={{0,0},{1,16},{2,32},{3,48},{4,64},{5,80},{6,96},{7,112},{8,128},{9... | collective-permute-start | bytes 1572872 | tf_op jit(solution)/shard_map/ppermute | solution.py:211
  26.0 95.3 %copy-start.5 = (f32[1024]{0:T(1024)S(1)}, f32[1024]{0:T(1024)}, u32[]{:S(2)}) copy-start(f32[1024]{0:T(1024)} %param.16) | copy-start | bytes 12292
  112.2 9.0 %copy-start = (bf16[16,128,2176]{2,1,0:T(8,128)(2,1)S(1)}, bf16[16,128,2176]{2,1,0:T(8,128)(2,1)}, u32[]{:S(2)}) copy-start(bf16[16,128,2176]{2,1,0:T(8,128)(2,1)} %shard_map.103) | copy-start | bytes 26738692
  112.3 11.9 %copy-start.6 = (bf16[256,1024]{1,0:T(8,128)(2,1)}, bf16[256,1024]{1,0:T(8,128)(2,1)S(1)}, u32[]{:S(2)}) copy-start(bf16[256,1024]{1,0:T(8,128)(2,1)S(1)} %collective-permute-done) | copy-start | bytes 1572868
  156.5 7.1 %copy-start.1 = (f32[2048,1024]{1,0:T(8,128)S(1)}, f32[2048,1024]{1,0:T(8,128)}, u32[]{:S(2)}) copy-start(f32[2048,1024]{1,0:T(8,128)} %get-tuple-element.34) | copy-start | bytes 25165828
  175.8 3.2 %copy-start.2 = (f32[2048,1024]{1,0:T(8,128)}, f32[2048,1024]{1,0:T(8,128)S(1)}, u32[]{:S(2)}) copy-start(f32[2048,1024]{1,0:T(8,128)S(1)} %get-tuple-element.42) | copy-start | bytes 25165828
  175.8 18.2 %copy-start.7 = (bf16[256,1024]{1,0:T(8,128)(2,1)S(1)}, bf16[256,1024]{1,0:T(8,128)(2,1)}, u32[]{:S(2)}) copy-start(bf16[256,1024]{1,0:T(8,128)(2,1)} %copy-done.6) | copy-start | bytes 1572868
  182.3 36.3 %all-to-all-start.2 = ((f32[256,16,64]{0,2,1:T(8,128)}), f32[256,16,64]{0,2,1:T(8,128)S(1)}, u32[]{:S(2)}, u32[]{:S(2)}) async-start(f32[256,16,64]{0,2,1:T(8,128)} %bitcast.9), calls=%async_computation.2 | async-start | bytes 2097152 | tf_op jit(solution)/shard_map/all_to_all | solution.py:249
  194.0 37.7 %copy-start.3 = (bf16[128,1024]{1,0:T(8,128)(2,1)S(1)}, bf16[128,1024]{1,0:T(8,128)(2,1)}, u32[]{:S(2)}) copy-start(bf16[128,1024]{1,0:T(8,128)(2,1)} %param.12) | copy-start | bytes 786436
  194.0 37.7 %copy-start.4 = (f32[128,1024]{1,0:T(8,128)S(1)}, f32[128,1024]{1,0:T(8,128)}, u32[]{:S(2)}) copy-start(f32[128,1024]{1,0:T(8,128)} %get-tuple-element.33) | copy-start | bytes 1572868
  218.6 32.3 %all-to-all-start.1 = ((bf16[16,128,256]{2,1,0:T(8,128)(2,1)}), bf16[16,128,256]{2,1,0:T(8,128)(2,1)S(1)}, u32[]{:S(2)}, u32[]{:S(2)}) async-start(bf16[16,128,256]{2,1,0:T(8,128)(2,1)} %bitcast.28), calls=%async_computation.1 | async-start | bytes 2097152 | tf_op jit(solution)/shard_map/all_to_all | solution.py:245
  231.9 20.0 %collective-permute-start.1 = (f32[256,64]{0,1:T(8,128)S(1)}, f32[256,64]{0,1:T(8,128)S(1)}, u32[]{:S(2)}, u32[]{:S(2)}) collective-permute-start(f32[256,64]{0,1:T(8,128)S(1)} %reduce_sum.115), channel_id=1, source_target_pairs={{0,0},{1,16},{2,32},{3,48},{4,64},{5,80},{6,96},{7,112},{8,128},{9... | collective-permute-start | bytes 196616 | tf_op jit(solution)/shard_map/ppermute | solution.py:251

commit v12 on v11

--- a/solution.py
+++ b/solution.py
@@ -140,7 +140,7 @@
 def contrast_group(scale, shift, own_slot, slot_g, image_b_g, caption_b_g):
     group_rows, width = caption_b_g.shape
     rows = own_slot.shape[0]
-    tc = 256
+    tc = 512
     return pl.pallas_call(
         contrast_kernel,
         grid=(group_rows // tc,),

time: 253 us -> 251 us (level)
  no operation moved by 1% of the time
where the time goes in v12:
time: 251 us; the launch traced here: 250 us
  Pallas kernels  111 us (44%)
  starting transfers between devices  44.5 us (18%)
  other arithmetic  41.2 us (16%)
  waiting for transfers between devices  31.8 us (13%)
  local copies, waits for them, and re-layouts  10.8 us (4%)
  matrix products  9.02 us (4%)
    pallas_call x1, Pallas kernels, gather_dp(): pl.pallas_call(functools.partial(gather_kernel, dp_size // 2), out_shape=...  85.7 us
    pallas_call x1, Pallas kernels, contrast_group(): pl.pallas_call(contrast_kernel, grid=(group_rows // tc,), out_shape=(jax....  25.3 us
    all_to_all x1, waiting for transfers between devices, shards(): lax.all_to_all(group_sum, 'zero', split_axis=1, concat_axis=0, tiled=True)  19.1 us
    all_to_all x1, waiting for transfers between devices, shards(): lax.all_to_all(hidden_part, 'dp', split_axis=0, concat_axis=1, tiled=True)  12.7 us
    all_to_all x1, starting transfers between devices, shards(): lax.all_to_all(hidden_part, 'dp', split_axis=0, concat_axis=1, tiled=True)  12.7 us
    all_to_all x1, starting transfers between devices, shards(): lax.all_to_all(group_sum, 'zero', split_axis=1, concat_axis=0, tiled=True)  11.7 us
    reduce_sum x2, other arithmetic, text_embed(): center = features - jnp.mean(features, axis=1, keepdims=True)  9.84 us
    all_to_all x1, starting transfers between devices, shards(): lax.all_to_all(feedforward_inner_activations, 'dp', split_axis=1, concat_...  7.59 us
  transfers between devices with their start and end apart: 5, of which 2 were waited for; matrix products, arithmetic and copies ran while one was open for 6% of the time, Pallas kernels for 34%

profile of v12, /device:TPU:57, one launch (start us, length us, event | category | flops | bytes accessed | tf_op | source)
XLA Modules:
  0.0 250.5 jit_solution(6138089491277070086)
XLA Ops:
  0.6 2.3 copy.20
  2.9 7.6 %all-to-all-start = ((bf16[128,16,256]{0,2,1:T(8,128)(2,1)}), bf16[128,16,256]{0,2,1:T(8,128)(2,1)S(1)}, u32[]{:S(2)}, u32[]{:S(2)}) async-start(bf16[128,16,256]{0,2,1:T(8,128)(2,1)} %bitcast.1), calls=%async_computation | async-start | bytes 2097152 | tf_op jit(solution)/shard_map/all_to_all | solution.py:208
  10.5 7.2 %collective-permute-start = (bf16[256,1024]{1,0:T(8,128)(2,1)}, bf16[256,1024]{1,0:T(8,128)(2,1)S(1)}, u32[]{:S(2)}, u32[]{:S(2)}) collective-permute-start(bf16[256,1024]{1,0:T(8,128)(2,1)} %param.17), channel_id=1, source_target_pairs={{0,0},{1,16},{2,32},{3,48},{4,64},{5,80},{6,96},{7,112},{8,128},{9... | collective-permute-start | bytes 1572872 | tf_op jit(solution)/shard_map/ppermute | solution.py:211
  19.0 0.6 compare_reduce_fusion.1
  19.6 0.6 compare_reduce_fusion
  20.3 2.0 fusion.21
  22.2 0.1 copy.23
  22.3 0.1 copy.22
  22.5 1.4 copy.24.own_slot_ref
  23.9 0.2 scatter.9
  24.1 1.9 pad_maximum_fusion.block_ref
  26.0 85.7 %shard_map.103 = bf16[16,128,2176]{2,1,0:T(8,128)(2,1)} custom-call(bf16[128,2176]{1,0:T(8,128)(2,1)} %pad_maximum_fusion.block_ref), custom_call_target="tpu_custom_call" | custom-call | tf_op jit(solution)/shard_map/pallas_call | solution.py:86
  111.7 0.0 all-to-all-done
  111.7 0.5 copy.21
  112.2 0.0 copy-start
  112.3 0.0 collective-permute-done
  112.3 0.0 copy-start.6
  112.3 3.0 %convert_reduce_fusion = f32[2048]{0:T(1024)S(1)} fusion(bf16[2048,2176]{1,0:T(8,128)(2,1)} %bitcast.17), kind=kLoop, calls=%fused_computation.3 | loop fusion | flops 4192256 | bytes 4202496 | tf_op jit(solution)/shard_map/jvp()/reduce_sum | solution.py:177
  115.3 3.0 %add_reduce_fusion = s32[2048]{0:T(1024)} fusion(bf16[2048,2176]{1,0:T(8,128)(2,1)} %bitcast.18), kind=kLoop, calls=%fused_computation.25 | loop fusion | flops 8192 | bytes 16384 | tf_op jit(solution)/shard_map/add | solution.py:219
  118.3 3.0 %fusion.6 = f32[2048]{0:T(1024)S(1)} fusion(f32[2048]{0:T(1024)S(1)} %broadcast_multiply_fusion, bf16[2048,2176]{1,0:T(8,128)(2,1)} %bitcast.19), kind=kLoop, calls=%fused_computation.12 | loop fusion | flops 8386560 | bytes 4210688 | tf_op jit(solution)/shard_map/jvp()/reduce_sum | solution.py:178
  121.3 0.0 copy-done.5
  121.3 0.0 copy-done
  121.3 2.8 %fusion.12 = (f32[2048]{0:T(1024)S(1)}, f32[2048]{0:T(1024)S(1)}) fusion(f32[1024]{0:T(1024)S(1)} %copy-done.5, f32[2048]{0:T(1024)S(1)} %fusion.19, f32[2048]{0:T(1024)S(1)} %broadcast_multiply_fusion, bf16[2048,2176]{1,0:T(8,128)(2,1)S(1)} %bitcast.23), kind=kLoop, calls=%fused_computation.18 | loop fusion | flops 18870272 | bytes 8425472 | tf_op jit(solution)/shard_map/jvp()/reduce_sum | solution.py:173
  124.1 0.0 copy-done.6
  124.2 4.9 %fusion.13 = (bf16[2048,1024]{1,0:T(8,128)(2,1)}, bf16[2048,1024]{1,0:T(8,128)(2,1)}) fusion(f32[2048]{0:T(1024)S(1)} %get-tuple-element.50, f32[1024]{0:T(1024)S(1)} %copy-done.5, f32[2048]{0:T(1024)S(1)} %fusion.19, f32[2048]{0:T(1024)S(1)} %broadcast_multiply_fusion, bf16[2048,2176]{1,0:T(8,128)(2,1)S(1)} %bitcast.24, f32[2048]{0:T(1024)S(1)} %get-tuple-element.49), kind=kLoop, calls=%fused_computation.19 | loop fusion | flops 18874368 | bytes 16814080 | tf_op jit(solution)/shard_map/convert_element_type | solution.py:227
  129.0 25.3 %shard_map.104 = (f32[2048,1024]{1,0:T(8,128)}, f32[128,1024]{1,0:T(8,128)}) custom-call(f32[1]{0:T(128)S(6)} %copy.31.scale_ref, f32[1]{0:T(128)S(6)} %copy.32.shift_ref, s32[128,1]{1,0:T(8,128)} %copy.24.own_slot_ref, s32[1,2048]{1,0:T(1,128)} %bitcast.30, bf16[2048,1024]{1,0:T(8,128)(2,1)} %get-tuple-element.44.images_ref, ...), custom_call_target="tpu_custom_call" | custom-call | flops 18253611008 | bytes 17301504 | tf_op jit(solution)/shard_map/pallas_call | solution.py:144
  154.4 5.8 %fusion.14 = f32[2048]{0:T(1024)S(1)} fusion(f32[2048,1024]{1,0:T(8,128)} %get-tuple-element.34, f32[1024]{0:T(1024)S(1)} %copy-done.5, f32[2048]{0:T(1024)S(1)} %fusion.19, f32[2048]{0:T(1024)S(1)} %broadcast_multiply_fusion, bf16[2048,2176]{1,0:T(8,128)(2,1)} %bitcast.20), kind=kLoop, calls=%fused_computation.20 | loop fusion | flops 12580864 | bytes 12611584 | tf_op jit(solution)/shard_map/transpose(jvp())/reduce_sum | solution.py:173
  160.3 1.2 copy-done.1
  161.4 5.4 %fusion.15 = f32[2048]{0:T(1024)S(1)} fusion(f32[2048,1024]{1,0:T(8,128)S(1)} %copy-done.1, f32[2048]{0:T(1024)S(1)} %multiply_multiply_fusion.1, f32[2048]{0:T(1024)S(1)} %get-tuple-element.50, f32[1024]{0:T(1024)S(1)} %copy-done.5, f32[2048]{0:T(1024)S(1)} %fusion.19, f32[2048]{0:T(1024)S(1)} %broadcast_multiply_fusion, bf16[2048,2176]{1,0:T(8,128)(2,1)} %bitcast.21), kind=kLoop, calls=%fused_computation.21 | loop fusion | flops 23066624 | bytes 12627968 | tf_op jit(solution)/shard_map/transpose(jvp())/reduce_sum | solution.py:179
  166.9 6.8 %fusion.24 = (f32[2048]{0:T(1024)S(1)}, f32[2048,1024]{1,0:T(8,128)S(1)}) fusion(f32[2048]{0:T(1024)S(1)} %multiply_multiply_fusion, f32[2048]{0:T(1024)S(1)} %multiply_multiply_fusion.1, f32[1024]{0:T(1024)S(1)} %copy-done.5, f32[2048]{0:T(1024)S(1)} %fusion.19, f32[2048]{0:T(1024)S(1)} %broadcast_multiply_fusion, bf16[2048,2176]{1,0:T(8,128)(2,1)} %bitcast.22, ...), kind=kLoop, calls=%fused_computation.57 | loop fusion | flops 29358080 | bytes 21024768 | tf_op jit(solution)/shard_map/transpose(jvp())/reduce_sum | solution.py:177
  173.7 0.0 copy-start.7
  173.7 3.2 %copy-done.2 = f32[2048,1024]{1,0:T(8,128)} copy-done((f32[2048,1024]{1,0:T(8,128)}, f32[2048,1024]{1,0:T(8,128)S(1)}, u32[]{:S(2)}) %copy-start.2) | copy-done | bytes 8388632
  176.9 3.3 %fusion.23 = f32[256,1024]{0,1:T(8,128)} fusion(bf16[2048,256]{1,0:T(8,128)(2,1)S(1)} %bitcast.27, f32[2048,1024]{1,0:T(8,128)S(1)} %get-tuple-element.42, f32[2048]{0:T(1024)S(1)} %negate_multiply_fusion), kind=kOutput, calls=%fused_computation.56 | convolution fusion | flops 1077936128 | bytes 10493952 | tf_op jit(solution)/shard_map/dot_general | solution.py:246
  180.2 11.7 %all-to-all-start.2 = ((f32[256,16,64]{0,2,1:T(8,128)}), f32[256,16,64]{0,2,1:T(8,128)S(1)}, u32[]{:S(2)}, u32[]{:S(2)}) async-start(f32[256,16,64]{0,2,1:T(8,128)} %bitcast.9), calls=%async_computation.2 | async-start | bytes 2097152 | tf_op jit(solution)/shard_map/all_to_all | solution.py:249
  192.0 0.0 copy-start.3
  192.0 0.0 copy-start.4
  192.0 5.7 %convolution_convert_fusion = bf16[2048,256]{1,0:T(8,128)(2,1)} fusion(bf16[256,1024]{1,0:T(8,128)(2,1)S(1)} %copy-done.7, f32[2048,1024]{1,0:T(8,128)} %copy-done.2, f32[2048]{0:T(1024)S(1)} %negate_multiply_fusion), kind=kOutput, calls=%fused_computation.24 | convolution fusion | flops 1078460416 | bytes 9969664 | tf_op jit(solution)/shard_map/dot_general | solution.py:239
  197.7 19.1 %all-to-all-done.2 = f32[256,16,64]{0,2,1:T(8,128)S(1)} async-done(((f32[256,16,64]{0,2,1:T(8,128)}), f32[256,16,64]{0,2,1:T(8,128)S(1)}, u32[]{:S(2)}, u32[]{:S(2)}) %all-to-all-start.2) | async-done | bytes 1048608 | tf_op jit(solution)/shard_map/all_to_all | solution.py:249
  216.8 12.7 %all-to-all-start.1 = ((bf16[16,128,256]{2,1,0:T(8,128)(2,1)}), bf16[16,128,256]{2,1,0:T(8,128)(2,1)S(1)}, u32[]{:S(2)}, u32[]{:S(2)}) async-start(bf16[16,128,256]{2,1,0:T(8,128)(2,1)} %bitcast.28), calls=%async_computation.1 | async-start | bytes 2097152 | tf_op jit(solution)/shard_map/all_to_all | solution.py:245
  229.6 0.0 copy-done.4
  229.6 0.2 fusion.17
  229.8 0.1 reduce_sum.115
  229.8 5.2 %collective-permute-start.1 = (f32[256,64]{0,1:T(8,128)S(1)}, f32[256,64]{0,1:T(8,128)S(1)}, u32[]{:S(2)}, u32[]{:S(2)}) collective-permute-start(f32[256,64]{0,1:T(8,128)S(1)} %reduce_sum.115), channel_id=1, source_target_pairs={{0,0},{1,16},{2,32},{3,48},{4,64},{5,80},{6,96},{7,112},{8,128},{9... | collective-permute-start | bytes 196616 | tf_op jit(solution)/shard_map/ppermute | solution.py:251
  235.1 0.9 add_add_fusion.2
  236.0 12.7 %all-to-all-done.1 = bf16[16,128,256]{2,1,0:T(8,128)(2,1)S(1)} async-done(((bf16[16,128,256]{2,1,0:T(8,128)(2,1)}), bf16[16,128,256]{2,1,0:T(8,128)(2,1)S(1)}, u32[]{:S(2)}, u32[]{:S(2)}) %all-to-all-start.1) | async-done | bytes 1048608 | tf_op jit(solution)/shard_map/all_to_all | solution.py:245
  248.7 1.1 copy.28
  249.8 0.0 collective-permute-done.1
  249.8 0.6 copy.33
  (13 shorter events, 0.1 us)
Async XLA Ops:
  2.9 108.8 %all-to-all-start = ((bf16[128,16,256]{0,2,1:T(8,128)(2,1)}), bf16[128,16,256]{0,2,1:T(8,128)(2,1)S(1)}, u32[]{:S(2)}, u32[]{:S(2)}) async-start(bf16[128,16,256]{0,2,1:T(8,128)(2,1)} %bitcast.1), calls=%async_computation | async-start | bytes 2097152 | tf_op jit(solution)/shard_map/all_to_all | solution.py:208
  10.5 101.8 %collective-permute-start = (bf16[256,1024]{1,0:T(8,128)(2,1)}, bf16[256,1024]{1,0:T(8,128)(2,1)S(1)}, u32[]{:S(2)}, u32[]{:S(2)}) collective-permute-start(bf16[256,1024]{1,0:T(8,128)(2,1)} %param.17), channel_id=1, source_target_pairs={{0,0},{1,16},{2,32},{3,48},{4,64},{5,80},{6,96},{7,112},{8,128},{9... | collective-permute-start | bytes 1572872 | tf_op jit(solution)/shard_map/ppermute | solution.py:211
  26.0 95.3 %copy-start.5 = (f32[1024]{0:T(1024)S(1)}, f32[1024]{0:T(1024)}, u32[]{:S(2)}) copy-start(f32[1024]{0:T(1024)} %param.16) | copy-start | bytes 12292
  112.2 9.0 %copy-start = (bf16[16,128,2176]{2,1,0:T(8,128)(2,1)S(1)}, bf16[16,128,2176]{2,1,0:T(8,128)(2,1)}, u32[]{:S(2)}) copy-start(bf16[16,128,2176]{2,1,0:T(8,128)(2,1)} %shard_map.103) | copy-start | bytes 26738692
  112.3 11.9 %copy-start.6 = (bf16[256,1024]{1,0:T(8,128)(2,1)}, bf16[256,1024]{1,0:T(8,128)(2,1)S(1)}, u32[]{:S(2)}) copy-start(bf16[256,1024]{1,0:T(8,128)(2,1)S(1)} %collective-permute-done) | copy-start | bytes 1572868
  154.4 7.1 %copy-start.1 = (f32[2048,1024]{1,0:T(8,128)S(1)}, f32[2048,1024]{1,0:T(8,128)}, u32[]{:S(2)}) copy-start(f32[2048,1024]{1,0:T(8,128)} %get-tuple-element.34) | copy-start | bytes 25165828
  173.7 3.2 %copy-start.2 = (f32[2048,1024]{1,0:T(8,128)}, f32[2048,1024]{1,0:T(8,128)S(1)}, u32[]{:S(2)}) copy-start(f32[2048,1024]{1,0:T(8,128)S(1)} %get-tuple-element.42) | copy-start | bytes 25165828
  173.7 18.2 %copy-start.7 = (bf16[256,1024]{1,0:T(8,128)(2,1)S(1)}, bf16[256,1024]{1,0:T(8,128)(2,1)}, u32[]{:S(2)}) copy-start(bf16[256,1024]{1,0:T(8,128)(2,1)} %copy-done.6) | copy-start | bytes 1572868
  180.2 36.6 %all-to-all-start.2 = ((f32[256,16,64]{0,2,1:T(8,128)}), f32[256,16,64]{0,2,1:T(8,128)S(1)}, u32[]{:S(2)}, u32[]{:S(2)}) async-start(f32[256,16,64]{0,2,1:T(8,128)} %bitcast.9), calls=%async_computation.2 | async-start | bytes 2097152 | tf_op jit(solution)/shard_map/all_to_all | solution.py:249
  192.0 37.6 %copy-start.3 = (bf16[128,1024]{1,0:T(8,128)(2,1)S(1)}, bf16[128,1024]{1,0:T(8,128)(2,1)}, u32[]{:S(2)}) copy-start(bf16[128,1024]{1,0:T(8,128)(2,1)} %param.12) | copy-start | bytes 786436
  192.0 37.6 %copy-start.4 = (f32[128,1024]{1,0:T(8,128)S(1)}, f32[128,1024]{1,0:T(8,128)}, u32[]{:S(2)}) copy-start(f32[128,1024]{1,0:T(8,128)} %get-tuple-element.33) | copy-start | bytes 1572868
  216.8 31.9 %all-to-all-start.1 = ((bf16[16,128,256]{2,1,0:T(8,128)(2,1)}), bf16[16,128,256]{2,1,0:T(8,128)(2,1)S(1)}, u32[]{:S(2)}, u32[]{:S(2)}) async-start(bf16[16,128,256]{2,1,0:T(8,128)(2,1)} %bitcast.28), calls=%async_computation.1 | async-start | bytes 2097152 | tf_op jit(solution)/shard_map/all_to_all | solution.py:245
  229.8 20.0 %collective-permute-start.1 = (f32[256,64]{0,1:T(8,128)S(1)}, f32[256,64]{0,1:T(8,128)S(1)}, u32[]{:S(2)}, u32[]{:S(2)}) collective-permute-start(f32[256,64]{0,1:T(8,128)S(1)} %reduce_sum.115), channel_id=1, source_target_pairs={{0,0},{1,16},{2,32},{3,48},{4,64},{5,80},{6,96},{7,112},{8,128},{9... | collective-permute-start | bytes 196616 | tf_op jit(solution)/shard_map/ppermute | solution.py:251

commit v13 on v12

--- a/solution.py
+++ b/solution.py
@@ -10,7 +10,9 @@
 MESH = pl.DeviceIdType.MESH
 
 
-def gather_kernel(chips, block_ref, out_ref, send_sem, recv_sem, local_sem):
+def gather_kernel(chips, m, *refs):
+    block_refs, out_refs = refs[:m], refs[m : 2 * m]
+    send_sem, recv_sem, local_sem = refs[2 * m :]
     me = lax.axis_index("dp")
     zz = lax.axis_index("zero")
     core = me % 2
@@ -29,72 +31,65 @@
         pl.semaphore_signal(barrier, inc=1, device_id=(peer(k), zz), device_id_type=MESH)
     pl.semaphore_wait(barrier, chips)
 
-    local = pltpu.make_async_copy(block_ref, out_ref.at[me], local_sem)
-    local.start()
-    sends = []
-    for k in range(1, chips):
-        copy = pltpu.make_async_remote_copy(
-            src_ref=block_ref,
-            dst_ref=out_ref.at[me],
-            send_sem=send_sem.at[k],
-            recv_sem=recv_sem.at[me],
-            device_id=(peer(k), zz),
+    def remote(i, src, slot, send_index, target):
+        return pltpu.make_async_remote_copy(
+            src_ref=src,
+            dst_ref=out_refs[i].at[slot],
+            send_sem=send_sem.at[i, send_index],
+            recv_sem=recv_sem.at[i, slot],
+            device_id=(target, zz),
             device_id_type=MESH,
         )
+
+    locals_ = []
+    sends = []
+    for i in range(m):
+        local = pltpu.make_async_copy(block_refs[i], out_refs[i].at[me], local_sem.at[i])
+        local.start()
+        locals_.append(local)
+    for k in range(1, chips):
+        for i in range(m):
+            copy = remote(i, block_refs[i], me, k, peer(k))
+            copy.start()
+            sends.append(copy)
+    for i in range(m):
+        copy = remote(i, block_refs[i], me, 0, sibling)
         copy.start()
         sends.append(copy)
-    copy = pltpu.make_async_remote_copy(
-        src_ref=block_ref,
-        dst_ref=out_ref.at[me],
-        send_sem=send_sem.at[0],
-        recv_sem=recv_sem.at[me],
-        device_id=(sibling, zz),
-        device_id_type=MESH,
-    )
-    copy.start()
-    sends.append(copy)
     for k in range(1, chips):
         s = source(k)
-        arrived = pltpu.make_async_remote_copy(
-            src_ref=out_ref.at[s],
-            dst_ref=out_ref.at[s],
-            send_sem=send_sem.at[chips + k],
-            recv_sem=recv_sem.at[s],
-            device_id=(sibling, zz),
-            device_id_type=MESH,
-        )
-        arrived.wait_recv()
-        arrived.start()
-        sends.append(arrived)
+        for i in range(m):
+            arrived = remote(i, out_refs[i].at[s], s, chips + k, sibling)
+            arrived.wait_recv()
+            arrived.start()
+            sends.append(arrived)
     for k in range(chips):
         t = ((chip + k) % chips) * 2 + (1 - core)
-        pltpu.make_async_remote_copy(
-            src_ref=out_ref.at[t],
-            dst_ref=out_ref.at[t],
-            send_sem=send_sem.at[0],
-            recv_sem=recv_sem.at[t],
-            device_id=(sibling, zz),
-            device_id_type=MESH,
-        ).wait_recv()
+        for i in range(m):
+            remote(i, out_refs[i].at[t], t, 0, sibling).wait_recv()
     for copy in sends:
         copy.wait_send()
-    local.wait()
-
-
-def gather_dp(block):
+    for local in locals_:
+        local.wait()
+
+
+def gather_dp(*blocks):
     dp_size = lax.axis_size("dp")
+    m = len(blocks)
     return pl.pallas_call(
-        functools.partial(gather_kernel, dp_size // 2),
-        out_shape=jax.ShapeDtypeStruct((dp_size,) + block.shape, block.dtype),
-        in_specs=[pl.BlockSpec(memory_space=pl.ANY)],
-        out_specs=pl.BlockSpec(memory_space=pl.ANY),
+        functools.partial(gather_kernel, dp_size // 2, m),
+        out_shape=tuple(
+            jax.ShapeDtypeStruct((dp_size,) + block.shape, block.dtype) for block in blocks
+        ),
+        in_specs=[pl.BlockSpec(memory_space=pl.ANY)] * m,
+        out_specs=tuple(pl.BlockSpec(memory_space=pl.ANY) for _ in blocks),
         scratch_shapes=[
-            pltpu.SemaphoreType.DMA((dp_size,)),
-            pltpu.SemaphoreType.DMA((dp_size,)),
-            pltpu.SemaphoreType.DMA(()),
+            pltpu.SemaphoreType.DMA((m, dp_size)),
+            pltpu.SemaphoreType.DMA((m, dp_size)),
+            pltpu.SemaphoreType.DMA((m,)),
         ],
         compiler_params=pltpu.CompilerParams(collective_id=0, has_side_effects=True),
-    )(block)
+    )(*blocks)
 
 
 def contrast_kernel(
@@ -210,15 +205,18 @@
     )
     weight_block = lax.ppermute(contracting_matrix, ("dp", "zero"), transpose_route)
 
-    digits = jnp.zeros((local_rows, 128), jnp.bfloat16)
-    digits = digits.at[:, 0].set((matched_slot // 256).astype(jnp.bfloat16))
-    digits = digits.at[:, 1].set((matched_slot % 256).astype(jnp.bfloat16))
-    both = jnp.concatenate([picture_embeds, summary_token_states, digits], axis=1)
-    both_g = gather_dp(both).reshape((-1, both.shape[1]))
-    ffa_cols, weight_block, both_g = lax.optimization_barrier((ffa_cols, weight_block, both_g))
-    slot_g = both_g[:, 2 * width].astype(jnp.int32) * 256 + both_g[:, 2 * width + 1].astype(
-        jnp.int32
-    )
+    digits = jnp.zeros((16, local_rows), jnp.bfloat16)
+    digits = digits.at[0].set((matched_slot // 256).astype(jnp.bfloat16))
+    digits = digits.at[1].set((matched_slot % 256).astype(jnp.bfloat16))
+    both = jnp.concatenate([picture_embeds, summary_token_states], axis=1)
+    both_g, digits_g = gather_dp(both, digits)
+    both_g = both_g.reshape((-1, both.shape[1]))
+    ffa_cols, weight_block, both_g, digits_g = lax.optimization_barrier(
+        (ffa_cols, weight_block, both_g, digits_g)
+    )
+    slot_g = (
+        digits_g[:, 0, :].astype(jnp.int32) * 256 + digits_g[:, 1, :].astype(jnp.int32)
+    ).reshape((-1,))
     image_b_g = unit_rows(both_g[:, :width].astype(jnp.float32)).astype(jnp.bfloat16)
     caption_g, caption_back = jax.vjp(
         lambda feats: text_embed(feats, closing_layernorm_multiplier),

time: 251 us -> 245 us (0.976)
  other arithmetic: 41.2 us -> 36.4 us
    another operation x3 -> x1, other arithmetic: 3.24 us -> 0.67 us
    unnamed x18 -> x20, local copies, waits for them, and re-layouts: 7.3 us -> 7.29 us
  transfers between devices with their start and end apart: 5 -> 5, of which waited for: 2 -> 2; matrix products, arithmetic and copies ran while one was open for 6% -> 5% of each run, Pallas kernels for 34% -> 35%
where the time goes in v13:
time: 245 us
  Pallas kernels  111 us (45%)
  starting transfers between devices  43.8 us (18%)
  other arithmetic  36.4 us (15%)
  waiting for transfers between devices  31.9 us (13%)
  local copies, waits for them, and re-layouts  10.3 us (4%)
  matrix products  9.01 us (4%)
    pallas_call x1, Pallas kernels, gather_dp(): pl.pallas_call(functools.partial(gather_kernel, dp_size // 2, m), out_sha...  85.9 us
    pallas_call x1, Pallas kernels, contrast_group(): pl.pallas_call(contrast_kernel, grid=(group_rows // tc,), out_shape=(jax....  25.3 us
    all_to_all x1, waiting for transfers between devices, shards(): lax.all_to_all(group_sum, 'zero', split_axis=1, concat_axis=0, tiled=True)  19.2 us
    all_to_all x1, starting transfers between devices, shards(): lax.all_to_all(group_sum, 'zero', split_axis=1, concat_axis=0, tiled=True)  13 us
    all_to_all x1, waiting for transfers between devices, shards(): lax.all_to_all(hidden_part, 'dp', split_axis=0, concat_axis=1, tiled=True)  12.7 us
    all_to_all x1, starting transfers between devices, shards(): lax.all_to_all(hidden_part, 'dp', split_axis=0, concat_axis=1, tiled=True)  10.8 us
    reduce_sum x2, other arithmetic, text_embed(): center = features - jnp.mean(features, axis=1, keepdims=True)  9.11 us
    all_to_all x1, starting transfers between devices, shards(): lax.all_to_all(feedforward_inner_activations, 'dp', split_axis=1, concat_...  7.59 us
  transfers between devices with their start and end apart: 5, of which 2 were waited for; matrix products, arithmetic and copies ran while one was open for 5% of the time, Pallas kernels for 35%

profile of v13, /device:TPU:57, one launch (start us, length us, event | category | flops | bytes accessed | tf_op | source)
XLA Modules:
  0.0 244.8 jit_solution(13873379813689825420)
XLA Ops:
  0.6 0.0 copy-start.5
  0.6 2.3 copy.16
  2.9 7.6 %all-to-all-start = ((bf16[128,16,256]{0,2,1:T(8,128)(2,1)}), bf16[128,16,256]{0,2,1:T(8,128)(2,1)S(1)}, u32[]{:S(2)}, u32[]{:S(2)}) async-start(bf16[128,16,256]{0,2,1:T(8,128)(2,1)} %bitcast.1), calls=%async_computation | async-start | bytes 2097152 | tf_op jit(solution)/shard_map/all_to_all | solution.py:203
  10.5 7.2 %collective-permute-start = (bf16[256,1024]{1,0:T(8,128)(2,1)}, bf16[256,1024]{1,0:T(8,128)(2,1)S(1)}, u32[]{:S(2)}, u32[]{:S(2)}) collective-permute-start(bf16[256,1024]{1,0:T(8,128)(2,1)} %param.17), channel_id=1, source_target_pairs={{0,0},{1,16},{2,32},{3,48},{4,64},{5,80},{6,96},{7,112},{8,128},{9... | collective-permute-start | bytes 1572872 | tf_op jit(solution)/shard_map/ppermute | solution.py:206
  19.0 1.4 copy.18.own_slot_ref
  20.4 0.7 fusion.21
  21.1 0.0 copy-start.6
  21.1 1.9 pad_maximum_fusion.refs_0_
  23.0 0.0 copy-done.6
  23.0 85.9 %shard_map.103 = (bf16[16,128,2048]{2,1,0:T(8,128)(2,1)}, bf16[16,16,128]{2,1,0:T(8,128)(2,1)}) custom-call(bf16[128,2048]{1,0:T(8,128)(2,1)} %pad_maximum_fusion.refs_0_, bf16[16,128]{1,0:T(8,128)(2,1)} %copy-done.6), custom_call_target="tpu_custom_call" | custom-call | tf_op jit(solution)/shard_map/pallas_call | solution.py:79
  108.9 0.0 all-to-all-done
  108.9 0.5 copy.17
  109.4 0.0 copy-start
  109.4 0.0 collective-permute-done
  109.5 1.6 add_bitcast_fusion.slot_ref
  111.0 3.2 %convert_reduce_fusion = f32[2048]{0:T(1024)S(1)} fusion(bf16[2048,2048]{1,0:T(8,128)(2,1)} %bitcast.18), kind=kLoop, calls=%fused_computation.3 | loop fusion | flops 4192256 | bytes 4202496 | tf_op jit(solution)/shard_map/jvp()/reduce_sum | solution.py:172
  114.2 3.0 %fusion.6 = f32[2048]{0:T(1024)S(1)} fusion(f32[2048]{0:T(1024)S(1)} %broadcast_multiply_fusion, bf16[2048,2048]{1,0:T(8,128)(2,1)} %bitcast.19), kind=kLoop, calls=%fused_computation.12 | loop fusion | flops 8386560 | bytes 4210688 | tf_op jit(solution)/shard_map/jvp()/reduce_sum | solution.py:173
  117.2 0.0 copy-done.5
  117.3 0.0 copy-done
  117.3 2.8 %fusion.12 = (f32[2048]{0:T(1024)S(1)}, f32[2048]{0:T(1024)S(1)}) fusion(f32[1024]{0:T(1024)S(1)} %copy-done.5, f32[2048]{0:T(1024)S(1)} %fusion.19, f32[2048]{0:T(1024)S(1)} %broadcast_multiply_fusion, bf16[2048,2048]{1,0:T(8,128)(2,1)S(1)} %bitcast.22), kind=kLoop, calls=%fused_computation.18 | loop fusion | flops 18870272 | bytes 8425472 | tf_op jit(solution)/shard_map/jvp()/reduce_sum | solution.py:168
  120.1 4.7 %fusion.13 = (bf16[2048,1024]{1,0:T(8,128)(2,1)}, bf16[2048,1024]{1,0:T(8,128)(2,1)}) fusion(f32[2048]{0:T(1024)S(1)} %get-tuple-element.56, f32[1024]{0:T(1024)S(1)} %copy-done.5, f32[2048]{0:T(1024)S(1)} %fusion.19, f32[2048]{0:T(1024)S(1)} %broadcast_multiply_fusion, bf16[2048,2048]{1,0:T(8,128)(2,1)S(1)} %bitcast.23, f32[2048]{0:T(1024)S(1)} %get-tuple-element.55), kind=kLoop, calls=%fused_computation.19 | loop fusion | flops 18874368 | bytes 16814080 | tf_op jit(solution)/shard_map/convert_element_type | solution.py:225
  124.8 25.3 %shard_map.104 = (f32[2048,1024]{1,0:T(8,128)}, f32[128,1024]{1,0:T(8,128)}) custom-call(f32[1]{0:T(128)S(6)} %copy.25.scale_ref, f32[1]{0:T(128)S(6)} %copy.26.shift_ref, s32[128,1]{1,0:T(8,128)} %copy.18.own_slot_ref, s32[1,2048]{1,0:T(1,128)} %add_bitcast_fusion.slot_ref, bf16[2048,1024]{1,0:T(8,128)(2,1)} %get-tuple-element.50.images_ref, ...), custom_call_target="tpu_custom_call" | custom-call | flops 18253611008 | bytes 17301504 | tf_op jit(solution)/shard_map/pallas_call | solution.py:139
  150.2 0.0 copy-start.1
  150.2 0.0 slice-start
  150.2 5.8 %fusion.14 = f32[2048]{0:T(1024)S(1)} fusion(f32[2048,1024]{1,0:T(8,128)} %get-tuple-element.40, f32[1024]{0:T(1024)S(1)} %copy-done.5, f32[2048]{0:T(1024)S(1)} %fusion.19, f32[2048]{0:T(1024)S(1)} %broadcast_multiply_fusion, bf16[2048,2048]{1,0:T(8,128)(2,1)} %bitcast.20), kind=kLoop, calls=%fused_computation.20 | loop fusion | flops 12580864 | bytes 12611584 | tf_op jit(solution)/shard_map/transpose(jvp())/reduce_sum | solution.py:168
  156.0 1.2 copy-done.1
  157.2 5.6 %fusion.15 = f32[2048]{0:T(1024)S(1)} fusion(f32[2048,1024]{1,0:T(8,128)S(1)} %copy-done.1, f32[2048]{0:T(1024)S(1)} %multiply_multiply_fusion.1, f32[2048]{0:T(1024)S(1)} %get-tuple-element.56, f32[1024]{0:T(1024)S(1)} %copy-done.5, f32[2048]{0:T(1024)S(1)} %fusion.19, f32[2048]{0:T(1024)S(1)} %broadcast_multiply_fusion, bf16[2048,2048]{1,0:T(8,128)(2,1)} %bitcast.21), kind=kLoop, calls=%fused_computation.21 | loop fusion | flops 23066624 | bytes 12627968 | tf_op jit(solution)/shard_map/transpose(jvp())/reduce_sum | solution.py:174
  162.9 0.0 slice-done
  162.9 0.0 slice-done.1
  162.9 5.9 %fusion.23 = (f32[2048]{0:T(1024)S(1)}, f32[2048,1024]{1,0:T(8,128)S(1)}) fusion(f32[2048]{0:T(1024)S(1)} %multiply_multiply_fusion, f32[2048]{0:T(1024)S(1)} %multiply_multiply_fusion.1, f32[1024]{0:T(1024)S(1)} %copy-done.5, f32[2048]{0:T(1024)S(1)} %fusion.19, f32[2048]{0:T(1024)S(1)} %broadcast_multiply_fusion, bf16[2048,2048]{1,0:T(8,128)(2,1)S(1)} %bitcast.26, ...), kind=kLoop, calls=%fused_computation.52 | loop fusion | flops 29358080 | bytes 21024768 | tf_op jit(solution)/shard_map/transpose(jvp())/reduce_sum | solution.py:172
  168.8 0.0 copy-start.2
  168.8 3.2 %copy-done.2 = f32[2048,1024]{1,0:T(8,128)} copy-done((f32[2048,1024]{1,0:T(8,128)}, f32[2048,1024]{1,0:T(8,128)S(1)}, u32[]{:S(2)}) %copy-start.2) | copy-done | bytes 8388632
  172.0 3.3 %fusion.22 = f32[256,1024]{0,1:T(8,128)} fusion(bf16[2048,256]{1,0:T(8,128)(2,1)S(1)} %bitcast.29, f32[2048,1024]{1,0:T(8,128)S(1)} %get-tuple-element.48, f32[2048]{0:T(1024)S(1)} %negate_multiply_fusion), kind=kOutput, calls=%fused_computation.51 | convolution fusion | flops 1077936128 | bytes 10493952 | tf_op jit(solution)/shard_map/dot_general | solution.py:244
  175.3 13.0 %all-to-all-start.2 = ((f32[256,16,64]{0,2,1:T(8,128)}), f32[256,16,64]{0,2,1:T(8,128)S(1)}, u32[]{:S(2)}, u32[]{:S(2)}) async-start(f32[256,16,64]{0,2,1:T(8,128)} %bitcast.32), calls=%async_computation.2 | async-start | bytes 2097152 | tf_op jit(solution)/shard_map/all_to_all | solution.py:247
  188.3 0.0 copy-start.4
  188.3 5.7 %convolution_convert_fusion = bf16[2048,256]{1,0:T(8,128)(2,1)} fusion(bf16[256,1024]{1,0:T(8,128)(2,1)S(1)} %collective-permute-done, f32[2048,1024]{1,0:T(8,128)} %copy-done.2, f32[2048]{0:T(1024)S(1)} %negate_multiply_fusion), kind=kOutput, calls=%fused_computation.24 | convolution fusion | flops 1078460416 | bytes 9969664 | tf_op jit(solution)/shard_map/dot_general | solution.py:237
  194.0 19.2 %all-to-all-done.2 = f32[256,16,64]{0,2,1:T(8,128)S(1)} async-done(((f32[256,16,64]{0,2,1:T(8,128)}), f32[256,16,64]{0,2,1:T(8,128)S(1)}, u32[]{:S(2)}, u32[]{:S(2)}) %all-to-all-start.2) | async-done | bytes 1048608 | tf_op jit(solution)/shard_map/all_to_all | solution.py:247
  213.2 10.8 %all-to-all-start.1 = ((bf16[16,128,256]{2,1,0:T(8,128)(2,1)}), bf16[16,128,256]{2,1,0:T(8,128)(2,1)S(1)}, u32[]{:S(2)}, u32[]{:S(2)}) async-start(bf16[16,128,256]{2,1,0:T(8,128)(2,1)} %bitcast.30), calls=%async_computation.1 | async-start | bytes 2097152 | tf_op jit(solution)/shard_map/all_to_all | solution.py:243
  224.0 0.0 copy-done.3
  224.0 0.0 copy-done.4
  224.0 0.2 fusion.17
  224.2 0.1 reduce_sum.115
  224.2 5.2 %collective-permute-start.1 = (f32[256,64]{0,1:T(8,128)S(1)}, f32[256,64]{0,1:T(8,128)S(1)}, u32[]{:S(2)}, u32[]{:S(2)}) collective-permute-start(f32[256,64]{0,1:T(8,128)S(1)} %reduce_sum.115), channel_id=1, source_target_pairs={{0,0},{1,16},{2,32},{3,48},{4,64},{5,80},{6,96},{7,112},{8,128},{9... | collective-permute-start | bytes 196616 | tf_op jit(solution)/shard_map/ppermute | solution.py:249
  229.5 0.9 add_add_fusion.2
  230.4 12.7 %all-to-all-done.1 = bf16[16,128,256]{2,1,0:T(8,128)(2,1)S(1)} async-done(((bf16[16,128,256]{2,1,0:T(8,128)(2,1)}), bf16[16,128,256]{2,1,0:T(8,128)(2,1)S(1)}, u32[]{:S(2)}, u32[]{:S(2)}) %all-to-all-start.1) | async-done | bytes 1048608 | tf_op jit(solution)/shard_map/all_to_all | solution.py:243
  243.1 1.1 copy.22
  244.2 0.0 collective-permute-done.1
  244.2 0.6 copy.27
  (12 shorter events, 0.1 us)
Async XLA Ops:
  0.6 116.6 %copy-start.5 = (f32[1024]{0:T(1024)S(1)}, f32[1024]{0:T(1024)}, u32[]{:S(2)}) copy-start(f32[1024]{0:T(1024)} %param.16) | copy-start | bytes 12292
  2.9 106.0 %all-to-all-start = ((bf16[128,16,256]{0,2,1:T(8,128)(2,1)}), bf16[128,16,256]{0,2,1:T(8,128)(2,1)S(1)}, u32[]{:S(2)}, u32[]{:S(2)}) async-start(bf16[128,16,256]{0,2,1:T(8,128)(2,1)} %bitcast.1), calls=%async_computation | async-start | bytes 2097152 | tf_op jit(solution)/shard_map/all_to_all | solution.py:203
  10.5 98.9 %collective-permute-start = (bf16[256,1024]{1,0:T(8,128)(2,1)}, bf16[256,1024]{1,0:T(8,128)(2,1)S(1)}, u32[]{:S(2)}, u32[]{:S(2)}) collective-permute-start(bf16[256,1024]{1,0:T(8,128)(2,1)} %param.17), channel_id=1, source_target_pairs={{0,0},{1,16},{2,32},{3,48},{4,64},{5,80},{6,96},{7,112},{8,128},{9... | collective-permute-start | bytes 1572872 | tf_op jit(solution)/shard_map/ppermute | solution.py:206
  21.1 1.9 copy-start.6
  109.4 7.8 %copy-start = (bf16[16,128,2048]{2,1,0:T(8,128)(2,1)S(1)}, bf16[16,128,2048]{2,1,0:T(8,128)(2,1)}, u32[]{:S(2)}) copy-start(bf16[16,128,2048]{2,1,0:T(8,128)(2,1)} %get-tuple-element.35) | copy-start | bytes 25165828
  150.2 7.0 %copy-start.1 = (f32[2048,1024]{1,0:T(8,128)S(1)}, f32[2048,1024]{1,0:T(8,128)}, u32[]{:S(2)}) copy-start(f32[2048,1024]{1,0:T(8,128)} %get-tuple-element.40) | copy-start | bytes 25165828
  150.2 12.7 %slice-start = ((s8[8388608]{0:T(1024)(128)(4,1)}), s8[4194304]{0:T(1024)(128)(4,1)S(1)}, s32[]{:S(2)}) async-start(s8[8388608]{0:T(1024)(128)(4,1)} %bitcast.24), calls=%async_computation.3 | async-start | bytes 8388608
  157.2 5.7 %slice-start.1 = ((s8[8388608]{0:T(1024)(128)(4,1)}), s8[4194304]{0:T(1024)(128)(4,1)S(1)}, s32[]{:S(2)}) async-start(s8[8388608]{0:T(1024)(128)(4,1)} %bitcast.24), calls=%async_computation.4 | async-start | bytes 8388608
  168.8 3.2 %copy-start.2 = (f32[2048,1024]{1,0:T(8,128)}, f32[2048,1024]{1,0:T(8,128)S(1)}, u32[]{:S(2)}) copy-start(f32[2048,1024]{1,0:T(8,128)S(1)} %get-tuple-element.48) | copy-start | bytes 25165828
  175.3 37.9 %all-to-all-start.2 = ((f32[256,16,64]{0,2,1:T(8,128)}), f32[256,16,64]{0,2,1:T(8,128)S(1)}, u32[]{:S(2)}, u32[]{:S(2)}) async-start(f32[256,16,64]{0,2,1:T(8,128)} %bitcast.32), calls=%async_computation.2 | async-start | bytes 2097152 | tf_op jit(solution)/shard_map/all_to_all | solution.py:247
  188.3 35.7 %copy-start.3 = (bf16[128,1024]{1,0:T(8,128)(2,1)S(1)}, bf16[128,1024]{1,0:T(8,128)(2,1)}, u32[]{:S(2)}) copy-start(bf16[128,1024]{1,0:T(8,128)(2,1)} %param.12) | copy-start | bytes 786436
  188.3 35.7 %copy-start.4 = (f32[128,1024]{1,0:T(8,128)S(1)}, f32[128,1024]{1,0:T(8,128)}, u32[]{:S(2)}) copy-start(f32[128,1024]{1,0:T(8,128)} %get-tuple-element.39) | copy-start | bytes 1572868
  213.2 29.9 %all-to-all-start.1 = ((bf16[16,128,256]{2,1,0:T(8,128)(2,1)}), bf16[16,128,256]{2,1,0:T(8,128)(2,1)S(1)}, u32[]{:S(2)}, u32[]{:S(2)}) async-start(bf16[16,128,256]{2,1,0:T(8,128)(2,1)} %bitcast.30), calls=%async_computation.1 | async-start | bytes 2097152 | tf_op jit(solution)/shard_map/all_to_all | solution.py:243
  224.2 20.0 %collective-permute-start.1 = (f32[256,64]{0,1:T(8,128)S(1)}, f32[256,64]{0,1:T(8,128)S(1)}, u32[]{:S(2)}, u32[]{:S(2)}) collective-permute-start(f32[256,64]{0,1:T(8,128)S(1)} %reduce_sum.115), channel_id=1, source_target_pairs={{0,0},{1,16},{2,32},{3,48},{4,64},{5,80},{6,96},{7,112},{8,128},{9... | collective-permute-start | bytes 196616 | tf_op jit(solution)/shard_map/ppermute | solution.py:249

commit v14 on v13

--- a/solution.py
+++ b/solution.py
@@ -93,16 +93,25 @@
 
 
 def contrast_kernel(
-    scale_ref, shift_ref, own_slot_ref, slot_ref, images_ref, captions_ref,
-    caption_out, image_out,
+    scale_ref, shift_ref, own_slot_ref, slot_ref, images_ref, feats_ref, gain_ref,
+    upstream_out, image_out,
 ):
     jb = pl.program_id(0)
-    tc = captions_ref.shape[0]
+    tc = feats_ref.shape[0]
+    width = feats_ref.shape[1]
     rows = own_slot_ref.shape[0]
     scale = scale_ref[0]
     half_scale = 0.5 * scale
     half_shift = 0.5 * shift_ref[0]
-    captions = captions_ref[...]
+    gain = gain_ref[...]
+
+    feats = feats_ref[...].astype(jnp.float32)
+    center = feats - jnp.sum(feats, axis=1, keepdims=True) / width
+    spread = jnp.sum(center * center, axis=1, keepdims=True) / width
+    inv_spread = lax.rsqrt(spread + 1e-05)
+    normed = center * inv_spread * gain
+    inv_norm = lax.rsqrt(jnp.sum(normed * normed, axis=1, keepdims=True) + 1e-06)
+    captions = (normed * inv_norm).astype(jnp.bfloat16)
     places = jb * tc + lax.broadcasted_iota(jnp.int32, (tc, 1), 0)
 
     def weights_of(products, positive):
@@ -114,8 +123,17 @@
         captions, images, (((1,), (1,)), ((), ())), preferred_element_type=jnp.float32
     )
     weights = weights_of(products, slot_ref[...] == places)
-    acc = jnp.dot(weights, images, preferred_element_type=jnp.float32)
-    caption_out[...] = scale * acc
+    caption_grad = scale * jnp.dot(weights, images, preferred_element_type=jnp.float32)
+
+    along = jnp.sum(caption_grad * normed, axis=1, keepdims=True)
+    normed_grad = inv_norm * caption_grad - inv_norm * inv_norm * inv_norm * along * normed
+    gained = gain * normed_grad
+    spread_grad = -0.5 * inv_spread * inv_spread * inv_spread * jnp.sum(
+        gained * center, axis=1, keepdims=True
+    )
+    center_grad = gained * inv_spread + (2.0 / width) * center * spread_grad
+    feats_grad = center_grad - jnp.sum(center_grad, axis=1, keepdims=True) / width
+    upstream_out[...] = feats_grad.astype(upstream_out.dtype)
 
     own_start = pl.multiple_of(lax.axis_index("dp") * rows, rows)
     own = images_ref[pl.ds(own_start, rows), :]
@@ -132,15 +150,15 @@
     image_out[...] += scale * jnp.dot(own_weights, captions, preferred_element_type=jnp.float32)
 
 
-def contrast_group(scale, shift, own_slot, slot_g, image_b_g, caption_b_g):
-    group_rows, width = caption_b_g.shape
+def contrast_group(scale, shift, own_slot, slot_g, image_b_g, both_g, gain):
+    group_rows, width = image_b_g.shape
     rows = own_slot.shape[0]
     tc = 512
     return pl.pallas_call(
         contrast_kernel,
         grid=(group_rows // tc,),
         out_shape=(
-            jax.ShapeDtypeStruct((group_rows, width), jnp.float32),
+            jax.ShapeDtypeStruct((group_rows, width), jnp.bfloat16),
             jax.ShapeDtypeStruct((rows, width), jnp.float32),
         ),
         in_specs=[
@@ -149,7 +167,8 @@
             pl.BlockSpec((rows, 1), lambda j: (0, 0)),
             pl.BlockSpec((1, group_rows), lambda j: (0, 0)),
             pl.BlockSpec((group_rows, width), lambda j: (0, 0)),
-            pl.BlockSpec((tc, width), lambda j: (j, 0)),
+            pl.BlockSpec((tc, width), lambda j: (j, 1)),
+            pl.BlockSpec((1, width), lambda j: (0, 0)),
         ],
         out_specs=(
             pl.BlockSpec((tc, width), lambda j: (j, 0)),
@@ -158,10 +177,18 @@
         compiler_params=pltpu.CompilerParams(dimension_semantics=("arbitrary",)),
         cost_estimate=pl.CostEstimate(
             flops=4 * group_rows * (group_rows + rows) * width,
-            bytes_accessed=2 * group_rows * width * 2 + (group_rows + rows) * width * 4,
+            bytes_accessed=3 * group_rows * width * 2 + rows * width * 4,
             transcendentals=group_rows * (group_rows + rows),
         ),
-    )(scale, shift, own_slot.reshape((rows, 1)), slot_g.reshape((1, group_rows)), image_b_g, caption_b_g)
+    )(
+        scale,
+        shift,
+        own_slot.reshape((rows, 1)),
+        slot_g.reshape((1, group_rows)),
+        image_b_g,
+        both_g,
+        gain.reshape((1, width)),
+    )
 
 
 def unit_rows(values):
@@ -218,21 +245,20 @@
         digits_g[:, 0, :].astype(jnp.int32) * 256 + digits_g[:, 1, :].astype(jnp.int32)
     ).reshape((-1,))
     image_b_g = unit_rows(both_g[:, :width].astype(jnp.float32)).astype(jnp.bfloat16)
-    caption_g, caption_back = jax.vjp(
-        lambda feats: text_embed(feats, closing_layernorm_multiplier),
-        both_g[:, width : 2 * width].astype(jnp.float32),
-    )
-    caption_b_g = caption_g.astype(jnp.bfloat16)
-    group_rows = caption_b_g.shape[0]
 
     unit_image, image_back = jax.vjp(unit_rows, picture_embeds.astype(jnp.float32))
 
-    caption_term, image_term = contrast_group(
-        sharpness_factor, additive_shift_learned, matched_slot, slot_g, image_b_g, caption_b_g
+    upstream_g, image_term = contrast_group(
+        sharpness_factor,
+        additive_shift_learned,
+        matched_slot,
+        slot_g,
+        image_b_g,
+        both_g,
+        closing_layernorm_multiplier,
     )
 
     image_grad = image_back(image_term)[0]
-    upstream_g = caption_back(caption_term)[0].astype(jnp.bfloat16)
 
     hidden_part = lax.dot_general(
         upstream_g,

time: 245 us -> 224 us (0.914)
  other arithmetic: 36.4 us -> 10.5 us
  Pallas kernels: 111 us -> 119 us
  local copies, waits for them, and re-layouts: 10.3 us -> 5.39 us
    reduce_sum x5 -> x0, other arithmetic: 23.6 us -> none  [the longest x2 9.11 us: text_embed(): center = features - jnp.mean(features, axis=1, keepdims=True)]
    pallas_call x1, Pallas kernels: 25.3 us -> 30.8 us  [contrast_group(): pl.pallas_call(contrast_kernel, grid=(group_rows // tc,), out_shape=(jax....]
    unnamed x20 -> x14, local copies, waits for them, and re-layouts: 7.29 us -> 3 us
  transfers between devices with their start and end apart: 5 -> 5, of which waited for: 2 -> 2; matrix products, arithmetic and copies ran while one was open for 5% -> 4% of each run, Pallas kernels for 35% -> 39%
where the time goes in v14:
time: 224 us; the launch traced here: 223 us
  Pallas kernels  119 us (53%)
  starting transfers between devices  43.8 us (20%)
  waiting for transfers between devices  33.1 us (15%)
  other arithmetic  10.5 us (5%)
  matrix products  9.4 us (4%)
  local copies, waits for them, and re-layouts  5.39 us (2%)
    pallas_call x1, Pallas kernels, gather_dp(): pl.pallas_call(functools.partial(gather_kernel, dp_size // 2, m), out_sha...  88.1 us
    pallas_call x1, Pallas kernels, contrast_group(): pl.pallas_call(contrast_kernel, grid=(group_rows // tc,), out_shape=(jax....  30.8 us
    all_to_all x1, waiting for transfers between devices, shards(): lax.all_to_all(group_sum, 'zero', split_axis=1, concat_axis=0, tiled=True)  20.4 us
    all_to_all x1, starting transfers between devices, shards(): lax.all_to_all(group_sum, 'zero', split_axis=1, concat_axis=0, tiled=True)  13.2 us
    all_to_all x1, waiting for transfers between devices, shards(): lax.all_to_all(hidden_part, 'dp', split_axis=0, concat_axis=1, tiled=True)  12.6 us
    all_to_all x1, starting transfers between devices, shards(): lax.all_to_all(hidden_part, 'dp', split_axis=0, concat_axis=1, tiled=True)  10.5 us
    all_to_all x1, starting transfers between devices, shards(): lax.all_to_all(feedforward_inner_activations, 'dp', split_axis=1, concat_...  7.59 us
    ppermute x1, starting transfers between devices, shards(): lax.ppermute(contracting_matrix, ('dp', 'zero'), transpose_route)  7.19 us
  transfers between devices with their start and end apart: 5, of which 2 were waited for; matrix products, arithmetic and copies ran while one was open for 4% of the time, Pallas kernels for 39%

profile of v14, /device:TPU:57, one launch (start us, length us, event | category | flops | bytes accessed | tf_op | source)
XLA Modules:
  0.0 223.2 jit_solution(9938612779858541284)
XLA Ops:
  0.6 0.0 copy-start.5
  0.6 0.0 copy-start.4
  0.7 0.0 copy-start
  0.7 0.0 copy-start.2
  0.7 2.3 %copy.16 = bf16[128,4096]{0,1:T(8,128)(2,1)} copy(bf16[128,4096]{1,0:T(8,128)(2,1)} %param.15) | data formatting | bytes 2097152 | tf_op args[3]
  3.0 7.6 %all-to-all-start = ((bf16[128,16,256]{0,2,1:T(8,128)(2,1)}), bf16[128,16,256]{0,2,1:T(8,128)(2,1)S(1)}, u32[]{:S(2)}, u32[]{:S(2)}) async-start(bf16[128,16,256]{0,2,1:T(8,128)(2,1)} %bitcast.1), calls=%async_computation | async-start | bytes 2097152 | tf_op jit(solution)/shard_map/all_to_all | solution.py:230
  10.6 0.0 copy-done.5
  10.6 7.2 %collective-permute-start = (bf16[256,1024]{1,0:T(8,128)(2,1)S(1)}, bf16[256,1024]{1,0:T(8,128)(2,1)S(1)}, u32[]{:S(2)}, u32[]{:S(2)}) collective-permute-start(bf16[256,1024]{1,0:T(8,128)(2,1)S(1)} %copy-done.5), channel_id=1, source_target_pairs={{0,0},{1,16},{2,32},{3,48},{4,64},{5,80},{6,96},{7,112},{8,128},{9... | collective-permute-start | bytes 1572872 | tf_op jit(solution)/shard_map/ppermute | solution.py:233
  19.1 0.0 copy-done.4
  19.1 0.7 copy.18.own_slot_ref
  19.9 0.0 copy-done
  19.9 0.0 copy-done.2
  19.9 0.0 copy-start.3
  19.9 0.8 pad_maximum_fusion.refs_0_
  20.8 0.0 copy-done.3
  20.8 88.1 %shard_map.103 = (bf16[16,128,2048]{2,1,0:T(8,128)(2,1)}, bf16[16,16,128]{2,1,0:T(8,128)(2,1)}) custom-call(bf16[128,2048]{1,0:T(8,128)(2,1)} %pad_maximum_fusion.refs_0_, bf16[16,128]{1,0:T(8,128)(2,1)} %copy-done.3), custom_call_target="tpu_custom_call" | custom-call | tf_op jit(solution)/shard_map/pallas_call | solution.py:79
  108.9 0.0 all-to-all-done
  108.9 0.5 copy.17
  109.5 0.0 collective-permute-done
  109.5 1.5 add_bitcast_fusion.slot_ref
  110.9 3.1 %fusion = f32[2048]{0:T(1024)S(1)} fusion(bf16[2048,2048]{1,0:T(8,128)(2,1)} %bitcast.21), kind=kLoop, calls=%fused_computation.2 | loop fusion | flops 6289408 | bytes 4202496 | tf_op jit(solution)/shard_map/reduce_sum | solution.py:195
  114.0 4.0 %fusion.1.images_ref = bf16[2048,1024]{1,0:T(8,128)(2,1)} fusion(f32[2048]{0:T(1024)S(1)} %add_rsqrt_fusion, bf16[2048,2048]{1,0:T(8,128)(2,1)} %bitcast.22), kind=kLoop, calls=%fused_computation.3 | loop fusion | flops 6291456 | bytes 8396800 | tf_op jit(solution)/shard_map/convert_element_type | solution.py:247
  118.0 30.8 %shard_map.104 = (bf16[2048,1024]{1,0:T(8,128)(2,1)}, f32[128,1024]{1,0:T(8,128)}) custom-call(f32[1]{0:T(128)S(6)} %copy.25.scale_ref, f32[1]{0:T(128)S(6)} %copy.26.shift_ref, s32[128,1]{1,0:T(8,128)} %copy.18.own_slot_ref, s32[1,2048]{1,0:T(1,128)} %add_bitcast_fusion.slot_ref, bf16[2048,1024]{1,0:T(8,128)(2,1)} %fusion.1.images_ref, ...), custom_call_target="tpu_custom_call" | custom-call | flops 18253611008 | bytes 13107200 | tf_op jit(solution)/shard_map/pallas_call | solution.py:157
  148.8 4.9 %fusion.6 = f32[256,1024]{0,1:T(8,128)} fusion(bf16[2048,256]{1,0:T(8,128)(2,1)S(1)} %bitcast.27, bf16[2048,1024]{1,0:T(8,128)(2,1)} %get-tuple-element.40), kind=kOutput, calls=%fused_computation.24 | convolution fusion | flops 1073741824 | bytes 6291456 | tf_op jit(solution)/shard_map/dot_general | solution.py:270
  153.7 13.2 %all-to-all-start.2 = ((f32[256,16,64]{0,2,1:T(8,128)}), f32[256,16,64]{0,2,1:T(8,128)S(1)}, u32[]{:S(2)}, u32[]{:S(2)}) async-start(f32[256,16,64]{0,2,1:T(8,128)} %bitcast.11), calls=%async_computation.2 | async-start | bytes 2097152 | tf_op jit(solution)/shard_map/all_to_all | solution.py:273
  166.9 0.0 copy-start.1
  166.9 4.5 %convolution_convert_fusion = bf16[2048,256]{1,0:T(8,128)(2,1)} fusion(bf16[2048,1024]{1,0:T(8,128)(2,1)} %get-tuple-element.40, bf16[256,1024]{1,0:T(8,128)(2,1)S(1)} %collective-permute-done), kind=kOutput, calls=%fused_computation.4 | convolution fusion | flops 1074266112 | bytes 5767168 | tf_op jit(solution)/shard_map/dot_general | solution.py:263
  171.4 20.4 %all-to-all-done.2 = f32[256,16,64]{0,2,1:T(8,128)S(1)} async-done(((f32[256,16,64]{0,2,1:T(8,128)}), f32[256,16,64]{0,2,1:T(8,128)S(1)}, u32[]{:S(2)}, u32[]{:S(2)}) %all-to-all-start.2) | async-done | bytes 1048608 | tf_op jit(solution)/shard_map/all_to_all | solution.py:273
  191.9 10.5 %all-to-all-start.1 = ((bf16[16,128,256]{2,1,0:T(8,128)(2,1)}), bf16[16,128,256]{2,1,0:T(8,128)(2,1)S(1)}, u32[]{:S(2)}, u32[]{:S(2)}) async-start(bf16[16,128,256]{2,1,0:T(8,128)(2,1)} %bitcast.26), calls=%async_computation.1 | async-start | bytes 2097152 | tf_op jit(solution)/shard_map/all_to_all | solution.py:269
  202.3 0.0 copy-done.1
  202.4 0.2 fusion.2
  202.5 0.1 reduce_sum.43
  202.6 5.3 %collective-permute-start.1 = (f32[256,64]{0,1:T(8,128)S(1)}, f32[256,64]{0,1:T(8,128)S(1)}, u32[]{:S(2)}, u32[]{:S(2)}) collective-permute-start(f32[256,64]{0,1:T(8,128)S(1)} %reduce_sum.43), channel_id=1, source_target_pairs={{0,0},{1,16},{2,32},{3,48},{4,64},{5,80},{6,96},{7,112},{8,128},{9... | collective-permute-start | bytes 196616 | tf_op jit(solution)/shard_map/ppermute | solution.py:275
  207.9 0.9 add_add_fusion
  208.9 12.6 %all-to-all-done.1 = bf16[16,128,256]{2,1,0:T(8,128)(2,1)S(1)} async-done(((bf16[16,128,256]{2,1,0:T(8,128)(2,1)}), bf16[16,128,256]{2,1,0:T(8,128)(2,1)S(1)}, u32[]{:S(2)}, u32[]{:S(2)}) %all-to-all-start.1) | async-done | bytes 1048608 | tf_op jit(solution)/shard_map/all_to_all | solution.py:269
  221.5 1.1 copy.22
  222.6 0.0 collective-permute-done.1
  222.6 0.6 copy.27
  (5 shorter events, 0.1 us)
Async XLA Ops:
  0.6 10.0 %copy-start.5 = (bf16[256,1024]{1,0:T(8,128)(2,1)S(1)}, bf16[256,1024]{1,0:T(8,128)(2,1)}, u32[]{:S(2)}) copy-start(bf16[256,1024]{1,0:T(8,128)(2,1)} %param.17) | copy-start | bytes 1572868
  0.6 18.5 %copy-start.4 = (s32[128]{0:T(128)S(1)}, s32[128]{0:T(128)}, u32[]{:S(2)}) copy-start(s32[128]{0:T(128)} %param.13) | copy-start | bytes 1540
  0.7 19.3 %copy-start = (bf16[128,1024]{1,0:T(8,128)(2,1)S(1)}, bf16[128,1024]{1,0:T(8,128)(2,1)}, u32[]{:S(2)}) copy-start(bf16[128,1024]{1,0:T(8,128)(2,1)} %param.12) | copy-start | bytes 786436
  0.7 19.3 %copy-start.2 = (bf16[128,1024]{1,0:T(8,128)(2,1)S(1)}, bf16[128,1024]{1,0:T(8,128)(2,1)}, u32[]{:S(2)}) copy-start(bf16[128,1024]{1,0:T(8,128)(2,1)} %param.14) | copy-start | bytes 786436
  3.0 105.9 %all-to-all-start = ((bf16[128,16,256]{0,2,1:T(8,128)(2,1)}), bf16[128,16,256]{0,2,1:T(8,128)(2,1)S(1)}, u32[]{:S(2)}, u32[]{:S(2)}) async-start(bf16[128,16,256]{0,2,1:T(8,128)(2,1)} %bitcast.1), calls=%async_computation | async-start | bytes 2097152 | tf_op jit(solution)/shard_map/all_to_all | solution.py:230
  10.6 98.9 %collective-permute-start = (bf16[256,1024]{1,0:T(8,128)(2,1)S(1)}, bf16[256,1024]{1,0:T(8,128)(2,1)S(1)}, u32[]{:S(2)}, u32[]{:S(2)}) collective-permute-start(bf16[256,1024]{1,0:T(8,128)(2,1)S(1)} %copy-done.5), channel_id=1, source_target_pairs={{0,0},{1,16},{2,32},{3,48},{4,64},{5,80},{6,96},{7,112},{8,128},{9... | collective-permute-start | bytes 1572872 | tf_op jit(solution)/shard_map/ppermute | solution.py:233
  19.9 0.8 copy-start.3
  153.7 38.1 %all-to-all-start.2 = ((f32[256,16,64]{0,2,1:T(8,128)}), f32[256,16,64]{0,2,1:T(8,128)S(1)}, u32[]{:S(2)}, u32[]{:S(2)}) async-start(f32[256,16,64]{0,2,1:T(8,128)} %bitcast.11), calls=%async_computation.2 | async-start | bytes 2097152 | tf_op jit(solution)/shard_map/all_to_all | solution.py:273
  166.9 35.4 %copy-start.1 = (f32[128,1024]{1,0:T(8,128)S(1)}, f32[128,1024]{1,0:T(8,128)}, u32[]{:S(2)}) copy-start(f32[128,1024]{1,0:T(8,128)} %get-tuple-element.39) | copy-start | bytes 1572868
  191.9 29.6 %all-to-all-start.1 = ((bf16[16,128,256]{2,1,0:T(8,128)(2,1)}), bf16[16,128,256]{2,1,0:T(8,128)(2,1)S(1)}, u32[]{:S(2)}, u32[]{:S(2)}) async-start(bf16[16,128,256]{2,1,0:T(8,128)(2,1)} %bitcast.26), calls=%async_computation.1 | async-start | bytes 2097152 | tf_op jit(solution)/shard_map/all_to_all | solution.py:269
  202.6 20.0 %collective-permute-start.1 = (f32[256,64]{0,1:T(8,128)S(1)}, f32[256,64]{0,1:T(8,128)S(1)}, u32[]{:S(2)}, u32[]{:S(2)}) collective-permute-start(f32[256,64]{0,1:T(8,128)S(1)} %reduce_sum.43), channel_id=1, source_target_pairs={{0,0},{1,16},{2,32},{3,48},{4,64},{5,80},{6,96},{7,112},{8,128},{9... | collective-permute-start | bytes 196616 | tf_op jit(solution)/shard_map/ppermute | solution.py:275

commit v15 on v14

--- a/solution.py
+++ b/solution.py
@@ -93,8 +93,8 @@
 
 
 def contrast_kernel(
-    scale_ref, shift_ref, own_slot_ref, slot_ref, images_ref, feats_ref, gain_ref,
-    upstream_out, image_out,
+    scale_ref, shift_ref, own_slot_ref, slot_ref, raw_images_ref, feats_ref, gain_ref,
+    upstream_out, image_out, images_ref,
 ):
     jb = pl.program_id(0)
     tc = feats_ref.shape[0]
@@ -118,6 +118,18 @@
         half = 0.5 * jnp.tanh(half_scale * products + half_shift)
         return jnp.where(positive, half - 0.5, half + 0.5).astype(jnp.bfloat16)
 
+    @pl.when(jb == 0)
+    def _():
+        def unit_chunk(c, carry):
+            at = pl.ds(pl.multiple_of(c * tc, tc), tc)
+            raw = raw_images_ref[at, :].astype(jnp.float32)
+            images_ref[at, :] = (
+                raw * lax.rsqrt(jnp.sum(raw * raw, axis=1, keepdims=True) + 1e-06)
+            ).astype(images_ref.dtype)
+            return carry
+
+        lax.fori_loop(0, images_ref.shape[0] // tc, unit_chunk, 0)
+
     images = images_ref[...]
     products = lax.dot_general(
         captions, images, (((1,), (1,)), ((), ())), preferred_element_type=jnp.float32
@@ -150,8 +162,8 @@
     image_out[...] += scale * jnp.dot(own_weights, captions, preferred_element_type=jnp.float32)
 
 
-def contrast_group(scale, shift, own_slot, slot_g, image_b_g, both_g, gain):
-    group_rows, width = image_b_g.shape
+def contrast_group(scale, shift, own_slot, slot_g, both_g, gain):
+    group_rows, width = both_g.shape[0], gain.shape[0]
     rows = own_slot.shape[0]
     tc = 512
     return pl.pallas_call(
@@ -174,6 +186,7 @@
             pl.BlockSpec((tc, width), lambda j: (j, 0)),
             pl.BlockSpec((rows, width), lambda j: (0, 0)),
         ),
+        scratch_shapes=[pltpu.VMEM((group_rows, width), jnp.bfloat16)],
         compiler_params=pltpu.CompilerParams(dimension_semantics=("arbitrary",)),
         cost_estimate=pl.CostEstimate(
             flops=4 * group_rows * (group_rows + rows) * width,
@@ -185,7 +198,7 @@
         shift,
         own_slot.reshape((rows, 1)),
         slot_g.reshape((1, group_rows)),
-        image_b_g,
+        both_g,
         both_g,
         gain.reshape((1, width)),
     )
@@ -244,8 +257,6 @@
     slot_g = (
         digits_g[:, 0, :].astype(jnp.int32) * 256 + digits_g[:, 1, :].astype(jnp.int32)
     ).reshape((-1,))
-    image_b_g = unit_rows(both_g[:, :width].astype(jnp.float32)).astype(jnp.bfloat16)
-
     unit_image, image_back = jax.vjp(unit_rows, picture_embeds.astype(jnp.float32))
 
     upstream_g, image_term = contrast_group(
@@ -253,7 +264,6 @@
         additive_shift_learned,
         matched_slot,
         slot_g,
-        image_b_g,
         both_g,
         closing_layernorm_multiplier,
     )

time: 224 us -> 219 us (0.978)
  other arithmetic: 10.5 us -> 3.49 us
    convert_element_type x1 -> x0, other arithmetic: 3.95 us -> none  [shards(): unit_rows(both_g[:, :width].astype(jnp.float32)).astype(jnp.bfloat16)]
    reduce_sum x2 -> x1, other arithmetic: 3.24 us -> 0.17 us  [unit_rows(): jnp.sum(values * values, axis=1, keepdims=True) + 1e-06]
  transfers between devices with their start and end apart: 5 -> 5, of which waited for: 2 -> 2; matrix products, arithmetic and copies ran while one was open for 4% -> 4% of each run, Pallas kernels for 39% -> 40%
where the time goes in v15:
time: 219 us; the launch traced here: 218 us
  Pallas kernels  121 us (55%)
  starting transfers between devices  43.8 us (20%)
  waiting for transfers between devices  33.2 us (15%)
  matrix products  9.41 us (4%)
  local copies, waits for them, and re-layouts  5.39 us (2%)
  other arithmetic  3.49 us (2%)
    pallas_call x1, Pallas kernels, gather_dp(): pl.pallas_call(functools.partial(gather_kernel, dp_size // 2, m), out_sha...  88.1 us
    pallas_call x1, Pallas kernels, contrast_group(): pl.pallas_call(contrast_kernel, grid=(group_rows // tc,), out_shape=(jax....  32.9 us
    all_to_all x1, waiting for transfers between devices, shards(): lax.all_to_all(group_sum, 'zero', split_axis=1, concat_axis=0, tiled=True)  20.4 us
    all_to_all x1, starting transfers between devices, shards(): lax.all_to_all(group_sum, 'zero', split_axis=1, concat_axis=0, tiled=True)  13.2 us
    all_to_all x1, waiting for transfers between devices, shards(): lax.all_to_all(hidden_part, 'dp', split_axis=0, concat_axis=1, tiled=True)  12.7 us
    all_to_all x1, starting transfers between devices, shards(): lax.all_to_all(hidden_part, 'dp', split_axis=0, concat_axis=1, tiled=True)  10.5 us
    all_to_all x1, starting transfers between devices, shards(): lax.all_to_all(feedforward_inner_activations, 'dp', split_axis=1, concat_...  7.59 us
    ppermute x1, starting transfers between devices, shards(): lax.ppermute(contracting_matrix, ('dp', 'zero'), transpose_route)  7.19 us
  transfers between devices with their start and end apart: 5, of which 2 were waited for; matrix products, arithmetic and copies ran while one was open for 4% of the time, Pallas kernels for 40%

profile of v15, /device:TPU:57, one launch (start us, length us, event | category | flops | bytes accessed | tf_op | source)
XLA Modules:
  0.0 218.3 jit_solution(17829903444382103926)
XLA Ops:
  0.6 0.0 copy-start.5
  0.6 0.0 copy-start.4
  0.7 0.0 copy-start
  0.7 0.0 copy-start.2
  0.7 2.3 %copy.16 = bf16[128,4096]{0,1:T(8,128)(2,1)} copy(bf16[128,4096]{1,0:T(8,128)(2,1)} %param.15) | data formatting | bytes 2097152 | tf_op args[3]
  3.0 7.6 %all-to-all-start = ((bf16[128,16,256]{0,2,1:T(8,128)(2,1)}), bf16[128,16,256]{0,2,1:T(8,128)(2,1)S(1)}, u32[]{:S(2)}, u32[]{:S(2)}) async-start(bf16[128,16,256]{0,2,1:T(8,128)(2,1)} %bitcast.1), calls=%async_computation | async-start | bytes 2097152 | tf_op jit(solution)/shard_map/all_to_all | solution.py:243
  10.6 0.0 copy-done.5
  10.6 7.2 %collective-permute-start = (bf16[256,1024]{1,0:T(8,128)(2,1)S(1)}, bf16[256,1024]{1,0:T(8,128)(2,1)S(1)}, u32[]{:S(2)}, u32[]{:S(2)}) collective-permute-start(bf16[256,1024]{1,0:T(8,128)(2,1)S(1)} %copy-done.5), channel_id=1, source_target_pairs={{0,0},{1,16},{2,32},{3,48},{4,64},{5,80},{6,96},{7,112},{8,128},{9... | collective-permute-start | bytes 1572872 | tf_op jit(solution)/shard_map/ppermute | solution.py:246
  19.1 0.0 copy-done.4
  19.1 0.7 copy.18.own_slot_ref
  19.9 0.0 copy-done
  19.9 0.0 copy-done.2
  19.9 0.0 copy-start.3
  19.9 0.8 pad_maximum_fusion.refs_0_
  20.8 0.0 copy-done.3
  20.8 88.1 %shard_map.103 = (bf16[16,128,2048]{2,1,0:T(8,128)(2,1)}, bf16[16,16,128]{2,1,0:T(8,128)(2,1)}) custom-call(bf16[128,2048]{1,0:T(8,128)(2,1)} %pad_maximum_fusion.refs_0_, bf16[16,128]{1,0:T(8,128)(2,1)} %copy-done.3), custom_call_target="tpu_custom_call" | custom-call | tf_op jit(solution)/shard_map/pallas_call | solution.py:79
  108.9 0.0 all-to-all-done
  108.9 0.5 copy.17
  109.5 0.0 collective-permute-done
  109.5 1.5 add_bitcast_fusion.slot_ref
  110.9 32.9 %shard_map.104 = (bf16[2048,1024]{1,0:T(8,128)(2,1)}, f32[128,1024]{1,0:T(8,128)}) custom-call(f32[1]{0:T(128)S(6)} %copy.25.scale_ref, f32[1]{0:T(128)S(6)} %copy.26.shift_ref, s32[128,1]{1,0:T(8,128)} %copy.18.own_slot_ref, s32[1,2048]{1,0:T(1,128)} %add_bitcast_fusion.slot_ref, bf16[2048,2048]{1,0:T(8,128)(2,1)} %bitcast.27, bf16[2048,2048]{1,0:T(8,128)(2,1)} %bitcast.28, ...), custom_call_target="tpu_custom_call" | custom-call | flops 18253611008 | bytes 13107200 | tf_op jit(solution)/shard_map/pallas_call | solution.py:169
  143.8 4.9 %fusion.4 = f32[256,1024]{0,1:T(8,128)} fusion(bf16[2048,256]{1,0:T(8,128)(2,1)S(1)} %bitcast.25, bf16[2048,1024]{1,0:T(8,128)(2,1)} %get-tuple-element.40), kind=kOutput, calls=%fused_computation.19 | convolution fusion | flops 1073741824 | bytes 6291456 | tf_op jit(solution)/shard_map/dot_general | solution.py:280
  148.7 13.2 %all-to-all-start.2 = ((f32[256,16,64]{0,2,1:T(8,128)}), f32[256,16,64]{0,2,1:T(8,128)S(1)}, u32[]{:S(2)}, u32[]{:S(2)}) async-start(f32[256,16,64]{0,2,1:T(8,128)} %bitcast.11), calls=%async_computation.2 | async-start | bytes 2097152 | tf_op jit(solution)/shard_map/all_to_all | solution.py:283
  161.9 0.0 copy-start.1
  161.9 4.5 %convolution_convert_fusion = bf16[2048,256]{1,0:T(8,128)(2,1)} fusion(bf16[2048,1024]{1,0:T(8,128)(2,1)} %get-tuple-element.40, bf16[256,1024]{1,0:T(8,128)(2,1)S(1)} %collective-permute-done), kind=kOutput, calls=%fused_computation | convolution fusion | flops 1074266112 | bytes 5767168 | tf_op jit(solution)/shard_map/dot_general | solution.py:273
  166.4 20.4 %all-to-all-done.2 = f32[256,16,64]{0,2,1:T(8,128)S(1)} async-done(((f32[256,16,64]{0,2,1:T(8,128)}), f32[256,16,64]{0,2,1:T(8,128)S(1)}, u32[]{:S(2)}, u32[]{:S(2)}) %all-to-all-start.2) | async-done | bytes 1048608 | tf_op jit(solution)/shard_map/all_to_all | solution.py:283
  186.9 10.5 %all-to-all-start.1 = ((bf16[16,128,256]{2,1,0:T(8,128)(2,1)}), bf16[16,128,256]{2,1,0:T(8,128)(2,1)S(1)}, u32[]{:S(2)}, u32[]{:S(2)}) async-start(bf16[16,128,256]{2,1,0:T(8,128)(2,1)} %bitcast.23), calls=%async_computation.1 | async-start | bytes 2097152 | tf_op jit(solution)/shard_map/all_to_all | solution.py:279
  197.4 0.0 copy-done.1
  197.4 0.2 fusion
  197.6 0.1 reduce_sum.33
  197.7 5.2 %collective-permute-start.1 = (f32[256,64]{0,1:T(8,128)S(1)}, f32[256,64]{0,1:T(8,128)S(1)}, u32[]{:S(2)}, u32[]{:S(2)}) collective-permute-start(f32[256,64]{0,1:T(8,128)S(1)} %reduce_sum.33), channel_id=1, source_target_pairs={{0,0},{1,16},{2,32},{3,48},{4,64},{5,80},{6,96},{7,112},{8,128},{9... | collective-permute-start | bytes 196616 | tf_op jit(solution)/shard_map/ppermute | solution.py:285
  202.9 0.9 add_add_fusion
  203.9 12.7 %all-to-all-done.1 = bf16[16,128,256]{2,1,0:T(8,128)(2,1)S(1)} async-done(((bf16[16,128,256]{2,1,0:T(8,128)(2,1)}), bf16[16,128,256]{2,1,0:T(8,128)(2,1)S(1)}, u32[]{:S(2)}, u32[]{:S(2)}) %all-to-all-start.1) | async-done | bytes 1048608 | tf_op jit(solution)/shard_map/all_to_all | solution.py:279
  216.6 1.1 copy.22
  217.7 0.0 collective-permute-done.1
  217.7 0.6 copy.27
  (4 shorter events, 0.1 us)
Async XLA Ops:
  0.6 10.0 %copy-start.5 = (bf16[256,1024]{1,0:T(8,128)(2,1)S(1)}, bf16[256,1024]{1,0:T(8,128)(2,1)}, u32[]{:S(2)}) copy-start(bf16[256,1024]{1,0:T(8,128)(2,1)} %param.17) | copy-start | bytes 1572868
  0.6 18.5 %copy-start.4 = (s32[128]{0:T(128)S(1)}, s32[128]{0:T(128)}, u32[]{:S(2)}) copy-start(s32[128]{0:T(128)} %param.13) | copy-start | bytes 1540
  0.7 19.3 %copy-start = (bf16[128,1024]{1,0:T(8,128)(2,1)S(1)}, bf16[128,1024]{1,0:T(8,128)(2,1)}, u32[]{:S(2)}) copy-start(bf16[128,1024]{1,0:T(8,128)(2,1)} %param.12) | copy-start | bytes 786436
  0.7 19.3 %copy-start.2 = (bf16[128,1024]{1,0:T(8,128)(2,1)S(1)}, bf16[128,1024]{1,0:T(8,128)(2,1)}, u32[]{:S(2)}) copy-start(bf16[128,1024]{1,0:T(8,128)(2,1)} %param.14) | copy-start | bytes 786436
  3.0 105.9 %all-to-all-start = ((bf16[128,16,256]{0,2,1:T(8,128)(2,1)}), bf16[128,16,256]{0,2,1:T(8,128)(2,1)S(1)}, u32[]{:S(2)}, u32[]{:S(2)}) async-start(bf16[128,16,256]{0,2,1:T(8,128)(2,1)} %bitcast.1), calls=%async_computation | async-start | bytes 2097152 | tf_op jit(solution)/shard_map/all_to_all | solution.py:243
  10.6 98.9 %collective-permute-start = (bf16[256,1024]{1,0:T(8,128)(2,1)S(1)}, bf16[256,1024]{1,0:T(8,128)(2,1)S(1)}, u32[]{:S(2)}, u32[]{:S(2)}) collective-permute-start(bf16[256,1024]{1,0:T(8,128)(2,1)S(1)} %copy-done.5), channel_id=1, source_target_pairs={{0,0},{1,16},{2,32},{3,48},{4,64},{5,80},{6,96},{7,112},{8,128},{9... | collective-permute-start | bytes 1572872 | tf_op jit(solution)/shard_map/ppermute | solution.py:246
  19.9 0.8 copy-start.3
  148.7 38.1 %all-to-all-start.2 = ((f32[256,16,64]{0,2,1:T(8,128)}), f32[256,16,64]{0,2,1:T(8,128)S(1)}, u32[]{:S(2)}, u32[]{:S(2)}) async-start(f32[256,16,64]{0,2,1:T(8,128)} %bitcast.11), calls=%async_computation.2 | async-start | bytes 2097152 | tf_op jit(solution)/shard_map/all_to_all | solution.py:283
  161.9 35.5 %copy-start.1 = (f32[128,1024]{1,0:T(8,128)S(1)}, f32[128,1024]{1,0:T(8,128)}, u32[]{:S(2)}) copy-start(f32[128,1024]{1,0:T(8,128)} %get-tuple-element.39) | copy-start | bytes 1572868
  186.9 29.7 %all-to-all-start.1 = ((bf16[16,128,256]{2,1,0:T(8,128)(2,1)}), bf16[16,128,256]{2,1,0:T(8,128)(2,1)S(1)}, u32[]{:S(2)}, u32[]{:S(2)}) async-start(bf16[16,128,256]{2,1,0:T(8,128)(2,1)} %bitcast.23), calls=%async_computation.1 | async-start | bytes 2097152 | tf_op jit(solution)/shard_map/all_to_all | solution.py:279
  197.7 20.0 %collective-permute-start.1 = (f32[256,64]{0,1:T(8,128)S(1)}, f32[256,64]{0,1:T(8,128)S(1)}, u32[]{:S(2)}, u32[]{:S(2)}) collective-permute-start(f32[256,64]{0,1:T(8,128)S(1)} %reduce_sum.33), channel_id=1, source_target_pairs={{0,0},{1,16},{2,32},{3,48},{4,64},{5,80},{6,96},{7,112},{8,128},{9... | collective-permute-start | bytes 196616 | tf_op jit(solution)/shard_map/ppermute | solution.py:285

commit v16 on v15

--- a/solution.py
+++ b/solution.py
@@ -94,7 +94,7 @@
 
 def contrast_kernel(
     scale_ref, shift_ref, own_slot_ref, slot_ref, raw_images_ref, feats_ref, gain_ref,
-    upstream_out, image_out, images_ref,
+    ffa_ref, weight_ref, hidden_out, sum_out, image_out, images_ref,
 ):
     jb = pl.program_id(0)
     tc = feats_ref.shape[0]
@@ -145,7 +145,21 @@
     )
     center_grad = gained * inv_spread + (2.0 / width) * center * spread_grad
     feats_grad = center_grad - jnp.sum(center_grad, axis=1, keepdims=True) / width
-    upstream_out[...] = feats_grad.astype(upstream_out.dtype)
+    upstream = feats_grad.astype(jnp.bfloat16)
+    hidden_out[...] = lax.dot_general(
+        upstream, weight_ref[...], (((1,), (1,)), ((), ())), preferred_element_type=jnp.float32
+    ).astype(hidden_out.dtype)
+    block_sum = lax.dot_general(
+        ffa_ref[...], upstream, (((0,), (0,)), ((), ())), preferred_element_type=jnp.float32
+    )
+
+    @pl.when(jb == 0)
+    def _():
+        sum_out[...] = block_sum
+
+    @pl.when(jb > 0)
+    def _():
+        sum_out[...] += block_sum
 
     own_start = pl.multiple_of(lax.axis_index("dp") * rows, rows)
     own = images_ref[pl.ds(own_start, rows), :]
@@ -162,15 +176,17 @@
     image_out[...] += scale * jnp.dot(own_weights, captions, preferred_element_type=jnp.float32)
 
 
-def contrast_group(scale, shift, own_slot, slot_g, both_g, gain):
+def contrast_group(scale, shift, own_slot, slot_g, both_g, gain, ffa_cols, weight_block):
     group_rows, width = both_g.shape[0], gain.shape[0]
+    block_cols = weight_block.shape[0]
     rows = own_slot.shape[0]
     tc = 512
     return pl.pallas_call(
         contrast_kernel,
         grid=(group_rows // tc,),
         out_shape=(
-            jax.ShapeDtypeStruct((group_rows, width), jnp.bfloat16),
+            jax.ShapeDtypeStruct((group_rows, block_cols), jnp.bfloat16),
+            jax.ShapeDtypeStruct((block_cols, width), jnp.float32),
             jax.ShapeDtypeStruct((rows, width), jnp.float32),
         ),
         in_specs=[
@@ -181,9 +197,12 @@
             pl.BlockSpec((group_rows, width), lambda j: (0, 0)),
             pl.BlockSpec((tc, width), lambda j: (j, 1)),
             pl.BlockSpec((1, width), lambda j: (0, 0)),
+            pl.BlockSpec((tc, block_cols), lambda j: (j, 0)),
+            pl.BlockSpec((block_cols, width), lambda j: (0, 0)),
         ],
         out_specs=(
-            pl.BlockSpec((tc, width), lambda j: (j, 0)),
+            pl.BlockSpec((tc, block_cols), lambda j: (j, 0)),
+            pl.BlockSpec((block_cols, width), lambda j: (0, 0)),
             pl.BlockSpec((rows, width), lambda j: (0, 0)),
         ),
         scratch_shapes=[pltpu.VMEM((group_rows, width), jnp.bfloat16)],
@@ -201,6 +220,8 @@
         both_g,
         both_g,
         gain.reshape((1, width)),
+        ffa_cols,
+        weight_block,
     )
 
 
@@ -259,27 +280,20 @@
     ).reshape((-1,))
     unit_image, image_back = jax.vjp(unit_rows, picture_embeds.astype(jnp.float32))
 
-    upstream_g, image_term = contrast_group(
+    hidden_part, group_sum, image_term = contrast_group(
         sharpness_factor,
         additive_shift_learned,
         matched_slot,
         slot_g,
         both_g,
         closing_layernorm_multiplier,
+        ffa_cols,
+        weight_block,
     )
 
     image_grad = image_back(image_term)[0]
 
-    hidden_part = lax.dot_general(
-        upstream_g,
-        weight_block,
-        (((1,), (1,)), ((), ())),
-        preferred_element_type=jnp.float32,
-    ).astype(jnp.bfloat16)
     hidden_grad = lax.all_to_all(hidden_part, "dp", split_axis=0, concat_axis=1, tiled=True)
-    group_sum = lax.dot_general(
-        ffa_cols, upstream_g, (((0,), (0,)), ((), ())), preferred_element_type=jnp.float32
-    )
     down_parts = lax.all_to_all(group_sum, "zero", split_axis=1, concat_axis=0, tiled=True)
     down_block = jnp.sum(down_parts.reshape((zero_size,) + (group_sum.shape[0], -1)), axis=0)
     down_grad = lax.ppermute(down_block, ("dp", "zero"), transpose_route)

time: 219 us -> 219 us (level)
  blocking collectives: 0 us -> 38.9 us
  waiting for transfers between devices: 33.2 us -> 11.3 us
  starting transfers between devices: 43.8 us -> 29.6 us
  matrix products: 9.41 us -> 0 us
  Pallas kernels: 121 us -> 124 us
  other arithmetic: 3.49 us -> 6.24 us
    all_to_all x0 -> x1, blocking collectives: none -> 38.9 us  [shards(): lax.all_to_all(group_sum, 'zero', split_axis=1, concat_axis=0, tiled=True)]
    all_to_all x1 -> x0, waiting for transfers between devices: 20.4 us -> none  [shards(): lax.all_to_all(group_sum, 'zero', split_axis=1, concat_axis=0, tiled=True)]
    all_to_all x1 -> x0, starting transfers between devices: 13.2 us -> none  [shards(): lax.all_to_all(group_sum, 'zero', split_axis=1, concat_axis=0, tiled=True)]
    dot_general x2 -> x0, matrix products: 9.41 us -> none  [the longest x1 4.9 us: shards(): lax.dot_general(ffa_cols, upstream_g, (((0,), (0,)), ((), ())), preferred...]
    pallas_call x1, Pallas kernels: 32.9 us -> 37.7 us  [contrast_group(): pl.pallas_call(contrast_kernel, grid=(group_rows // tc,), out_shape=(jax....]
    unnamed x14 -> x11, local copies, waits for them, and re-layouts: 3 us -> 0.65 us
    pallas_call x1, Pallas kernels: 88.1 us -> 85.9 us  [gather_dp(): pl.pallas_call(functools.partial(gather_kernel, dp_size // 2, m), out_sha...]
  transfers between devices with their start and end apart: 5 -> 4, of which waited for: 2 -> 1; matrix products, arithmetic and copies ran while one was open for 4% -> 3% of each run, Pallas kernels for 40% -> 39%
where the time goes in v16:
time: 219 us
  Pallas kernels  124 us (57%)
  blocking collectives  38.9 us (18%)
  starting transfers between devices  29.6 us (14%)
  waiting for transfers between devices  11.3 us (5%)
  local copies, waits for them, and re-layouts  7.08 us (3%)
  other arithmetic  6.24 us (3%)
    pallas_call x1, Pallas kernels, gather_dp(): pl.pallas_call(functools.partial(gather_kernel, dp_size // 2, m), out_sha...  85.9 us
    all_to_all x1, blocking collectives, shards(): lax.all_to_all(group_sum, 'zero', split_axis=1, concat_axis=0, tiled=True)  38.9 us
    pallas_call x1, Pallas kernels, contrast_group(): pl.pallas_call(contrast_kernel, grid=(group_rows // tc,), out_shape=(jax....  37.7 us
    all_to_all x1, waiting for transfers between devices, shards(): lax.all_to_all(hidden_part, 'dp', split_axis=0, concat_axis=1, tiled=True)  11.3 us
    all_to_all x1, starting transfers between devices, shards(): lax.all_to_all(hidden_part, 'dp', split_axis=0, concat_axis=1, tiled=True)  9.85 us
    all_to_all x1, starting transfers between devices, shards(): lax.all_to_all(feedforward_inner_activations, 'dp', split_axis=1, concat_...  7.59 us
    ppermute x1, starting transfers between devices, shards(): lax.ppermute(contracting_matrix, ('dp', 'zero'), transpose_route)  7.18 us
    ppermute x1, starting transfers between devices, shards(): down_grad = lax.ppermute(down_block, ('dp', 'zero'), transpose_route)  5 us
  transfers between devices with their start and end apart: 4, of which 1 were waited for; matrix products, arithmetic and copies ran while one was open for 3% of the time, Pallas kernels for 39%

profile of v16, /device:TPU:57, one launch (start us, length us, event | category | flops | bytes accessed | tf_op | source)
XLA Modules:
  0.0 218.8 jit_solution(12530850948216517051)
XLA Ops:
  0.6 2.3 %copy.21 = bf16[16,16,8,256]{3,2,0,1:T(8,128)(2,1)} copy(bf16[16,16,8,256]{3,2,1,0:T(8,128)(2,1)} %bitcast.23) | data formatting | bytes 2097152 | tf_op jit(solution)/shard_map/all_to_all | solution.py:264
  2.9 7.6 %all-to-all-start = ((bf16[128,16,256]{2,0,1:T(8,128)(2,1)}), bf16[128,16,256]{2,0,1:T(8,128)(2,1)S(1)}, u32[]{:S(2)}, u32[]{:S(2)}) async-start(bf16[128,16,256]{2,0,1:T(8,128)(2,1)} %bitcast.20), calls=%async_computation | async-start | bytes 2097152 | tf_op jit(solution)/shard_map/all_to_all | solution.py:264
  10.5 7.2 %collective-permute-start = (bf16[256,1024]{1,0:T(8,128)(2,1)}, bf16[256,1024]{1,0:T(8,128)(2,1)S(1)}, u32[]{:S(2)}, u32[]{:S(2)}) collective-permute-start(bf16[256,1024]{1,0:T(8,128)(2,1)} %param.17), channel_id=1, source_target_pairs={{0,0},{1,16},{2,32},{3,48},{4,64},{5,80},{6,96},{7,112},{8,128},{9... | collective-permute-start | bytes 1572872 | tf_op jit(solution)/shard_map/ppermute | solution.py:267
  19.0 1.4 copy.15.own_slot_ref
  20.4 0.7 fusion.3
  21.1 0.0 copy-start.3
  21.1 1.9 pad_maximum_fusion.refs_0_
  23.0 0.0 copy-done.3
  23.0 85.9 %shard_map.103 = (bf16[16,128,2048]{2,1,0:T(8,128)(2,1)}, bf16[16,16,128]{2,1,0:T(8,128)(2,1)}) custom-call(bf16[128,2048]{1,0:T(8,128)(2,1)} %pad_maximum_fusion.refs_0_, bf16[16,128]{1,0:T(8,128)(2,1)} %copy-done.3), custom_call_target="tpu_custom_call" | custom-call | tf_op jit(solution)/shard_map/pallas_call | solution.py:79
  108.9 0.0 collective-permute-done.weight_ref
  108.9 0.0 copy-start.4
  108.9 0.0 all-to-all-done
  108.9 0.0 copy-start.2
  109.0 1.5 add_bitcast_fusion.slot_ref
  110.4 0.0 copy-done.4
  110.4 0.0 copy-done.2
  110.4 0.0 copy-start
  110.4 37.7 %shard_map.104 = (bf16[2048,256]{1,0:T(8,128)(2,1)}, f32[256,1024]{1,0:T(8,128)}, f32[128,1024]{1,0:T(8,128)}) custom-call(f32[1]{0:T(128)S(6)} %copy.24.scale_ref, f32[1]{0:T(128)S(6)} %copy.25.shift_ref, s32[128,1]{1,0:T(8,128)} %copy.15.own_slot_ref, s32[1,2048]{1,0:T(1,128)} %add_bitcast_fusion.slot_ref, bf16[2048,2048]{1,0:T(8,128)(2,1)} %bitcast.28, ...), custom_call_target="tpu_custom_call" | custom-call | flops 18253611008 | bytes 13107200 | tf_op jit(solution)/shard_map/pallas_call | solution.py:184
  148.1 0.0 copy-start.1
  148.1 1.6 copy.17
  149.7 38.9 %all_to_all.51 = f32[256,16,64]{0,2,1:T(8,128)S(1)} all-to-all(f32[256,16,64]{0,2,1:T(8,128)S(1)} %bitcast.22), channel_id=1, replica_groups=mesh['dp'=16,'zero'=16] {'zero'}, dimensions={1} | all-to-all | bytes 2097152 | tf_op jit(solution)/shard_map/all_to_all | solution.py:297
  188.6 9.9 %all-to-all-start.1 = ((bf16[16,128,256]{2,1,0:T(8,128)(2,1)}), bf16[16,128,256]{2,1,0:T(8,128)(2,1)S(1)}, u32[]{:S(2)}, u32[]{:S(2)}) async-start(bf16[16,128,256]{2,1,0:T(8,128)(2,1)} %bitcast.25), calls=%async_computation.1 | async-start | bytes 2097152 | tf_op jit(solution)/shard_map/all_to_all | solution.py:296
  198.5 0.0 copy-done
  198.5 1.2 fusion
  199.7 0.1 reduce_sum.33
  199.8 5.0 %collective-permute-start.1 = (f32[256,64]{0,1:T(8,128)S(1)}, f32[256,64]{0,1:T(8,128)S(1)}, u32[]{:S(2)}, u32[]{:S(2)}) collective-permute-start(f32[256,64]{0,1:T(8,128)S(1)} %reduce_sum.33), channel_id=1, source_target_pairs={{0,0},{1,16},{2,32},{3,48},{4,64},{5,80},{6,96},{7,112},{8,128},{9... | collective-permute-start | bytes 196616 | tf_op jit(solution)/shard_map/ppermute | solution.py:299
  204.8 0.0 copy-done.1
  204.8 0.9 add_add_fusion
  205.7 11.3 %all-to-all-done.1 = bf16[16,128,256]{2,1,0:T(8,128)(2,1)S(1)} async-done(((bf16[16,128,256]{2,1,0:T(8,128)(2,1)}), bf16[16,128,256]{2,1,0:T(8,128)(2,1)S(1)}, u32[]{:S(2)}, u32[]{:S(2)}) %all-to-all-start.1) | async-done | bytes 1048608 | tf_op jit(solution)/shard_map/all_to_all | solution.py:296
  217.1 1.1 copy.19
  218.2 0.0 collective-permute-done.1
  218.2 0.6 copy.26
  (3 shorter events, 0.1 us)
Async XLA Ops:
  2.9 106.0 %all-to-all-start = ((bf16[128,16,256]{2,0,1:T(8,128)(2,1)}), bf16[128,16,256]{2,0,1:T(8,128)(2,1)S(1)}, u32[]{:S(2)}, u32[]{:S(2)}) async-start(bf16[128,16,256]{2,0,1:T(8,128)(2,1)} %bitcast.20), calls=%async_computation | async-start | bytes 2097152 | tf_op jit(solution)/shard_map/all_to_all | solution.py:264
  10.5 98.4 %collective-permute-start = (bf16[256,1024]{1,0:T(8,128)(2,1)}, bf16[256,1024]{1,0:T(8,128)(2,1)S(1)}, u32[]{:S(2)}, u32[]{:S(2)}) collective-permute-start(bf16[256,1024]{1,0:T(8,128)(2,1)} %param.17), channel_id=1, source_target_pairs={{0,0},{1,16},{2,32},{3,48},{4,64},{5,80},{6,96},{7,112},{8,128},{9... | collective-permute-start | bytes 1572872 | tf_op jit(solution)/shard_map/ppermute | solution.py:267
  21.1 1.9 copy-start.3
  108.9 1.5 copy-start.4
  108.9 1.5 copy-start.2
  110.4 88.0 %copy-start = (bf16[128,1024]{1,0:T(8,128)(2,1)S(1)}, bf16[128,1024]{1,0:T(8,128)(2,1)}, u32[]{:S(2)}) copy-start(bf16[128,1024]{1,0:T(8,128)(2,1)} %param.12) | copy-start | bytes 786436
  148.1 56.7 %copy-start.1 = (f32[128,1024]{1,0:T(8,128)S(1)}, f32[128,1024]{1,0:T(8,128)}, u32[]{:S(2)}) copy-start(f32[128,1024]{1,0:T(8,128)} %get-tuple-element.42) | copy-start | bytes 1572868
  188.6 28.5 %all-to-all-start.1 = ((bf16[16,128,256]{2,1,0:T(8,128)(2,1)}), bf16[16,128,256]{2,1,0:T(8,128)(2,1)S(1)}, u32[]{:S(2)}, u32[]{:S(2)}) async-start(bf16[16,128,256]{2,1,0:T(8,128)(2,1)} %bitcast.25), calls=%async_computation.1 | async-start | bytes 2097152 | tf_op jit(solution)/shard_map/all_to_all | solution.py:296
  199.8 18.4 %collective-permute-start.1 = (f32[256,64]{0,1:T(8,128)S(1)}, f32[256,64]{0,1:T(8,128)S(1)}, u32[]{:S(2)}, u32[]{:S(2)}) collective-permute-start(f32[256,64]{0,1:T(8,128)S(1)} %reduce_sum.33), channel_id=1, source_target_pairs={{0,0},{1,16},{2,32},{3,48},{4,64},{5,80},{6,96},{7,112},{8,128},{9... | collective-permute-start | bytes 196616 | tf_op jit(solution)/shard_map/ppermute | solution.py:299

commit v17 on v15

--- a/solution.py
+++ b/solution.py
@@ -165,7 +165,7 @@
 def contrast_group(scale, shift, own_slot, slot_g, both_g, gain):
     group_rows, width = both_g.shape[0], gain.shape[0]
     rows = own_slot.shape[0]
-    tc = 512
+    tc = 1024
     return pl.pallas_call(
         contrast_kernel,
         grid=(group_rows // tc,),

time: 219 us -> 219 us (level)
  no operation moved by 1% of the time
where the time goes in v17:
time: 219 us; the launch traced here: 218 us
  Pallas kernels  121 us (55%)
  starting transfers between devices  43.8 us (20%)
  waiting for transfers between devices  33.1 us (15%)
  matrix products  9.41 us (4%)
  local copies, waits for them, and re-layouts  5.39 us (2%)
  other arithmetic  3.49 us (2%)
    pallas_call x1, Pallas kernels, gather_dp(): pl.pallas_call(functools.partial(gather_kernel, dp_size // 2, m), out_sha...  88.1 us
    pallas_call x1, Pallas kernels, contrast_group(): pl.pallas_call(contrast_kernel, grid=(group_rows // tc,), out_shape=(jax....  32.7 us
    all_to_all x1, waiting for transfers between devices, shards(): lax.all_to_all(group_sum, 'zero', split_axis=1, concat_axis=0, tiled=True)  20.4 us
    all_to_all x1, starting transfers between devices, shards(): lax.all_to_all(group_sum, 'zero', split_axis=1, concat_axis=0, tiled=True)  13.2 us
    all_to_all x1, waiting for transfers between devices, shards(): lax.all_to_all(hidden_part, 'dp', split_axis=0, concat_axis=1, tiled=True)  12.6 us
    all_to_all x1, starting transfers between devices, shards(): lax.all_to_all(hidden_part, 'dp', split_axis=0, concat_axis=1, tiled=True)  10.5 us
    all_to_all x1, starting transfers between devices, shards(): lax.all_to_all(feedforward_inner_activations, 'dp', split_axis=1, concat_...  7.59 us
    ppermute x1, starting transfers between devices, shards(): lax.ppermute(contracting_matrix, ('dp', 'zero'), transpose_route)  7.19 us
  transfers between devices with their start and end apart: 5, of which 2 were waited for; matrix products, arithmetic and copies ran while one was open for 4% of the time, Pallas kernels for 40%

profile of v17, /device:TPU:57, one launch (start us, length us, event | category | flops | bytes accessed | tf_op | source)
XLA Modules:
  0.0 218.0 jit_solution(8926260908809124388)
XLA Ops:
  0.6 0.0 copy-start.5
  0.6 0.0 copy-start.4
  0.7 0.0 copy-start
  0.7 0.0 copy-start.2
  0.7 2.3 %copy.16 = bf16[128,4096]{0,1:T(8,128)(2,1)} copy(bf16[128,4096]{1,0:T(8,128)(2,1)} %param.15) | data formatting | bytes 2097152 | tf_op args[3]
  3.0 7.6 %all-to-all-start = ((bf16[128,16,256]{0,2,1:T(8,128)(2,1)}), bf16[128,16,256]{0,2,1:T(8,128)(2,1)S(1)}, u32[]{:S(2)}, u32[]{:S(2)}) async-start(bf16[128,16,256]{0,2,1:T(8,128)(2,1)} %bitcast.1), calls=%async_computation | async-start | bytes 2097152 | tf_op jit(solution)/shard_map/all_to_all | solution.py:243
  10.6 0.0 copy-done.5
  10.6 7.2 %collective-permute-start = (bf16[256,1024]{1,0:T(8,128)(2,1)S(1)}, bf16[256,1024]{1,0:T(8,128)(2,1)S(1)}, u32[]{:S(2)}, u32[]{:S(2)}) collective-permute-start(bf16[256,1024]{1,0:T(8,128)(2,1)S(1)} %copy-done.5), channel_id=1, source_target_pairs={{0,0},{1,16},{2,32},{3,48},{4,64},{5,80},{6,96},{7,112},{8,128},{9... | collective-permute-start | bytes 1572872 | tf_op jit(solution)/shard_map/ppermute | solution.py:246
  19.1 0.0 copy-done.4
  19.1 0.7 copy.18.own_slot_ref
  19.9 0.0 copy-done
  19.9 0.0 copy-done.2
  19.9 0.0 copy-start.3
  19.9 0.8 pad_maximum_fusion.refs_0_
  20.8 0.0 copy-done.3
  20.8 88.1 %shard_map.103 = (bf16[16,128,2048]{2,1,0:T(8,128)(2,1)}, bf16[16,16,128]{2,1,0:T(8,128)(2,1)}) custom-call(bf16[128,2048]{1,0:T(8,128)(2,1)} %pad_maximum_fusion.refs_0_, bf16[16,128]{1,0:T(8,128)(2,1)} %copy-done.3), custom_call_target="tpu_custom_call" | custom-call | tf_op jit(solution)/shard_map/pallas_call | solution.py:79
  108.9 0.0 all-to-all-done
  108.9 0.5 copy.17
  109.5 0.0 collective-permute-done
  109.5 1.5 add_bitcast_fusion.slot_ref
  110.9 32.7 %shard_map.104 = (bf16[2048,1024]{1,0:T(8,128)(2,1)}, f32[128,1024]{1,0:T(8,128)}) custom-call(f32[1]{0:T(128)S(6)} %copy.25.scale_ref, f32[1]{0:T(128)S(6)} %copy.26.shift_ref, s32[128,1]{1,0:T(8,128)} %copy.18.own_slot_ref, s32[1,2048]{1,0:T(1,128)} %add_bitcast_fusion.slot_ref, bf16[2048,2048]{1,0:T(8,128)(2,1)} %bitcast.27, bf16[2048,2048]{1,0:T(8,128)(2,1)} %bitcast.28, ...), custom_call_target="tpu_custom_call" | custom-call | flops 18253611008 | bytes 13107200 | tf_op jit(solution)/shard_map/pallas_call | solution.py:169
  143.6 4.9 %fusion.4 = f32[256,1024]{0,1:T(8,128)} fusion(bf16[2048,256]{1,0:T(8,128)(2,1)S(1)} %bitcast.25, bf16[2048,1024]{1,0:T(8,128)(2,1)} %get-tuple-element.40), kind=kOutput, calls=%fused_computation.19 | convolution fusion | flops 1073741824 | bytes 6291456 | tf_op jit(solution)/shard_map/dot_general | solution.py:280
  148.5 13.2 %all-to-all-start.2 = ((f32[256,16,64]{0,2,1:T(8,128)}), f32[256,16,64]{0,2,1:T(8,128)S(1)}, u32[]{:S(2)}, u32[]{:S(2)}) async-start(f32[256,16,64]{0,2,1:T(8,128)} %bitcast.11), calls=%async_computation.2 | async-start | bytes 2097152 | tf_op jit(solution)/shard_map/all_to_all | solution.py:283
  161.7 0.0 copy-start.1
  161.7 4.5 %convolution_convert_fusion = bf16[2048,256]{1,0:T(8,128)(2,1)} fusion(bf16[2048,1024]{1,0:T(8,128)(2,1)} %get-tuple-element.40, bf16[256,1024]{1,0:T(8,128)(2,1)S(1)} %collective-permute-done), kind=kOutput, calls=%fused_computation | convolution fusion | flops 1074266112 | bytes 5767168 | tf_op jit(solution)/shard_map/dot_general | solution.py:273
  166.2 20.4 %all-to-all-done.2 = f32[256,16,64]{0,2,1:T(8,128)S(1)} async-done(((f32[256,16,64]{0,2,1:T(8,128)}), f32[256,16,64]{0,2,1:T(8,128)S(1)}, u32[]{:S(2)}, u32[]{:S(2)}) %all-to-all-start.2) | async-done | bytes 1048608 | tf_op jit(solution)/shard_map/all_to_all | solution.py:283
  186.6 10.5 %all-to-all-start.1 = ((bf16[16,128,256]{2,1,0:T(8,128)(2,1)}), bf16[16,128,256]{2,1,0:T(8,128)(2,1)S(1)}, u32[]{:S(2)}, u32[]{:S(2)}) async-start(bf16[16,128,256]{2,1,0:T(8,128)(2,1)} %bitcast.23), calls=%async_computation.1 | async-start | bytes 2097152 | tf_op jit(solution)/shard_map/all_to_all | solution.py:279
  197.2 0.0 copy-done.1
  197.2 0.2 fusion
  197.4 0.1 reduce_sum.33
  197.4 5.3 %collective-permute-start.1 = (f32[256,64]{0,1:T(8,128)S(1)}, f32[256,64]{0,1:T(8,128)S(1)}, u32[]{:S(2)}, u32[]{:S(2)}) collective-permute-start(f32[256,64]{0,1:T(8,128)S(1)} %reduce_sum.33), channel_id=1, source_target_pairs={{0,0},{1,16},{2,32},{3,48},{4,64},{5,80},{6,96},{7,112},{8,128},{9... | collective-permute-start | bytes 196616 | tf_op jit(solution)/shard_map/ppermute | solution.py:285
  202.7 0.9 add_add_fusion
  203.7 12.6 %all-to-all-done.1 = bf16[16,128,256]{2,1,0:T(8,128)(2,1)S(1)} async-done(((bf16[16,128,256]{2,1,0:T(8,128)(2,1)}), bf16[16,128,256]{2,1,0:T(8,128)(2,1)S(1)}, u32[]{:S(2)}, u32[]{:S(2)}) %all-to-all-start.1) | async-done | bytes 1048608 | tf_op jit(solution)/shard_map/all_to_all | solution.py:279
  216.3 1.1 copy.22
  217.4 0.0 collective-permute-done.1
  217.4 0.6 copy.27
  (4 shorter events, 0.1 us)
Async XLA Ops:
  0.6 10.0 %copy-start.5 = (bf16[256,1024]{1,0:T(8,128)(2,1)S(1)}, bf16[256,1024]{1,0:T(8,128)(2,1)}, u32[]{:S(2)}) copy-start(bf16[256,1024]{1,0:T(8,128)(2,1)} %param.17) | copy-start | bytes 1572868
  0.6 18.5 %copy-start.4 = (s32[128]{0:T(128)S(1)}, s32[128]{0:T(128)}, u32[]{:S(2)}) copy-start(s32[128]{0:T(128)} %param.13) | copy-start | bytes 1540
  0.7 19.3 %copy-start = (bf16[128,1024]{1,0:T(8,128)(2,1)S(1)}, bf16[128,1024]{1,0:T(8,128)(2,1)}, u32[]{:S(2)}) copy-start(bf16[128,1024]{1,0:T(8,128)(2,1)} %param.12) | copy-start | bytes 786436
  0.7 19.3 %copy-start.2 = (bf16[128,1024]{1,0:T(8,128)(2,1)S(1)}, bf16[128,1024]{1,0:T(8,128)(2,1)}, u32[]{:S(2)}) copy-start(bf16[128,1024]{1,0:T(8,128)(2,1)} %param.14) | copy-start | bytes 786436
  3.0 105.9 %all-to-all-start = ((bf16[128,16,256]{0,2,1:T(8,128)(2,1)}), bf16[128,16,256]{0,2,1:T(8,128)(2,1)S(1)}, u32[]{:S(2)}, u32[]{:S(2)}) async-start(bf16[128,16,256]{0,2,1:T(8,128)(2,1)} %bitcast.1), calls=%async_computation | async-start | bytes 2097152 | tf_op jit(solution)/shard_map/all_to_all | solution.py:243
  10.6 98.9 %collective-permute-start = (bf16[256,1024]{1,0:T(8,128)(2,1)S(1)}, bf16[256,1024]{1,0:T(8,128)(2,1)S(1)}, u32[]{:S(2)}, u32[]{:S(2)}) collective-permute-start(bf16[256,1024]{1,0:T(8,128)(2,1)S(1)} %copy-done.5), channel_id=1, source_target_pairs={{0,0},{1,16},{2,32},{3,48},{4,64},{5,80},{6,96},{7,112},{8,128},{9... | collective-permute-start | bytes 1572872 | tf_op jit(solution)/shard_map/ppermute | solution.py:246
  19.9 0.8 copy-start.3
  148.5 38.1 %all-to-all-start.2 = ((f32[256,16,64]{0,2,1:T(8,128)}), f32[256,16,64]{0,2,1:T(8,128)S(1)}, u32[]{:S(2)}, u32[]{:S(2)}) async-start(f32[256,16,64]{0,2,1:T(8,128)} %bitcast.11), calls=%async_computation.2 | async-start | bytes 2097152 | tf_op jit(solution)/shard_map/all_to_all | solution.py:283
  161.7 35.4 %copy-start.1 = (f32[128,1024]{1,0:T(8,128)S(1)}, f32[128,1024]{1,0:T(8,128)}, u32[]{:S(2)}) copy-start(f32[128,1024]{1,0:T(8,128)} %get-tuple-element.39) | copy-start | bytes 1572868
  186.6 29.7 %all-to-all-start.1 = ((bf16[16,128,256]{2,1,0:T(8,128)(2,1)}), bf16[16,128,256]{2,1,0:T(8,128)(2,1)S(1)}, u32[]{:S(2)}, u32[]{:S(2)}) async-start(bf16[16,128,256]{2,1,0:T(8,128)(2,1)} %bitcast.23), calls=%async_computation.1 | async-start | bytes 2097152 | tf_op jit(solution)/shard_map/all_to_all | solution.py:279
  197.4 20.0 %collective-permute-start.1 = (f32[256,64]{0,1:T(8,128)S(1)}, f32[256,64]{0,1:T(8,128)S(1)}, u32[]{:S(2)}, u32[]{:S(2)}) collective-permute-start(f32[256,64]{0,1:T(8,128)S(1)} %reduce_sum.33), channel_id=1, source_target_pairs={{0,0},{1,16},{2,32},{3,48},{4,64},{5,80},{6,96},{7,112},{8,128},{9... | collective-permute-start | bytes 196616 | tf_op jit(solution)/shard_map/ppermute | solution.py:285

commit v18 on v17

--- a/solution.py
+++ b/solution.py
@@ -243,17 +243,16 @@
     ffa_cols = lax.all_to_all(
         feedforward_inner_activations, "dp", split_axis=1, concat_axis=0, tiled=True
     )
-    weight_block = lax.ppermute(contracting_matrix, ("dp", "zero"), transpose_route)
-
     digits = jnp.zeros((16, local_rows), jnp.bfloat16)
     digits = digits.at[0].set((matched_slot // 256).astype(jnp.bfloat16))
     digits = digits.at[1].set((matched_slot % 256).astype(jnp.bfloat16))
     both = jnp.concatenate([picture_embeds, summary_token_states], axis=1)
     both_g, digits_g = gather_dp(both, digits)
     both_g = both_g.reshape((-1, both.shape[1]))
-    ffa_cols, weight_block, both_g, digits_g = lax.optimization_barrier(
-        (ffa_cols, weight_block, both_g, digits_g)
-    )
+    ffa_cols, weight_in, both_g, digits_g = lax.optimization_barrier(
+        (ffa_cols, contracting_matrix, both_g, digits_g)
+    )
+    weight_block = lax.ppermute(weight_in, ("dp", "zero"), transpose_route)
     slot_g = (
         digits_g[:, 0, :].astype(jnp.int32) * 256 + digits_g[:, 1, :].astype(jnp.int32)
     ).reshape((-1,))

time: 219 us -> 242 us (1.11)
  waiting for transfers between devices: 33.1 us -> 69 us
  starting transfers between devices: 43.8 us -> 35.9 us
  Pallas kernels: 121 us -> 114 us
    ppermute x1, waiting for transfers between devices: 0.01 us -> 52.9 us  [shards(): weight_block = lax.ppermute(weight_in, ('dp', 'zero'), transpose_route)]
    all_to_all x1, waiting for transfers between devices: 20.4 us -> 0.01 us  [shards(): lax.all_to_all(group_sum, 'zero', split_axis=1, concat_axis=0, tiled=True)]
    pallas_call x1, Pallas kernels: 88.1 us -> 81.8 us  [gather_dp(): pl.pallas_call(functools.partial(gather_kernel, dp_size // 2, m), out_sha...]
    all_to_all x1, starting transfers between devices: 13.2 us -> 8.93 us  [shards(): lax.all_to_all(group_sum, 'zero', split_axis=1, concat_axis=0, tiled=True)]
    all_to_all x1, waiting for transfers between devices: 12.6 us -> 16.1 us  [shards(): lax.all_to_all(hidden_part, 'dp', split_axis=0, concat_axis=1, tiled=True)]
    ppermute x1, starting transfers between devices: 5.29 us -> 1.92 us  [shards(): down_grad = lax.ppermute(down_block, ('dp', 'zero'), transpose_route)]
    ppermute x1, starting transfers between devices: 7.19 us -> 3.93 us  [shards(): weight_block = lax.ppermute(weight_in, ('dp', 'zero'), transpose_route)]
    all_to_all x1, starting transfers between devices: 10.5 us -> 13.6 us  [shards(): lax.all_to_all(hidden_part, 'dp', split_axis=0, concat_axis=1, tiled=True)]
  transfers between devices with their start and end apart: 5 -> 5, of which waited for: 2 -> 2; matrix products, arithmetic and copies ran while one was open for 4% -> 3% of each run, Pallas kernels for 40% -> 34%
where the time goes in v18:
time: 242 us; the launch traced here: 240 us
  Pallas kernels  114 us (47%)
  waiting for transfers between devices  69 us (29%)
  starting transfers between devices  35.9 us (15%)
  matrix products  9.41 us (4%)
  local copies, waits for them, and re-layouts  5.37 us (2%)
  other arithmetic  3.49 us (1%)
    pallas_call x1, Pallas kernels, gather_dp(): pl.pallas_call(functools.partial(gather_kernel, dp_size // 2, m), out_sha...  81.8 us
    ppermute x1, waiting for transfers between devices, shards(): weight_block = lax.ppermute(weight_in, ('dp', 'zero'), transpose_route)  52.9 us
    pallas_call x1, Pallas kernels, contrast_group(): pl.pallas_call(contrast_kernel, grid=(group_rows // tc,), out_shape=(jax....  32.7 us
    all_to_all x1, waiting for transfers between devices, shards(): lax.all_to_all(hidden_part, 'dp', split_axis=0, concat_axis=1, tiled=True)  16.1 us
    all_to_all x1, starting transfers between devices, shards(): lax.all_to_all(hidden_part, 'dp', split_axis=0, concat_axis=1, tiled=True)  13.6 us
    all_to_all x1, starting transfers between devices, shards(): lax.all_to_all(group_sum, 'zero', split_axis=1, concat_axis=0, tiled=True)  8.93 us
    all_to_all x1, starting transfers between devices, shards(): lax.all_to_all(feedforward_inner_activations, 'dp', split_axis=1, concat_...  7.59 us
    dot_general x1, matrix products, shards(): lax.dot_general(ffa_cols, upstream_g, (((0,), (0,)), ((), ())), preferred...  4.96 us
  transfers between devices with their start and end apart: 5, of which 2 were waited for; matrix products, arithmetic and copies ran while one was open for 3% of the time, Pallas kernels for 34%

profile of v18, /device:TPU:57, one launch (start us, length us, event | category | flops | bytes accessed | tf_op | source)
XLA Modules:
  0.0 239.7 jit_solution(9977589851302198704)
XLA Ops:
  0.6 0.0 copy-start.4
  0.6 0.0 copy-start
  0.7 0.0 copy-start.2
  0.7 2.3 copy.16
  3.0 7.6 %all-to-all-start = ((bf16[128,16,256]{0,2,1:T(8,128)(2,1)}), bf16[128,16,256]{0,2,1:T(8,128)(2,1)S(1)}, u32[]{:S(2)}, u32[]{:S(2)}) async-start(bf16[128,16,256]{0,2,1:T(8,128)(2,1)} %bitcast.1), calls=%async_computation | async-start | bytes 2097152 | tf_op jit(solution)/shard_map/all_to_all | solution.py:243
  11.9 0.0 copy-done.4
  11.9 0.7 copy.18.own_slot_ref
  12.7 0.0 copy-done
  12.7 0.0 copy-done.2
  12.7 0.0 copy-start.3
  12.7 0.8 pad_maximum_fusion.refs_0_
  13.5 0.0 copy-done.3
  13.5 81.8 %shard_map.103 = (bf16[16,128,2048]{2,1,0:T(8,128)(2,1)}, bf16[16,16,128]{2,1,0:T(8,128)(2,1)}) custom-call(bf16[128,2048]{1,0:T(8,128)(2,1)} %pad_maximum_fusion.refs_0_, bf16[16,128]{1,0:T(8,128)(2,1)} %copy-done.3), custom_call_target="tpu_custom_call" | custom-call | tf_op jit(solution)/shard_map/pallas_call | solution.py:79
  95.3 0.0 all-to-all-done
  95.3 0.5 copy.17
  95.9 1.5 add_bitcast_fusion.slot_ref
  97.3 32.7 %shard_map.104 = (bf16[2048,1024]{1,0:T(8,128)(2,1)}, f32[128,1024]{1,0:T(8,128)}) custom-call(f32[1]{0:T(128)S(6)} %copy.25.scale_ref, f32[1]{0:T(128)S(6)} %copy.26.shift_ref, s32[128,1]{1,0:T(8,128)} %copy.18.own_slot_ref, s32[1,2048]{1,0:T(1,128)} %add_bitcast_fusion.slot_ref, bf16[2048,2048]{1,0:T(8,128)(2,1)} %bitcast.27, bf16[2048,2048]{1,0:T(8,128)(2,1)} %bitcast.28, ...), custom_call_target="tpu_custom_call" | custom-call | flops 18253611008 | bytes 13107200 | tf_op jit(solution)/shard_map/pallas_call | solution.py:169
  130.0 0.0 copy-start.5
  130.0 5.0 %fusion.4 = f32[256,1024]{0,1:T(8,128)} fusion(bf16[2048,256]{1,0:T(8,128)(2,1)S(1)} %bitcast.25, bf16[2048,1024]{1,0:T(8,128)(2,1)} %get-tuple-element.40), kind=kOutput, calls=%fused_computation.19 | convolution fusion | flops 1073741824 | bytes 6291456 | tf_op jit(solution)/shard_map/dot_general | solution.py:279
  135.0 8.9 %all-to-all-start.2 = ((f32[256,16,64]{0,2,1:T(8,128)}), f32[256,16,64]{0,2,1:T(8,128)S(1)}, u32[]{:S(2)}, u32[]{:S(2)}) async-start(f32[256,16,64]{0,2,1:T(8,128)} %bitcast.11), calls=%async_computation.2 | async-start | bytes 2097152 | tf_op jit(solution)/shard_map/all_to_all | solution.py:282
  143.9 0.0 copy-done.5
  143.9 0.0 copy-start.1
  143.9 3.9 %collective-permute-start = (bf16[256,1024]{1,0:T(8,128)(2,1)S(1)}, bf16[256,1024]{1,0:T(8,128)(2,1)S(1)}, u32[]{:S(2)}, u32[]{:S(2)}) collective-permute-start(bf16[256,1024]{1,0:T(8,128)(2,1)S(1)} %copy-done.5), channel_id=1, source_target_pairs={{0,0},{1,16},{2,32},{3,48},{4,64},{5,80},{6,96},{7,112},{8,128},{9... | collective-permute-start | bytes 1572872 | tf_op jit(solution)/shard_map/ppermute | solution.py:255
  147.9 52.9 %collective-permute-done = bf16[256,1024]{1,0:T(8,128)(2,1)S(1)} collective-permute-done((bf16[256,1024]{1,0:T(8,128)(2,1)S(1)}, bf16[256,1024]{1,0:T(8,128)(2,1)S(1)}, u32[]{:S(2)}, u32[]{:S(2)}) %collective-permute-start) | collective-permute-done | bytes 524320 | tf_op jit(solution)/shard_map/ppermute | solution.py:255
  200.7 4.5 %convolution_convert_fusion = bf16[2048,256]{1,0:T(8,128)(2,1)} fusion(bf16[2048,1024]{1,0:T(8,128)(2,1)} %get-tuple-element.40, bf16[256,1024]{1,0:T(8,128)(2,1)S(1)} %collective-permute-done), kind=kOutput, calls=%fused_computation | convolution fusion | flops 1074266112 | bytes 5767168 | tf_op jit(solution)/shard_map/dot_general | solution.py:272
  205.2 0.0 all-to-all-done.2
  205.2 13.6 %all-to-all-start.1 = ((bf16[16,128,256]{2,1,0:T(8,128)(2,1)}), bf16[16,128,256]{2,1,0:T(8,128)(2,1)S(1)}, u32[]{:S(2)}, u32[]{:S(2)}) async-start(bf16[16,128,256]{2,1,0:T(8,128)(2,1)} %bitcast.23), calls=%async_computation.1 | async-start | bytes 2097152 | tf_op jit(solution)/shard_map/all_to_all | solution.py:278
  218.8 0.0 copy-done.1
  218.8 0.2 fusion
  219.0 0.1 reduce_sum.33
  219.0 1.9 collective-permute-start.1
  221.0 0.9 add_add_fusion
  221.9 16.1 %all-to-all-done.1 = bf16[16,128,256]{2,1,0:T(8,128)(2,1)S(1)} async-done(((bf16[16,128,256]{2,1,0:T(8,128)(2,1)}), bf16[16,128,256]{2,1,0:T(8,128)(2,1)S(1)}, u32[]{:S(2)}, u32[]{:S(2)}) %all-to-all-start.1) | async-done | bytes 1048608 | tf_op jit(solution)/shard_map/all_to_all | solution.py:278
  238.0 1.1 copy.22
  239.1 0.0 collective-permute-done.1
  239.1 0.6 copy.27
  (4 shorter events, 0.1 us)
Async XLA Ops:
  0.6 11.2 %copy-start.4 = (s32[128]{0:T(128)S(1)}, s32[128]{0:T(128)}, u32[]{:S(2)}) copy-start(s32[128]{0:T(128)} %param.13) | copy-start | bytes 1540
  0.6 12.0 %copy-start = (bf16[128,1024]{1,0:T(8,128)(2,1)S(1)}, bf16[128,1024]{1,0:T(8,128)(2,1)}, u32[]{:S(2)}) copy-start(bf16[128,1024]{1,0:T(8,128)(2,1)} %param.12) | copy-start | bytes 786436
  0.7 12.0 %copy-start.2 = (bf16[128,1024]{1,0:T(8,128)(2,1)S(1)}, bf16[128,1024]{1,0:T(8,128)(2,1)}, u32[]{:S(2)}) copy-start(bf16[128,1024]{1,0:T(8,128)(2,1)} %param.14) | copy-start | bytes 786436
  3.0 92.3 %all-to-all-start = ((bf16[128,16,256]{0,2,1:T(8,128)(2,1)}), bf16[128,16,256]{0,2,1:T(8,128)(2,1)S(1)}, u32[]{:S(2)}, u32[]{:S(2)}) async-start(bf16[128,16,256]{0,2,1:T(8,128)(2,1)} %bitcast.1), calls=%async_computation | async-start | bytes 2097152 | tf_op jit(solution)/shard_map/all_to_all | solution.py:243
  12.7 0.8 copy-start.3
  130.0 13.9 %copy-start.5 = (bf16[256,1024]{1,0:T(8,128)(2,1)S(1)}, bf16[256,1024]{1,0:T(8,128)(2,1)}, u32[]{:S(2)}) copy-start(bf16[256,1024]{1,0:T(8,128)(2,1)} %param.17) | copy-start | bytes 1572868
  135.0 70.2 %all-to-all-start.2 = ((f32[256,16,64]{0,2,1:T(8,128)}), f32[256,16,64]{0,2,1:T(8,128)S(1)}, u32[]{:S(2)}, u32[]{:S(2)}) async-start(f32[256,16,64]{0,2,1:T(8,128)} %bitcast.11), calls=%async_computation.2 | async-start | bytes 2097152 | tf_op jit(solution)/shard_map/all_to_all | solution.py:282
  143.9 74.9 %copy-start.1 = (f32[128,1024]{1,0:T(8,128)S(1)}, f32[128,1024]{1,0:T(8,128)}, u32[]{:S(2)}) copy-start(f32[128,1024]{1,0:T(8,128)} %get-tuple-element.39) | copy-start | bytes 1572868
  143.9 56.8 %collective-permute-start = (bf16[256,1024]{1,0:T(8,128)(2,1)S(1)}, bf16[256,1024]{1,0:T(8,128)(2,1)S(1)}, u32[]{:S(2)}, u32[]{:S(2)}) collective-permute-start(bf16[256,1024]{1,0:T(8,128)(2,1)S(1)} %copy-done.5), channel_id=1, source_target_pairs={{0,0},{1,16},{2,32},{3,48},{4,64},{5,80},{6,96},{7,112},{8,128},{9... | collective-permute-start | bytes 1572872 | tf_op jit(solution)/shard_map/ppermute | solution.py:255
  205.2 32.8 %all-to-all-start.1 = ((bf16[16,128,256]{2,1,0:T(8,128)(2,1)}), bf16[16,128,256]{2,1,0:T(8,128)(2,1)S(1)}, u32[]{:S(2)}, u32[]{:S(2)}) async-start(bf16[16,128,256]{2,1,0:T(8,128)(2,1)} %bitcast.23), calls=%async_computation.1 | async-start | bytes 2097152 | tf_op jit(solution)/shard_map/all_to_all | solution.py:278
  219.0 20.0 %collective-permute-start.1 = (f32[256,64]{0,1:T(8,128)S(1)}, f32[256,64]{0,1:T(8,128)S(1)}, u32[]{:S(2)}, u32[]{:S(2)}) collective-permute-start(f32[256,64]{0,1:T(8,128)S(1)} %reduce_sum.33), channel_id=1, source_target_pairs={{0,0},{1,16},{2,32},{3,48},{4,64},{5,80},{6,96},{7,112},{8,128},{9... | collective-permute-start | bytes 196616 | tf_op jit(solution)/shard_map/ppermute | solution.py:284
